TPU v7x, 32 devices: a whole 2x2x4 slice. The times are simulated.
32 devices in a mesh: dp: 2 (over x), ctx: 4 (over z), tp: 4 (over y, core).
Axes of the slice: x: 2, y: 2, z: 4, core: 2. Of those that a mesh axis runs over, the one named last changes fastest.
Arguments:
- inputs: bfloat16 [16, 1024, 512], P('dp', 'ctx'), may hold values from -6 to 6
- memory: bfloat16 [16, 1024, 512], P('dp', 'ctx'), may hold values from -6 to 6
- cotangent: bfloat16 [16, 1024, 512], P('dp', 'ctx'), may hold values from -6 to 6
- wq_self: bfloat16 [512, 512], P(('dp', 'ctx'), 'tp'), may hold values from -0.25 to 0.25
- wk_self: bfloat16 [512, 512], P(('dp', 'ctx'), 'tp'), may hold values from -0.25 to 0.25
- wv_self: bfloat16 [512, 512], P(('dp', 'ctx'), 'tp'), may hold values from -0.25 to 0.25
- wo_self: bfloat16 [512, 512], P('tp', ('dp', 'ctx')), may hold values from -1 to 1
- wq_cross: bfloat16 [512, 512], P(('dp', 'ctx'), 'tp'), may hold values from -0.25 to 0.25
- wk_cross: bfloat16 [512, 512], P(('dp', 'ctx'), 'tp'), may hold values from -0.25 to 0.25
- wv_cross: bfloat16 [512, 512], P(('dp', 'ctx'), 'tp'), may hold values from -0.25 to 0.25
- wo_cross: bfloat16 [512, 512], P('tp', ('dp', 'ctx')), may hold values from -1 to 1
- w_in: bfloat16 [512, 2048], P(('dp', 'ctx'), 'tp'), may hold values from -0.25 to 0.25
- w_out: bfloat16 [2048, 512], P('tp', ('dp', 'ctx')), may hold values from -0.125 to 0.125
- gains: bfloat16 [3, 512], P(None, ('dp', 'ctx', 'tp')), may hold values from 0.25 to 1.75
- shifts: bfloat16 [10, 512], P(None, ('dp', 'ctx', 'tp')), may hold values from -1 to 1
- ffn_bias: bfloat16 [2048], P(('dp', 'ctx', 'tp')), may hold values from -1 to 1
Outputs:
- output: bfloat16 [16, 1024, 512], P('dp', 'ctx')
- grad_inputs: float32 [16, 1024, 512], P('dp', 'ctx')
- grad_memory: float32 [16, 1024, 512], P('dp', 'ctx')
- grad_wq_self: float32 [512, 512], P(('dp', 'ctx'), 'tp')
- grad_wk_self: float32 [512, 512], P(('dp', 'ctx'), 'tp')
- grad_wv_self: float32 [512, 512], P(('dp', 'ctx'), 'tp')
- grad_wo_self: float32 [512, 512], P('tp', ('dp', 'ctx'))
- grad_wq_cross: float32 [512, 512], P(('dp', 'ctx'), 'tp')
- grad_wk_cross: float32 [512, 512], P(('dp', 'ctx'), 'tp')
- grad_wv_cross: float32 [512, 512], P(('dp', 'ctx'), 'tp')
- grad_wo_cross: float32 [512, 512], P('tp', ('dp', 'ctx'))
- grad_w_in: float32 [512, 2048], P(('dp', 'ctx'), 'tp')
- grad_w_out: float32 [2048, 512], P('tp', ('dp', 'ctx'))
- grad_gains: float32 [3, 512], P(None, ('dp', 'ctx', 'tp'))
- grad_shifts: float32 [10, 512], P(None, ('dp', 'ctx', 'tp'))
- grad_ffn_bias: float32 [2048], P(('dp', 'ctx', 'tp'))
All inputs are finite; a program needn't handle non-finite values.
Results may differ from a plain program's by a relative error of at most 0.022.
Values may be sent and summed in bfloat16 or wider, within the bound.
No kernel may reach another device: no remote copies, remote signals or barrier semaphores. Data moves between devices by JAX's collectives and lax.ppermute only.
A program may use at most 128 MiB of HBM per device.

v0:
```python
import jax
import jax.numpy as jnp
from jax import lax
from jax.sharding import PartitionSpec as P

HD = 64


EPS = 1e-05


def as_sent(array):

    def short(part):
        return part.astype(jnp.bfloat16) if part.dtype == jnp.float32 else part

    return jax.tree.map(short, array)


def cut_along(array, dim, devices):
    dims = array.shape
    parts = array.reshape(*dims[:dim], devices, dims[dim] // devices, *dims[dim + 1 :])
    return jnp.moveaxis(parts, dim, 0)


def summed_on_arrival(array, axis, dim):
    devices = lax.axis_size(axis)
    parts = lax.all_to_all(cut_along(array, dim, devices), axis, 0, 0, tiled=True)
    return jnp.sum(parts.astype(jnp.float32), axis=0)


def side_by_side(arrays, axis, dim, along):
    both = jnp.concatenate(arrays, axis=along)
    filled, at, outs = (summed_on_arrival(both, axis, dim), 0, [])
    for a in arrays:
        outs.append(lax.slice_in_dim(filled, at, at + a.shape[along], axis=along))
        at += a.shape[along]
    return tuple(outs)


def layer_norm(values, weight, offset):
    average = jnp.mean(values, axis=-1, keepdims=True)
    centered = values - average
    variance = jnp.mean(centered * centered, axis=-1, keepdims=True)
    return centered * lax.rsqrt(variance + EPS) * weight + offset


def matmul(left, right):
    return jnp.dot(left, right, preferred_element_type=jnp.float32)


def matmul_left(left, right):
    return lax.dot_general(
        left, right, (((0,), (0,)), ((), ())), preferred_element_type=jnp.float32
    )


def matmul_right(left, right):
    return lax.dot_general(
        left, right, (((1,), (1,)), ((), ())), preferred_element_type=jnp.float32
    )


def to_low(values):
    return values.astype(jnp.bfloat16)


def head_sum(values):
    return lax.psum(values, "tp")


def head_grad(values):
    return jax.tree.map(lambda part: part.astype(jnp.float32), lax.psum(as_sent(values), "tp"))


def attend_forward(queries, key_rows, values, allowed):
    scores = jnp.einsum(
        "qhe,khe->hqk", queries, key_rows, preferred_element_type=jnp.float32
    ) * HD ** (-0.5)
    scores = jnp.where(allowed[None], scores, -1e30)
    highest = jnp.max(scores, axis=-1, keepdims=True)
    exp_scores = jnp.exp(scores - highest)
    totals = jnp.sum(exp_scores, axis=-1, keepdims=True)
    soft_weights = exp_scores / totals
    mixed_heads = jnp.einsum(
        "hqk,khe->qhe", to_low(soft_weights), values, preferred_element_type=jnp.float32
    )
    return (to_low(mixed_heads), (highest + jnp.log(totals))[..., 0])


def attend_backward(queries, key_rows, values, allowed, grad_mixed, log_totals):
    scores = jnp.einsum(
        "qhe,khe->hqk", queries, key_rows, preferred_element_type=jnp.float32
    ) * HD ** (-0.5)
    scores = jnp.where(allowed[None], scores, -1e30)
    soft_weights = jnp.exp(scores - log_totals[..., None])
    grad_soft = jnp.einsum("qhe,khe->hqk", grad_mixed, values, preferred_element_type=jnp.float32)
    row_inner = jnp.sum(grad_soft * soft_weights, axis=-1, keepdims=True)
    grad_scores = to_low(soft_weights * (grad_soft - row_inner) * HD ** (-0.5))
    grad_queries = to_low(
        jnp.einsum("hqk,khe->qhe", grad_scores, key_rows, preferred_element_type=jnp.float32)
    )
    grad_keys = jnp.einsum("hqk,qhe->khe", grad_scores, queries, preferred_element_type=jnp.float32)
    grad_values = jnp.einsum(
        "hqk,qhe->khe", to_low(soft_weights), grad_mixed, preferred_element_type=jnp.float32
    )
    return (grad_queries, grad_keys, grad_values)


def shards(
    inputs,
    memory,
    cotangent,
    wq_self,
    wk_self,
    wv_self,
    wo_self,
    wq_cross,
    wk_cross,
    wv_cross,
    wo_cross,
    w_in,
    w_out,
    gains,
    shifts,
    ffn_bias,
):
    seqs_here, block_rows, model_width = inputs.shape
    mem_rows = memory.shape[1]
    local_width = wq_self.shape[1]
    hidden_here = w_in.shape[1]
    head_count = local_width // HD
    tensor_rank = lax.axis_index("tp")
    context_rank = lax.axis_index("ctx")
    gathered = (
        lax.all_gather(wq_self, ("dp", "ctx"), axis=0, tiled=True),
        lax.all_gather(wk_self, ("dp", "ctx"), axis=0, tiled=True),
        lax.all_gather(wv_self, ("dp", "ctx"), axis=0, tiled=True),
        lax.all_gather(wq_cross, ("dp", "ctx"), axis=0, tiled=True),
        lax.all_gather(wk_cross, ("dp", "ctx"), axis=0, tiled=True),
        lax.all_gather(wv_cross, ("dp", "ctx"), axis=0, tiled=True),
        lax.all_gather(w_in, ("dp", "ctx"), axis=0, tiled=True),
        lax.all_gather(wo_self, ("dp", "ctx"), axis=1, tiled=True),
        lax.all_gather(wo_cross, ("dp", "ctx"), axis=1, tiled=True),
        lax.all_gather(w_out, ("dp", "ctx"), axis=1, tiled=True),
    )
    full_qs, full_ks, full_vs, full_qc, full_kc, full_vc, full_in, full_os, full_oc, full_out = (
        gathered
    )
    all_gains, all_shifts, all_bias = (
        lax.all_gather(gains, ("dp", "ctx", "tp"), axis=1, tiled=True),
        lax.all_gather(shifts, ("dp", "ctx", "tp"), axis=1, tiled=True),
        lax.all_gather(ffn_bias, ("dp", "ctx", "tp"), axis=0, tiled=True),
    )
    all_gains = all_gains.astype(jnp.float32)
    all_shifts = all_shifts.astype(jnp.float32)
    ffn_here = lax.dynamic_slice_in_dim(
        all_bias.astype(jnp.float32), tensor_rank * hidden_here, hidden_here, 0
    )

    def own_heads(vector):
        return lax.dynamic_slice_in_dim(vector, tensor_rank * local_width, local_width, 0)

    def by_heads(array, rows):
        return array.reshape(seqs_here, rows, head_count, HD)

    flat_x = inputs.reshape(-1, model_width)
    flat_m = memory.reshape(-1, model_width)
    queries = to_low(matmul(flat_x, full_qs) + own_heads(all_shifts[0]))
    key_rows = to_low(matmul(flat_x, full_ks))
    value_rows = to_low(matmul(flat_x, full_vs) + own_heads(all_shifts[1]))
    mem_keys = to_low(matmul(flat_m, full_kc))
    mem_values = to_low(matmul(flat_m, full_vc) + own_heads(all_shifts[5]))
    seen_keys, seen_values, seen_mkeys, seen_mvalues = (
        lax.all_gather(
            key_rows.reshape(seqs_here, block_rows, local_width), "ctx", axis=1, tiled=True
        ),
        lax.all_gather(
            value_rows.reshape(seqs_here, block_rows, local_width), "ctx", axis=1, tiled=True
        ),
        lax.all_gather(
            mem_keys.reshape(seqs_here, mem_rows, local_width), "ctx", axis=1, tiled=True
        ),
        lax.all_gather(
            mem_values.reshape(seqs_here, mem_rows, local_width), "ctx", axis=1, tiled=True
        ),
    )
    total_keys = seen_keys.shape[1]
    total_mem = seen_mkeys.shape[1]
    key_ok = jnp.arange(total_keys) // block_rows <= context_rank
    causal = jnp.broadcast_to(key_ok[None, :], (block_rows, total_keys))
    open_mask = jnp.ones((block_rows, total_mem), jnp.bool_)
    self_parts = (
        by_heads(queries, block_rows),
        by_heads(seen_keys, total_keys),
        by_heads(seen_values, total_keys),
    )
    self_mixed, self_logs = lax.map(lambda t: attend_forward(t[0], t[1], t[2], causal), self_parts)
    self_flat = self_mixed.reshape(-1, local_width)
    z_first = flat_x.astype(jnp.float32) + head_sum(matmul(self_flat, full_os)) + all_shifts[2]
    normed_one = layer_norm(z_first, all_gains[0], all_shifts[3])
    normed_low = to_low(normed_one)
    cross_q = to_low(matmul(normed_low, full_qc) + own_heads(all_shifts[4]))
    cross_parts = (
        by_heads(cross_q, block_rows),
        by_heads(seen_mkeys, total_mem),
        by_heads(seen_mvalues, total_mem),
    )
    cross_mixed, cross_logs = lax.map(
        lambda t: attend_forward(t[0], t[1], t[2], open_mask), cross_parts
    )
    cross_flat = cross_mixed.reshape(-1, local_width)
    z_second = normed_one + head_sum(matmul(cross_flat, full_oc)) + all_shifts[6]
    normed_two = layer_norm(z_second, all_gains[1], all_shifts[7])
    hidden_in = to_low(normed_two)
    pre_act = matmul(hidden_in, full_in) + ffn_here
    activated = to_low(jax.nn.gelu(pre_act))
    z_third = normed_two + head_sum(matmul(activated, full_out)) + all_shifts[8]
    result = layer_norm(z_third, all_gains[2], all_shifts[9])
    held = lax.optimization_barrier(
        (
            (
                wq_self,
                wk_self,
                wv_self,
                wq_cross,
                wk_cross,
                wv_cross,
                w_in,
                wo_self,
                wo_cross,
                w_out,
            ),
            result,
        )
    )[0]
    regathered = (
        lax.all_gather(held[0], ("dp", "ctx"), axis=0, tiled=True),
        lax.all_gather(held[1], ("dp", "ctx"), axis=0, tiled=True),
        lax.all_gather(held[2], ("dp", "ctx"), axis=0, tiled=True),
        lax.all_gather(held[3], ("dp", "ctx"), axis=0, tiled=True),
        lax.all_gather(held[4], ("dp", "ctx"), axis=0, tiled=True),
        lax.all_gather(held[5], ("dp", "ctx"), axis=0, tiled=True),
        lax.all_gather(held[6], ("dp", "ctx"), axis=0, tiled=True),
        lax.all_gather(held[7], ("dp", "ctx"), axis=1, tiled=True),
        lax.all_gather(held[8], ("dp", "ctx"), axis=1, tiled=True),
        lax.all_gather(held[9], ("dp", "ctx"), axis=1, tiled=True),
    )
    full_qs, full_ks, full_vs, full_qc, full_kc, full_vc, full_in, full_os, full_oc, full_out = (
        regathered
    )
    grad_top = cotangent.reshape(-1, model_width).astype(jnp.float32)
    dz_third, gain_grad_three, shift_grad_nine = jax.vjp(
        layer_norm, z_third, all_gains[2], all_shifts[9]
    )[1](grad_top)
    grad_branch = to_low(dz_third)
    grad_full_out = matmul_left(activated, grad_branch)
    grad_act = to_low(matmul_right(grad_branch, full_out))
    grad_pre = to_low(jax.vjp(jax.nn.gelu, pre_act)[1](grad_act.astype(jnp.float32))[0])
    grad_full_in = matmul_left(hidden_in, grad_pre)
    grad_normed_two = dz_third + head_grad(matmul_right(grad_pre, full_in))
    dz_second, gain_grad_two, shift_grad_seven = jax.vjp(
        layer_norm, z_second, all_gains[1], all_shifts[7]
    )[1](grad_normed_two)
    grad_cross_branch = to_low(dz_second)
    grad_full_oc = matmul_left(cross_flat, grad_cross_branch)
    grad_cross_mixed = to_low(matmul_right(grad_cross_branch, full_oc))
    cross_back = (
        cross_parts[0],
        cross_parts[1],
        cross_parts[2],
        by_heads(grad_cross_mixed, block_rows),
        cross_logs,
    )
    grad_cq, grad_mk_part, grad_mv_part = lax.map(
        lambda t: attend_backward(t[0], t[1], t[2], open_mask, t[3], t[4]), cross_back
    )
    grad_cq = grad_cq.reshape(-1, local_width)
    grad_full_qc = matmul_left(normed_low, grad_cq)
    grad_normed_one = dz_second + head_grad(matmul_right(grad_cq, full_qc))
    dz_first, gain_grad_one, shift_grad_three = jax.vjp(
        layer_norm, z_first, all_gains[0], all_shifts[3]
    )[1](grad_normed_one)
    grad_self_branch = to_low(dz_first)
    grad_full_os = matmul_left(self_flat, grad_self_branch)
    grad_self_mixed = to_low(matmul_right(grad_self_branch, full_os))
    self_back = (
        self_parts[0],
        self_parts[1],
        self_parts[2],
        by_heads(grad_self_mixed, block_rows),
        self_logs,
    )
    grad_q, grad_k_part, grad_v_part = lax.map(
        lambda t: attend_backward(t[0], t[1], t[2], causal, t[3], t[4]), self_back
    )
    sum_k, sum_v, sum_mk, sum_mv = (
        lax.psum_scatter(
            grad_k_part.reshape(seqs_here, total_keys, local_width).astype(jnp.bfloat16),
            "ctx",
            scatter_dimension=1,
            tiled=True,
        ).astype(jnp.float32),
        lax.psum_scatter(
            grad_v_part.reshape(seqs_here, total_keys, local_width).astype(jnp.bfloat16),
            "ctx",
            scatter_dimension=1,
            tiled=True,
        ).astype(jnp.float32),
        lax.psum_scatter(
            grad_mk_part.reshape(seqs_here, total_mem, local_width).astype(jnp.bfloat16),
            "ctx",
            scatter_dimension=1,
            tiled=True,
        ).astype(jnp.float32),
        lax.psum_scatter(
            grad_mv_part.reshape(seqs_here, total_mem, local_width).astype(jnp.bfloat16),
            "ctx",
            scatter_dimension=1,
            tiled=True,
        ).astype(jnp.float32),
    )
    grad_k = to_low(sum_k.reshape(-1, local_width))
    grad_v = to_low(sum_v.reshape(-1, local_width))
    grad_mk = to_low(sum_mk.reshape(-1, local_width))
    grad_mv = to_low(sum_mv.reshape(-1, local_width))
    grad_q = grad_q.reshape(-1, local_width)
    grad_full_qs = matmul_left(flat_x, grad_q)
    grad_full_ks = matmul_left(flat_x, grad_k)
    grad_full_vs = matmul_left(flat_x, grad_v)
    grad_full_kc = matmul_left(flat_m, grad_mk)
    grad_full_vc = matmul_left(flat_m, grad_mv)
    input_part = (
        matmul_right(grad_q, full_qs)
        + matmul_right(grad_k, full_ks)
        + matmul_right(grad_v, full_vs)
    )
    memory_part = matmul_right(grad_mk, full_kc) + matmul_right(grad_mv, full_vc)
    input_total, memory_total = head_grad((input_part, memory_part))
    grad_x = dz_first + input_total
    owned = jnp.arange(model_width) // local_width == tensor_rank

    def keep_owned(vector):
        return jnp.where(owned, vector, jnp.zeros_like(vector))

    def widen_heads(vector):
        return lax.dynamic_update_slice_in_dim(
            jnp.zeros((model_width,), jnp.float32), vector, tensor_rank * local_width, 0
        )

    def row_total(array):
        return jnp.sum(array.astype(jnp.float32), axis=0)

    gain_rows = jnp.stack(
        [keep_owned(gain_grad_one), keep_owned(gain_grad_two), keep_owned(gain_grad_three)]
    )
    shift_rows = jnp.stack(
        [
            widen_heads(row_total(grad_q)),
            widen_heads(row_total(grad_v)),
            keep_owned(row_total(dz_first)),
            keep_owned(shift_grad_three),
            widen_heads(row_total(grad_cq)),
            widen_heads(row_total(grad_mv)),
            keep_owned(row_total(dz_second)),
            keep_owned(shift_grad_seven),
            keep_owned(row_total(dz_third)),
            keep_owned(shift_grad_nine),
        ]
    )
    ffn_total = jnp.zeros((hidden_here * lax.axis_size("tp"),), jnp.float32)
    ffn_total = lax.dynamic_update_slice_in_dim(
        ffn_total, row_total(grad_pre), tensor_rank * hidden_here, 0
    )
    weight_parts = (
        *side_by_side(
            (
                grad_full_qs.astype(jnp.bfloat16),
                grad_full_ks.astype(jnp.bfloat16),
                grad_full_vs.astype(jnp.bfloat16),
                grad_full_qc.astype(jnp.bfloat16),
                grad_full_kc.astype(jnp.bfloat16),
                grad_full_vc.astype(jnp.bfloat16),
                grad_full_in.astype(jnp.bfloat16),
            ),
            ("dp", "ctx"),
            0,
            1,
        ),
        *side_by_side(
            (
                grad_full_os.astype(jnp.bfloat16),
                grad_full_oc.astype(jnp.bfloat16),
                grad_full_out.astype(jnp.bfloat16),
            ),
            ("dp", "ctx"),
            1,
            0,
        ),
    )
    gain_out, shift_out, ffn_out = (
        lax.psum_scatter(gain_rows, ("dp", "ctx", "tp"), scatter_dimension=1, tiled=True),
        lax.psum_scatter(shift_rows, ("dp", "ctx", "tp"), scatter_dimension=1, tiled=True),
        lax.psum_scatter(ffn_total, ("dp", "ctx", "tp"), scatter_dimension=0, tiled=True),
    )
    return (
        to_low(result).reshape(seqs_here, block_rows, model_width),
        grad_x.reshape(seqs_here, block_rows, model_width),
        memory_total.reshape(seqs_here, mem_rows, model_width),
        weight_parts[0],
        weight_parts[1],
        weight_parts[2],
        weight_parts[7],
        weight_parts[3],
        weight_parts[4],
        weight_parts[5],
        weight_parts[8],
        weight_parts[6],
        weight_parts[9],
        gain_out,
        shift_out,
        ffn_out,
    )


def solution(mesh):
    return jax.shard_map(
        shards,
        mesh=mesh,
        in_specs=(
            P("dp", "ctx", None),
            P("dp", "ctx", None),
            P("dp", "ctx", None),
            P(("dp", "ctx"), "tp"),
            P(("dp", "ctx"), "tp"),
            P(("dp", "ctx"), "tp"),
            P("tp", ("dp", "ctx")),
            P(("dp", "ctx"), "tp"),
            P(("dp", "ctx"), "tp"),
            P(("dp", "ctx"), "tp"),
            P("tp", ("dp", "ctx")),
            P(("dp", "ctx"), "tp"),
            P("tp", ("dp", "ctx")),
            P(None, ("dp", "ctx", "tp")),
            P(None, ("dp", "ctx", "tp")),
            P(("dp", "ctx", "tp")),
        ),
        out_specs=(
            P("dp", "ctx", None),
            P("dp", "ctx", None),
            P("dp", "ctx", None),
            P(("dp", "ctx"), "tp"),
            P(("dp", "ctx"), "tp"),
            P(("dp", "ctx"), "tp"),
            P("tp", ("dp", "ctx")),
            P(("dp", "ctx"), "tp"),
            P(("dp", "ctx"), "tp"),
            P(("dp", "ctx"), "tp"),
            P("tp", ("dp", "ctx")),
            P(("dp", "ctx"), "tp"),
            P("tp", ("dp", "ctx")),
            P(None, ("dp", "ctx", "tp")),
            P(None, ("dp", "ctx", "tp")),
            P(("dp", "ctx", "tp")),
        ),
        check_vma=False,
    )
```

profile of v0, /device:TPU:0, one launch (start us, length us, event | category | flops | bytes accessed | tf_op | source)
XLA Modules:
  0.0 1859.8 jit_solution(18212366963563769408)
XLA Ops:
  8.2 43.6 %all_gather.82 = bf16[10,512]{0,1:T(8,128)(2,1)S(1)} all-gather(bf16[10,16]{0,1:T(8,128)(2,1)S(1)} %copy.148), channel_id=1, replica_groups=mesh['dp'=2,'ctx'=4,'tp'=4] {'dp','ctx','tp'}, dimensions={1}, use_global_device_ids=true | all-gather | bytes 10560 | tf_op jit(solution)/shard_map/all_gather | solution.py:152
  51.9 30.7 %all_gather.81 = bf16[512,128]{1,0:T(8,128)(2,1)S(1)} all-gather(bf16[64,128]{1,0:T(8,128)(2,1)S(1)} %copy-done.54), channel_id=1, replica_groups=mesh['dp'=2,'ctx'=4,'tp'=4] {'dp','ctx'}, dimensions={0}, use_global_device_ids=true | all-gather | bytes 147456 | tf_op jit(solution)/shard_map/all_gather | solution.py:138
  85.9 31.5 %all_gather.85 = bf16[512,128]{1,0:T(8,128)(2,1)S(1)} all-gather(bf16[64,128]{1,0:T(8,128)(2,1)S(1)} %copy-done.50), channel_id=1, replica_groups=mesh['dp'=2,'ctx'=4,'tp'=4] {'dp','ctx'}, dimensions={0}, use_global_device_ids=true | all-gather | bytes 147456 | tf_op jit(solution)/shard_map/all_gather | solution.py:137
  120.7 31.2 %all_gather.89 = bf16[512,128]{1,0:T(8,128)(2,1)S(1)} all-gather(bf16[64,128]{1,0:T(8,128)(2,1)S(1)} %copy-done.48), channel_id=1, replica_groups=mesh['dp'=2,'ctx'=4,'tp'=4] {'dp','ctx'}, dimensions={0}, use_global_device_ids=true | all-gather | bytes 147456 | tf_op jit(solution)/shard_map/all_gather | solution.py:141
  153.5 31.4 %all_gather.92 = bf16[512,128]{1,0:T(8,128)(2,1)S(1)} all-gather(bf16[64,128]{1,0:T(8,128)(2,1)S(1)} %copy-done.46), channel_id=1, replica_groups=mesh['dp'=2,'ctx'=4,'tp'=4] {'dp','ctx'}, dimensions={0}, use_global_device_ids=true | all-gather | bytes 147456 | tf_op jit(solution)/shard_map/all_gather | solution.py:140
  186.6 31.6 %all_gather.84 = bf16[512,128]{1,0:T(8,128)(2,1)S(1)} all-gather(bf16[64,128]{1,0:T(8,128)(2,1)S(1)} %copy-done.52), channel_id=1, replica_groups=mesh['dp'=2,'ctx'=4,'tp'=4] {'dp','ctx'}, dimensions={0}, use_global_device_ids=true | all-gather | bytes 147456 | tf_op jit(solution)/shard_map/all_gather | solution.py:136
  225.6 31.6 %all_gather.87 = bf16[128,512]{0,1:T(8,128)(2,1)S(1)} all-gather(bf16[128,64]{0,1:T(8,128)(2,1)} %param.30), channel_id=1, replica_groups=mesh['dp'=2,'ctx'=4,'tp'=4] {'dp','ctx'}, dimensions={1}, use_global_device_ids=true | all-gather | bytes 147456 | tf_op jit(solution)/shard_map/all_gather | solution.py:143
  265.2 30.5 %while.56 = (s32[]{:T(128)}, bf16[8,256,2,64]{1,3,2,0:T(8,128)(2,1)S(1)}, f32[8,2,256]{2,1,0:T(2,128)S(1)}, bf16[8,1024,2,64]{1,3,2,0:T(8,128)(2,1)}, bf16[8,256...) while((s32[]{:T(128)}, ...), condition=%wide.region_3.4_spmd.clone, body=%wide.region_0.3_spmd.clone.sunk | while | flops 140541440 | bytes 6968409 | solution.py:198
  299.6 36.4 %all-gather = bf16[32,16,3]{1,2,0:T(4,128)(2,1)S(1)} all-gather(bf16[1,16,3]{1,2,0:T(4,128)(2,1)S(1)} %bitcast.435), channel_id=1, replica_groups=mesh['dp'=2,'ctx'=4,'tp'=4] {'dp','ctx','tp'}, dimensions={0}, use_global_device_ids=true | all-gather | bytes 3168 | tf_op jit(solution)/shard_map/all_gather | solution.py:151
  336.9 32.7 %all_gather.91 = bf16[512,128]{1,0:T(8,128)(2,1)} all-gather(bf16[64,128]{1,0:T(8,128)(2,1)S(1)} %copy-done.43), channel_id=1, replica_groups=mesh['dp'=2,'ctx'=4,'tp'=4] {'dp','ctx'}, dimensions={0}, use_global_device_ids=true | all-gather | bytes 147456 | tf_op jit(solution)/shard_map/all_gather | solution.py:139
  369.6 30.9 %all_gather.94 = bf16[128,512]{0,1:T(8,128)(2,1)S(1)} all-gather(bf16[128,64]{0,1:T(8,128)(2,1)S(1)} %copy-done.41), channel_id=1, replica_groups=mesh['dp'=2,'ctx'=4,'tp'=4] {'dp','ctx'}, dimensions={1}, use_global_device_ids=true | all-gather | bytes 147456 | tf_op jit(solution)/shard_map/all_gather | solution.py:144
  423.3 34.4 %while.54 = (s32[]{:T(128)}, bf16[8,256,2,64]{1,3,2,0:T(8,128)(2,1)}, f32[8,2,256]{2,1,0:T(2,128)S(1)}, bf16[8,1024,2,64]{1,3,2,0:T(8,128)(2,1)}, bf16[8,256,2,6...) while((s32[]{:T(128)}, bf16[8,256,2,64]{1,3,2,0:T(8,128)(2,1)}, ...), condition=%wide.region_10.11_spmd, body=%wide.region_7.10_spmd.sunk | while | flops 138968576 | bytes 6965329 | solution.py:209
  462.9 39.1 %all-reduce = bf16[2048]{0:T(1024)(128)(2,1)S(1)} all-reduce(bf16[2048]{0:T(1024)(128)(2,1)S(1)} %dynamic-update-slice), channel_id=1, replica_groups=mesh['dp'=2,'ctx'=4,'tp'=4] {'dp','ctx','tp'}, use_global_device_ids=true, to_apply=%add | all-reduce | flops 2048 | bytes 8192
  502.1 35.5 %all_gather.95 = bf16[512,512]{1,0:T(8,128)(2,1)} all-gather(bf16[64,512]{1,0:T(8,128)(2,1)S(1)} %copy-done.40), channel_id=1, replica_groups=mesh['dp'=2,'ctx'=4,'tp'=4] {'dp','ctx'}, dimensions={0}, use_global_device_ids=true | all-gather | bytes 589824 | tf_op jit(solution)/shard_map/all_gather | solution.py:142
  537.6 34.4 %all_gather.97 = bf16[512,512]{0,1:T(8,128)(2,1)} all-gather(bf16[512,64]{0,1:T(8,128)(2,1)S(1)} %copy-done.39), channel_id=1, replica_groups=mesh['dp'=2,'ctx'=4,'tp'=4] {'dp','ctx'}, dimensions={1}, use_global_device_ids=true | all-gather | bytes 589824 | tf_op jit(solution)/shard_map/all_gather | solution.py:145
  587.4 85.3 %all-reduce.14.cloned.1.call-done = f32[2048,512]{1,0:T(8,128)} async-done(((f32[2048,512]{1,0:T(8,128)}), f32[2048,512]{1,0:T(8,128)}) %all-reduce.14.cloned.1.call-update) | async-done | bytes 4194320 | tf_op jit(solution)/shard_map/psum | solution.py:69
  684.6 32.6 %all_gather.98 = bf16[512,512]{0,1:T(8,128)(2,1)S(1)} all-gather(bf16[512,64]{0,1:T(8,128)(2,1)S(1)} %copy-done.39), channel_id=1, replica_groups=mesh['dp'=2,'ctx'=4,'tp'=4] {'dp','ctx'}, dimensions={1}, use_global_device_ids=true | all-gather | bytes 589824 | tf_op jit(solution)/shard_map/all_gather | solution.py:247
  717.1 32.1 %all_gather.99 = bf16[512,512]{1,0:T(8,128)(2,1)S(1)} all-gather(bf16[64,512]{1,0:T(8,128)(2,1)S(1)} %copy-done.40), channel_id=1, replica_groups=mesh['dp'=2,'ctx'=4,'tp'=4] {'dp','ctx'}, dimensions={0}, use_global_device_ids=true | all-gather | bytes 589824 | tf_op jit(solution)/shard_map/all_gather | solution.py:244
  759.2 31.0 %all_gather.100 = bf16[128,512]{0,1:T(8,128)(2,1)S(1)} all-gather(bf16[128,64]{0,1:T(8,128)(2,1)S(1)} %copy-done.42), channel_id=1, replica_groups=mesh['dp'=2,'ctx'=4,'tp'=4] {'dp','ctx'}, dimensions={1}, use_global_device_ids=true | all-gather | bytes 147456 | tf_op jit(solution)/shard_map/all_gather | solution.py:246
  790.2 30.9 %all_gather.101 = bf16[512,128]{1,0:T(8,128)(2,1)S(1)} all-gather(bf16[64,128]{1,0:T(8,128)(2,1)S(1)} %copy-done.44), channel_id=1, replica_groups=mesh['dp'=2,'ctx'=4,'tp'=4] {'dp','ctx'}, dimensions={0}, use_global_device_ids=true | all-gather | bytes 147456 | tf_op jit(solution)/shard_map/all_gather | solution.py:241
  844.9 149.5 %while.55 = (s32[]{:T(128)}, bf16[8,256,2,64]{1,3,2,0:T(8,128)(2,1)}, bf16[8,1024,2,64]{1,3,2,0:T(8,128)(2,1)}, bf16[8,1024,2,64]{1,3,2,0:T(8,128)(2,1)}, bf16[8...) while((s32[]{:T(128)}, ...), condition=%wide.region_24.25_spmd, body=%wide.region_22.24_spmd.sunk | while | flops 342395904 | bytes 25242728 | solution.py:275
  999.4 30.7 %all_gather.102 = bf16[128,512]{0,1:T(8,128)(2,1)S(1)} all-gather(bf16[128,64]{0,1:T(8,128)(2,1)S(1)} %copy-done.45), channel_id=1, replica_groups=mesh['dp'=2,'ctx'=4,'tp'=4] {'dp','ctx'}, dimensions={1}, use_global_device_ids=true | all-gather | bytes 147456 | tf_op jit(solution)/shard_map/all_gather | solution.py:245
  1074.4 149.9 %while.57 = (s32[]{:T(128)}, bf16[8,256,2,64]{1,3,2,0:T(8,128)(2,1)}, bf16[8,1024,2,64]{1,3,2,0:T(8,128)(2,1)}, bf16[8,1024,2,64]{1,3,2,0:T(8,128)(2,1)}, bf16[8...) while((s32[]{:T(128)}, ...), condition=%wide.region_30.31_spmd.clone, body=%wide.region_28.30_spmd.clone.sunk | while | flops 342920192 | bytes 25243760 | solution.py:294
  1226.7 43.6 %all-reduce.1 = f32[2048]{0:T(1024)S(1)} all-reduce(f32[2048]{0:T(1024)S(1)} %dynamic_update_slice.56), channel_id=8, replica_groups=mesh['dp'=2,'ctx'=4,'tp'=4] {'dp','ctx','tp'}, use_global_device_ids=true, to_apply=%region_55.56.clone | all-reduce | flops 2048 | bytes 16384
  1271.0 33.1 %all_gather.106 = bf16[512,128]{1,0:T(8,128)(2,1)} all-gather(bf16[64,128]{1,0:T(8,128)(2,1)S(1)} %copy-done.47), channel_id=1, replica_groups=mesh['dp'=2,'ctx'=4,'tp'=4] {'dp','ctx'}, dimensions={0}, use_global_device_ids=true | all-gather | bytes 147456 | tf_op jit(solution)/shard_map/all_gather | solution.py:242
  1304.1 32.8 %all_gather.107 = bf16[512,128]{1,0:T(8,128)(2,1)} all-gather(bf16[64,128]{1,0:T(8,128)(2,1)S(1)} %copy-done.49), channel_id=1, replica_groups=mesh['dp'=2,'ctx'=4,'tp'=4] {'dp','ctx'}, dimensions={0}, use_global_device_ids=true | all-gather | bytes 147456 | tf_op jit(solution)/shard_map/all_gather | solution.py:243
  1336.9 32.7 %all_gather.104 = bf16[512,128]{1,0:T(8,128)(2,1)} all-gather(bf16[64,128]{1,0:T(8,128)(2,1)S(1)} %copy-done.51), channel_id=1, replica_groups=mesh['dp'=2,'ctx'=4,'tp'=4] {'dp','ctx'}, dimensions={0}, use_global_device_ids=true | all-gather | bytes 147456 | tf_op jit(solution)/shard_map/all_gather | solution.py:239
  1369.7 32.9 %all_gather.103 = bf16[512,128]{1,0:T(8,128)(2,1)} all-gather(bf16[64,128]{1,0:T(8,128)(2,1)S(1)} %copy-done.53), channel_id=1, replica_groups=mesh['dp'=2,'ctx'=4,'tp'=4] {'dp','ctx'}, dimensions={0}, use_global_device_ids=true | all-gather | bytes 147456 | tf_op jit(solution)/shard_map/all_gather | solution.py:238
  1402.5 33.1 %all_gather.105 = bf16[512,128]{1,0:T(8,128)(2,1)} all-gather(bf16[64,128]{1,0:T(8,128)(2,1)S(1)} %copy-done.55), channel_id=1, replica_groups=mesh['dp'=2,'ctx'=4,'tp'=4] {'dp','ctx'}, dimensions={0}, use_global_device_ids=true | all-gather | bytes 147456 | tf_op jit(solution)/shard_map/all_gather | solution.py:240
  1515.5 62.3 %all-reduce.20.cloned.1.call-done = (bf16[2048,512]{1,0:T(8,128)(2,1)}, bf16[8,256,512]{2,1,0:T(8,128)(2,1)}) async-done(((bf16[2048,512]{1,0:T(8,128)(2,1)}, bf16[8,256,512]{2,1,0:T(8,128)(2,1)}), (bf16[2048,512]{1,0:T(8,128)(2,1)}, bf16[8,256,512]{2,1,0:T(8,128)(2,1)})) %all-reduce.20.cloned.1.call-update) | async-done | bytes 4194320 | tf_op jit(solution)/shard_map/psum | solution.py:73
  1592.5 125.5 %reduce-scatter.19.cloned.1.call-done = f32[16,3]{1,0:T(8,128)} async-done(((f32[512,3]{1,0:T(8,128)}), f32[16,3]{1,0:T(8,128)}) %reduce-scatter.19.cloned.1.call-update) | async-done | bytes 208
  1719.4 130.6 %reduce-scatter.21.cloned.1.call-done = f32[16,10]{1,0:T(8,128)} async-done(((f32[512,10]{1,0:T(8,128)}), f32[16,10]{1,0:T(8,128)}) %reduce-scatter.21.cloned.1.call-update) | async-done | bytes 656
  (527 shorter events, 634.6 us)
Async XLA Ops:
  7.2 144.7 %copy-start = (bf16[8,256,512]{2,1,0:T(8,128)(2,1)S(1)}, bf16[8,256,512]{2,1,0:T(8,128)(2,1)}, u32[]{:S(2)}) copy-start(bf16[8,256,512]{2,1,0:T(8,128)(2,1)} %param.25) | copy-start | bytes 6291460
  7.2 250.1 %all-gather.6.cloned.1.call-start = ((), (), s32[]{:S(2)}) async-start(), calls=%async_computation.8 | async-start | bytes 2621440 | tf_op jit(solution)/shard_map/all_gather | solution.py:178
  85.8 175.4 %all-gather.8.cloned.1.call-start = ((), (), s32[]{:S(2)}) async-start(), calls=%async_computation.9 | async-start | bytes 2621440 | tf_op jit(solution)/shard_map/all_gather | solution.py:175
  120.5 282.0 %all-gather.10.cloned.1.call-start = ((), (), s32[]{:S(2)}) async-start(), calls=%async_computation.11 | async-start | bytes 2621440 | tf_op jit(solution)/shard_map/all_gather | solution.py:184
  153.4 253.0 %all-gather.12.cloned.1.call-start = ((), (), s32[]{:S(2)}) async-start(), calls=%async_computation.12 | async-start | bytes 2621440 | tf_op jit(solution)/shard_map/all_gather | solution.py:181
  186.4 223.9 %all-reduce.10.cloned.1.call-start = ((), (), s32[]{:S(2)}) async-start(), calls=%async_computation.10 | async-start | bytes 8388608 | tf_op jit(solution)/shard_map/psum | solution.py:69
  299.0 70.6 %copy-start.41 = (bf16[128,64]{0,1:T(8,128)(2,1)S(1)}, bf16[128,64]{0,1:T(8,128)(2,1)}, u32[]{:S(2)}) copy-start(bf16[128,64]{0,1:T(8,128)(2,1)} %param.34) | copy-start | bytes 49156
  299.0 273.0 %all-reduce.12.cloned.1.call-start = ((), (), s32[]{:S(2)}) async-start(), calls=%async_computation.13 | async-start | bytes 8388608 | tf_op jit(solution)/shard_map/psum | solution.py:69
  402.5 270.2 %copy-start.56 = (f32[1,512]{1,0:T(1,128)}, f32[1,512]{1,0:T(1,128)S(1)}, u32[]{:S(2)}) copy-start(f32[1,512]{1,0:T(1,128)S(1)} %get-tuple-element.565) | copy-start | bytes 6148
  462.1 75.5 %copy-start.39 = (bf16[512,64]{0,1:T(8,128)(2,1)S(1)}, bf16[512,64]{0,1:T(8,128)(2,1)}, u32[]{:S(2)}) copy-start(bf16[512,64]{0,1:T(8,128)(2,1)} %param.36) | copy-start | bytes 196612
  462.1 109.9 %copy-start.63 = (f32[512]{0:T(512)S(1)}, f32[512]{0:T(512)}, u32[]{:S(2)}) copy-start(f32[512]{0:T(512)} %copy-done.62) | copy-start | bytes 6148
  462.1 109.9 %copy-start.77 = (f32[512]{0:T(512)S(1)}, f32[512]{0:T(512)}, u32[]{:S(2)}) copy-start(f32[512]{0:T(512)} %get-tuple-element.465) | copy-start | bytes 6148
  462.1 210.6 %all-reduce.14.cloned.1.call-start = ((), (), s32[]{:S(2)}) async-start(), calls=%async_computation.14 | async-start | bytes 8388608 | tf_op jit(solution)/shard_map/psum | solution.py:69
  502.1 247.1 %copy-start.79 = (f32[512]{0:T(512)}, f32[512]{0:T(512)S(1)}, u32[]{:S(2)}) copy-start(f32[512]{0:T(512)S(1)} %dynamic-slice_convert_fusion) | copy-start | bytes 6148
  587.3 85.4 %copy-start.76 = (f32[512]{0:T(512)S(1)}, f32[512]{0:T(512)}, u32[]{:S(2)}) copy-start(f32[512]{0:T(512)} %get-tuple-element.463) | copy-start | bytes 6148
  587.3 233.7 %all-reduce.16.cloned.1.call-start = ((), (), s32[]{:S(2)}) async-start(), calls=%async_computation.15 | async-start | bytes 4194304 | tf_op jit(solution)/shard_map/psum | solution.py:73
  682.7 66.5 %copy-start.10 = (f32[2048,512]{1,0:T(8,128)}, f32[2048,512]{1,0:T(8,128)S(1)}, u32[]{:S(2)}) copy-start(f32[2048,512]{1,0:T(8,128)S(1)} %get-tuple-element.539) | copy-start | bytes 12582916
  758.5 292.1 %all-reduce.18.cloned.1.call-start = ((), (), s32[]{:S(2)}) async-start(), calls=%async_computation.16 | async-start | bytes 4194304 | tf_op jit(solution)/shard_map/psum | solution.py:73
  998.7 461.0 %reduce-scatter.15.cloned.1.call-start = ((), (), s32[]{:S(2)}) async-start(), calls=%async_computation.19 | async-start | bytes 2621440 | tf_op jit(solution)/shard_map/reduce_scatter | solution.py:310
  999.3 461.8 %reduce-scatter.17.cloned.1.call-start = ((), (), s32[]{:S(2)}) async-start(), calls=%async_computation.20 | async-start | bytes 2621440 | tf_op jit(solution)/shard_map/reduce_scatter | solution.py:316
  1030.2 435.2 %reduce-scatter.11.cloned.1.call-start = ((), (), s32[]{:S(2)}) async-start(), calls=%async_computation.17 | async-start | bytes 2621440 | tf_op jit(solution)/shard_map/reduce_scatter | solution.py:298
  1224.4 79.7 %copy-start.49 = (bf16[64,128]{1,0:T(8,128)(2,1)S(1)}, bf16[64,128]{1,0:T(8,128)(2,1)}, u32[]{:S(2)}) copy-start(bf16[64,128]{1,0:T(8,128)(2,1)} %param.33) | copy-start | bytes 49156
  1224.4 112.5 %copy-start.51 = (bf16[64,128]{1,0:T(8,128)(2,1)S(1)}, bf16[64,128]{1,0:T(8,128)(2,1)}, u32[]{:S(2)}) copy-start(bf16[64,128]{1,0:T(8,128)(2,1)} %param.28) | copy-start | bytes 49156
  1224.4 145.3 %copy-start.53 = (bf16[64,128]{1,0:T(8,128)(2,1)S(1)}, bf16[64,128]{1,0:T(8,128)(2,1)}, u32[]{:S(2)}) copy-start(bf16[64,128]{1,0:T(8,128)(2,1)} %param.27) | copy-start | bytes 49156
  1224.4 178.1 %copy-start.55 = (bf16[64,128]{1,0:T(8,128)(2,1)S(1)}, bf16[64,128]{1,0:T(8,128)(2,1)}, u32[]{:S(2)}) copy-start(bf16[64,128]{1,0:T(8,128)(2,1)} %param.29) | copy-start | bytes 49156
  1224.4 260.5 %reduce-scatter.13.cloned.1.call-start = ((), (), s32[]{:S(2)}) async-start(), calls=%async_computation.18 | async-start | bytes 2621440 | tf_op jit(solution)/shard_map/reduce_scatter | solution.py:304
  1224.5 211.2 %copy-start.80 = (f32[512]{0:T(512)S(1)}, f32[512]{0:T(512)}, u32[]{:S(2)}) copy-start(f32[512]{0:T(512)} %copy-done.79) | copy-start | bytes 6148
  1448.3 56.5 %all-to-all-start.1 = ((bf16[8,768,64]{1,2,0:T(8,128)(2,1)}), bf16[8,768,64]{1,2,0:T(8,128)(2,1)}, u32[]{:S(2)}, u32[]{:S(2)}) async-start(bf16[8,768,64]{1,2,0:T(8,128)(2,1)} %bitcast.56), calls=%async_computation.5 | async-start | bytes 1572864 | tf_op jit(solution)/shard_map/all_to_all | solution.py:28
  1453.0 124.8 %all-reduce.20.cloned.1.call-start = ((), (), s32[]{:S(2)}) async-start(), calls=%async_computation.23 | async-start | bytes 8388608 | tf_op jit(solution)/shard_map/psum | solution.py:73
  1504.8 346.5 %all-to-all-start = ((bf16[8,64,1280]{2,1,0:T(8,128)(2,1)}), bf16[8,64,1280]{2,1,0:T(8,128)(2,1)S(1)}, u32[]{:S(2)}, u32[]{:S(2)}) async-start(bf16[8,64,1280]{2,1,0:T(8,128)(2,1)} %bitcast.54), calls=%async_computation.4 | async-start | bytes 2621440 | tf_op jit(solution)/shard_map/all_to_all | solution.py:28
  1509.8 208.2 %reduce-scatter.19.cloned.1.call-start = ((), (), s32[]{:S(2)}) async-start(), calls=%async_computation.21 | async-start | bytes 270336
  1584.3 265.6 %reduce-scatter.21.cloned.1.call-start = ((), (), s32[]{:S(2)}) async-start(), calls=%async_computation.22 | async-start | bytes 270336
  (72 other events, 703.3 us)
Sparse Core Ops, SparseCore 0:
  85.9 45.0 all-gather.5
  132.6 47.6 all-gather.7
  182.4 47.0 all-gather.9
  231.0 45.5 all-gather.11
  299.1 82.1 all-reduce.9
  462.2 84.7 all-reduce.11
  587.4 85.2 all-reduce.13
  758.6 52.0 all-reduce.15
  998.9 51.6 all-reduce.17
  1052.8 43.9 reduce-scatter.14
  1099.1 43.0 reduce-scatter.16
  1224.6 45.3 reduce-scatter.10
  1435.8 49.1 reduce-scatter.12
  1491.9 85.8 all-reduce.19
  1584.5 133.5 reduce-scatter.18
  1720.2 129.7 reduce-scatter.20
where the time goes:
time: 1870 us; the launch traced here: 1860 us
  blocking collectives  806 us (43%)
  waiting for transfers between devices  440 us (24%)
  matrix products  416 us (22%)
  local copies, waits for them, and re-layouts  105 us (6%)
  other arithmetic  66.5 us (4%)
    unnamed x18, waiting for transfers between devices  257 us
    psum x3, waiting for transfers between devices, head_sum(): return lax.psum(values, 'tp')  85.3 us
    unnamed x2, blocking collectives  82.8 us
    psum x3, waiting for transfers between devices, head_grad(): lax.psum(as_sent(values), 'tp')  82.4 us
    dot_general x16, matrix products, attend_backward(): jnp.einsum('hqk,khe->qhe', grad_scores, key_rows, preferred_element_type=...  78.1 us
    dot_general x16, matrix products, attend_backward(): jnp.einsum('hqk,qhe->khe', grad_scores, queries, preferred_element_type=j...  77.7 us
    dot_general x16, matrix products, attend_backward(): jnp.einsum('qhe,khe->hqk', queries, key_rows, preferred_element_type=jnp....  45.4 us
    dot_general x16, matrix products, attend_backward(): jnp.einsum('qhe,khe->hqk', grad_mixed, values, preferred_element_type=jnp...  45 us
  transfers between devices with their start and end apart: 18, of which 6 were waited for; matrix products, arithmetic and copies ran while one was open for 17% of the time, Pallas kernels for 0%

commit v1 on v0

v1 whole, which is shorter than its diff:
```python
import functools

import jax
import jax.numpy as jnp
from jax import lax
from jax.experimental import pallas as pl
from jax.experimental.pallas import tpu as pltpu
from jax.sharding import PartitionSpec as P

HD = 64
EPS = 1e-05
BF = jnp.bfloat16
F32 = jnp.float32
PAIR = 2 * HD
VMEM_LIMIT = 56 << 20
GELU_C = 0.7978845608028654
GELU_A = 0.044715


def nn(left, right):
    return lax.dot_general(left, right, (((1,), (0,)), ((), ())), preferred_element_type=F32)


def nt(left, right):
    return lax.dot_general(left, right, (((1,), (1,)), ((), ())), preferred_element_type=F32)


def params(**kw):
    return pltpu.CompilerParams(vmem_limit_bytes=VMEM_LIMIT, dimension_semantics=kw.pop("sem"), **kw)


def full(shape):
    return pl.BlockSpec(shape, lambda *_: (0,) * len(shape))


def norm_stats(z):
    mean = jnp.mean(z, axis=-1, keepdims=True)
    cent = z - mean
    var = jnp.mean(cent * cent, axis=-1, keepdims=True)
    inv = lax.rsqrt(var + EPS)
    return cent * inv, inv


def norm_back(grad, gain, normed, inv):
    e = grad * gain
    me = jnp.mean(e, axis=-1, keepdims=True)
    men = jnp.mean(e * normed, axis=-1, keepdims=True)
    return inv * (e - me - normed * men)


def rows_sum(a):
    return jnp.sum(a, axis=0, keepdims=True)


def split_pair(block):
    lane = lax.broadcasted_iota(jnp.int32, block.shape, 1)
    zero = jnp.zeros_like(block)
    return jnp.concatenate(
        [jnp.where(lane < HD, block, zero), jnp.where(lane < HD, zero, block)], axis=0
    )


def join_pair(both):
    q = both.shape[1] // 2
    row = lax.broadcasted_iota(jnp.int32, (both.shape[0], q), 0)
    return jnp.where(row < HD, both[:, :q], both[:, q:])


def attn_fwd_body(
    causal, q_rows, kv_parts, w_ref, vecp_ref, q_row, v_row,
    q_ref, k_ref, v_ref, p_refs, ot_ref, o_ref, il_ref, acc_ref,
):
    d = q_rows.shape[1]
    wq = w_ref[:, 0, 0].reshape(d, PAIR)
    wkv = jnp.concatenate(
        [w_ref[:, 0, 1].reshape(d, PAIR), w_ref[:, 0, 2].reshape(d, PAIR)], axis=1
    )
    wo = w_ref[:, 0, 3].reshape(d, PAIR)
    kv = nn(kv_parts, wkv)
    k = kv[:, :PAIR].astype(BF)
    v = (kv[:, PAIR:] + vecp_ref[v_row : v_row + 1]).astype(BF)
    q = (nn(q_rows, wq) + vecp_ref[q_row : q_row + 1]).astype(BF) * HD ** (-0.5)
    q_ref[0] = q
    k_ref[0] = k
    v_ref[0] = v
    vt = v.T
    blocks = len(p_refs)
    rows = q.shape[0] // blocks
    keys = k.shape[0]
    for b in range(blocks):
        n = keys // blocks * (b + 1) if causal else keys
        s = nt(k[:n], split_pair(q[b * rows : (b + 1) * rows]))
        top = jnp.max(s, axis=0, keepdims=True)
        p = jnp.exp(s - top)
        inv = 1.0 / jnp.sum(p, axis=0, keepdims=True)
        pb = p.astype(BF)
        p_refs[b][0] = pb
        ot = join_pair(nn(vt[:, :n], pb) * inv)
        span = slice(b * rows, (b + 1) * rows)
        ot_ref[0, :, span] = ot.astype(BF)
        o_ref[0, span, :] = ot.T.astype(BF)
        il_ref[0, 0:1, span] = inv[:, :rows]
        il_ref[0, 1:2, span] = inv[:, rows:]
    acc_ref[...] += nt(o_ref[0], wo)


def self_fwd(xo_ref, xp_ref, w_ref, vecp_ref, vec_ref, q_ref, k_ref, v_ref, p0, p1, p2, p3,
             ot_ref, o_ref, il_ref, n_ref, r_ref, x_all, acc_ref):
    t = pl.program_id(0)
    blocks = 4
    half = xo_ref.shape[0] // blocks

    @pl.when(t == 0)
    def _():
        for b in range(blocks):
            x_all[2 * b * half : (2 * b + 1) * half] = xo_ref[b * half : (b + 1) * half]
            x_all[(2 * b + 1) * half : (2 * b + 2) * half] = xp_ref[b * half : (b + 1) * half]
        acc_ref[...] = xo_ref[...].astype(F32) + vec_ref[5:6]

    attn_fwd_body(True, xo_ref[...], x_all[...], w_ref, vecp_ref, 3, 4,
                  q_ref, k_ref, v_ref, (p0, p1, p2, p3), ot_ref, o_ref, il_ref, acc_ref)

    @pl.when(t == pl.num_programs(0) - 1)
    def _():
        normed, inv = norm_stats(acc_ref[...])
        n_ref[...] = normed
        r_ref[...] = jnp.broadcast_to(inv, r_ref.shape)


def cross_fwd(n1_ref, mo_ref, mp_ref, w_ref, vecp_ref, vec_ref, q_ref, k_ref, v_ref, p0, p1, p2, p3,
              ot_ref, o_ref, il_ref, n_ref, r_ref, m_all, h_low, acc_ref):
    t = pl.program_id(0)
    half = mo_ref.shape[0]

    @pl.when(t == 0)
    def _():
        m_all[:half] = mo_ref[...]
        m_all[half:] = mp_ref[...]
        h1 = n1_ref[...] * vec_ref[0:1] + vec_ref[6:7]
        h_low[...] = h1.astype(BF)
        acc_ref[...] = h1 + vec_ref[9:10]

    attn_fwd_body(False, h_low[...], m_all[...], w_ref, vecp_ref, 7, 8,
                  q_ref, k_ref, v_ref, (p0, p1, p2, p3), ot_ref, o_ref, il_ref, acc_ref)

    @pl.when(t == pl.num_programs(0) - 1)
    def _():
        normed, inv = norm_stats(acc_ref[...])
        n_ref[...] = normed
        r_ref[...] = jnp.broadcast_to(inv, r_ref.shape)


def ffn_both(n2_ref, r2_ref, cot_ref, w_ref, bias_ref, vec_ref,
             out_ref, gin_ref, gout_ref, dz2_ref, vg_ref, bg_ref,
             h_low, h_t, act, slope, acc, dz3_low, dz3_t, dh2):
    phase = pl.program_id(0)
    t = pl.program_id(1)
    d = n2_ref.shape[1]
    last = pl.num_programs(1) - 1
    w_in = w_ref[:, 0, 0].reshape(d, -1)
    w_out = w_ref[:, 0, 1].reshape(d, -1)

    @pl.when((phase == 0) & (t == 0))
    def _():
        h2 = n2_ref[...] * vec_ref[1:2] + vec_ref[10:11]
        h_low[...] = h2.astype(BF)
        h_t[...] = h2.astype(BF).T
        acc[...] = h2 + vec_ref[11:12]

    @pl.when(phase == 0)
    def _():
        u = nn(h_low[...], w_in) + bias_ref[0]
        cube = GELU_A * u * u
        th = jnp.tanh(GELU_C * u * (1.0 + cube))
        low = 0.5 * (1.0 + th)
        f = (u * low).astype(BF)
        act[t] = f
        slope[t] = low + 0.5 * u * (1.0 - th * th) * (GELU_C * (1.0 + 3.0 * cube))
        acc[...] += nt(f, w_out)

    @pl.when((phase == 0) & (t == last))
    def _():
        n3, r3 = norm_stats(acc[...])
        out_ref[...] = (n3 * vec_ref[2:3] + vec_ref[12:13]).astype(BF)
        g = cot_ref[...].astype(F32)
        vg_ref[0:1] = rows_sum(g * n3)
        vg_ref[1:2] = rows_sum(g)
        dz3 = norm_back(g, vec_ref[2:3], n3, r3)
        vg_ref[2:3] = rows_sum(dz3)
        low = dz3.astype(BF)
        dz3_low[...] = low
        dz3_t[...] = low.T
        dh2[...] = dz3

    @pl.when(phase == 1)
    def _():
        f = act[t]
        df = nn(dz3_low[...], w_out).astype(BF).astype(F32)
        du = (df * slope[t]).astype(BF)
        gout_ref[...] = nn(dz3_t[...], f).astype(BF).reshape(gout_ref.shape)
        gin_ref[...] = nn(h_t[...], du).astype(BF).reshape(gin_ref.shape)
        bg_ref[0] = rows_sum(du.astype(F32))
        dh2[...] += nt(du, w_in)

    @pl.when((phase == 1) & (t == last))
    def _():
        g = dh2[...]
        n2 = n2_ref[...]
        vg_ref[3:4] = rows_sum(g * n2)
        vg_ref[4:5] = rows_sum(g)
        dz2 = norm_back(g, vec_ref[1:2], n2, r2_ref[:, 0:1])
        vg_ref[5:6] = rows_sum(dz2)
        vg_ref[6:8] = jnp.zeros_like(vg_ref[6:8])
        dz2_ref[...] = dz2


def attn_bwd(causal, act_ref, dz_ref, w_ref, vec_ref, q_ref, k_ref, v_ref, p0, p1, p2, p3,
             ot_ref, o_ref, il_ref, n_ref, r_ref,
             gq_ref, go_ref, own_ref, peer_ref, out_ref, vg_ref, qg_ref,
             dy, dy_t, act_t, acc, dk_ref, dv_ref):
    t = pl.program_id(0)
    d = dz_ref.shape[1]
    p_refs = (p0, p1, p2, p3)
    blocks = len(p_refs)
    wq = w_ref[:, 0, 0].reshape(d, PAIR)
    wo = w_ref[:, 0, 3].reshape(d, PAIR)

    @pl.when(t == 0)
    def _():
        dz = dz_ref[...]
        low = dz.astype(BF)
        dy[...] = low
        dy_t[...] = low.T
        acc[...] = dz
        if causal:
            act_t[...] = act_ref[...].T
        else:
            h = n_ref[...] * vec_ref[0:1] + vec_ref[6:7]
            act_t[...] = h.astype(BF).T

    q = q_ref[0]
    k = k_ref[0]
    v = v_ref[0]
    keys = k.shape[0]
    rows = q.shape[0] // blocks
    do = nn(dy[...], wo).astype(BF)
    go_ref[...] = nn(dy_t[...], o_ref[0]).astype(BF).reshape(go_ref.shape)
    do_t = do.T.astype(F32)
    prod = do_t * ot_ref[0].astype(F32)
    inv_a, inv_b = il_ref[0, 0:1], il_ref[0, 1:2]
    inner_a = jnp.sum(prod[:HD], axis=0, keepdims=True) * inv_a
    inner_b = jnp.sum(prod[HD:], axis=0, keepdims=True) * inv_b
    row = lax.broadcasted_iota(jnp.int32, do_t.shape, 0)
    dos = (do_t * jnp.where(row < HD, inv_a, inv_b)).astype(BF).T
    kt = k.T
    dqs = [None] * blocks
    for b in reversed(range(blocks)):
        n = keys // blocks * (b + 1) if causal else keys
        span = slice(b * rows, (b + 1) * rows)
        dob = split_pair(dos[span])
        qb = split_pair(q[span])
        pb = p_refs[b][0]
        dp = nt(v[:n], dob)
        inner = jnp.concatenate([inner_a[:, span], inner_b[:, span]], axis=1)
        ds = (pb.astype(F32) * (dp - inner)).astype(BF)
        dv = nn(pb, dob)
        dk = nn(ds, qb)
        if b == blocks - 1:
            dv_ref[...] = dv
            dk_ref[...] = dk
        else:
            dv_ref[:n] += dv
            dk_ref[:n] += dk
        dqs[b] = (join_pair(nn(kt[:, :n], ds)) * HD ** (-0.5)).T.astype(BF)
    dq = jnp.concatenate(dqs, axis=0)
    gq_ref[...] = nn(act_t[...], dq).astype(BF).reshape(gq_ref.shape)
    qg_ref[0] = rows_sum(dq.astype(F32))
    acc[...] += nt(dq, wq)
    for i, ref in enumerate((dk_ref, dv_ref)):
        if causal:
            for b in range(blocks):
                at = 2 * b * rows
                own_ref[i, 0, b * rows : (b + 1) * rows] = ref[at : at + rows]
                peer_ref[i, 0, b * rows : (b + 1) * rows] = ref[at + rows : at + 2 * rows].astype(BF)
        else:
            own_ref[i, 0] = ref[: keys // 2]
            peer_ref[i, 0] = ref[keys // 2 :].astype(BF)

    @pl.when(t == pl.num_programs(0) - 1)
    def _():
        g = acc[...]
        if causal:
            out_ref[...] = g
            vg_ref[...] = jnp.zeros_like(vg_ref)
        else:
            normed = n_ref[...]
            vg_ref[0:1] = rows_sum(g * normed)
            vg_ref[1:2] = rows_sum(g)
            dz1 = norm_back(g, vec_ref[0:1], normed, r_ref[:, 0:1])
            vg_ref[2:3] = rows_sum(dz1)
            vg_ref[3:8] = jnp.zeros_like(vg_ref[3:8])
            out_ref[...] = dz1


def kv_back(with_base, act_ref, own_ref, got_ref, w_ref, *rest):
    if with_base:
        base_ref, out_ref, gk_ref, gv_ref, vgrad_ref, act_t, acc = rest
    else:
        out_ref, gk_ref, gv_ref, vgrad_ref, act_t, acc = rest
    t = pl.program_id(0)
    d = act_ref.shape[1]
    wk = w_ref[:, 0, 1].reshape(d, PAIR)
    wv = w_ref[:, 0, 2].reshape(d, PAIR)

    @pl.when(t == 0)
    def _():
        act_t[...] = act_ref[...].T
        if with_base:
            acc[...] = base_ref[...]
        else:
            acc[...] = jnp.zeros_like(acc)

    dk = (own_ref[0, 0] + got_ref[0, 0].astype(F32)).astype(BF)
    dv = (own_ref[1, 0] + got_ref[1, 0].astype(F32)).astype(BF)
    dkv = jnp.concatenate([dk, dv], axis=1)
    gkv = nn(act_t[...], dkv).astype(BF)
    gk_ref[...] = gkv[:, :PAIR].reshape(gk_ref.shape)
    gv_ref[...] = gkv[:, PAIR:].reshape(gv_ref.shape)
    vgrad_ref[0] = rows_sum(dv.astype(F32))
    acc[...] += nt(dkv, jnp.concatenate([wk, wv], axis=1))

    @pl.when(t == pl.num_programs(0) - 1)
    def _():
        out_ref[...] = acc[...].astype(BF)


def pair_spec(rows):
    return pl.BlockSpec((1, rows, PAIR), lambda t: (t, 0, 0))


def struct(shape, dtype):
    return jax.ShapeDtypeStruct(shape, dtype)


def weight_spec(w):
    return pl.BlockSpec((w.shape[0], 1) + w.shape[2:], lambda t: (0, t, 0, 0, 0))


def grad_spec(dc, rows):
    return pl.BlockSpec((dc, 1, rows, PAIR), lambda t: (0, t, 0, 0))


def run_attn_fwd(causal, rows_in, w, vec):
    d = vec.shape[1]
    own = rows_in[0].shape[0]
    keys = 2 * own
    pairs = w.shape[1]
    blocks = 4
    ns = [keys // blocks * (b + 1) if causal else keys for b in range(blocks)]
    qn = 2 * own // blocks
    out_shape = (
        struct((pairs, own, PAIR), BF),
        struct((pairs, keys, PAIR), BF),
        struct((pairs, keys, PAIR), BF),
        *[struct((pairs, n, qn), BF) for n in ns],
        struct((pairs, PAIR, own), BF),
        struct((pairs, own, PAIR), BF),
        struct((pairs, 8, own), F32),
        struct((own, d), F32),
        struct((own, PAIR), F32),
    )
    out_specs = (
        pair_spec(own),
        pair_spec(keys),
        pair_spec(keys),
        *[pl.BlockSpec((1, n, qn), lambda t: (t, 0, 0)) for n in ns],
        pl.BlockSpec((1, PAIR, own), lambda t: (t, 0, 0)),
        pair_spec(own),
        pl.BlockSpec((1, 8, own), lambda t: (t, 0, 0)),
        full((own, d)),
        full((own, PAIR)),
    )
    in_specs = [full(a.shape) for a in rows_in] + [
        weight_spec(w),
        pl.BlockSpec((vec.shape[0], PAIR), lambda t: (0, t)),
        full(vec.shape),
    ]
    scratch = [pltpu.VMEM((keys, d), BF)]
    if not causal:
        scratch.append(pltpu.VMEM((own, d), BF))
    scratch.append(pltpu.VMEM((own, d), F32))
    area = sum(ns) * qn
    return pl.pallas_call(
        self_fwd if causal else cross_fwd,
        grid=(pairs,),
        in_specs=in_specs,
        out_specs=out_specs,
        out_shape=out_shape,
        scratch_shapes=scratch,
        compiler_params=params(sem=("arbitrary",)),
        cost_estimate=pl.CostEstimate(
            flops=2 * own * d * d * 6 + 4 * area * PAIR * pairs,
            bytes_accessed=2 * area * pairs + 8 * own * d,
            transcendentals=area * pairs,
        ),
        name="self_fwd" if causal else "cross_fwd",
    )(*rows_in, w, vec, vec)


def run_ffn(n2, r2, cot, w, bias, vec):
    own, d = n2.shape
    dc, parts, _, prows, hid = w.shape
    back = lambda p, t: (0, p * t, 0, 0)
    return pl.pallas_call(
        ffn_both,
        grid=(2, parts),
        in_specs=[
            full(n2.shape),
            full(r2.shape),
            full(cot.shape),
            pl.BlockSpec((dc, 1, 2, prows, hid), lambda p, t: (0, t, 0, 0, 0)),
            pl.BlockSpec((1, 1, hid), lambda p, t: (t, 0, 0)),
            full(vec.shape),
        ],
        out_specs=(
            full((own, d)),
            pl.BlockSpec((dc, 1, prows, hid), back),
            pl.BlockSpec((dc, 1, prows, hid), back),
            full((own, d)),
            full((8, d)),
            pl.BlockSpec((1, 1, hid), lambda p, t: (p * t, 0, 0)),
        ),
        out_shape=(
            struct((own, d), BF),
            struct((dc, parts, prows, hid), BF),
            struct((dc, parts, prows, hid), BF),
            struct((own, d), F32),
            struct((8, d), F32),
            struct((parts, 1, hid), F32),
        ),
        scratch_shapes=[
            pltpu.VMEM((own, d), BF),
            pltpu.VMEM((d, own), BF),
            pltpu.VMEM((parts, own, hid), BF),
            pltpu.VMEM((parts, own, hid), F32),
            pltpu.VMEM((own, d), F32),
            pltpu.VMEM((own, d), BF),
            pltpu.VMEM((d, own), BF),
            pltpu.VMEM((own, d), F32),
        ],
        compiler_params=params(sem=("arbitrary", "arbitrary")),
        cost_estimate=pl.CostEstimate(
            flops=12 * own * d * hid * parts,
            bytes_accessed=4 * dc * parts * 2 * prows * hid + 20 * own * d,
            transcendentals=own * hid * parts,
        ),
        name="ffn_both",
    )(n2, r2, cot, w, bias, vec)


def run_attn_bwd(causal, act, dz, w, vec, saved, n, r):
    q, k, v, p0, p1, p2, p3, ot, o, il = saved
    pairs, own, _ = q.shape
    keys = k.shape[1]
    d = dz.shape[1]
    dc, _, _, prows, _ = w.shape
    ps = (p0, p1, p2, p3)
    area = sum(p.shape[1] * p.shape[2] for p in ps)
    kv_spec = pl.BlockSpec((2, 1, own, PAIR), lambda t: (0, t, 0, 0))
    return pl.pallas_call(
        functools.partial(attn_bwd, causal),
        grid=(pairs,),
        in_specs=[
            full(act.shape),
            full(dz.shape),
            weight_spec(w),
            full(vec.shape),
            pair_spec(own),
            pair_spec(keys),
            pair_spec(keys),
            *[pl.BlockSpec((1,) + p.shape[1:], lambda t: (t, 0, 0)) for p in ps],
            pl.BlockSpec((1, PAIR, own), lambda t: (t, 0, 0)),
            pair_spec(own),
            pl.BlockSpec((1, 8, own), lambda t: (t, 0, 0)),
            full(n.shape),
            full(r.shape),
        ],
        out_specs=(
            grad_spec(dc, prows),
            grad_spec(dc, prows),
            kv_spec,
            kv_spec,
            full((own, d)),
            full((8, d)),
            pl.BlockSpec((1, 1, PAIR), lambda t: (t, 0, 0)),
        ),
        out_shape=(
            struct((dc, pairs, prows, PAIR), BF),
            struct((dc, pairs, prows, PAIR), BF),
            struct((2, pairs, own, PAIR), F32),
            struct((2, pairs, own, PAIR), BF),
            struct((own, d), F32),
            struct((8, d), F32),
            struct((pairs, 1, PAIR), F32),
        ),
        scratch_shapes=[
            pltpu.VMEM((own, d), BF),
            pltpu.VMEM((d, own), BF),
            pltpu.VMEM((d, own), BF),
            pltpu.VMEM((own, d), F32),
            pltpu.VMEM((keys, PAIR), F32),
            pltpu.VMEM((keys, PAIR), F32),
        ],
        compiler_params=params(sem=("arbitrary",)),
        cost_estimate=pl.CostEstimate(
            flops=2 * own * d * d * 4 + 8 * area * PAIR * pairs,
            bytes_accessed=2 * area * pairs + 16 * own * d,
            transcendentals=0,
        ),
        name="self_bwd" if causal else "cross_bwd",
    )(act, dz, w, vec, *saved, n, r)


def run_kv_back(name, act, own_part, got, w, base):
    own, d = act.shape
    dc, pairs, _, prows, _ = w.shape
    kv_spec = pl.BlockSpec((2, 1, own, PAIR), lambda t: (0, t, 0, 0))
    ins = [act, own_part, got, w]
    specs = [full(act.shape), kv_spec, kv_spec, weight_spec(w)]
    if base is not None:
        ins.append(base)
        specs.append(full(base.shape))
    return pl.pallas_call(
        functools.partial(kv_back, base is not None),
        grid=(pairs,),
        in_specs=specs,
        out_specs=(
            full((own, d)),
            grad_spec(dc, prows),
            grad_spec(dc, prows),
            pl.BlockSpec((1, 1, PAIR), lambda t: (t, 0, 0)),
        ),
        out_shape=(
            struct((own, d), BF),
            struct((dc, pairs, prows, PAIR), BF),
            struct((dc, pairs, prows, PAIR), BF),
            struct((pairs, 1, PAIR), F32),
        ),
        scratch_shapes=[pltpu.VMEM((d, own), BF), pltpu.VMEM((own, d), F32)],
        compiler_params=params(sem=("arbitrary",)),
        cost_estimate=pl.CostEstimate(
            flops=8 * own * d * d, bytes_accessed=20 * own * d, transcendentals=0
        ),
        name=name,
    )(*ins)


ALL = ("dp", "ctx", "ty", "tc")


def shards(
    inputs, memory, cotangent, wq_self, wk_self, wv_self, wo_self, wq_cross, wk_cross, wv_cross,
    wo_cross, w_in, w_out, gains, shifts, ffn_bias,
):
    seqs, block, d = inputs.shape
    n_dp, n_ctx, n_y, n_c = (lax.axis_size(a) for a in ALL)
    dc, pairs = n_dp * n_ctx, n_y * n_c
    half = block // n_c
    y_rank, c_rank = lax.axis_index("ty"), lax.axis_index("tc")
    own = n_ctx * half
    swap = [(i, i ^ 1) for i in range(n_c)]

    def mine(array):
        part = lax.dynamic_slice(array, (y_rank * n_ctx, c_rank * half, 0), (n_ctx, half, d))
        return lax.all_to_all(part, "ctx", 0, 0, tiled=True).reshape(own, d)

    def peer(array):
        return lax.ppermute(array, "tc", swap)

    def gather(array):
        got = lax.all_gather(array, ALL, axis=0, tiled=False)
        return got.reshape(dc, pairs, *array.shape)

    prows = wq_self.shape[0]
    vec_local = jnp.concatenate([gains.reshape(-1), shifts.reshape(-1), ffn_bias.reshape(-1)])
    used = vec_local.shape[0]
    vec_rows = -(-used // (8 * PAIR)) * 8
    vec_pack = jnp.pad(vec_local, (0, vec_rows * PAIR - used)).reshape(vec_rows, PAIR)
    first = jnp.concatenate([wq_self, wk_self, wv_self, wo_self.T, vec_pack], axis=0)
    got = gather(first)
    w_self = got[:, :, : 4 * prows].reshape(dc, pairs, 4, prows, PAIR)
    vec_all = got[:, :, 4 * prows :].reshape(dc * pairs, -1)[:, :used].astype(F32)
    lanes = gains.shape[1]
    cut = 13 * lanes
    vec = vec_all[:, :cut].reshape(-1, 13, lanes).transpose(1, 0, 2).reshape(13, d)
    vec = jnp.pad(vec, ((0, 3), (0, 0)))
    bias = vec_all[:, cut:].reshape(pairs, 1, -1)
    w_cross = gather(jnp.stack([wq_cross, wk_cross, wv_cross, wo_cross.T]))
    w_ffn = gather(jnp.stack([w_in, w_out.T]))

    xo = mine(inputs)
    xp = peer(xo)
    mo = mine(memory)
    mp = peer(mo)
    cot = mine(cotangent)

    *saved_self, n1, r1 = run_attn_fwd(True, (xo, xp), w_self, vec)
    *saved_cross, n2, r2 = run_attn_fwd(False, (n1, mo, mp), w_cross, vec)
    out, g_in, g_out, dz2, vg_ffn, bg = run_ffn(n2, r2, cot, w_ffn, bias, vec)
    gqc, goc, ownc, peerc, dz1, vg_cross, qgc = run_attn_bwd(
        False, mo, dz2, w_cross, vec, saved_cross, n1, r1
    )
    gotc = peer(peerc)
    gqs, gos, owns, peers, base, _, qgs = run_attn_bwd(
        True, xo, dz1, w_self, vec, saved_self, n1, r1
    )
    gots = peer(peers)
    gmem, gkc, gvc, vgc = run_kv_back("mem_back", mo, ownc, gotc, w_cross, None)
    gx, gks, gvs, vgs = run_kv_back("in_back", xo, owns, gots, w_self, base)

    def home(array, dtype):
        part = lax.all_to_all(array.reshape(n_ctx, half, d), "ctx", 0, 0, tiled=True)
        every = lax.all_gather(part, ("ty", "tc"), axis=0, tiled=False)
        every = every.reshape(n_y, n_c, n_ctx, half, d).transpose(0, 2, 1, 3, 4)
        return every.reshape(seqs, block, d).astype(dtype)

    def scatter(array):
        return lax.psum_scatter(
            array.reshape(dc * pairs, *array.shape[2:]), ALL, scatter_dimension=0, tiled=False
        )

    ffn_sum = scatter(jnp.stack([g_in, g_out], axis=2)).astype(F32)

    def line(a):
        return a.reshape(1, -1)

    vec_grads = jnp.concatenate(
        [
            vg_cross[0:1], vg_ffn[3:4], vg_ffn[0:1],
            line(qgs), line(vgs), vg_cross[2:3], vg_cross[1:2], line(qgc), line(vgc),
            vg_ffn[5:6], vg_ffn[4:5], vg_ffn[2:3], vg_ffn[1:2],
        ],
        axis=0,
    )
    vec_grads = vec_grads.reshape(13, dc * pairs, lanes).transpose(1, 0, 2).reshape(dc * pairs, cut)
    vec_grads = jnp.concatenate([vec_grads, bg.reshape(dc * pairs, -1)], axis=1)
    vec_grads = jnp.pad(vec_grads, ((0, 0), (0, vec_rows * PAIR - used)))
    vec_grads = vec_grads.reshape(dc, pairs, vec_rows, PAIR).astype(BF)
    rest = jnp.concatenate([gqs, gks, gvs, gos, gqc, gkc, gvc, goc, vec_grads], axis=2)
    rest = scatter(rest).astype(F32)
    mats = [rest[i * prows : (i + 1) * prows] for i in range(8)]
    vec_mine = rest[8 * prows :].reshape(-1)[:used]
    n_gain, n_shift = gains.size, shifts.size
    return (
        home(out, BF),
        home(gx, F32),
        home(gmem, F32),
        mats[0],
        mats[1],
        mats[2],
        mats[3].T,
        mats[4],
        mats[5],
        mats[6],
        mats[7].T,
        ffn_sum[0],
        ffn_sum[1].T,
        vec_mine[:n_gain].reshape(gains.shape),
        vec_mine[n_gain : n_gain + n_shift].reshape(shifts.shape),
        vec_mine[n_gain + n_shift :],
    )


def solution(mesh):
    sizes = mesh.devices.shape
    inner = jax.sharding.Mesh(
        mesh.devices.reshape(sizes[0], sizes[1], sizes[2] // 2, 2), ALL
    )
    rows = P("dp", "ctx", None)
    tp = ("ty", "tc")
    col = P(("dp", "ctx"), tp)
    row = P(tp, ("dp", "ctx"))
    small = P(None, ALL)
    weights = (col, col, col, row, col, col, col, row, col, row)
    tail = (small, small, P(ALL))
    return jax.shard_map(
        shards,
        mesh=inner,
        in_specs=(rows, rows, rows) + weights + tail,
        out_specs=(rows, rows, rows) + weights + tail,
        check_vma=False,
    )
```

time: 1870 us -> 658 us (0.35)
  blocking collectives: 806 us -> 57.9 us
  matrix products: 416 us -> 0 us
  Pallas kernels: 0 us -> 93.9 us
  local copies, waits for them, and re-layouts: 105 us -> 43.3 us
  other arithmetic: 66.5 us -> 14.2 us
  waiting for transfers between devices: 440 us -> 418 us
    all_gather x22 -> x0, blocking collectives: 723 us -> none  [the longest x1 43.6 us: shards(): lax.all_gather(shifts, ('dp', 'ctx', 'tp'), axis=1, tiled=True)]
    dot_general x142 -> x0, matrix products: 416 us -> none  [the longest x16 78.1 us: attend_backward(): jnp.einsum('hqk,khe->qhe', grad_scores, key_rows, preferred_element_type=...]
    psum x6 -> x0, waiting for transfers between devices: 168 us -> none  [the longest x3 85.3 us: head_sum(): return lax.psum(values, 'tp')]
    reduce_scatter x4 -> x1, waiting for transfers between devices: 15.6 us -> 135 us  [scatter(): lax.psum_scatter(array.reshape(dc * pairs, *array.shape[2:]), ALL, scatte...]
    unnamed x18 -> x9, waiting for transfers between devices: 257 us -> 145 us
    all_gather x4 -> x6, waiting for transfers between devices: 0.01 us -> 102 us  [the longest x3 102 us: gather(): got = lax.all_gather(array, ALL, axis=0, tiled=False)]
    pallas_call x0 -> x7, Pallas kernels: none -> 93.9 us  [the longest x2 33 us: run_attn_bwd(): pl.pallas_call(functools.partial(attn_bwd, causal), grid=(pairs,), in_spe...]
    unnamed x2 -> x0, blocking collectives: 82.8 us -> none
  transfers between devices with their start and end apart: 18 -> 15, of which waited for: 6 -> 9; matrix products, arithmetic and copies ran while one was open for 17% -> 7% of each run, Pallas kernels for 0% -> 12%
where the time goes in v1:
time: 658 us; the launch traced here: 656 us
  waiting for transfers between devices  418 us (64%)
  Pallas kernels  93.9 us (14%)
  blocking collectives  57.9 us (9%)
  local copies, waits for them, and re-layouts  43.3 us (7%)
  between operations  14.6 us (2%)
  other arithmetic  14.2 us (2%)
  starting transfers between devices  14 us (2%)
    unnamed x9, waiting for transfers between devices  145 us
    reduce_scatter x1, waiting for transfers between devices, scatter(): lax.psum_scatter(array.reshape(dc * pairs, *array.shape[2:]), ALL, scatte...  135 us
    all_gather x3, waiting for transfers between devices, gather(): got = lax.all_gather(array, ALL, axis=0, tiled=False)  102 us
    all_to_all x3, blocking collectives, home(): lax.all_to_all(array.reshape(n_ctx, half, d), 'ctx', 0, 0, tiled=True)  57.9 us
    pallas_call x2, Pallas kernels, run_attn_bwd(): pl.pallas_call(functools.partial(attn_bwd, causal), grid=(pairs,), in_spe...  33 us
    pallas_call x2, Pallas kernels, run_attn_fwd(): pl.pallas_call(self_fwd if causal else cross_fwd, grid=(pairs,), in_specs...  32.9 us
    all_to_all x3, waiting for transfers between devices, mine(): return lax.all_to_all(part, 'ctx', 0, 0, tiled=True).reshape(own, d)  30.6 us
    unnamed x74, local copies, waits for them, and re-layouts  16.5 us
  transfers between devices with their start and end apart: 15, of which 9 were waited for; matrix products, arithmetic and copies ran while one was open for 7% of the time, Pallas kernels for 12%

profile of v1, /device:TPU:0, one launch (start us, length us, event | category | flops | bytes accessed | tf_op | source)
XLA Modules:
  0.0 656.4 jit_solution(6890786192727316169)
XLA Ops:
  17.2 6.3 all-to-all-start
  25.3 14.0 %all-to-all-done = bf16[4,128,512]{2,1,0:T(8,128)(2,1)S(1)} async-done(((bf16[4,128,512]{2,1,0:T(8,128)(2,1)}), bf16[4,128,512]{2,1,0:T(8,128)(2,1)S(1)}, u32[]{:S(2)}, u32[]{:S(2)}) %all-to-all-start) | async-done | bytes 524320 | tf_op jit(solution)/shard_map/all_to_all | solution.py:575
  39.4 3.5 all-to-all-start.1
  42.9 16.6 %all-to-all-done.1 = bf16[4,128,512]{2,1,0:T(8,128)(2,1)S(1)} async-done(((bf16[4,128,512]{2,1,0:T(8,128)(2,1)}), bf16[4,128,512]{2,1,0:T(8,128)(2,1)S(1)}, u32[]{:S(2)}, u32[]{:S(2)}) %all-to-all-start.1) | async-done | bytes 524320 | tf_op jit(solution)/shard_map/all_to_all | solution.py:575
  59.6 2.1 constant_dynamic-slice_fusion
  61.6 3.5 all-to-all-start.2
  65.2 14.9 %all-gather.13.cloned.1.call-done = bf16[8448,128]{1,0:T(8,128)(2,1)} async-done(((bf16[264,128]{1,0:T(8,128)(2,1)}), bf16[8448,128]{1,0:T(8,128)(2,1)}) %all-gather.13.cloned.1.call-update) | async-done | bytes 2162704 | tf_op jit(solution)/shard_map/all_gather | solution.py:581
  81.0 3.1 slice.165
  86.7 14.9 %self_fwd.1 = (bf16[4,512,128]{2,1,0:T(8,128)(2,1)}, bf16[4,1024,128]{2,1,0:T(8,128)(2,1)}, bf16[4,1024,128]{2,1,0:T(8,128)(2,1)}, bf16[4,256,256]{2,1,0:T(8,128...) custom-call(bf16[512,512]{1,0:T(8,128)(2,1)} %bitcast.94, ...), custom_call_target="tpu_custom_call" | custom-call | flops 2952790016 | bytes 7340032 | tf_op jit(solution)/shard_map/self_fwd/pallas_call | solution.py:393
  101.6 41.1 %all-gather.15.cloned.1.call-done = bf16[128,64,128]{2,1,0:T(8,128)(2,1)} async-done(((bf16[4,64,128]{2,1,0:T(8,128)(2,1)}), bf16[128,64,128]{2,1,0:T(8,128)(2,1)}) %all-gather.15.cloned.1.call-update) | async-done | bytes 2097168 | tf_op jit(solution)/shard_map/all_gather | solution.py:581
  142.7 18.0 %cross_fwd.1 = (bf16[4,512,128]{2,1,0:T(8,128)(2,1)}, bf16[4,1024,128]{2,1,0:T(8,128)(2,1)}, bf16[4,1024,128]{2,1,0:T(8,128)(2,1)}, bf16[4,1024,256]{2,1,0:T(8,1...) custom-call(f32[512,512]{1,0:T(8,128)} %get-tuple-element.67.n1_ref., ...), custom_call_target="tpu_custom_call" | custom-call | flops 3758096384 | bytes 10485760 | tf_op jit(solution)/shard_map/cross_fwd/pallas_call | solution.py:393
  160.8 46.3 %all-gather.17.cloned.1.call-done = bf16[64,64,512]{2,1,0:T(8,128)(2,1)} async-done(((bf16[2,64,512]{2,1,0:T(8,128)(2,1)}), bf16[64,64,512]{2,1,0:T(8,128)(2,1)}) %all-gather.17.cloned.1.call-update) | async-done | bytes 4194320 | tf_op jit(solution)/shard_map/all_gather | solution.py:581
  207.1 16.1 %ffn_both.1 = (bf16[512,512]{1,0:T(8,128)(2,1)}, bf16[8,4,64,512]{3,2,1,0:T(8,128)(2,1)}, bf16[8,4,64,512]{3,2,1,0:T(8,128)(2,1)}, f32[512,512]{1,0:T(8,128)}, f32[8,512]{1,0:T(8,128)}, /*index=5*/f32[4,1,512]{2,1,0:T(1,128)}) custom-call(f32[512,512]{1,0:T(8,128)} %get-tuple-element.68.n2_ref, f32[512,128]{1,0:T(8,128)} %get-tuple-element.69.r2_ref, ...), custom_call_target="tpu_custom_call" | custom-call | flops 6442450944 | bytes 13631488 | tf_op jit(solution)/shard_map/ffn_both/pallas_call | solution.py:414
  223.2 19.4 %all_to_all.30 = bf16[4,128,512]{2,1,0:T(8,128)(2,1)} all-to-all(bf16[4,128,512]{2,1,0:T(8,128)(2,1)} %bitcast.115), channel_id=1, replica_groups=mesh['dp'=2,'ctx'=4,'ty'=2,'tc'=2] {'ctx'}, dimensions={0} | all-to-all | bytes 1048576 | tf_op jit(solution)/shard_map/all_to_all | solution.py:622
  242.7 17.9 %cross_bwd.1 = (bf16[8,4,64,128]{3,2,1,0:T(8,128)(2,1)}, bf16[8,4,64,128]{3,2,1,0:T(8,128)(2,1)}, f32[2,4,512,128]{3,2,1,0:T(8,128)}, bf16[2,4,512,128]{3,2,1,0:...) custom-call(bf16[512,512]{1,0:T(8,128)(2,1)} %bitcast.112, ...), custom_call_target="tpu_custom_call" | custom-call | flops 5368709120 | bytes 12582912 | tf_op jit(solution)/shard_map/cross_bwd/pallas_call | solution.py:470
  260.7 2.9 collective-permute-done.3.got_ref
  264.6 5.7 mem_back.1
  270.2 19.3 %all_to_all.31 = bf16[4,128,512]{2,1,0:T(8,128)(2,1)} all-to-all(bf16[4,128,512]{2,1,0:T(8,128)(2,1)} %bitcast.117), channel_id=1, replica_groups=mesh['dp'=2,'ctx'=4,'ty'=2,'tc'=2] {'ctx'}, dimensions={0} | all-to-all | bytes 1048576 | tf_op jit(solution)/shard_map/all_to_all | solution.py:622
  289.6 15.1 %self_bwd.1 = (bf16[8,4,64,128]{3,2,1,0:T(8,128)(2,1)}, bf16[8,4,64,128]{3,2,1,0:T(8,128)(2,1)}, f32[2,4,512,128]{3,2,1,0:T(8,128)}, bf16[2,4,512,128]{3,2,1,0:T...) custom-call(bf16[512,512]{1,0:T(8,128)(2,1)} %bitcast.95, ...), custom_call_target="tpu_custom_call" | custom-call | flops 3758096384 | bytes 9437184 | tf_op jit(solution)/shard_map/self_bwd/pallas_call | solution.py:470
  304.7 2.9 collective-permute-done.2.got_ref
  308.5 6.2 in_back.1
  314.8 19.3 %all_to_all.32 = bf16[4,128,512]{2,1,0:T(8,128)(2,1)} all-to-all(bf16[4,128,512]{2,1,0:T(8,128)(2,1)} %bitcast.116), channel_id=1, replica_groups=mesh['dp'=2,'ctx'=4,'ty'=2,'tc'=2] {'ctx'}, dimensions={0} | all-to-all | bytes 1048576 | tf_op jit(solution)/shard_map/all_to_all | solution.py:622
  334.1 4.0 pad_maximum_fusion
  340.1 2.0 constant_dynamic-update-slice_fusion.26
  342.8 2.0 constant_dynamic-update-slice_fusion.25
  351.2 3.1 copy.60
  354.3 2.1 convert_bitcast_fusion
  356.5 2.7 copy.62
  359.2 2.3 convert_bitcast_fusion.1
  361.5 2.7 copy.61
  364.2 134.7 %reduce-scatter.6.cloned.1.call-done = bf16[1,2,64,512]{3,2,1,0:T(8,128)(2,1)} async-done(((bf16[32,2,64,512]{3,2,1,0:T(8,128)(2,1)}), bf16[1,2,64,512]{3,2,1,0:T(8,128)(2,1)}) %reduce-scatter.6.cloned.1.call-update) | async-done | bytes 131088 | tf_op jit(solution)/shard_map/reduce_scatter | solution.py:628
  500.6 144.8 %reduce-scatter.8.cloned.1.call-done = bf16[1,520,128]{2,1,0:T(8,128)(2,1)} async-done(((bf16[32,520,128]{2,1,0:T(8,128)(2,1)}), bf16[1,520,128]{2,1,0:T(8,128)(2,1)}) %reduce-scatter.8.cloned.1.call-update) | async-done | bytes 133136
  (152 shorter events, 32.2 us)
Async XLA Ops:
  7.2 9.1 %copy-start = (bf16[8,256,512]{2,1,0:T(8,128)(2,1)S(1)}, bf16[8,256,512]{2,1,0:T(8,128)(2,1)}, u32[]{:S(2)}) copy-start(bf16[8,256,512]{2,1,0:T(8,128)(2,1)} %param.16) | copy-start | bytes 6291460
  7.2 72.9 %all-gather.13.cloned.1.call-start = ((), (), s32[]{:S(2)}) async-start(), calls=%async_computation.9 | async-start | bytes 2230272 | tf_op jit(solution)/shard_map/all_gather | solution.py:581
  13.2 129.5 %all-gather.15.cloned.1.call-start = ((), (), s32[]{:S(2)}) async-start(), calls=%async_computation.10 | async-start | bytes 2162688 | tf_op jit(solution)/shard_map/all_gather | solution.py:581
  14.7 192.4 %all-gather.17.cloned.1.call-start = ((), (), s32[]{:S(2)}) async-start(), calls=%async_computation.11 | async-start | bytes 4325376 | tf_op jit(solution)/shard_map/all_gather | solution.py:581
  17.2 22.2 %all-to-all-start = ((bf16[4,128,512]{2,1,0:T(8,128)(2,1)}), bf16[4,128,512]{2,1,0:T(8,128)(2,1)S(1)}, u32[]{:S(2)}, u32[]{:S(2)}) async-start(bf16[4,128,512]{2,1,0:T(8,128)(2,1)} %constant_dynamic-slice_fusion.2), calls=%async_computation | async-start | bytes 1048576 | tf_op jit(solution)/shard_map/all_to_all | solution.py:575
  39.4 45.9 %copy-start.2 = (bf16[4,128,512]{2,1,0:T(8,128)(2,1)}, bf16[4,128,512]{2,1,0:T(8,128)(2,1)S(1)}, u32[]{:S(2)}) copy-start(bf16[4,128,512]{2,1,0:T(8,128)(2,1)S(1)} %all-to-all-done) | copy-start | bytes 1572868
  39.4 20.2 %all-to-all-start.1 = ((bf16[4,128,512]{2,1,0:T(8,128)(2,1)}), bf16[4,128,512]{2,1,0:T(8,128)(2,1)S(1)}, u32[]{:S(2)}, u32[]{:S(2)}) async-start(bf16[4,128,512]{2,1,0:T(8,128)(2,1)} %constant_dynamic-slice_fusion.1), calls=%async_computation.1 | async-start | bytes 1048576 | tf_op jit(solution)/shard_map/all_to_all | solution.py:575
  42.8 43.0 %collective-permute-start = (bf16[512,512]{1,0:T(8,128)(2,1)S(1)}, bf16[512,512]{1,0:T(8,128)(2,1)S(1)}, u32[]{:S(2)}, u32[]{:S(2)}) collective-permute-start(bf16[512,512]{1,0:T(8,128)(2,1)S(1)} %bitcast.93), channel_id=1, source_target_pairs={{0,1},{1,0},{2,3},{3,2},{4,5},{5,4},{6,7},{7,6},{8,9},{9,8},{10,11... | collective-permute-start | bytes 1572872 | tf_op jit(solution)/shard_map/ppermute | solution.py:578
  59.6 42.0 %copy-start.4 = (bf16[4,128,512]{2,1,0:T(8,128)(2,1)}, bf16[4,128,512]{2,1,0:T(8,128)(2,1)S(1)}, u32[]{:S(2)}) copy-start(bf16[4,128,512]{2,1,0:T(8,128)(2,1)S(1)} %all-to-all-done.1) | copy-start | bytes 1572868
  59.6 42.0 %collective-permute-start.1 = (bf16[512,512]{1,0:T(8,128)(2,1)S(1)}, bf16[512,512]{1,0:T(8,128)(2,1)S(1)}, u32[]{:S(2)}, u32[]{:S(2)}) collective-permute-start(bf16[512,512]{1,0:T(8,128)(2,1)S(1)} %bitcast.110), channel_id=1, source_target_pairs={{0,1},{1,0},{2,3},{3,2},{4,5},{5,4},{6,7},{7,6},{8,9},{9,8},{10,11... | collective-permute-start | bytes 1572872 | tf_op jit(solution)/shard_map/ppermute | solution.py:578
  61.6 99.2 %all-to-all-start.2 = ((bf16[4,128,512]{2,1,0:T(8,128)(2,1)}), bf16[4,128,512]{2,1,0:T(8,128)(2,1)S(1)}, u32[]{:S(2)}, u32[]{:S(2)}) async-start(bf16[4,128,512]{2,1,0:T(8,128)(2,1)} %constant_dynamic-slice_fusion), calls=%async_computation.2 | async-start | bytes 1048576 | tf_op jit(solution)/shard_map/all_to_all | solution.py:575
  65.1 286.1 %all-gather.19.cloned.1.call-start = ((), (), s32[]{:S(2)}) async-start(), calls=%async_computation.12 | async-start | bytes 2621440 | tf_op jit(solution)/shard_map/all_gather | solution.py:623
  101.6 41.2 %copy-start.22 = (bf16[512,512]{1,0:T(8,128)(2,1)}, bf16[512,512]{1,0:T(8,128)(2,1)S(1)}, u32[]{:S(2)}) copy-start(bf16[512,512]{1,0:T(8,128)(2,1)S(1)} %collective-permute-done.1.mp_ref) | copy-start | bytes 1572868
  160.8 46.3 %copy-start.13 = (bf16[4,128,512]{2,1,0:T(8,128)(2,1)}, bf16[4,128,512]{2,1,0:T(8,128)(2,1)S(1)}, u32[]{:S(2)}) copy-start(bf16[4,128,512]{2,1,0:T(8,128)(2,1)S(1)} %all-to-all-done.2) | copy-start | bytes 1572868
  242.7 111.6 %all-gather.23.cloned.1.call-start = ((), (), s32[]{:S(2)}) async-start(), calls=%async_computation.14 | async-start | bytes 2621440 | tf_op jit(solution)/shard_map/all_gather | solution.py:623
  260.7 2.9 collective-permute-start.3
  289.5 69.7 %all-gather.21.cloned.1.call-start = ((), (), s32[]{:S(2)}) async-start(), calls=%async_computation.13 | async-start | bytes 2621440 | tf_op jit(solution)/shard_map/all_gather | solution.py:623
  304.6 2.9 collective-permute-start.2
  308.5 25.6 %copy-start.3 = (bf16[8,4,64,512]{3,2,1,0:T(8,128)(2,1)S(1)}, bf16[8,4,64,512]{3,2,1,0:T(8,128)(2,1)}, u32[]{:S(2)}) copy-start(bf16[8,4,64,512]{3,2,1,0:T(8,128)(2,1)} %get-tuple-element.116) | copy-start | bytes 6291460
  334.1 164.8 %reduce-scatter.6.cloned.1.call-start = ((), (), s32[]{:S(2)}) async-start(), calls=%async_computation.8 | async-start | bytes 4325376 | tf_op jit(solution)/shard_map/reduce_scatter | solution.py:628
  338.1 1.0 copy-start.16
  338.1 1.3 copy-start.15
  338.2 4.0 copy-start.20
  338.2 4.1 copy-start.18
  338.2 6.6 %copy-start.12 = (bf16[8,4,64,128]{3,2,1,0:T(8,128)(2,1)S(1)}, bf16[8,4,64,128]{3,2,1,0:T(8,128)(2,1)}, u32[]{:S(2)}) copy-start(bf16[8,4,64,128]{3,2,1,0:T(8,128)(2,1)} %get-tuple-element.103) | copy-start | bytes 1572868
  338.2 7.5 %copy-start.11 = (bf16[8,4,64,128]{3,2,1,0:T(8,128)(2,1)S(1)}, bf16[8,4,64,128]{3,2,1,0:T(8,128)(2,1)}, u32[]{:S(2)}) copy-start(bf16[8,4,64,128]{3,2,1,0:T(8,128)(2,1)} %get-tuple-element.104) | copy-start | bytes 1572868
  338.2 8.5 %copy-start.8 = (bf16[8,4,64,128]{3,2,1,0:T(8,128)(2,1)S(1)}, bf16[8,4,64,128]{3,2,1,0:T(8,128)(2,1)}, u32[]{:S(2)}) copy-start(bf16[8,4,64,128]{3,2,1,0:T(8,128)(2,1)} %get-tuple-element.105) | copy-start | bytes 1572868
  338.2 9.4 %copy-start.10 = (bf16[8,4,64,128]{3,2,1,0:T(8,128)(2,1)S(1)}, bf16[8,4,64,128]{3,2,1,0:T(8,128)(2,1)}, u32[]{:S(2)}) copy-start(bf16[8,4,64,128]{3,2,1,0:T(8,128)(2,1)} %get-tuple-element.106) | copy-start | bytes 1572868
  338.2 10.4 %copy-start.9 = (bf16[8,4,64,128]{3,2,1,0:T(8,128)(2,1)S(1)}, bf16[8,4,64,128]{3,2,1,0:T(8,128)(2,1)}, u32[]{:S(2)}) copy-start(bf16[8,4,64,128]{3,2,1,0:T(8,128)(2,1)} %get-tuple-element.107) | copy-start | bytes 1572868
  338.3 11.3 %copy-start.7 = (bf16[8,4,64,128]{3,2,1,0:T(8,128)(2,1)S(1)}, bf16[8,4,64,128]{3,2,1,0:T(8,128)(2,1)}, u32[]{:S(2)}) copy-start(bf16[8,4,64,128]{3,2,1,0:T(8,128)(2,1)} %get-tuple-element.108) | copy-start | bytes 1572868
  338.3 307.1 %reduce-scatter.8.cloned.1.call-start = ((), (), s32[]{:S(2)}) async-start(), calls=%async_computation.15 | async-start | bytes 4392960
  359.2 290.4 %copy-start.1 = (bf16[8,256,512]{2,1,0:T(8,128)(2,1)S(1)}, bf16[8,256,512]{2,1,0:T(8,128)(2,1)}, u32[]{:S(2)}) copy-start(bf16[8,256,512]{2,1,0:T(8,128)(2,1)} %param.16) | copy-start | bytes 6291460
  (7 other events, 5.8 us)
Sparse Core Ops, SparseCore 0:
  13.3 66.7 all-gather.12
  83.0 59.6 all-gather.14
  146.2 60.8 all-gather.16
  242.8 20.7 all-gather.18
  289.6 20.8 all-gather.22
  334.2 20.8 all-gather.20
  357.4 141.4 reduce-scatter.5
  501.2 144.1 reduce-scatter.7

commit v2 on v1

v2 whole, which is shorter than its diff:
```python
import functools

import jax
import jax.numpy as jnp
from jax import lax
from jax.experimental import pallas as pl
from jax.experimental.pallas import tpu as pltpu
from jax.sharding import PartitionSpec as P

HD = 64
EPS = 1e-05
BF = jnp.bfloat16
F32 = jnp.float32
PAIR = 2 * HD
VMEM_LIMIT = 40 << 20
SMALL_LIMIT = 16 << 20
GELU_C = 0.7978845608028654
GELU_A = 0.044715


def nn(left, right):
    return lax.dot_general(left, right, (((1,), (0,)), ((), ())), preferred_element_type=F32)


def nt(left, right):
    return lax.dot_general(left, right, (((1,), (1,)), ((), ())), preferred_element_type=F32)


def norm_stats(z):
    mean = jnp.mean(z, axis=-1, keepdims=True)
    cent = z - mean
    var = jnp.mean(cent * cent, axis=-1, keepdims=True)
    inv = lax.rsqrt(var + EPS)
    return cent * inv, inv


def norm_back(grad, gain, normed, inv):
    e = grad * gain
    me = jnp.mean(e, axis=-1, keepdims=True)
    men = jnp.mean(e * normed, axis=-1, keepdims=True)
    return inv * (e - me - normed * men)


def rows_sum(a):
    return jnp.sum(a, axis=0, keepdims=True)


def split_pair(block):
    lane = lax.broadcasted_iota(jnp.int32, block.shape, 1)
    zero = jnp.zeros_like(block)
    return jnp.concatenate(
        [jnp.where(lane < HD, block, zero), jnp.where(lane < HD, zero, block)], axis=0
    )


def join_pair(both):
    q = both.shape[1] // 2
    row = lax.broadcasted_iota(jnp.int32, (both.shape[0], q), 0)
    return jnp.where(row < HD, both[:, :q], both[:, q:])


def vrow(vec_ref, row):
    return jnp.concatenate([vec_ref[j, row : row + 1] for j in range(vec_ref.shape[0])], axis=1)


def pick(own_ref, peer_ref, mat, odd):
    shape = own_ref.shape
    own = own_ref[0, mat].reshape(shape[2] * shape[3], shape[4])
    other = peer_ref[0, mat].reshape(shape[2] * shape[3], shape[4])
    return jnp.where(odd, other, own)


def put_pieces(ref, at, first, value, ranks_ref):
    n_x, n_z = ref.shape[1], ref.shape[2]
    rows = value.shape[0] // (n_x * n_z)
    for d in range(n_x):
        for z in range(n_z):
            i = d * n_z + z
            ref[at, d ^ ranks_ref[0], z ^ ranks_ref[1], first : first + rows] = value[
                i * rows : (i + 1) * rows
            ]


def attn_fwd_body(
    causal, q_rows, kv_parts, w, biases,
    q_ref, k_ref, v_ref, p_refs, ot_ref, o_ref, il_ref, acc_ref,
):
    wq, wk, wv, wo = w
    kv = nn(kv_parts, jnp.concatenate([wk, wv], axis=1))
    k = kv[:, :PAIR].astype(BF)
    v = (kv[:, PAIR:] + biases[1]).astype(BF)
    q = (nn(q_rows, wq) + biases[0]).astype(BF) * HD ** (-0.5)
    q_ref[0] = q
    k_ref[0] = k
    v_ref[0] = v
    vt = v.T
    blocks = len(p_refs)
    rows = q.shape[0] // blocks
    keys = k.shape[0]
    for b in range(blocks):
        n = keys // blocks * (b + 1) if causal else keys
        s = nt(k[:n], split_pair(q[b * rows : (b + 1) * rows]))
        top = jnp.max(s, axis=0, keepdims=True)
        p = jnp.exp(s - top)
        inv = 1.0 / jnp.sum(p, axis=0, keepdims=True)
        pb = p.astype(BF)
        p_refs[b][0] = pb
        ot = join_pair(nn(vt[:, :n], pb) * inv)
        span = slice(b * rows, (b + 1) * rows)
        ot_ref[0, :, span] = ot.astype(BF)
        o_ref[0, span, :] = ot.T.astype(BF)
        il_ref[0, 0:1, span] = inv[:, :rows]
        il_ref[0, 1:2, span] = inv[:, rows:]
    acc_ref[...] += nt(o_ref[0], wo)


def self_fwd(ranks_ref, xo_ref, xp_ref, wa_ref, wb_ref, va_ref, vb_ref,
             q_ref, k_ref, v_ref, p0, p1, p2, p3, ot_ref, o_ref, il_ref,
             n_ref, r_ref, vec_ref, bias_ref, x_all, acc_ref):
    s = pl.program_id(0)
    blocks = 4
    half = xo_ref.shape[0] // blocks
    tiles = vec_ref.shape[0]

    @pl.when(s == 0)
    def _():
        for b in range(blocks):
            x_all[2 * b * half : (2 * b + 1) * half] = xo_ref[b * half : (b + 1) * half]
            x_all[(2 * b + 1) * half : (2 * b + 2) * half] = xp_ref[b * half : (b + 1) * half]
        both = va_ref[...].astype(F32) + vb_ref[...].astype(F32)
        vec_ref[...] = both[:tiles]
        bias_ref[...] = both[tiles]
        acc_ref[...] = xo_ref[...].astype(F32) + vrow(vec_ref, 5)

    odd = s % 2 == 1
    w = [pick(wa_ref, wb_ref, i, odd) for i in range(4)]
    t = s ^ ranks_ref[4]
    attn_fwd_body(True, xo_ref[...], x_all[...], w, (vec_ref[t, 3:4], vec_ref[t, 4:5]),
                  q_ref, k_ref, v_ref, (p0, p1, p2, p3), ot_ref, o_ref, il_ref, acc_ref)

    @pl.when(s == pl.num_programs(0) - 1)
    def _():
        normed, inv = norm_stats(acc_ref[...])
        n_ref[...] = normed
        r_ref[...] = jnp.broadcast_to(inv, r_ref.shape)


def cross_fwd(ranks_ref, n1_ref, mo_ref, mp_ref, wa_ref, wb_ref, vec_ref,
              q_ref, k_ref, v_ref, p0, p1, p2, p3, ot_ref, o_ref, il_ref,
              n_ref, r_ref, m_all, h_low, acc_ref):
    s = pl.program_id(0)
    half = mo_ref.shape[0]

    @pl.when(s == 0)
    def _():
        m_all[:half] = mo_ref[...]
        m_all[half:] = mp_ref[...]
        h1 = n1_ref[...] * vrow(vec_ref, 0) + vrow(vec_ref, 6)
        h_low[...] = h1.astype(BF)
        acc_ref[...] = h1 + vrow(vec_ref, 9)

    odd = s % 2 == 1
    w = [pick(wa_ref, wb_ref, i, odd) for i in range(4)]
    t = s ^ ranks_ref[4]
    attn_fwd_body(False, h_low[...], m_all[...], w, (vec_ref[t, 7:8], vec_ref[t, 8:9]),
                  q_ref, k_ref, v_ref, (p0, p1, p2, p3), ot_ref, o_ref, il_ref, acc_ref)

    @pl.when(s == pl.num_programs(0) - 1)
    def _():
        normed, inv = norm_stats(acc_ref[...])
        n_ref[...] = normed
        r_ref[...] = jnp.broadcast_to(inv, r_ref.shape)


def ffn_both(ranks_ref, n2_ref, r2_ref, cot_ref, w_ref, bias_ref, vec_ref,
             h0, h1, h2, h3, keep_ref, send_ref, dz2_ref, vg_ref, bg_ref,
             h_low, h_t, act, slope, acc, dz3_low, dz3_t, dh2):
    phase = pl.program_id(0)
    t = pl.program_id(1)
    d = n2_ref.shape[1]
    last = pl.num_programs(1) - 1
    w_in = w_ref[:, 0, 0].reshape(d, -1)
    w_out = w_ref[:, 0, 1].reshape(d, -1)
    hid = w_in.shape[1]
    strips = hid // PAIR

    @pl.when((phase == 0) & (t == 0))
    def _():
        h = n2_ref[...] * vrow(vec_ref, 1) + vrow(vec_ref, 10)
        h_low[...] = h.astype(BF)
        h_t[...] = h.astype(BF).T
        acc[...] = h + vrow(vec_ref, 11)

    @pl.when(phase == 0)
    def _():
        bias = jnp.concatenate(
            [bias_ref[pl.ds(t * strips + j, 1), :] for j in range(strips)], axis=1
        )
        u = nn(h_low[...], w_in) + bias
        cube = GELU_A * u * u
        th = jnp.tanh(GELU_C * u * (1.0 + cube))
        low = 0.5 * (1.0 + th)
        f = (u * low).astype(BF)
        act[t] = f
        slope[t] = low + 0.5 * u * (1.0 - th * th) * (GELU_C * (1.0 + 3.0 * cube))
        acc[...] += nt(f, w_out)

    @pl.when((phase == 0) & (t == last))
    def _():
        n3, r3 = norm_stats(acc[...])
        acc[...] = n3 * vrow(vec_ref, 2) + vrow(vec_ref, 12)
        put_home(acc, (h0, h1, h2, h3), ranks_ref)
        g = cot_ref[...].astype(F32)
        vg_ref[0:1] = rows_sum(g * n3)
        vg_ref[1:2] = rows_sum(g)
        dz3 = norm_back(g, vrow(vec_ref, 2), n3, r3)
        vg_ref[2:3] = rows_sum(dz3)
        low = dz3.astype(BF)
        dz3_low[...] = low
        dz3_t[...] = low.T
        dh2[...] = dz3

    @pl.when(phase == 1)
    def _():
        f = act[t]
        df = nn(dz3_low[...], w_out).astype(BF).astype(F32)
        du = (df * slope[t]).astype(BF)
        g_out = nn(dz3_t[...], f).astype(BF)
        g_in = nn(h_t[...], du).astype(BF)
        sums = rows_sum(du.astype(F32))
        for j in range(strips):
            bg_ref[pl.ds(t * strips + j, 1), :] = sums[:, j * PAIR : (j + 1) * PAIR]
        dh2[...] += nt(du, w_in)
        mine = t % 2 == ranks_ref[3]
        shape = keep_ref.shape[:1] + keep_ref.shape[3:]

        @pl.when(mine)
        def _():
            keep_ref[:, 0, 0] = g_in.reshape(shape)
            keep_ref[:, 0, 1] = g_out.reshape(shape)

        @pl.when(jnp.logical_not(mine))
        def _():
            send_ref[:, 0, 0] = g_in.reshape(shape)
            send_ref[:, 0, 1] = g_out.reshape(shape)

    @pl.when((phase == 1) & (t == last))
    def _():
        g = dh2[...]
        n2 = n2_ref[...]
        vg_ref[3:4] = rows_sum(g * n2)
        vg_ref[4:5] = rows_sum(g)
        dz2 = norm_back(g, vrow(vec_ref, 1), n2, r2_ref[:, 0:1])
        vg_ref[5:6] = rows_sum(dz2)
        vg_ref[6:8] = jnp.zeros_like(vg_ref[6:8])
        dz2_ref[...] = dz2


def put_home(acc, refs, ranks_ref):
    rows = refs[0].shape[0]
    for r, ref in enumerate(refs):
        at = pl.multiple_of((r ^ ranks_ref[1]) * rows, rows)
        ref[...] = acc[pl.ds(at, rows), :].astype(BF)


def attn_bwd(causal, ranks_ref, act_ref, dz_ref, wa_ref, wb_ref, vec_ref,
             q_ref, k_ref, v_ref, p0, p1, p2, p3, ot_ref, o_ref, il_ref, n_ref, r_ref,
             keep_ref, send_ref, own_ref, peer_ref, out_ref, vg_ref, qg_ref,
             dy, dy_t, act_t, acc, dk_ref, dv_ref):
    s = pl.program_id(0)
    p_refs = (p0, p1, p2, p3)
    blocks = len(p_refs)
    odd = s % 2 == 1
    wq = pick(wa_ref, wb_ref, 0, odd)
    wo = pick(wa_ref, wb_ref, 3, odd)

    @pl.when(s == 0)
    def _():
        dz = dz_ref[...]
        low = dz.astype(BF)
        dy[...] = low
        dy_t[...] = low.T
        acc[...] = dz
        if causal:
            act_t[...] = act_ref[...].T
        else:
            h = n_ref[...] * vrow(vec_ref, 0) + vrow(vec_ref, 6)
            act_t[...] = h.astype(BF).T

    q = q_ref[0]
    k = k_ref[0]
    v = v_ref[0]
    keys = k.shape[0]
    rows = q.shape[0] // blocks
    do = nn(dy[...], wo).astype(BF)
    g_o = nn(dy_t[...], o_ref[0]).astype(BF)
    do_t = do.T.astype(F32)
    prod = do_t * ot_ref[0].astype(F32)
    inv_a, inv_b = il_ref[0, 0:1], il_ref[0, 1:2]
    inner_a = jnp.sum(prod[:HD], axis=0, keepdims=True) * inv_a
    inner_b = jnp.sum(prod[HD:], axis=0, keepdims=True) * inv_b
    row = lax.broadcasted_iota(jnp.int32, do_t.shape, 0)
    dos = (do_t * jnp.where(row < HD, inv_a, inv_b)).astype(BF).T
    kt = k.T
    dqs = [None] * blocks
    for b in reversed(range(blocks)):
        n = keys // blocks * (b + 1) if causal else keys
        span = slice(b * rows, (b + 1) * rows)
        dob = split_pair(dos[span])
        qb = split_pair(q[span])
        pb = p_refs[b][0]
        dp = nt(v[:n], dob)
        inner = jnp.concatenate([inner_a[:, span], inner_b[:, span]], axis=1)
        ds = (pb.astype(F32) * (dp - inner)).astype(BF)
        dv = nn(pb, dob)
        dk = nn(ds, qb)
        if b == blocks - 1:
            dv_ref[...] = dv
            dk_ref[...] = dk
        else:
            dv_ref[:n] += dv
            dk_ref[:n] += dk
        dqs[b] = (join_pair(nn(kt[:, :n], ds)) * HD ** (-0.5)).T.astype(BF)
    dq = jnp.concatenate(dqs, axis=0)
    g_q = nn(act_t[...], dq).astype(BF)
    piece = keep_ref.shape[3] // 2

    @pl.when(jnp.logical_not(odd))
    def _():
        put_pieces(keep_ref, 0, 0, g_q, ranks_ref)
        put_pieces(keep_ref, 0, piece, g_o, ranks_ref)

    @pl.when(odd)
    def _():
        put_pieces(send_ref, 0, 0, g_q, ranks_ref)
        put_pieces(send_ref, 0, piece, g_o, ranks_ref)

    qg_ref[0] = rows_sum(dq.astype(F32))
    acc[...] += nt(dq, wq)
    for i, ref in enumerate((dk_ref, dv_ref)):
        if causal:
            for b in range(blocks):
                at = 2 * b * rows
                own_ref[i, 0, b * rows : (b + 1) * rows] = ref[at : at + rows]
                peer_ref[i, 0, b * rows : (b + 1) * rows] = ref[at + rows : at + 2 * rows].astype(BF)
        else:
            own_ref[i, 0] = ref[: keys // 2]
            peer_ref[i, 0] = ref[keys // 2 :].astype(BF)

    @pl.when(s == pl.num_programs(0) - 1)
    def _():
        g = acc[...]
        if causal:
            out_ref[...] = g
            vg_ref[...] = jnp.zeros_like(vg_ref)
        else:
            normed = n_ref[...]
            vg_ref[0:1] = rows_sum(g * normed)
            vg_ref[1:2] = rows_sum(g)
            dz1 = norm_back(g, vrow(vec_ref, 0), normed, r_ref[:, 0:1])
            vg_ref[2:3] = rows_sum(dz1)
            vg_ref[3:8] = jnp.zeros_like(vg_ref[3:8])
            out_ref[...] = dz1


def kv_back(final, lanes, blen, ranks_ref, act_ref, own_ref, got_ref, wa_ref, wb_ref, *rest):
    if final:
        (base_ref, vgc_ref, vgf_ref, bg_ref, qgs_ref, qgc_ref, vg_mem_ref,
         h0, h1, h2, h3, keep_ref, send_ref, act_t, acc, vg_self, tiles) = rest
    else:
        h0, h1, h2, h3, keep_ref, send_ref, vgrad_ref, act_t, acc = rest
    s = pl.program_id(0)
    odd = s % 2 == 1
    wk = pick(wa_ref, wb_ref, 1, odd)
    wv = pick(wa_ref, wb_ref, 2, odd)

    @pl.when(s == 0)
    def _():
        act_t[...] = act_ref[...].T
        if final:
            acc[...] = base_ref[...]
        else:
            acc[...] = jnp.zeros_like(acc)

    dk = (own_ref[0, 0] + got_ref[0, 0].astype(F32)).astype(BF)
    dv = (own_ref[1, 0] + got_ref[1, 0].astype(F32)).astype(BF)
    dkv = jnp.concatenate([dk, dv], axis=1)
    gkv = nn(act_t[...], dkv).astype(BF)
    piece = gkv.shape[0] // (keep_ref.shape[1] * keep_ref.shape[2])
    at = s // 2 if final else 0

    @pl.when(jnp.logical_not(odd))
    def _():
        put_pieces(keep_ref, at, 0, gkv[:, :PAIR], ranks_ref)
        put_pieces(keep_ref, at, piece, gkv[:, PAIR:], ranks_ref)

    @pl.when(odd)
    def _():
        put_pieces(send_ref, at, 0, gkv[:, :PAIR], ranks_ref)
        put_pieces(send_ref, at, piece, gkv[:, PAIR:], ranks_ref)

    sums = rows_sum(dv.astype(F32))
    acc[...] += nt(dkv, jnp.concatenate([wk, wv], axis=1))
    if not final:
        vgrad_ref[0] = sums
    else:
        vg_self[s] = sums
        pairs = vg_self.shape[0]

        @pl.when(s == 0)
        def _():
            for j in range(pairs):
                at = slice(j * PAIR, (j + 1) * PAIR)
                rel = j ^ ranks_ref[4]
                tiles[j, 0:1] = vgc_ref[0:1, at]
                tiles[j, 1:2] = vgf_ref[3:4, at]
                tiles[j, 2:3] = vgf_ref[0:1, at]
                tiles[j, 3:4] = qgs_ref[rel]
                tiles[j, 5:6] = vgc_ref[2:3, at]
                tiles[j, 6:7] = vgc_ref[1:2, at]
                tiles[j, 7:8] = qgc_ref[rel]
                tiles[j, 8:9] = vg_mem_ref[rel]
                tiles[j, 9:10] = vgf_ref[5:6, at]
                tiles[j, 10:11] = vgf_ref[4:5, at]
                tiles[j, 11:12] = vgf_ref[2:3, at]
                tiles[j, 12:13] = vgf_ref[1:2, at]
                tiles[j, 13:16] = jnp.zeros((3, PAIR), F32)

        tiles[s ^ ranks_ref[4], 4:5] = sums
        rows_at = lax.broadcasted_iota(jnp.int32, (16, PAIR), 0)
        n_x, n_z = keep_ref.shape[1], keep_ref.shape[2]

        @pl.when(s == pairs - 1)
        def _():
            for ry in range(2):
                for rc, ref in enumerate((keep_ref, send_ref)):
                    for i in range(n_x):
                        for k in range(n_z):
                            dc = (i ^ ranks_ref[0]) * n_z + (k ^ ranks_ref[1])
                            p = dc * pairs + ((2 * ry + rc) ^ ranks_ref[4])
                            tile = tiles[lax.div(p * lanes, PAIR)]
                            bias = bg_ref[pl.ds(lax.div(p * blen, PAIR), 1), :]
                            both = jnp.where(rows_at == 13, bias, tile).astype(BF)
                            ref[ry, i, k, 2 * piece : 2 * piece + 16] = both

    @pl.when(s == pl.num_programs(0) - 1)
    def _():
        put_home(acc, (h0, h1, h2, h3), ranks_ref)


def pack_rows(*refs):
    ins, outs = refs[1 : 1 + len(refs) // 2], refs[1 + len(refs) // 2 :]
    for ref, out in zip(ins, outs):
        out[...] = ref[0]


def pack_pairs(*refs):
    m_refs, c_refs, outs = refs[1:5], refs[5:9], refs[9:13]
    for m, c, out in zip(m_refs, c_refs, outs):
        out[0] = m[0]
        out[1] = c[0]


def pack_weights(lanes, blen, ranks_ref, wqs, wks, wvs, wos, wqc, wkc, wvc, woc, win, wout,
                 gains, shifts, bias, s_ref, c_ref, f_ref, va, vb):
    n = wqs.shape[0]
    for i, ref in enumerate((wqs, wks, wvs, wos)):
        s_ref[i * n : (i + 1) * n] = ref[...]
    for i, ref in enumerate((wqc, wkc, wvc, woc)):
        c_ref[i * n : (i + 1) * n] = ref[...]
    p = (ranks_ref[0] * 4 + ranks_ref[1]) * 4 + ranks_ref[4]
    at = 4 * n
    va[...] = jnp.zeros_like(va)
    va[0:3, 0:lanes] = gains[...].astype(F32)
    va[3:13, 0:lanes] = shifts[...].astype(F32)
    s_ref[at : at + 16] = pltpu.roll(va[...], lax.rem(p * lanes, PAIR), 1).astype(BF)
    vb[...] = jnp.zeros_like(vb)
    vb[pl.ds(lax.div(p * blen, PAIR), 1), 0:blen] = bias[...].astype(F32)
    s_ref[at + 16 : at + 32] = pltpu.roll(vb[...], lax.rem(p * blen, PAIR), 1).astype(BF)
    f_ref[0] = win[...]
    f_ref[1] = wout[...]


def whole(a):
    return pl.BlockSpec(a.shape, lambda *_: (0,) * len(a.shape))


def without(body, at, count):
    return lambda *refs: body(*refs[:at], *refs[at + count :])


def launch(body, name, grid, ranks, ins, outs, scratch=(), deps=(), limit=VMEM_LIMIT, cost=(0, 0, 0)):
    first = 0 if ranks is None else 1
    deps = list(deps)
    if deps:
        body = without(body, first + len(ins), len(deps))
    call = pl.pallas_call(
        body,
        grid_spec=pltpu.PrefetchScalarGridSpec(
            num_scalar_prefetch=first,
            grid=grid,
            in_specs=[i[1] for i in ins] + [pl.BlockSpec(memory_space=pl.ANY)] * len(deps),
            out_specs=tuple(o[1] for o in outs),
            scratch_shapes=list(scratch),
        ),
        out_shape=tuple(
            pltpu.HBM(o[0].shape, o[0].dtype) if len(o) > 2 else o[0] for o in outs
        ),
        compiler_params=pltpu.CompilerParams(
            vmem_limit_bytes=limit, dimension_semantics=("arbitrary",) * len(grid)
        ),
        cost_estimate=pl.CostEstimate(
            flops=cost[0], bytes_accessed=cost[1], transcendentals=cost[2]
        ),
        name=name,
    )
    args = [
        pltpu.with_memory_space_constraint(i[0], pltpu.HBM) if len(i) > 2 else i[0] for i in ins
    ] + deps
    return call(*args) if ranks is None else call(ranks, *args)


def local(body, name, outs, *ins, ranks=None, scratch=(), in_specs=None, deps=()):
    specs = in_specs or [whole(a) for a in ins]
    size = sum(o.size * o.dtype.itemsize for o in outs)
    return launch(
        body, name, (1,), ranks, list(zip(ins, specs)), [(o, whole(o)) for o in outs],
        scratch, deps, SMALL_LIMIT, (size, 2 * size, 0),
    )


def struct(shape, dtype):
    return jax.ShapeDtypeStruct(shape, dtype)


def restack(ins, outs, cuts):
    for out, (lo, hi) in zip(outs, cuts):
        for r, ref in enumerate(ins):
            out[0, 0, r] = ref[lo:hi]


def double(own, got, out, axis):
    m = own.shape[axis]
    if axis == 0:
        out[:m] = own[...]
        out[m:] = got[...]
    else:
        out[:, :m] = own[...]
        out[:, m:] = got[...]


def order(ranks_ref, parts, outs):
    for r, ref in enumerate(parts):
        rows = ref.shape[-2]
        at = pl.multiple_of((r ^ ranks_ref[1]) * rows, rows)
        for i, out in enumerate(outs):
            out[pl.ds(at, rows), :] = ref[...] if len(outs) == 1 else ref[i]


def assemble(lanes, ranks_ref, a0, a1, b0, b1, w_ref, v_ref=None, scr=None):
    pairs = 4
    n_x, n_z = a0.shape[1], a0.shape[2]
    prows = w_ref.shape[3]
    if v_ref is not None:
        scr[...] = jnp.zeros_like(scr)
    for ry in range(2):
        a_ref = (a0, a1)[ry]
        for i in range(n_x):
            for k in range(n_z):
                dc = (i ^ ranks_ref[0]) * n_z + (k ^ ranks_ref[1])
                b_ref, bi = (b0, i) if i < n_x // 2 else (b1, i - n_x // 2)
                for m in range(2):
                    span = slice(m * prows, (m + 1) * prows)
                    w_ref[ry, m, dc] = a_ref[0, i, k, span]
                    w_ref[ry, 2 + m, dc] = b_ref[ry, bi, k, span]
                if v_ref is not None:
                    at = 2 * prows
                    p = dc * pairs + ((2 * ry) ^ ranks_ref[4])
                    tile = lax.div(p * lanes, PAIR)
                    scr[tile] += b_ref[ry, bi, k, at : at + 16].astype(F32)
                    scr[pairs] += b_ref[ry, bi, k, at + 16 : at + 32].astype(F32)
    if v_ref is not None:
        v_ref[...] = scr[...].astype(BF)


def start_one(cuts, ranks_ref, *refs):
    restack(refs[0:4], refs[8:10], cuts)
    order(ranks_ref, refs[4:8], refs[10:11])


def start_two(axes, cuts, a, ga, b, gb, *refs):
    double(a, ga, refs[4], axes[0])
    double(b, gb, refs[5], axes[1])
    restack(refs[0:4], refs[6:8], cuts)


def double_both(axes, a, ga, b, gb, out_a, out_b):
    double(a, ga, out_a, axes[0])
    double(b, gb, out_b, axes[1])


def start_five(lanes, ranks_ref, *refs):
    assemble(lanes, ranks_ref, *refs[0:4], refs[8])
    order(ranks_ref, refs[4:8], refs[9:11])


def order_home(ranks_ref, *refs):
    order(ranks_ref, refs[:4], refs[4:])


def add_body(keep, got, out):
    out[...] = (keep[...].astype(F32) + got[...].astype(F32)).astype(BF)


def halve_body(axis_a, axis_b, cuts, *refs):
    n = len(cuts)
    ins, (sa, ka, sb, kb) = refs[: len(refs) - 4], refs[len(refs) - 4 :]

    def place(axis, send, keep, at, value):
        rows = value.shape[3]
        m = value.shape[axis] // 2
        lo = value[:m] if axis == 0 else value[:, :m]
        hi = value[m:] if axis == 0 else value[:, m:]
        keep[:, :, :, at : at + rows] = lo
        send[:, :, :, at : at + rows] = hi.astype(BF)

    at_a = at_b = 0
    for i, cut in enumerate(cuts):
        if cut is None:
            continue
        keep, got = ins[2 * i], ins[2 * i + 1]
        total = keep[...].astype(F32) + got[...].astype(F32)
        place(axis_a, sa, ka, at_a, total[:, :, :, :cut])
        place(axis_b, sb, kb, at_b, total[:, :, :, cut:])
        at_a += cut
        at_b += total.shape[3] - cut
    if cuts[0] is None:
        place(axis_a, sa, ka, 0, ins[0][...] + ins[1][...].astype(F32))
        place(axis_b, sb, kb, 0, ins[2][...] + ins[3][...].astype(F32))


def spread_body(ka, ra, kb, rb, s1, s2, s3, keep):
    rows = ka.shape[3]
    for r, ref in enumerate((keep, s1, s2, s3)):
        ref[:rows] = (ka[0, 0, r] + ra[0, 0, r].astype(F32)).astype(ref.dtype)
        ref[rows:] = (kb[0, 0, r] + rb[0, 0, r].astype(F32)).astype(ref.dtype)


def finish_body(plan, lanes, blen, ranks_ref, keep, r1, r2, r3, *outs):
    total = keep[...] + r1[...].astype(F32) + r2[...].astype(F32) + r3[...].astype(F32)
    at = 0
    outs = list(outs)
    for turn, rows in plan:
        part = total[at : at + rows]
        at += rows
        if turn == 2:
            p = (ranks_ref[0] * 4 + ranks_ref[1]) * 4 + ranks_ref[4]
            vec = pltpu.roll(part, lax.rem(PAIR - lax.rem(p * lanes, PAIR), PAIR), 1)
            outs.pop(0)[...] = vec[0:3, :lanes]
            outs.pop(0)[...] = vec[3:13, :lanes]
            own = pltpu.roll(part, lax.rem(PAIR - lax.rem(p * blen, PAIR), PAIR), 1)
            outs.pop(0)[...] = own[13:14, :blen]
        else:
            outs.pop(0)[...] = part


def home_body(ranks_ref, own, other, got_own, got_other, out_ref):
    y = pl.program_id(0)
    n_z, rows, _ = own.shape
    here = pl.multiple_of(ranks_ref[3] * rows, rows)
    there = pl.multiple_of((1 - ranks_ref[3]) * rows, rows)
    for same, a, b in ((True, own, got_own), (False, other, got_other)):
        @pl.when((y == ranks_ref[2]) == same)
        def _():
            for z in range(n_z):
                out_ref[z, pl.ds(here, rows), :] = a[z].astype(out_ref.dtype)
                out_ref[z, pl.ds(there, rows), :] = b[z].astype(out_ref.dtype)


def pair_spec(rows):
    return pl.BlockSpec((1, rows, PAIR), lambda s, _: (s, 0, 0))


def half_spec(w):
    return pl.BlockSpec((1,) + w.shape[1:], lambda s, _: (s // 2, 0, 0, 0, 0))


def slot_shape(n_x, n_z, rows):
    return struct((2, n_x, n_z, rows, PAIR), BF)


def slot_spec(n_x, n_z, rows):
    return pl.BlockSpec((1, n_x, n_z, rows, PAIR), lambda s, _: (s // 2, 0, 0, 0, 0))


def full(shape):
    return pl.BlockSpec(shape, lambda *_: (0,) * len(shape))


def run_attn_fwd(causal, ranks, rows_in, w_own, w_peer, vecs, pairs, deps):
    own, d = rows_in[0].shape
    keys = 2 * own
    blocks = 4
    ns = [keys // blocks * (b + 1) if causal else keys for b in range(blocks)]
    qn = 2 * own // blocks
    outs = [
        (struct((pairs, own, PAIR), BF), pair_spec(own), True),
        (struct((pairs, keys, PAIR), BF), pair_spec(keys), True),
        (struct((pairs, keys, PAIR), BF), pair_spec(keys), True),
        *[
            (struct((pairs, n, qn), BF), pl.BlockSpec((1, n, qn), lambda s, _: (s, 0, 0)), True)
            for n in ns
        ],
        (struct((pairs, PAIR, own), BF), pl.BlockSpec((1, PAIR, own), lambda s, _: (s, 0, 0)), True),
        (struct((pairs, own, PAIR), BF), pair_spec(own), True),
        (struct((pairs, 8, own), F32), pl.BlockSpec((1, 8, own), lambda s, _: (s, 0, 0)), True),
        (struct((own, d), F32), full((own, d))),
        (struct((own, PAIR), F32), full((own, PAIR))),
    ]
    if causal:
        outs.append((struct((pairs, 16, PAIR), F32), full((pairs, 16, PAIR))))
        outs.append((struct((16, PAIR), F32), full((16, PAIR))))
    scratch = [pltpu.VMEM((keys, d), BF)]
    if not causal:
        scratch.append(pltpu.VMEM((own, d), BF))
    scratch.append(pltpu.VMEM((own, d), F32))
    area = sum(ns) * qn
    ins = [(a, whole(a)) for a in rows_in] + [(w_own, half_spec(w_own)), (w_peer, half_spec(w_peer))]
    return launch(
        self_fwd if causal else cross_fwd,
        "self_fwd" if causal else "cross_fwd",
        (pairs,), ranks, ins + [(a, whole(a)) for a in vecs], outs, scratch, deps,
        cost=(
            2 * own * d * d * 6 + 4 * area * PAIR * pairs,
            2 * area * pairs + 8 * own * d,
            area * pairs,
        ),
    )


def run_ffn(ranks, n2, r2, cot, w, bias, vec):
    own, d = n2.shape
    dc, parts, _, prows, hid = w.shape
    half = own // 4
    back = lambda p, t, _: (0, p * (t // 2), 0, 0, 0)
    outs = [(struct((half, d), BF), full((half, d)))] * 4 + [
        (struct((dc, 2, 2, prows, hid), BF), pl.BlockSpec((dc, 1, 2, prows, hid), back)),
        (struct((dc, 2, 2, prows, hid), BF), pl.BlockSpec((dc, 1, 2, prows, hid), back)),
        (struct((own, d), F32), full((own, d))),
        (struct((8, d), F32), full((8, d))),
        (struct((16, PAIR), F32), full((16, PAIR))),
    ]
    ins = [
        (n2, whole(n2)),
        (r2, whole(r2)),
        (cot, whole(cot)),
        (w, pl.BlockSpec((dc, 1, 2, prows, hid), lambda p, t, _: (0, t, 0, 0, 0)), True),
        (bias, whole(bias)),
        (vec, whole(vec)),
    ]
    scratch = [
        pltpu.VMEM((own, d), BF),
        pltpu.VMEM((d, own), BF),
        pltpu.VMEM((parts, own, hid), BF),
        pltpu.VMEM((parts, own, hid), F32),
        pltpu.VMEM((own, d), F32),
        pltpu.VMEM((own, d), BF),
        pltpu.VMEM((d, own), BF),
        pltpu.VMEM((own, d), F32),
    ]
    return launch(
        ffn_both, "ffn_both", (2, parts), ranks, ins, outs, scratch,
        cost=(
            12 * own * d * hid * parts,
            4 * dc * parts * 2 * prows * hid + 20 * own * d,
            own * hid * parts,
        ),
    )


def run_attn_bwd(causal, ranks, act, dz, w_own, w_peer, vec, saved, n, r, n_x, n_z, deps):
    q, k, v, p0, p1, p2, p3, ot, o, il = saved
    pairs, own, _ = q.shape
    keys = k.shape[1]
    d = dz.shape[1]
    prows = w_own.shape[3]
    ps = (p0, p1, p2, p3)
    area = sum(p.shape[1] * p.shape[2] for p in ps)
    kv_spec = pl.BlockSpec((2, 1, own, PAIR), lambda s, _: (0, s, 0, 0))
    outs = [
        (slot_shape(n_x, n_z, 2 * prows), slot_spec(n_x, n_z, 2 * prows)),
        (slot_shape(n_x, n_z, 2 * prows), slot_spec(n_x, n_z, 2 * prows)),
        (struct((2, pairs, own, PAIR), F32), kv_spec),
        (struct((2, pairs, own, PAIR), BF), kv_spec),
        (struct((own, d), F32), full((own, d))),
        (struct((8, d), F32), full((8, d))),
        (struct((pairs, 1, PAIR), F32), pl.BlockSpec((1, 1, PAIR), lambda s, _: (s, 0, 0))),
    ]
    ins = [
        (act, whole(act)),
        (dz, whole(dz)),
        (w_own, half_spec(w_own)),
        (w_peer, half_spec(w_peer)),
        (vec, whole(vec)),
        (q, pair_spec(own), True),
        (k, pair_spec(keys), True),
        (v, pair_spec(keys), True),
        *[(p, pl.BlockSpec((1,) + p.shape[1:], lambda s, _: (s, 0, 0)), True) for p in ps],
        (ot, pl.BlockSpec((1, PAIR, own), lambda s, _: (s, 0, 0)), True),
        (o, pair_spec(own), True),
        (il, pl.BlockSpec((1, 8, own), lambda s, _: (s, 0, 0)), True),
        (n, whole(n)),
        (r, whole(r)),
    ]
    scratch = [
        pltpu.VMEM((own, d), BF),
        pltpu.VMEM((d, own), BF),
        pltpu.VMEM((d, own), BF),
        pltpu.VMEM((own, d), F32),
        pltpu.VMEM((keys, PAIR), F32),
        pltpu.VMEM((keys, PAIR), F32),
    ]
    return launch(
        functools.partial(attn_bwd, causal), "self_bwd" if causal else "cross_bwd",
        (pairs,), ranks, ins, outs, scratch, deps,
        cost=(
            2 * own * d * d * 4 + 8 * area * PAIR * pairs,
            2 * area * pairs + 16 * own * d,
            0,
        ),
    )


def run_kv_back(name, ranks, act, own_part, got, w_own, w_peer, extra, lanes, blen, n_x, n_z,
                deps):
    own, d = act.shape
    pairs = own_part.shape[1]
    prows = w_own.shape[3]
    final = bool(extra)
    rows = 2 * prows + (16 if final else 0)
    half = own // 4
    outs = [(struct((half, d), BF), full((half, d)))] * 4
    scratch = [pltpu.VMEM((d, own), BF), pltpu.VMEM((own, d), F32)]
    if final:
        outs += [(slot_shape(n_x, n_z, rows), full((2, n_x, n_z, rows, PAIR)))] * 2
        scratch += [pltpu.VMEM((pairs, 1, PAIR), F32), pltpu.VMEM((pairs, 16, PAIR), F32)]
    else:
        outs += [(slot_shape(n_x, n_z, rows), slot_spec(n_x, n_z, rows))] * 2
        outs.append(
            (struct((pairs, 1, PAIR), F32), pl.BlockSpec((1, 1, PAIR), lambda s, _: (s, 0, 0)))
        )
    ins = [
        (act, whole(act)),
        (own_part, pl.BlockSpec((2, 1, own, PAIR), lambda s, _: (0, s, 0, 0))),
        (got, pl.BlockSpec((2, 1, own, PAIR), lambda s, _: (0, s ^ 1, 0, 0))),
        (w_own, half_spec(w_own)),
        (w_peer, half_spec(w_peer)),
    ] + [(a, whole(a)) for a in extra]
    return launch(
        functools.partial(kv_back, final, lanes, blen), name, (pairs,), ranks, ins, outs,
        scratch, deps, cost=(8 * own * d * d, 20 * own * d, 0),
    )


ALL = ("dp", "ctx", "ty", "tc")


def shards(
    inputs, memory, cotangent, wq_self, wk_self, wv_self, wo_self, wq_cross, wk_cross, wv_cross,
    wo_cross, w_in, w_out, gains, shifts, ffn_bias,
):
    seqs, block, d = inputs.shape
    n_x, n_z, n_y, n_c = (lax.axis_size(a) for a in ALL)
    pairs = n_y * n_c
    half = block // n_c
    own = n_z * half
    x_rank, z_rank, y_rank, c_rank = (lax.axis_index(a) for a in ALL)
    ranks = jnp.stack([x_rank, z_rank, y_rank, c_rank, y_rank * n_c + c_rank]).astype(jnp.int32)
    prows, lanes, blen = wq_self.shape[0], gains.shape[1], ffn_bias.shape[0]
    hid = w_in.shape[1]
    x_bits = [1 << i for i in range((n_x - 1).bit_length())]

    def send(array, axis, bit):
        return lax.ppermute(array, axis, [(i, i ^ bit) for i in range(lax.axis_size(axis))])

    def rows_of(r):
        return pl.BlockSpec((1, half, d), lambda i, ref: (ref[2] * 4 + (ref[1] ^ r), ref[3], 0))

    def packed_rows(array, turns):
        return [(array, rows_of(r), True) for r in turns]

    def around_z(parts):
        return [parts[0]] + [send(parts[r], "ctx", r) for r in range(1, n_z)]

    row_part = struct((half, d), BF)
    pair_part = struct((2, half, d), BF)
    turns = range(n_z)
    xs = launch(
        pack_rows, "pack_rows", (1,), ranks, packed_rows(inputs, turns),
        [(row_part, whole(row_part))] * n_z, limit=SMALL_LIMIT,
    )
    x_got = around_z(xs)
    weights = (wq_self, wk_self, wv_self, wo_self.T, wq_cross, wk_cross, wv_cross, wo_cross.T,
               w_in, w_out.T, gains, shifts, ffn_bias.reshape(1, -1))
    s_pack, c_pack, f_pack = local(
        functools.partial(pack_weights, lanes, blen), "pack_weights",
        [struct((4 * prows + 32, PAIR), BF), struct((4 * prows, PAIR), BF),
         struct((2, prows, hid), BF)],
        *weights, ranks=ranks, deps=[xs[0]],
        scratch=[pltpu.VMEM((16, PAIR), F32), pltpu.VMEM((16, PAIR), F32)],
    )
    s_got = around_z([s_pack] * n_z)
    w_ffn = lax.all_gather(f_pack, ALL, axis=0, tiled=False).reshape(
        n_x * n_z, pairs, 2, prows, hid
    )
    cuts_s = ((0, 2 * prows), (2 * prows, 4 * prows + 32))
    cuts_c = ((0, 2 * prows), (2 * prows, 4 * prows))

    def z_slots(cuts):
        return [struct((1, 1, n_z, hi - lo, PAIR), BF) for lo, hi in cuts]

    def doubled(array, axis):
        shape = list(array.shape)
        shape[axis] *= 2
        return struct(tuple(shape), BF)

    steps_a = [("dp", bit) for bit in x_bits] + [("ty", 1)]
    steps_b = [("ty", 1)] + [("dp", bit) for bit in x_bits]
    axis_of = {"ty": 0, "dp": 1}
    axes_at = [(axis_of[sa[0]], axis_of[sb[0]]) for sa, sb in zip(steps_a, steps_b)]

    def step(i, a, b):
        return [a, send(a, *steps_a[i]), b, send(b, *steps_b[i])]

    def more(i, a, b):
        while i < len(steps_a) - 1:
            ga, gb = axes_at[i]
            a, b = local(
                functools.partial(double_both, axes_at[i]), "double",
                [doubled(a, ga), doubled(b, gb)], *step(i, a, b),
            )
            i += 1
        return a, b

    sa, sb, xo = local(
        functools.partial(start_one, cuts_s), "start_one",
        z_slots(cuts_s) + [struct((own, d), BF)], *s_got, *x_got, ranks=ranks,
    )
    xp = send(xo, "tc", 1)
    c_parts = around_z([c_pack] * n_z)
    sa, sb, ca, cb = local(
        functools.partial(start_two, axes_at[0], cuts_c), "start_two",
        [doubled(sa, axes_at[0][0]), doubled(sb, axes_at[0][1])] + z_slots(cuts_c),
        *step(0, sa, sb), *c_parts,
    )
    sa, sb = more(1, sa, sb)
    s_last = step(len(steps_a) - 1, sa, sb)
    mcs = launch(
        pack_pairs, "pack_pairs", (1,), ranks,
        packed_rows(memory, turns) + packed_rows(cotangent, turns),
        [(pair_part, whole(pair_part))] * n_z, deps=[sa], limit=SMALL_LIMIT,
    )
    mc_got = around_z(mcs)
    w_shape = struct((2, 4, n_x * n_z, prows, PAIR), BF)
    ws_own, v_own = local(
        functools.partial(assemble, lanes), "assemble",
        [w_shape, struct((pairs + 1, 16, PAIR), BF)], *s_last, ranks=ranks,
        scratch=[pltpu.VMEM((pairs + 1, 16, PAIR), F32)], deps=[mcs[0]],
    )
    ws_peer, v_peer = send(ws_own, "tc", 1), send(v_own, "tc", 1)
    ca, cb = more(0, ca, cb)
    c_last = step(len(steps_a) - 1, ca, cb)
    *saved_self, n1, r1, vec, bias = run_attn_fwd(
        True, ranks, (xo, xp), ws_own, ws_peer, (v_own, v_peer), pairs, [ca]
    )
    wc_own, mo, cot = local(
        functools.partial(start_five, lanes), "start_five",
        [w_shape, struct((own, d), BF), struct((own, d), BF)], *c_last, *mc_got,
        ranks=ranks, deps=[r1],
    )
    wc_peer = send(wc_own, "tc", 1)
    mp = send(mo, "tc", 1)
    *saved_cross, n2, r2 = run_attn_fwd(
        False, ranks, (n1, mo, mp), wc_own, wc_peer, (vec,), pairs, []
    )
    *out_rows, f_keep, f_send, dz2, vg_ffn, bg = run_ffn(ranks, n2, r2, cot, w_ffn, bias, vec)

    def home_rows(got, deps):
        (here,) = local(
            order_home, "order_home", [struct((own, d), BF)], *got, ranks=ranks, deps=deps
        )
        return here.reshape(n_z, half, d)

    def home_last(here, there, dtype, deps):
        ins = [here, there, send(here, "tc", 1), send(there, "tc", 1)]
        (result,) = launch(
            home_body, "home", (n_y,), ranks, [(a, whole(a)) for a in ins],
            [(struct((seqs, block, d), dtype),
              pl.BlockSpec((n_z, block, d), lambda y, _: (y, 0, 0)), True)],
            deps=deps, limit=2 * SMALL_LIMIT,
            cost=(seqs * block * d, 6 * seqs * block * d, 0),
        )
        return result

    back_a = [("ty", 1)] + [("dp", bit) for bit in reversed(x_bits)]
    back_b = [("dp", bit) for bit in reversed(x_bits)] + [("ty", 1)]

    def shape_at(i, rows, steps):
        shape = [2, n_x, n_z, rows, PAIR]
        for axis, _ in steps[: i + 1]:
            shape[axis_of[axis]] //= 2
        return tuple(shape)

    def halve(i, ins, cuts, rows, deps):
        shape_a, shape_b = shape_at(i, rows[0], back_a), shape_at(i, rows[1], back_b)
        to_a, keep_a, to_b, keep_b = local(
            functools.partial(
                halve_body, axis_of[back_a[i][0]], axis_of[back_b[i][0]], cuts
            ),
            "halve",
            [struct(shape_a, BF), struct(shape_a, F32), struct(shape_b, BF), struct(shape_b, F32)],
            *ins, deps=deps,
        )
        return [keep_a, send(to_a, *back_a[i]), keep_b, send(to_b, *back_b[i])]

    def halve_more(i, ins, rows, stop, deps):
        while i < stop:
            ins = halve(i, ins, (None,), rows, deps)
            i, deps = i + 1, []
        return ins

    def spread(ins, deps):
        rows = ins[0].shape[3] + ins[2].shape[3]
        *sends, keep = local(
            spread_body, "spread",
            [struct((rows, PAIR), BF)] * 3 + [struct((rows, PAIR), F32)], *ins, deps=deps,
        )
        return [keep] + [send(sends[r - 1], "ctx", r) for r in range(1, n_z)]

    def finish(ins, plan, extra, deps):
        outs = [struct((size, PAIR), F32) for turn, size in plan if turn != 2] + extra
        return local(
            functools.partial(finish_body, plan, lanes, blen), "finish", outs, *ins,
            ranks=ranks, deps=deps,
        )

    rounds = len(back_a)
    out_got = around_z(out_rows)
    f_shape = f_keep.shape
    f_block = pl.BlockSpec((f_shape[0] // 2,) + f_shape[1:], lambda i: (i, 0, 0, 0, 0))
    (f_sum,) = launch(
        add_body, "add", (2,), None,
        [(f_keep, f_block), (send(f_send, "tc", 1), f_block)], [(struct(f_shape, BF), f_block, True)],
        cost=(f_keep.size, 6 * f_keep.size, 0),
    )
    f_done = lax.psum_scatter(
        f_sum.reshape(-1, 2, prows, hid), ("dp", "ctx", "ty"), scatter_dimension=0, tiled=False
    ).astype(F32)
    c_keep, c_send, c_own, c_peer, dz1, vg_cross, qgc = run_attn_bwd(
        False, ranks, mo, dz2, wc_own, wc_peer, vec, saved_cross, n1, r1, n_x, n_z, [f_sum]
    )
    c_got, c_add = send(c_peer, "tc", 1), send(c_send, "tc", 1)
    out_here = home_rows(out_got, [dz1])
    out_there = send(out_here, "ty", 1)
    s_keep, s_send, s_own, s_peer, base, _, qgs = run_attn_bwd(
        True, ranks, xo, dz1, ws_own, ws_peer, vec, saved_self, n1, r1, n_x, n_z, [out_here]
    )
    s_got, s_add = send(s_peer, "tc", 1), send(s_send, "tc", 1)
    *mem_rows, m_keep, m_send, vgc = run_kv_back(
        "mem_back", ranks, mo, c_own, c_got, wc_own, wc_peer, (), lanes, blen, n_x, n_z, [base]
    )
    mem_got, m_add = around_z(mem_rows), send(m_send, "tc", 1)
    rows_one = (2 * prows, 2 * prows)
    rows_two = (2 * prows, 2 * prows + 16)
    one = halve(0, [c_keep, c_add, s_keep, s_add], (prows, prows), rows_one, [vgc])
    *in_rows, i_keep, i_send = run_kv_back(
        "in_back", ranks, xo, s_own, s_got, ws_own, ws_peer,
        (base, vg_cross, vg_ffn, bg, qgs, qgc, vgc), lanes, blen, n_x, n_z, [one[0]],
    )
    in_got, i_add = around_z(in_rows), send(i_send, "tc", 1)
    mem_here = home_rows(mem_got, [in_rows[0]])
    mem_there = send(mem_here, "ty", 1)
    one = halve_more(1, one, rows_one, rounds, [mem_here])
    two = halve(0, [m_keep, m_add, i_keep, i_add], (prows, prows), rows_two, [one[0]])
    one = spread(one, [two[0]])
    in_here = home_rows(in_got, [one[0]])
    in_there = send(in_here, "ty", 1)
    two = halve_more(1, two, rows_two, rounds, [in_here])
    out = home_last(out_here, out_there, BF, [two[0]])
    gqc, gqs, goc, gos = finish(one, ((0, prows),) * 4, [], [out])
    two = spread(two, [gqc])
    grad_memory = home_last(mem_here, mem_there, F32, [two[0]])
    grad_inputs = home_last(in_here, in_there, F32, [grad_memory])
    gkc, gks, gvc, gvs, g_gains, g_shifts, g_bias = finish(
        two, ((0, prows),) * 4 + ((2, 16),),
        [struct(gains.shape, F32), struct(shifts.shape, F32), struct((1, blen), F32)],
        [grad_inputs],
    )
    return (
        out, grad_inputs, grad_memory, gqs, gks, gvs, gos.T, gqc, gkc, gvc, goc.T,
        f_done[0], f_done[1].T, g_gains, g_shifts, g_bias.reshape(-1),
    )


def solution(mesh):
    sizes = mesh.devices.shape
    inner = jax.sharding.Mesh(
        mesh.devices.reshape(sizes[0], sizes[1], sizes[2] // 2, 2), ALL
    )
    rows = P("dp", "ctx", None)
    tp = ("ty", "tc")
    col = P(("dp", "ctx"), tp)
    row = P(tp, ("dp", "ctx"))
    small = P(None, ALL)
    weights = (col, col, col, row, col, col, col, row, col, row)
    tail = (small, small, P(ALL))
    return jax.shard_map(
        shards,
        mesh=inner,
        in_specs=(rows, rows, rows) + weights + tail,
        out_specs=(rows, rows, rows) + weights + tail,
        check_vma=False,
    )
```

time: 658 us -> 310 us (0.47)
  waiting for transfers between devices: 418 us -> 96.1 us
  blocking collectives: 57.9 us -> 0 us
  starting transfers between devices: 14 us -> 67.6 us
  local copies, waits for them, and re-layouts: 43.3 us -> 18.7 us
  Pallas kernels: 93.9 us -> 111 us
  other arithmetic: 14.2 us -> 0.92 us
    unnamed x9 -> x2, waiting for transfers between devices: 145 us -> 0.03 us
    reduce_scatter x1, waiting for transfers between devices: 135 us -> 0.01 us  [shards(): lax.psum_scatter(f_sum.reshape(-1, 2, prows, hid), ('dp', 'ctx', 'ty'), s...]
    all_gather x6 -> x1, waiting for transfers between devices: 102 us -> 0.01 us  [shards(): lax.all_gather(f_pack, ALL, axis=0, tiled=False)]
    ppermute x4 -> x64, waiting for transfers between devices: 5.72 us -> 96 us  [send(): lax.ppermute(array, axis, [(i, i ^ bit) for i in range(lax.axis_size(axis...]
    ppermute x4 -> x64, starting transfers between devices: 0.21 us -> 67.5 us  [send(): lax.ppermute(array, axis, [(i, i ^ bit) for i in range(lax.axis_size(axis...]
    all_to_all x3 -> x0, blocking collectives: 57.9 us -> none  [home(): lax.all_to_all(array.reshape(n_ctx, half, d), 'ctx', 0, 0, tiled=True)]
    all_to_all x3 -> x0, waiting for transfers between devices: 30.6 us -> none  [mine(): return lax.all_to_all(part, 'ctx', 0, 0, tiled=True).reshape(own, d)]
    pallas_call x7 -> x30, Pallas kernels: 93.9 us -> 111 us  [launch(): return call(*args) if ranks is None else call(ranks, *args)]
  transfers between devices with their start and end apart: 15 -> 66, of which waited for: 9 -> 23; matrix products, arithmetic and copies ran while one was open for 7% -> 0% of each run, Pallas kernels for 12% -> 30%
where the time goes in v2:
time: 310 us; the launch traced here: 309 us
  Pallas kernels  111 us (36%)
  waiting for transfers between devices  96.1 us (31%)
  starting transfers between devices  67.6 us (22%)
  local copies, waits for them, and re-layouts  18.7 us (6%)
  between operations  14.7 us (5%)
    pallas_call x30, Pallas kernels, launch(): return call(*args) if ranks is None else call(ranks, *args)  111 us
    ppermute x64, waiting for transfers between devices, send(): lax.ppermute(array, axis, [(i, i ^ bit) for i in range(lax.axis_size(axis...  96 us
    ppermute x64, starting transfers between devices, send(): lax.ppermute(array, axis, [(i, i ^ bit) for i in range(lax.axis_size(axis...  67.5 us
    unnamed x88, local copies, waits for them, and re-layouts  17.9 us
  transfers between devices with their start and end apart: 66, of which 23 were waited for; matrix products, arithmetic and copies ran while one was open for 0% of the time, Pallas kernels for 30%

profile of v2, /device:TPU:0, one launch (start us, length us, event | category | flops | bytes accessed | tf_op | source)
XLA Modules:
  0.0 309.1 jit_solution(4211262209981068199)
XLA Ops:
  10.6 5.1 %collective-permute-start.2 = (bf16[288,128]{1,0:T(8,128)(2,1)S(1)}, bf16[288,128]{1,0:T(8,128)(2,1)S(1)}, u32[]{:S(2)}, u32[]{:S(2)}) collective-permute-start(bf16[288,128]{1,0:T(8,128)(2,1)S(1)} %get-tuple-element.138.refs_0_), channel_id=1, source_target_pairs={{0,12},{4,8},{8,4},{12,0},{1,13},{5,9},{9,5},{13,1},{2,14},{6,10},... | collective-permute-start | bytes 221192 | tf_op jit(solution)/shard_map/ppermute | solution.py:884
  16.3 3.7 %collective-permute-start.5 = (bf16[128,512]{1,0:T(8,128)(2,1)S(1)}, bf16[128,512]{1,0:T(8,128)(2,1)S(1)}, u32[]{:S(2)}, u32[]{:S(2)}) collective-permute-start(bf16[128,512]{1,0:T(8,128)(2,1)S(1)} %get-tuple-element.141), channel_id=1, source_target_pairs={{0,12},{4,8},{8,4},{12,0},{1,13},{5,9},{9,5},{13,1},{2,14},{6,10},... | collective-permute-start | bytes 393224 | tf_op jit(solution)/shard_map/ppermute | solution.py:884
  20.7 14.8 %collective-permute-done.1.refs_2_ = bf16[288,128]{1,0:T(8,128)(2,1)S(1)} collective-permute-done((bf16[288,128]{1,0:T(8,128)(2,1)S(1)}, bf16[288,128]{1,0:T(8,128)(2,1)S(1)}, u32[]{:S(2)}, u32[]{:S(2)}) %collective-permute-start.1) | collective-permute-done | bytes 73760 | tf_op jit(solution)/shard_map/ppermute | solution.py:884
  39.6 2.8 collective-permute-start.11
  45.9 3.2 %collective-permute-done.10.refs_2_ = bf16[256,128]{1,0:T(8,128)(2,1)S(1)} collective-permute-done((bf16[256,128]{1,0:T(8,128)(2,1)S(1)}, bf16[256,128]{1,0:T(8,128)(2,1)S(1)}, u32[]{:S(2)}, u32[]{:S(2)}) %collective-permute-start.10) | collective-permute-done | bytes 65568 | tf_op jit(solution)/shard_map/ppermute | solution.py:884
  52.3 3.9 %collective-permute-done.12.refs_2_ = bf16[1,2,4,128,128]{4,3,2,1,0:T(8,128)(2,1)S(1)} collective-permute-done((bf16[1,2,4,128,128]{4,3,2,1,0:T(8,128)(2,1)S(1)}, bf16[1,2,4,128,128]{4,3,2,1,0:T(8,128)(2,1)S(1)}, u32[]{:S(2)}, u32[]{:S(2)}) %collective-permute-start.12) | collective-permute-done | bytes 262176 | tf_op jit(solution)/shard_map/ppermute | solution.py:884
  59.5 3.7 %collective-permute-done.16.ga = bf16[1,1,4,128,128]{4,3,2,1,0:T(8,128)(2,1)S(1)} collective-permute-done((bf16[1,1,4,128,128]{4,3,2,1,0:T(8,128)(2,1)S(1)}, bf16[1,1,4,128,128]{4,3,2,1,0:T(8,128)(2,1)S(1)}, u32[]{:S(2)}, u32[]{:S(2)}) %collective-permute-start.16) | collective-permute-done | bytes 131104 | tf_op jit(solution)/shard_map/ppermute | solution.py:884
  69.5 13.8 %self_fwd.1 = (bf16[4,512,128]{2,1,0:T(8,128)(2,1)}, bf16[4,1024,128]{2,1,0:T(8,128)(2,1)}, bf16[4,1024,128]{2,1,0:T(8,128)(2,1)}, bf16[4,256,256]{2,1,0:T(8,128...) custom-call(s32[5]{0:T(128)S(1)} %stack.23.refs_0_.ranks_ref, ...), custom_call_target="tpu_custom_call" | custom-call | flops 2952790016 | bytes 7340032 | tf_op jit(solution)/shard_map/self_fwd/pallas_call | solution.py:520
  85.1 3.7 %collective-permute-done.21.refs_7_ = bf16[2,128,512]{2,1,0:T(8,128)(2,1)S(1)} collective-permute-done((bf16[2,128,512]{2,1,0:T(8,128)(2,1)S(1)}, bf16[2,128,512]{2,1,0:T(8,128)(2,1)S(1)}, u32[]{:S(2)}, u32[]{:S(2)}) %collective-permute-start.21) | collective-permute-done | bytes 262176 | tf_op jit(solution)/shard_map/ppermute | solution.py:884
  88.8 5.2 %collective-permute-done.22.refs_8_ = bf16[2,128,512]{2,1,0:T(8,128)(2,1)S(1)} collective-permute-done((bf16[2,128,512]{2,1,0:T(8,128)(2,1)S(1)}, bf16[2,128,512]{2,1,0:T(8,128)(2,1)S(1)}, u32[]{:S(2)}, u32[]{:S(2)}) %collective-permute-start.22) | collective-permute-done | bytes 262176 | tf_op jit(solution)/shard_map/ppermute | solution.py:884
  95.3 3.2 %collective-permute-done.23.mp_ref = bf16[512,512]{1,0:T(8,128)(2,1)S(1)} collective-permute-done((bf16[512,512]{1,0:T(8,128)(2,1)S(1)}, bf16[512,512]{1,0:T(8,128)(2,1)S(1)}, u32[]{:S(2)}, u32[]{:S(2)}) %collective-permute-start.23) | collective-permute-done | bytes 524320 | tf_op jit(solution)/shard_map/ppermute | solution.py:884
  98.6 16.4 %cross_fwd.1 = (bf16[4,512,128]{2,1,0:T(8,128)(2,1)}, bf16[4,1024,128]{2,1,0:T(8,128)(2,1)}, bf16[4,1024,128]{2,1,0:T(8,128)(2,1)}, bf16[4,1024,256]{2,1,0:T(8,1...) custom-call(s32[5]{0:T(128)S(1)} %stack.23.refs_0_.ranks_ref, ...), custom_call_target="tpu_custom_call" | custom-call | flops 3758096384 | bytes 10485760 | tf_op jit(solution)/shard_map/cross_fwd/pallas_call | solution.py:520
  117.7 15.1 %ffn_both.1 = (bf16[128,512]{1,0:T(8,128)(2,1)S(1)}, bf16[128,512]{1,0:T(8,128)(2,1)S(1)}, bf16[128,512]{1,0:T(8,128)(2,1)S(1)}, bf16[128,512]{1,0:T(8,128)(2,1)...) custom-call(s32[5]{0:T(128)S(1)} %stack.23.refs_0_.ranks_ref, ...), custom_call_target="tpu_custom_call" | custom-call | flops 6442450944 | bytes 13631488 | tf_op jit(solution)/shard_map/ffn_both/pallas_call | solution.py:520
  134.1 3.9 %collective-permute-done.28.got = bf16[8,2,2,64,512]{4,3,2,1,0:T(8,128)(2,1)S(1)} collective-permute-done((bf16[8,2,2,64,512]{4,3,2,1,0:T(8,128)(2,1)S(1)}, bf16[8,2,2,64,512]{4,3,2,1,0:T(8,128)(2,1)S(1)}, u32[]{:S(2)}, u32[]{:S(2)}) %collective-permute-start.28) | collective-permute-done | bytes 2097184 | tf_op jit(solution)/shard_map/ppermute | solution.py:884
  139.6 5.1 %collective-permute-start.25 = (bf16[128,512]{1,0:T(8,128)(2,1)}, bf16[128,512]{1,0:T(8,128)(2,1)S(1)}, u32[]{:S(2)}, u32[]{:S(2)}) collective-permute-start(bf16[128,512]{1,0:T(8,128)(2,1)} %copy-done.41), channel_id=1, source_target_pairs={{0,4},{4,0},{8,12},{12,8},{1,5},{5,1},{9,13},{13,9},{2,6},{6,2},{1... | collective-permute-start | bytes 393224 | tf_op jit(solution)/shard_map/ppermute | solution.py:884
  144.7 2.4 collective-permute-start.27
  153.9 18.5 %cross_bwd.1 = (bf16[2,2,4,128,128]{4,3,2,1,0:T(8,128)(2,1)S(1)}, bf16[2,2,4,128,128]{4,3,2,1,0:T(8,128)(2,1)S(1)}, f32[2,4,512,128]{3,2,1,0:T(8,128)S(1)}, bf16...) custom-call(s32[5]{0:T(128)S(1)} %stack.23.refs_0_.ranks_ref, ...), custom_call_target="tpu_custom_call" | custom-call | flops 5368709120 | bytes 12582912 | tf_op jit(solution)/shard_map/cross_bwd/pallas_call | solution.py:520
  173.7 16.1 %self_bwd.1 = (bf16[2,2,4,128,128]{4,3,2,1,0:T(8,128)(2,1)S(1)}, bf16[2,2,4,128,128]{4,3,2,1,0:T(8,128)(2,1)S(1)}, f32[2,4,512,128]{3,2,1,0:T(8,128)S(1)}, bf16[...) custom-call(s32[5]{0:T(128)S(1)} %stack.23.refs_0_.ranks_ref, ...), custom_call_target="tpu_custom_call" | custom-call | flops 3758096384 | bytes 9437184 | tf_op jit(solution)/shard_map/self_bwd/pallas_call | solution.py:520
  191.9 5.0 %mem_back.1 = (bf16[128,512]{1,0:T(8,128)(2,1)S(1)}, bf16[128,512]{1,0:T(8,128)(2,1)S(1)}, bf16[128,512]{1,0:T(8,128)(2,1)S(1)}, bf16[128,512]{1,0:T(8,128)(2,1)...) custom-call(s32[5]{0:T(128)S(1)} %stack.23.refs_0_.ranks_ref, ...), custom_call_target="tpu_custom_call" | custom-call | flops 1073741824 | bytes 5242880 | tf_op jit(solution)/shard_map/mem_back/pallas_call | solution.py:520
  198.3 5.5 %in_back.1 = (bf16[128,512]{1,0:T(8,128)(2,1)S(1)}, bf16[128,512]{1,0:T(8,128)(2,1)S(1)}, bf16[128,512]{1,0:T(8,128)(2,1)S(1)}, bf16[128,512]{1,0:T(8,128)(2,1)S...) custom-call(s32[5]{0:T(128)S(1)} %stack.23.refs_0_.ranks_ref, ...), custom_call_target="tpu_custom_call" | custom-call | flops 1073741824 | bytes 5242880 | tf_op jit(solution)/shard_map/in_back/pallas_call | solution.py:520
  207.3 10.0 %collective-permute-done.41.refs_3_ = bf16[128,512]{1,0:T(8,128)(2,1)S(1)} collective-permute-done((bf16[128,512]{1,0:T(8,128)(2,1)S(1)}, bf16[128,512]{1,0:T(8,128)(2,1)S(1)}, u32[]{:S(2)}, u32[]{:S(2)}) %collective-permute-start.41) | collective-permute-done | bytes 131104 | tf_op jit(solution)/shard_map/ppermute | solution.py:884
  220.9 5.7 %collective-permute-done.38.refs_1_ = bf16[1,2,4,128,128]{4,3,2,1,0:T(8,128)(2,1)S(1)} collective-permute-done((bf16[1,2,4,128,128]{4,3,2,1,0:T(8,128)(2,1)S(1)}, bf16[1,2,4,128,128]{4,3,2,1,0:T(8,128)(2,1)S(1)}, u32[]{:S(2)}, u32[]{:S(2)}) %collective-permute-start.38) | collective-permute-done | bytes 262176 | tf_op jit(solution)/shard_map/ppermute | solution.py:884
  234.5 2.7 collective-permute-start.46
  239.8 7.6 %collective-permute-done.46.refs_3_ = bf16[128,512]{1,0:T(8,128)(2,1)S(1)} collective-permute-done((bf16[128,512]{1,0:T(8,128)(2,1)S(1)}, bf16[128,512]{1,0:T(8,128)(2,1)S(1)}, u32[]{:S(2)}, u32[]{:S(2)}) %collective-permute-start.46) | collective-permute-done | bytes 131104 | tf_op jit(solution)/shard_map/ppermute | solution.py:884
  253.6 2.4 collective-permute-done.58.refs_2_
  256.1 2.6 collective-permute-done.59.refs_3_
  258.7 7.3 %collective-permute-done.43.refs_1_ = bf16[1,2,4,128,128]{4,3,2,1,0:T(8,128)(2,1)S(1)} collective-permute-done((bf16[1,2,4,128,128]{4,3,2,1,0:T(8,128)(2,1)S(1)}, bf16[1,2,4,128,128]{4,3,2,1,0:T(8,128)(2,1)S(1)}, u32[]{:S(2)}, u32[]{:S(2)}) %collective-permute-start.43) | collective-permute-done | bytes 262176 | tf_op jit(solution)/shard_map/ppermute | solution.py:884
  267.0 5.6 %collective-permute-done.60.refs_4_ = bf16[256,128]{1,0:T(8,128)(2,1)S(1)} collective-permute-done((bf16[256,128]{1,0:T(8,128)(2,1)S(1)}, bf16[256,128]{1,0:T(8,128)(2,1)S(1)}, u32[]{:S(2)}, u32[]{:S(2)}) %collective-permute-start.60) | collective-permute-done | bytes 65568 | tf_op jit(solution)/shard_map/ppermute | solution.py:884
  272.6 5.0 %collective-permute-done.56.refs_1_ = bf16[1,1,4,128,128]{4,3,2,1,0:T(8,128)(2,1)S(1)} collective-permute-done((bf16[1,1,4,128,128]{4,3,2,1,0:T(8,128)(2,1)S(1)}, bf16[1,1,4,128,128]{4,3,2,1,0:T(8,128)(2,1)S(1)}, u32[]{:S(2)}, u32[]{:S(2)}) %collective-permute-start.56) | collective-permute-done | bytes 131104 | tf_op jit(solution)/shard_map/ppermute | solution.py:884
  287.1 2.4 collective-permute-start.63
  289.5 2.7 home.4.refs_5_
  294.5 2.7 home.5.refs_5_
  (223 shorter events, 86.4 us)
Async XLA Ops:
  7.2 110.5 %all-gather.3.cloned.1.call-start = ((), (), s32[]{:S(2)}) async-start(), calls=%async_computation.2 | async-start | bytes 4325376 | tf_op jit(solution)/shard_map/all_gather | solution.py:913
  10.5 290.1 %reduce-scatter.2.cloned.1.call-start = ((), (), s32[]{:S(2)}) async-start(), calls=%async_computation.1 | async-start | bytes 2228224 | tf_op jit(solution)/shard_map/reduce_scatter | solution.py:1056
  15.7 19.8 %collective-permute-start.3 = (bf16[128,512]{1,0:T(8,128)(2,1)S(1)}, bf16[128,512]{1,0:T(8,128)(2,1)S(1)}, u32[]{:S(2)}, u32[]{:S(2)}) collective-permute-start(bf16[128,512]{1,0:T(8,128)(2,1)S(1)} %get-tuple-element.139), channel_id=1, source_target_pairs={{0,4},{4,0},{8,12},{12,8},{1,5},{5,1},{9,13},{13,9},{2,6},{6,2},{1... | collective-permute-start | bytes 393224 | tf_op jit(solution)/shard_map/ppermute | solution.py:884
  15.7 19.8 %collective-permute-start.4 = (bf16[128,512]{1,0:T(8,128)(2,1)S(1)}, bf16[128,512]{1,0:T(8,128)(2,1)S(1)}, u32[]{:S(2)}, u32[]{:S(2)}) collective-permute-start(bf16[128,512]{1,0:T(8,128)(2,1)S(1)} %get-tuple-element.140), channel_id=1, source_target_pairs={{0,8},{4,12},{8,0},{12,4},{1,9},{5,13},{9,1},{13,5},{2,10},{6,14},... | collective-permute-start | bytes 393224 | tf_op jit(solution)/shard_map/ppermute | solution.py:884
  16.3 19.2 %collective-permute-start.5 = (bf16[128,512]{1,0:T(8,128)(2,1)S(1)}, bf16[128,512]{1,0:T(8,128)(2,1)S(1)}, u32[]{:S(2)}, u32[]{:S(2)}) collective-permute-start(bf16[128,512]{1,0:T(8,128)(2,1)S(1)} %get-tuple-element.141), channel_id=1, source_target_pairs={{0,12},{4,8},{8,4},{12,0},{1,13},{5,9},{9,5},{13,1},{2,14},{6,10},... | collective-permute-start | bytes 393224 | tf_op jit(solution)/shard_map/ppermute | solution.py:884
  20.1 15.4 %collective-permute-start.1 = (bf16[288,128]{1,0:T(8,128)(2,1)S(1)}, bf16[288,128]{1,0:T(8,128)(2,1)S(1)}, u32[]{:S(2)}, u32[]{:S(2)}) collective-permute-start(bf16[288,128]{1,0:T(8,128)(2,1)S(1)} %get-tuple-element.138.refs_0_), channel_id=1, source_target_pairs={{0,8},{4,12},{8,0},{12,4},{1,9},{5,13},{9,1},{13,5},{2,10},{6,14},... | collective-permute-start | bytes 221192 | tf_op jit(solution)/shard_map/ppermute | solution.py:884
  20.1 15.4 %collective-permute-start = (bf16[288,128]{1,0:T(8,128)(2,1)S(1)}, bf16[288,128]{1,0:T(8,128)(2,1)S(1)}, u32[]{:S(2)}, u32[]{:S(2)}) collective-permute-start(bf16[288,128]{1,0:T(8,128)(2,1)S(1)} %get-tuple-element.138.refs_0_), channel_id=1, source_target_pairs={{0,4},{4,0},{8,12},{12,8},{1,5},{5,1},{9,13},{13,9},{2,6},{6,2},{1... | collective-permute-start | bytes 221192 | tf_op jit(solution)/shard_map/ppermute | solution.py:884
  36.1 13.0 %collective-permute-start.8 = (bf16[1,1,4,160,128]{4,3,2,1,0:T(8,128)(2,1)S(1)}, bf16[1,1,4,160,128]{4,3,2,1,0:T(8,128)(2,1)S(1)}, u32[]{:S(2)}, u32[]{:S(2)}) collective-permute-start(bf16[1,1,4,160,128]{4,3,2,1,0:T(8,128)(2,1)S(1)} %get-tuple-element.144.b), channel_id=1, source_target_pairs={{0,2},{2,0},{1,3},{3,1},{4,6},{6,4},{5,7},{7,5},{8,10},{10,8},{9,1... | collective-permute-start | bytes 491528 | tf_op jit(solution)/shard_map/ppermute | solution.py:884
  63.1 22.0 %collective-permute-start.20 = (bf16[2,128,512]{2,1,0:T(8,128)(2,1)S(1)}, bf16[2,128,512]{2,1,0:T(8,128)(2,1)S(1)}, u32[]{:S(2)}, u32[]{:S(2)}) collective-permute-start(bf16[2,128,512]{2,1,0:T(8,128)(2,1)S(1)} %get-tuple-element.156), channel_id=1, source_target_pairs={{0,4},{4,0},{8,12},{12,8},{1,5},{5,1},{9,13},{13,9},{2,6},{6,2},{1... | collective-permute-start | bytes 786440 | tf_op jit(solution)/shard_map/ppermute | solution.py:884
  65.0 23.8 %collective-permute-start.21 = (bf16[2,128,512]{2,1,0:T(8,128)(2,1)S(1)}, bf16[2,128,512]{2,1,0:T(8,128)(2,1)S(1)}, u32[]{:S(2)}, u32[]{:S(2)}) collective-permute-start(bf16[2,128,512]{2,1,0:T(8,128)(2,1)S(1)} %get-tuple-element.157), channel_id=1, source_target_pairs={{0,8},{4,12},{8,0},{12,4},{1,9},{5,13},{9,1},{13,5},{2,10},{6,14},... | collective-permute-start | bytes 786440 | tf_op jit(solution)/shard_map/ppermute | solution.py:884
  66.4 27.7 %collective-permute-start.22 = (bf16[2,128,512]{2,1,0:T(8,128)(2,1)S(1)}, bf16[2,128,512]{2,1,0:T(8,128)(2,1)S(1)}, u32[]{:S(2)}, u32[]{:S(2)}) collective-permute-start(bf16[2,128,512]{2,1,0:T(8,128)(2,1)S(1)} %get-tuple-element.158), channel_id=1, source_target_pairs={{0,12},{4,8},{8,4},{12,0},{1,13},{5,9},{9,5},{13,1},{2,14},{6,10},... | collective-permute-start | bytes 786440 | tf_op jit(solution)/shard_map/ppermute | solution.py:884
  67.6 26.4 %collective-permute-start.19 = (bf16[2,1,4,128,128]{4,3,2,1,0:T(8,128)(2,1)S(1)}, bf16[2,1,4,128,128]{4,3,2,1,0:T(8,128)(2,1)S(1)}, u32[]{:S(2)}, u32[]{:S(2)}) collective-permute-start(bf16[2,1,4,128,128]{4,3,2,1,0:T(8,128)(2,1)S(1)} %get-tuple-element.155.refs_3_), channel_id=1, source_target_pairs={{0,16},{16,0},{1,17},{17,1},{2,18},{18,2},{3,19},{19,3},{4,20},{20... | collective-permute-start | bytes 786440 | tf_op jit(solution)/shard_map/ppermute | solution.py:884
  69.2 24.8 %collective-permute-start.18 = (bf16[1,2,4,128,128]{4,3,2,1,0:T(8,128)(2,1)S(1)}, bf16[1,2,4,128,128]{4,3,2,1,0:T(8,128)(2,1)S(1)}, u32[]{:S(2)}, u32[]{:S(2)}) collective-permute-start(bf16[1,2,4,128,128]{4,3,2,1,0:T(8,128)(2,1)S(1)} %get-tuple-element.153.refs_7_.refs_1_), channel_id=1, source_target_pairs={{0,2},{2,0},{1,3},{3,1},{4,6},{6,4},{5,7},{7,5},{8,10},{10,8},{9,1... | collective-permute-start | bytes 786440 | tf_op jit(solution)/shard_map/ppermute | solution.py:884
  139.6 32.9 %collective-permute-start.25 = (bf16[128,512]{1,0:T(8,128)(2,1)}, bf16[128,512]{1,0:T(8,128)(2,1)S(1)}, u32[]{:S(2)}, u32[]{:S(2)}) collective-permute-start(bf16[128,512]{1,0:T(8,128)(2,1)} %copy-done.41), channel_id=1, source_target_pairs={{0,4},{4,0},{8,12},{12,8},{1,5},{5,1},{9,13},{13,9},{2,6},{6,2},{1... | collective-permute-start | bytes 393224 | tf_op jit(solution)/shard_map/ppermute | solution.py:884
  144.7 27.8 %collective-permute-start.26 = (bf16[128,512]{1,0:T(8,128)(2,1)}, bf16[128,512]{1,0:T(8,128)(2,1)S(1)}, u32[]{:S(2)}, u32[]{:S(2)}) collective-permute-start(bf16[128,512]{1,0:T(8,128)(2,1)} %copy-done.40), channel_id=1, source_target_pairs={{0,8},{4,12},{8,0},{12,4},{1,9},{5,13},{9,1},{13,5},{2,10},{6,14},... | collective-permute-start | bytes 393224 | tf_op jit(solution)/shard_map/ppermute | solution.py:884
  144.7 27.8 %collective-permute-start.27 = (bf16[128,512]{1,0:T(8,128)(2,1)}, bf16[128,512]{1,0:T(8,128)(2,1)S(1)}, u32[]{:S(2)}, u32[]{:S(2)}) collective-permute-start(bf16[128,512]{1,0:T(8,128)(2,1)} %copy-done.39), channel_id=1, source_target_pairs={{0,12},{4,8},{8,4},{12,0},{1,13},{5,9},{9,5},{13,1},{2,14},{6,10},... | collective-permute-start | bytes 393224 | tf_op jit(solution)/shard_map/ppermute | solution.py:884
  172.4 19.5 %collective-permute-start.32 = (bf16[2,4,512,128]{3,2,1,0:T(8,128)(2,1)S(1)}, bf16[2,4,512,128]{3,2,1,0:T(8,128)(2,1)S(1)}, u32[]{:S(2)}, u32[]{:S(2)}) collective-permute-start(bf16[2,4,512,128]{3,2,1,0:T(8,128)(2,1)S(1)} %get-tuple-element.187), channel_id=1, source_target_pairs={{0,1},{1,0},{2,3},{3,2},{4,5},{5,4},{6,7},{7,6},{8,9},{9,8},{10,11... | collective-permute-start | bytes 3145736 | tf_op jit(solution)/shard_map/ppermute | solution.py:884
  190.4 38.2 %collective-permute-start.29 = (bf16[4,128,512]{2,1,0:T(8,128)(2,1)S(1)}, bf16[4,128,512]{2,1,0:T(8,128)(2,1)S(1)}, u32[]{:S(2)}, u32[]{:S(2)}) collective-permute-start(bf16[4,128,512]{2,1,0:T(8,128)(2,1)S(1)} %bitcast.25), channel_id=1, source_target_pairs={{0,2},{2,0},{1,3},{3,1},{4,6},{6,4},{5,7},{7,5},{8,10},{10,8},{9,1... | collective-permute-start | bytes 1572872 | tf_op jit(solution)/shard_map/ppermute | solution.py:884
  203.9 33.3 %collective-permute-start.37 = (bf16[2,2,4,144,128]{4,3,2,1,0:T(8,128)(2,1)S(1)}, bf16[2,2,4,144,128]{4,3,2,1,0:T(8,128)(2,1)S(1)}, u32[]{:S(2)}, u32[]{:S(2)}) collective-permute-start(bf16[2,2,4,144,128]{4,3,2,1,0:T(8,128)(2,1)S(1)} %get-tuple-element.215), channel_id=1, source_target_pairs={{0,1},{1,0},{2,3},{3,2},{4,5},{5,4},{6,7},{7,6},{8,9},{9,8},{10,11... | collective-permute-start | bytes 1769480 | tf_op jit(solution)/shard_map/ppermute | solution.py:884
  203.9 13.4 %collective-permute-start.41 = (bf16[128,512]{1,0:T(8,128)(2,1)S(1)}, bf16[128,512]{1,0:T(8,128)(2,1)S(1)}, u32[]{:S(2)}, u32[]{:S(2)}) collective-permute-start(bf16[128,512]{1,0:T(8,128)(2,1)S(1)} %get-tuple-element.221), channel_id=1, source_target_pairs={{0,8},{4,12},{8,0},{12,4},{1,9},{5,13},{9,1},{13,5},{2,10},{6,14},... | collective-permute-start | bytes 393224 | tf_op jit(solution)/shard_map/ppermute | solution.py:884
  205.0 14.5 %collective-permute-start.42 = (bf16[128,512]{1,0:T(8,128)(2,1)S(1)}, bf16[128,512]{1,0:T(8,128)(2,1)S(1)}, u32[]{:S(2)}, u32[]{:S(2)}) collective-permute-start(bf16[128,512]{1,0:T(8,128)(2,1)S(1)} %get-tuple-element.222), channel_id=1, source_target_pairs={{0,12},{4,8},{8,4},{12,0},{1,13},{5,9},{9,5},{13,1},{2,14},{6,10},... | collective-permute-start | bytes 393224 | tf_op jit(solution)/shard_map/ppermute | solution.py:884
  207.3 27.2 %collective-permute-start.33 = (bf16[2,2,4,128,128]{4,3,2,1,0:T(8,128)(2,1)S(1)}, bf16[2,2,4,128,128]{4,3,2,1,0:T(8,128)(2,1)S(1)}, u32[]{:S(2)}, u32[]{:S(2)}) collective-permute-start(bf16[2,2,4,128,128]{4,3,2,1,0:T(8,128)(2,1)S(1)} %get-tuple-element.200), channel_id=1, source_target_pairs={{0,1},{1,0},{2,3},{3,2},{4,5},{5,4},{6,7},{7,6},{8,9},{9,8},{10,11... | collective-permute-start | bytes 1572872 | tf_op jit(solution)/shard_map/ppermute | solution.py:884
  231.6 18.5 %collective-permute-start.30 = (bf16[4,128,512]{2,1,0:T(8,128)(2,1)S(1)}, bf16[4,128,512]{2,1,0:T(8,128)(2,1)S(1)}, u32[]{:S(2)}, u32[]{:S(2)}) collective-permute-start(bf16[4,128,512]{2,1,0:T(8,128)(2,1)S(1)} %bitcast.26), channel_id=1, source_target_pairs={{0,1},{1,0},{2,3},{3,2},{4,5},{5,4},{6,7},{7,6},{8,9},{9,8},{10,11... | collective-permute-start | bytes 1572872 | tf_op jit(solution)/shard_map/ppermute | solution.py:884
  232.8 18.3 %collective-permute-start.31 = (bf16[4,128,512]{2,1,0:T(8,128)(2,1)S(1)}, bf16[4,128,512]{2,1,0:T(8,128)(2,1)S(1)}, u32[]{:S(2)}, u32[]{:S(2)}) collective-permute-start(bf16[4,128,512]{2,1,0:T(8,128)(2,1)S(1)} %collective-permute-done.29.refs_2_), channel_id=1, source_target_pairs={{0,1},{1,0},{2,3},{3,2},{4,5},{5,4},{6,7},{7,6},{8,9},{9,8},{10,11... | collective-permute-start | bytes 1572872 | tf_op jit(solution)/shard_map/ppermute | solution.py:884
  233.6 19.4 %collective-permute-start.53 = (bf16[4,128,512]{2,1,0:T(8,128)(2,1)S(1)}, bf16[4,128,512]{2,1,0:T(8,128)(2,1)S(1)}, u32[]{:S(2)}, u32[]{:S(2)}) collective-permute-start(bf16[4,128,512]{2,1,0:T(8,128)(2,1)S(1)} %bitcast.29), channel_id=1, source_target_pairs={{0,2},{2,0},{1,3},{3,1},{4,6},{6,4},{5,7},{7,5},{8,10},{10,8},{9,1... | collective-permute-start | bytes 1572872 | tf_op jit(solution)/shard_map/ppermute | solution.py:884
  247.9 18.0 %collective-permute-start.50 = (bf16[4,128,512]{2,1,0:T(8,128)(2,1)S(1)}, bf16[4,128,512]{2,1,0:T(8,128)(2,1)S(1)}, u32[]{:S(2)}, u32[]{:S(2)}) collective-permute-start(bf16[4,128,512]{2,1,0:T(8,128)(2,1)S(1)} %bitcast.32), channel_id=1, source_target_pairs={{0,2},{2,0},{1,3},{3,1},{4,6},{6,4},{5,7},{7,5},{8,10},{10,8},{9,1... | collective-permute-start | bytes 1572872 | tf_op jit(solution)/shard_map/ppermute | solution.py:884
  249.1 16.8 %collective-permute-start.43 = (bf16[1,2,4,128,128]{4,3,2,1,0:T(8,128)(2,1)S(1)}, bf16[1,2,4,128,128]{4,3,2,1,0:T(8,128)(2,1)S(1)}, u32[]{:S(2)}, u32[]{:S(2)}) collective-permute-start(bf16[1,2,4,128,128]{4,3,2,1,0:T(8,128)(2,1)S(1)} %get-tuple-element.226), channel_id=1, source_target_pairs={{0,2},{2,0},{1,3},{3,1},{4,6},{6,4},{5,7},{7,5},{8,10},{10,8},{9,1... | collective-permute-start | bytes 786440 | tf_op jit(solution)/shard_map/ppermute | solution.py:884
  250.0 16.4 %collective-permute-start.44 = (bf16[2,1,4,144,128]{4,3,2,1,0:T(8,128)(2,1)S(1)}, bf16[2,1,4,144,128]{4,3,2,1,0:T(8,128)(2,1)S(1)}, u32[]{:S(2)}, u32[]{:S(2)}) collective-permute-start(bf16[2,1,4,144,128]{4,3,2,1,0:T(8,128)(2,1)S(1)} %get-tuple-element.228), channel_id=1, source_target_pairs={{0,16},{16,0},{1,17},{17,1},{2,18},{18,2},{3,19},{19,3},{4,20},{20... | collective-permute-start | bytes 884744 | tf_op jit(solution)/shard_map/ppermute | solution.py:884
  256.1 31.0 %collective-permute-start.54 = (bf16[4,128,512]{2,1,0:T(8,128)(2,1)S(1)}, bf16[4,128,512]{2,1,0:T(8,128)(2,1)S(1)}, u32[]{:S(2)}, u32[]{:S(2)}) collective-permute-start(bf16[4,128,512]{2,1,0:T(8,128)(2,1)S(1)} %bitcast.30), channel_id=1, source_target_pairs={{0,1},{1,0},{2,3},{3,2},{4,5},{5,4},{6,7},{7,6},{8,9},{9,8},{10,11... | collective-permute-start | bytes 1572872 | tf_op jit(solution)/shard_map/ppermute | solution.py:884
  258.7 28.4 %collective-permute-start.55 = (bf16[4,128,512]{2,1,0:T(8,128)(2,1)S(1)}, bf16[4,128,512]{2,1,0:T(8,128)(2,1)S(1)}, u32[]{:S(2)}, u32[]{:S(2)}) collective-permute-start(bf16[4,128,512]{2,1,0:T(8,128)(2,1)S(1)} %collective-permute-done.53.refs_2_), channel_id=1, source_target_pairs={{0,1},{1,0},{2,3},{3,2},{4,5},{5,4},{6,7},{7,6},{8,9},{9,8},{10,11... | collective-permute-start | bytes 1572872 | tf_op jit(solution)/shard_map/ppermute | solution.py:884
  266.0 26.3 %collective-permute-start.51 = (bf16[4,128,512]{2,1,0:T(8,128)(2,1)S(1)}, bf16[4,128,512]{2,1,0:T(8,128)(2,1)S(1)}, u32[]{:S(2)}, u32[]{:S(2)}) collective-permute-start(bf16[4,128,512]{2,1,0:T(8,128)(2,1)S(1)} %bitcast.33), channel_id=1, source_target_pairs={{0,1},{1,0},{2,3},{3,2},{4,5},{5,4},{6,7},{7,6},{8,9},{9,8},{10,11... | collective-permute-start | bytes 1572872 | tf_op jit(solution)/shard_map/ppermute | solution.py:884
  266.0 26.3 %collective-permute-start.52 = (bf16[4,128,512]{2,1,0:T(8,128)(2,1)S(1)}, bf16[4,128,512]{2,1,0:T(8,128)(2,1)S(1)}, u32[]{:S(2)}, u32[]{:S(2)}) collective-permute-start(bf16[4,128,512]{2,1,0:T(8,128)(2,1)S(1)} %collective-permute-done.50.refs_2_), channel_id=1, source_target_pairs={{0,1},{1,0},{2,3},{3,2},{4,5},{5,4},{6,7},{7,6},{8,9},{9,8},{10,11... | collective-permute-start | bytes 1572872 | tf_op jit(solution)/shard_map/ppermute | solution.py:884
  (78 other events, 505.5 us)
Sparse Core Ops, SparseCore 0:
  11.5 87.0 all-gather.2
  139.7 85.6 reduce-scatter.1

commit v3 on v2

v3 whole, which is shorter than its diff:
```python
import functools

import jax
import jax.numpy as jnp
from jax import lax
from jax.experimental import pallas as pl
from jax.experimental.pallas import tpu as pltpu
from jax.sharding import PartitionSpec as P

HD = 64
EPS = 1e-05
BF = jnp.bfloat16
F32 = jnp.float32
PAIR = 2 * HD
VMEM_LIMIT = 40 << 20
SMALL_LIMIT = 16 << 20
SMALL_COST = 1_000_000_000
COVER = 10 * SMALL_COST
COSTS = dict(
    self_fwd=24_000_000_000, cross_fwd=28_000_000_000, ffn_both=25_000_000_000,
    cross_bwd=30_000_000_000, self_bwd=16_000_000_000, mem_back=9_000_000_000,
    in_back=9_000_000_000,
)
GELU_C = 0.7978845608028654
GELU_A = 0.044715


def nn(left, right):
    return lax.dot_general(left, right, (((1,), (0,)), ((), ())), preferred_element_type=F32)


def nt(left, right):
    return lax.dot_general(left, right, (((1,), (1,)), ((), ())), preferred_element_type=F32)


def norm_stats(z):
    mean = jnp.mean(z, axis=-1, keepdims=True)
    cent = z - mean
    var = jnp.mean(cent * cent, axis=-1, keepdims=True)
    inv = lax.rsqrt(var + EPS)
    return cent * inv, inv


def norm_back(grad, gain, normed, inv):
    e = grad * gain
    me = jnp.mean(e, axis=-1, keepdims=True)
    men = jnp.mean(e * normed, axis=-1, keepdims=True)
    return inv * (e - me - normed * men)


def rows_sum(a):
    return jnp.sum(a, axis=0, keepdims=True)


def split_pair(block):
    lane = lax.broadcasted_iota(jnp.int32, block.shape, 1)
    zero = jnp.zeros_like(block)
    return jnp.concatenate(
        [jnp.where(lane < HD, block, zero), jnp.where(lane < HD, zero, block)], axis=0
    )


def join_pair(both):
    q = both.shape[1] // 2
    row = lax.broadcasted_iota(jnp.int32, (both.shape[0], q), 0)
    return jnp.where(row < HD, both[:, :q], both[:, q:])


def vrow(vec_ref, row):
    return jnp.concatenate([vec_ref[j, row : row + 1] for j in range(vec_ref.shape[0])], axis=1)


def swap(pair):
    return (pair % 2) * 2 + pair // 2


def pick(own_ref, peer_ref, mat, other_half):
    shape = own_ref.shape
    own = own_ref[0, mat].reshape(shape[2] * shape[3], shape[4])
    other = peer_ref[0, mat].reshape(shape[2] * shape[3], shape[4])
    return jnp.where(other_half, other, own)


def put_pieces(ref, at, first, value, ranks_ref):
    n_x, n_z = ref.shape[1], ref.shape[2]
    rows = value.shape[0] // (n_x * n_z)
    for d in range(n_x):
        for z in range(n_z):
            i = d * n_z + z
            ref[at, d ^ ranks_ref[0], z ^ ranks_ref[1], first : first + rows] = value[
                i * rows : (i + 1) * rows
            ]


def attn_fwd_body(
    causal, q_rows, kv_parts, w, biases,
    q_ref, k_ref, v_ref, p_refs, ot_ref, o_ref, il_ref, acc_ref,
):
    wq, wk, wv, wo = w
    kv = nn(kv_parts, jnp.concatenate([wk, wv], axis=1))
    k = kv[:, :PAIR].astype(BF)
    v = (kv[:, PAIR:] + biases[1]).astype(BF)
    q = (nn(q_rows, wq) + biases[0]).astype(BF) * HD ** (-0.5)
    q_ref[0] = q
    k_ref[0] = k
    v_ref[0] = v
    vt = v.T
    blocks = len(p_refs)
    rows = q.shape[0] // blocks
    keys = k.shape[0]
    for b in range(blocks):
        n = keys // blocks * (b + 1) if causal else keys
        s = nt(k[:n], split_pair(q[b * rows : (b + 1) * rows]))
        top = jnp.max(s, axis=0, keepdims=True)
        p = jnp.exp(s - top)
        inv = 1.0 / jnp.sum(p, axis=0, keepdims=True)
        pb = p.astype(BF)
        p_refs[b][0] = pb
        ot = join_pair(nn(vt[:, :n], pb) * inv)
        span = slice(b * rows, (b + 1) * rows)
        ot_ref[0, :, span] = ot.astype(BF)
        o_ref[0, span, :] = ot.T.astype(BF)
        il_ref[0, 0:1, span] = inv[:, :rows]
        il_ref[0, 1:2, span] = inv[:, rows:]
    acc_ref[...] += nt(o_ref[0], wo)


def finish_norm(acc_ref, n_ref, r_ref):
    normed, inv = norm_stats(acc_ref[...])
    n_ref[...] = normed
    r_ref[...] = jnp.broadcast_to(inv, r_ref.shape)


def self_fwd(ranks_ref, xo_ref, xp_ref, wa_ref, wb_ref, va_ref, vb_ref, *refs):
    saved, (n_ref, r_ref, vec_ref, bias_ref, x_all, acc_ref) = refs[:10], refs[10:]
    q_ref, k_ref, v_ref, *p_refs, ot_ref, o_ref, il_ref = saved
    s = pl.program_id(0)
    blocks = 4
    half = xo_ref.shape[0] // blocks
    tiles = vec_ref.shape[0]

    @pl.when(s == 0)
    def _():
        for b in range(blocks):
            x_all[2 * b * half : (2 * b + 1) * half] = xo_ref[b * half : (b + 1) * half]
            x_all[(2 * b + 1) * half : (2 * b + 2) * half] = xp_ref[b * half : (b + 1) * half]
        both = va_ref[...].astype(F32) + vb_ref[...].astype(F32)
        vec_ref[...] = both[:tiles]
        bias_ref[...] = both[tiles]
        acc_ref[...] = xo_ref[...].astype(F32) + vrow(vec_ref, 5)

    w = [pick(wa_ref, wb_ref, i, s >= 2) for i in range(4)]
    t = swap(s) ^ ranks_ref[4]
    attn_fwd_body(True, xo_ref[...], x_all[...], w, (vec_ref[t, 3:4], vec_ref[t, 4:5]),
                  q_ref, k_ref, v_ref, p_refs, ot_ref, o_ref, il_ref, acc_ref)

    @pl.when(s == pl.num_programs(0) - 1)
    def _():
        finish_norm(acc_ref, n_ref, r_ref)


def cross_fwd(ranks_ref, n1_ref, mo_ref, mp_ref, wa_ref, wb_ref, vec_ref, *refs):
    saved, (n_ref, r_ref, m_all, h_low, acc_ref) = refs[:10], refs[10:]
    q_ref, k_ref, v_ref, *p_refs, ot_ref, o_ref, il_ref = saved
    s = pl.program_id(0)
    half = mo_ref.shape[0]

    @pl.when(s == 0)
    def _():
        m_all[:half] = mo_ref[...]
        m_all[half:] = mp_ref[...]
        h1 = n1_ref[...] * vrow(vec_ref, 0) + vrow(vec_ref, 6)
        h_low[...] = h1.astype(BF)
        acc_ref[...] = h1 + vrow(vec_ref, 9)

    w = [pick(wa_ref, wb_ref, i, s >= 2) for i in range(4)]
    t = swap(s) ^ ranks_ref[4]
    attn_fwd_body(False, h_low[...], m_all[...], w, (vec_ref[t, 7:8], vec_ref[t, 8:9]),
                  q_ref, k_ref, v_ref, p_refs, ot_ref, o_ref, il_ref, acc_ref)

    @pl.when(s == pl.num_programs(0) - 1)
    def _():
        finish_norm(acc_ref, n_ref, r_ref)


def ffn_both(ranks_ref, n2_ref, r2_ref, c0, c1, c2, c3, w_ref, bias_ref, vec_ref,
             h0, h1, h2, h3, keep_ref, send_ref, dz2_ref, vg_ref, bg_ref,
             h_low, h_t, act, slope, acc, dz3_low, dz3_t, dh2):
    phase = pl.program_id(0)
    t = pl.program_id(1)
    d = n2_ref.shape[1]
    last = pl.num_programs(1) - 1
    w_in = w_ref[:, 0, 0].reshape(d, -1)
    w_out = w_ref[:, 0, 1].reshape(d, -1)
    hid = w_in.shape[1]
    strips = hid // PAIR

    @pl.when((phase == 0) & (t == 0))
    def _():
        h = n2_ref[...] * vrow(vec_ref, 1) + vrow(vec_ref, 10)
        h_low[...] = h.astype(BF)
        h_t[...] = h.astype(BF).T
        acc[...] = h + vrow(vec_ref, 11)

    @pl.when(phase == 0)
    def _():
        bias = jnp.concatenate(
            [bias_ref[pl.ds(t * strips + j, 1), :] for j in range(strips)], axis=1
        )
        u = nn(h_low[...], w_in) + bias
        cube = GELU_A * u * u
        th = jnp.tanh(GELU_C * u * (1.0 + cube))
        low = 0.5 * (1.0 + th)
        f = (u * low).astype(BF)
        act[t] = f
        slope[t] = low + 0.5 * u * (1.0 - th * th) * (GELU_C * (1.0 + 3.0 * cube))
        acc[...] += nt(f, w_out)

    @pl.when((phase == 0) & (t == last))
    def _():
        n3, r3 = norm_stats(acc[...])
        acc[...] = n3 * vrow(vec_ref, 2) + vrow(vec_ref, 12)
        put_home(acc, (h0, h1, h2, h3), ranks_ref)
        for r, ref in enumerate((c0, c1, c2, c3)):
            rows = ref.shape[0]
            at = pl.multiple_of((r ^ ranks_ref[1]) * rows, rows)
            dh2[pl.ds(at, rows), :] = ref[...].astype(F32)
        g = dh2[...]
        vg_ref[0:1] = rows_sum(g * n3)
        vg_ref[1:2] = rows_sum(g)
        dz3 = norm_back(g, vrow(vec_ref, 2), n3, r3)
        vg_ref[2:3] = rows_sum(dz3)
        low = dz3.astype(BF)
        dz3_low[...] = low
        dz3_t[...] = low.T
        dh2[...] = dz3

    @pl.when(phase == 1)
    def _():
        f = act[t]
        df = nn(dz3_low[...], w_out).astype(BF).astype(F32)
        du = (df * slope[t]).astype(BF)
        g_out = nn(dz3_t[...], f).astype(BF)
        g_in = nn(h_t[...], du).astype(BF)
        sums = rows_sum(du.astype(F32))
        for j in range(strips):
            bg_ref[pl.ds(t * strips + j, 1), :] = sums[:, j * PAIR : (j + 1) * PAIR]
        dh2[...] += nt(du, w_in)
        mine = t % 2 == ranks_ref[3]
        piece = keep_ref.shape[3] // 2

        @pl.when(mine)
        def _():
            put_pieces(keep_ref, 0, 0, g_in, ranks_ref)
            put_pieces(keep_ref, 0, piece, g_out, ranks_ref)

        @pl.when(jnp.logical_not(mine))
        def _():
            put_pieces(send_ref, 0, 0, g_in, ranks_ref)
            put_pieces(send_ref, 0, piece, g_out, ranks_ref)

    @pl.when((phase == 1) & (t == last))
    def _():
        g = dh2[...]
        n2 = n2_ref[...]
        vg_ref[3:4] = rows_sum(g * n2)
        vg_ref[4:5] = rows_sum(g)
        dz2 = norm_back(g, vrow(vec_ref, 1), n2, r2_ref[:, 0:1])
        vg_ref[5:6] = rows_sum(dz2)
        vg_ref[6:8] = jnp.zeros_like(vg_ref[6:8])
        dz2_ref[...] = dz2


def put_home(acc, refs, ranks_ref):
    rows = refs[0].shape[0]
    for r, ref in enumerate(refs):
        at = pl.multiple_of((r ^ ranks_ref[1]) * rows, rows)
        ref[...] = acc[pl.ds(at, rows), :].astype(BF)


def self_bwd(ranks_ref, act_ref, dz_ref, part_ref, w_ref, *refs):
    saved, (slot_ref, own_ref, peer_ref, out_ref, qg_ref, *scratch) = refs[:10], refs[10:]
    shape = w_ref.shape
    w = [w_ref[0, i].reshape(shape[2] * shape[3], shape[4]) for i in (0, 3)]

    def first():
        dz = dz_ref[...]
        return act_ref[...].T, dz, part_ref[...]

    def store(g_q, g_o, piece):
        put_pieces(slot_ref, 0, 0, g_q, ranks_ref)
        put_pieces(slot_ref, 0, piece, g_o, ranks_ref)

    def last(total):
        out_ref[...] = total

    attn_bwd(True, first, w, saved, store, last, slot_ref.shape[3] // 2,
             own_ref, peer_ref, qg_ref, *scratch)


def cross_bwd(ranks_ref, n_ref, r_ref, dz_ref, wa_ref, wb_ref, vec_ref, *refs):
    saved = refs[:10]
    keep_ref, send_ref, own_ref, peer_ref, out_ref, vg_ref, qg_ref, *scratch = refs[10:]
    s = pl.program_id(0)
    odd = s >= 2

    def first():
        h = n_ref[...] * vrow(vec_ref, 0) + vrow(vec_ref, 6)
        dz = dz_ref[...]
        return h.astype(BF).T, dz, dz

    def store(g_q, g_o, piece):
        @pl.when(jnp.logical_not(odd))
        def _():
            put_pieces(keep_ref, 0, 0, g_q, ranks_ref)
            put_pieces(keep_ref, 0, piece, g_o, ranks_ref)

        @pl.when(odd)
        def _():
            put_pieces(send_ref, 0, 0, g_q, ranks_ref)
            put_pieces(send_ref, 0, piece, g_o, ranks_ref)

    def last(g):
        normed = n_ref[...]
        vg_ref[0:1] = rows_sum(g * normed)
        vg_ref[1:2] = rows_sum(g)
        dz1 = norm_back(g, vrow(vec_ref, 0), normed, r_ref[:, 0:1])
        vg_ref[2:3] = rows_sum(dz1)
        vg_ref[3:8] = jnp.zeros_like(vg_ref[3:8])
        out_ref[...] = dz1

    w = [pick(wa_ref, wb_ref, i, odd) for i in (0, 3)]
    attn_bwd(False, first, w, saved, store, last, keep_ref.shape[3] // 2,
             own_ref, peer_ref, qg_ref, *scratch)


def attn_bwd(causal, first, w, saved, store, last, piece, own_ref, peer_ref, qg_ref,
             dy, dy_t, act_t, acc, dk_ref, dv_ref):
    s = pl.program_id(0)
    q_ref, k_ref, v_ref, p0, p1, p2, p3, ot_ref, o_ref, il_ref = saved
    p_refs = (p0, p1, p2, p3)
    blocks = len(p_refs)
    wq, wo = w

    @pl.when(s == 0)
    def _():
        act_t[...], dz, acc[...] = first()
        low = dz.astype(BF)
        dy[...] = low
        dy_t[...] = low.T

    q = q_ref[0]
    k = k_ref[0]
    v = v_ref[0]
    keys = k.shape[0]
    rows = q.shape[0] // blocks
    do = nn(dy[...], wo).astype(BF)
    g_o = nn(dy_t[...], o_ref[0]).astype(BF)
    do_t = do.T.astype(F32)
    prod = do_t * ot_ref[0].astype(F32)
    inv_a, inv_b = il_ref[0, 0:1], il_ref[0, 1:2]
    inner_a = jnp.sum(prod[:HD], axis=0, keepdims=True) * inv_a
    inner_b = jnp.sum(prod[HD:], axis=0, keepdims=True) * inv_b
    row = lax.broadcasted_iota(jnp.int32, do_t.shape, 0)
    dos = (do_t * jnp.where(row < HD, inv_a, inv_b)).astype(BF).T
    kt = k.T
    dqs = [None] * blocks
    for b in reversed(range(blocks)):
        n = keys // blocks * (b + 1) if causal else keys
        span = slice(b * rows, (b + 1) * rows)
        dob = split_pair(dos[span])
        qb = split_pair(q[span])
        pb = p_refs[b][0]
        dp = nt(v[:n], dob)
        inner = jnp.concatenate([inner_a[:, span], inner_b[:, span]], axis=1)
        ds = (pb.astype(F32) * (dp - inner)).astype(BF)
        dv = nn(pb, dob)
        dk = nn(ds, qb)
        if b == blocks - 1:
            dv_ref[...] = dv
            dk_ref[...] = dk
        else:
            dv_ref[:n] += dv
            dk_ref[:n] += dk
        dqs[b] = (join_pair(nn(kt[:, :n], ds)) * HD ** (-0.5)).T.astype(BF)
    dq = jnp.concatenate(dqs, axis=0)
    g_q = nn(act_t[...], dq).astype(BF)
    store(g_q, g_o, piece)
    qg_ref[0] = rows_sum(dq.astype(F32))
    acc[...] += nt(dq, wq)
    for i, ref in enumerate((dk_ref, dv_ref)):
        if causal:
            for b in range(blocks):
                at = 2 * b * rows
                own_ref[i, 0, b * rows : (b + 1) * rows] = ref[at : at + rows]
                peer_ref[i, 0, b * rows : (b + 1) * rows] = ref[at + rows : at + 2 * rows].astype(BF)
        else:
            own_ref[i, 0] = ref[: keys // 2]
            peer_ref[i, 0] = ref[keys // 2 :].astype(BF)

    @pl.when(s == pl.num_programs(0) - 1)
    def _():
        last(acc[...])


def kv_back(final, lanes, blen, ranks_ref, act_ref, wa_ref, wb_ref, *rest):
    if final:
        (own_ref, got_ref, own_hi, got_hi, base_ref, vgc_ref, vgf_ref, bg_ref, qgs_ref, qgs_hi,
         qgc_ref, vg_mem_ref,
         h0, h1, h2, h3, keep_ref, send_ref, act_t, acc, vg_self, tiles) = rest
    else:
        own_ref, got_ref, h0, h1, h2, h3, keep_ref, send_ref, vgrad_ref, act_t, acc = rest
    s = pl.program_id(0)
    odd = s >= 2
    wk = pick(wa_ref, wb_ref, 1, odd)
    wv = pick(wa_ref, wb_ref, 2, odd)

    @pl.when(s == 0)
    def _():
        act_t[...] = act_ref[...].T
        if final:
            acc[...] = base_ref[...]
        else:
            acc[...] = jnp.zeros_like(acc)

    dk, dv = (own_ref[i, 0] + got_ref[i, 0].astype(F32) for i in range(2))
    if final:
        dk = jnp.where(odd, own_hi[0, 0] + got_hi[0, 0].astype(F32), dk)
        dv = jnp.where(odd, own_hi[1, 0] + got_hi[1, 0].astype(F32), dv)
    dk, dv = dk.astype(BF), dv.astype(BF)
    dkv = jnp.concatenate([dk, dv], axis=1)
    gkv = nn(act_t[...], dkv).astype(BF)
    piece = gkv.shape[0] // (keep_ref.shape[1] * keep_ref.shape[2])
    at = s % 2 if final else 0

    @pl.when(jnp.logical_not(odd))
    def _():
        put_pieces(keep_ref, at, 0, gkv[:, :PAIR], ranks_ref)
        put_pieces(keep_ref, at, piece, gkv[:, PAIR:], ranks_ref)

    @pl.when(odd)
    def _():
        put_pieces(send_ref, at, 0, gkv[:, :PAIR], ranks_ref)
        put_pieces(send_ref, at, piece, gkv[:, PAIR:], ranks_ref)

    sums = rows_sum(dv.astype(F32))
    acc[...] += nt(dkv, jnp.concatenate([wk, wv], axis=1))
    if not final:
        vgrad_ref[0] = sums
    else:
        vg_self[s] = sums
        pairs = vg_self.shape[0]

        @pl.when(s == 0)
        def _():
            for j in range(pairs):
                at = slice(j * PAIR, (j + 1) * PAIR)
                rel = swap(j ^ ranks_ref[4])
                tiles[j, 0:1] = vgc_ref[0:1, at]
                tiles[j, 1:2] = vgf_ref[3:4, at]
                tiles[j, 2:3] = vgf_ref[0:1, at]
                tiles[j, 3:4] = jnp.where(rel < 2, qgs_ref[rel % 2], qgs_hi[rel % 2])
                tiles[j, 5:6] = vgc_ref[2:3, at]
                tiles[j, 6:7] = vgc_ref[1:2, at]
                tiles[j, 7:8] = qgc_ref[rel]
                tiles[j, 8:9] = vg_mem_ref[rel]
                tiles[j, 9:10] = vgf_ref[5:6, at]
                tiles[j, 10:11] = vgf_ref[4:5, at]
                tiles[j, 11:12] = vgf_ref[2:3, at]
                tiles[j, 12:13] = vgf_ref[1:2, at]
                tiles[j, 13:16] = jnp.zeros((3, PAIR), F32)

        tiles[swap(s) ^ ranks_ref[4], 4:5] = sums
        rows_at = lax.broadcasted_iota(jnp.int32, (16, PAIR), 0)
        n_x, n_z = keep_ref.shape[1], keep_ref.shape[2]

        @pl.when(s == pairs - 1)
        def _():
            for ry in range(2):
                for rc, ref in enumerate((keep_ref, send_ref)):
                    for i in range(n_x):
                        for k in range(n_z):
                            dc = (i ^ ranks_ref[0]) * n_z + (k ^ ranks_ref[1])
                            p = dc * pairs + ((2 * ry + rc) ^ ranks_ref[4])
                            tile = tiles[lax.div(p * lanes, PAIR)]
                            bias = bg_ref[pl.ds(lax.div(p * blen, PAIR), 1), :]
                            both = jnp.where(rows_at == 13, bias, tile).astype(BF)
                            ref[ry, i, k, 2 * piece : 2 * piece + 16] = both

    @pl.when(s == pl.num_programs(0) - 1)
    def _():
        put_home(acc, (h0, h1, h2, h3), ranks_ref)


def pack_rows(*refs):
    ins, outs = refs[1 : 1 + len(refs) // 2], refs[1 + len(refs) // 2 :]
    for ref, out in zip(ins, outs):
        out[...] = ref[0]


def pack_rest(*refs):
    ins, (win, wout), outs, f_ref = refs[1:9], refs[9:11], refs[11:19], refs[19]
    for ref, out in zip(ins, outs):
        out[...] = ref[0]
    f_ref[0] = win[...]
    f_ref[1] = wout[...]


def pack_weights(lanes, blen, ranks_ref, wqs, wks, wvs, wos, wqc, wkc, wvc, woc,
                 gains, shifts, bias, s_ref, c_ref, va, vb):
    n = wqs.shape[0]
    for i, ref in enumerate((wqc, wkc, wvc, woc)):
        c_ref[i * n : (i + 1) * n] = ref[...]
    for i, ref in enumerate((wqs, wks, wvs, wos)):
        s_ref[i * n : (i + 1) * n] = ref[...]
    p = (ranks_ref[0] * 4 + ranks_ref[1]) * 4 + ranks_ref[4]
    at = 4 * n
    va[...] = jnp.zeros_like(va)
    va[0:3, 0:lanes] = gains[...].astype(F32)
    va[3:13, 0:lanes] = shifts[...].astype(F32)
    s_ref[at : at + 16] = pltpu.roll(va[...], lax.rem(p * lanes, PAIR), 1).astype(BF)
    vb[...] = jnp.zeros_like(vb)
    vb[pl.ds(lax.div(p * blen, PAIR), 1), 0:blen] = bias[...].astype(F32)
    s_ref[at + 16 : at + 32] = pltpu.roll(vb[...], lax.rem(p * blen, PAIR), 1).astype(BF)


def whole(a):
    return pl.BlockSpec(a.shape, lambda *_: (0,) * len(a.shape))


def without(body, at, count):
    return lambda *refs: body(*refs[:at], *refs[at + count :])


def launch(body, name, grid, ranks, ins, outs, scratch=(), deps=(), limit=VMEM_LIMIT, cost=SMALL_COST):
    first = 0 if ranks is None else 1
    deps = list(deps)
    n_in, n_out = first + len(ins), len(outs)

    def with_token(*refs):
        kept = refs[:n_in] + refs[n_in + len(deps) :]
        kept[n_in + n_out][...] = jnp.zeros((8, PAIR), F32)
        body(*kept[: n_in + n_out], *kept[n_in + n_out + 1 :])

    token = struct((8, PAIR), F32)
    call = pl.pallas_call(
        with_token,
        grid_spec=pltpu.PrefetchScalarGridSpec(
            num_scalar_prefetch=first,
            grid=grid,
            in_specs=[i[1] for i in ins] + [pl.BlockSpec(memory_space=pl.ANY)] * len(deps),
            out_specs=tuple(o[1] for o in outs) + (whole(token),),
            scratch_shapes=list(scratch),
        ),
        out_shape=tuple(
            pltpu.HBM(o[0].shape, o[0].dtype) if len(o) > 2 else o[0] for o in outs
        ) + (token,),
        compiler_params=pltpu.CompilerParams(
            vmem_limit_bytes=limit, dimension_semantics=("arbitrary",) * len(grid)
        ),
        cost_estimate=pl.CostEstimate(flops=cost, bytes_accessed=1, transcendentals=0),
        name=name,
    )
    args = [
        pltpu.with_memory_space_constraint(i[0], pltpu.HBM) if len(i) > 2 else i[0] for i in ins
    ] + deps
    return call(*args) if ranks is None else call(ranks, *args)


def local(body, name, outs, *ins, ranks=None, scratch=(), deps=(), pinned=(), limit=SMALL_LIMIT,
          cost=SMALL_COST):
    return launch(
        body, name, (1,), ranks, [(a, whole(a)) for a in ins],
        [(o, whole(o), True) if i in pinned else (o, whole(o)) for i, o in enumerate(outs)],
        scratch, deps, limit, cost,
    )


def struct(shape, dtype):
    return jax.ShapeDtypeStruct(shape, dtype)


def restack(ins, outs, cuts):
    for out, (lo, hi) in zip(outs, cuts):
        for r, ref in enumerate(ins):
            out[0, 0, r] = ref[lo:hi]


def double(own, got, out, axis):
    m = own.shape[axis]
    if axis == 0:
        out[:m] = own[...]
        out[m:] = got[...]
    else:
        out[:, :m] = own[...]
        out[:, m:] = got[...]


def order(ranks_ref, parts, outs):
    for r, ref in enumerate(parts):
        rows = ref.shape[-2]
        at = pl.multiple_of((r ^ ranks_ref[1]) * rows, rows)
        for i, out in enumerate(outs):
            out[pl.ds(at, rows), :] = ref[...] if len(outs) == 1 else ref[i]


def assemble(lanes, ranks_ref, a0, a1, b0, b1, w_ref, v_ref=None, scr=None):
    pairs = 4
    n_x, n_z = a0.shape[1], a0.shape[2]
    prows = w_ref.shape[3]
    if v_ref is not None:
        scr[...] = jnp.zeros_like(scr)
    for ry in range(2):
        a_ref = (a0, a1)[ry]
        for i in range(n_x):
            for k in range(n_z):
                dc = (i ^ ranks_ref[0]) * n_z + (k ^ ranks_ref[1])
                b_ref, bi = (b0, i) if i < n_x // 2 else (b1, i - n_x // 2)
                for m in range(2):
                    span = slice(m * prows, (m + 1) * prows)
                    w_ref[ry, m, dc] = a_ref[0, i, k, span]
                    w_ref[ry, 2 + m, dc] = b_ref[ry, bi, k, span]
                if v_ref is not None:
                    at = 2 * prows
                    p = dc * pairs + ((2 * ry) ^ ranks_ref[4])
                    tile = lax.div(p * lanes, PAIR)
                    scr[tile] += b_ref[ry, bi, k, at : at + 16].astype(F32)
                    scr[pairs] += b_ref[ry, bi, k, at + 16 : at + 32].astype(F32)
    if v_ref is not None:
        v_ref[...] = scr[...].astype(BF)


def start_one(cuts, ranks_ref, *refs):
    restack(refs[0:4], refs[8:10], cuts)
    order(ranks_ref, refs[4:8], refs[10:11])


def start_two(axes, cuts, a, ga, b, gb, *refs):
    double(a, ga, refs[4], axes[0])
    double(b, gb, refs[5], axes[1])
    restack(refs[0:4], refs[6:8], cuts)


def start_five(lanes, ranks_ref, *refs):
    assemble(lanes, ranks_ref, *refs[0:4], refs[8])
    order(ranks_ref, refs[4:8], refs[9:10])


def double_both(axes, a, ga, b, gb, out_a, out_b):
    double(a, ga, out_a, axes[0])
    double(b, gb, out_b, axes[1])


def order_home(ranks_ref, *refs):
    order(ranks_ref, refs[:4], refs[4:])


def halve_body(axis_a, axis_b, cuts, *refs):
    ins, (sa, ka, sb, kb) = refs[: len(refs) - 4], refs[len(refs) - 4 :]

    def place(axis, send, keep, at, value):
        rows = value.shape[3]
        m = value.shape[axis] // 2
        lo = value[:m] if axis == 0 else value[:, :m]
        hi = value[m:] if axis == 0 else value[:, m:]
        keep[:, :, :, at : at + rows] = lo
        send[:, :, :, at : at + rows] = hi.astype(BF)

    at_a = at_b = 0
    for cut in cuts:
        if cut is None:
            keep_a, got_a, keep_b, got_b, *ins = ins
            parts = (keep_a[...] + got_a[...].astype(F32), keep_b[...] + got_b[...].astype(F32))
        else:
            keep, got, *ins = ins
            total = keep[...].astype(F32) + got[...].astype(F32)
            parts = (total[:, :, :, :cut], total[:, :, :, cut:])
        place(axis_a, sa, ka, at_a, parts[0])
        place(axis_b, sb, kb, at_b, parts[1])
        at_a += parts[0].shape[3]
        at_b += parts[1].shape[3]


def spread_body(*refs):
    ins, (s1, s2, s3, keep) = refs[:-4], refs[-4:]
    at = 0
    for own, got in zip(ins[::2], ins[1::2]):
        rows = own.shape[3]
        for r, ref in enumerate((keep, s1, s2, s3)):
            total = own[0, 0, r] + got[0, 0, r].astype(F32)
            ref[at : at + rows] = total.astype(ref.dtype)
        at += rows


def finish_body(plan, lanes, blen, ranks_ref, keep, r1, r2, r3, *outs):
    total = keep[...] + r1[...].astype(F32) + r2[...].astype(F32) + r3[...].astype(F32)
    at = 0
    outs = list(outs)
    for turn, rows in plan:
        part = total[at : at + rows]
        at += rows
        if turn == 2:
            p = (ranks_ref[0] * 4 + ranks_ref[1]) * 4 + ranks_ref[4]
            vec = pltpu.roll(part, lax.rem(PAIR - lax.rem(p * lanes, PAIR), PAIR), 1)
            outs.pop(0)[...] = vec[0:3, :lanes]
            outs.pop(0)[...] = vec[3:13, :lanes]
            own = pltpu.roll(part, lax.rem(PAIR - lax.rem(p * blen, PAIR), PAIR), 1)
            outs.pop(0)[...] = own[13:14, :blen]
        else:
            outs.pop(0)[...] = part


def home_body(every, out_ref):
    n_c, n_z, rows, _ = every.shape
    for c in range(n_c):
        for z in range(n_z):
            out_ref[z, c * rows : (c + 1) * rows, :] = every[c, z].astype(out_ref.dtype)


def half_spec(w, other):
    if other:
        return pl.BlockSpec((1,) + w.shape[1:], lambda s, _: (jnp.maximum(s - 2, 0), 0, 0, 0, 0))
    return pl.BlockSpec((1,) + w.shape[1:], lambda s, _: (jnp.minimum(s, 1), 0, 0, 0, 0))


def slot_outs(n_x, n_z, rows):
    shape = struct((2, n_x, n_z, rows, PAIR), BF)
    block = (1, n_x, n_z, rows, PAIR)
    return [
        (shape, pl.BlockSpec(block, lambda s, _: (jnp.minimum(s, 1), 0, 0, 0, 0))),
        (shape, pl.BlockSpec(block, lambda s, _: (jnp.maximum(s - 2, 0), 0, 0, 0, 0))),
    ]


def full(shape):
    return pl.BlockSpec(shape, lambda *_: (0,) * len(shape))


def run_attn_fwd(causal, ranks, rows_in, w_own, w_peer, vecs, pairs, deps):
    own, d = rows_in[0].shape
    keys = 2 * own
    blocks = 4
    ns = [keys // blocks * (b + 1) if causal else keys for b in range(blocks)]
    qn = 2 * own // blocks

    def saved(shape, dtype):
        return (struct((pairs,) + shape, dtype),
                pl.BlockSpec((1,) + shape, lambda s, _: (s, 0, 0)), True)

    outs = [
        saved((own, PAIR), BF), saved((keys, PAIR), BF), saved((keys, PAIR), BF),
        *[saved((n, qn), BF) for n in ns],
        saved((PAIR, own), BF), saved((own, PAIR), BF), saved((8, own), F32),
        (struct((own, d), F32), full((own, d))),
        (struct((own, PAIR), F32), full((own, PAIR))),
    ]
    if causal:
        outs.append((struct((pairs, 16, PAIR), F32), full((pairs, 16, PAIR))))
        outs.append((struct((16, PAIR), F32), full((16, PAIR))))
    ins = [(a, whole(a)) for a in rows_in]
    ins += [(w_own, half_spec(w_own, False), True), (w_peer, half_spec(w_peer, True), True)]
    ins += [(a, whole(a)) for a in vecs]
    scratch = [pltpu.VMEM((keys, d), BF)] + ([] if causal else [pltpu.VMEM((own, d), BF)])
    scratch.append(pltpu.VMEM((own, d), F32))

    return launch(
        self_fwd if causal else cross_fwd, "self_fwd" if causal else "cross_fwd",
        (pairs,), ranks, ins, outs, scratch, deps,
        cost=COSTS["self_fwd" if causal else "cross_fwd"],
    )


def run_ffn(ranks, n2, r2, cots, w, bias, vec, n_x, n_z):
    own, d = n2.shape
    dc, parts, _, prows, hid = w.shape
    half = own // 4
    back = lambda p, t, ref: ((p * (t // 2)) ^ ref[2], 0, 0, 0, 0)
    slots = struct((2, n_x, n_z, 2 * prows, hid), BF)
    slot_block = pl.BlockSpec((1, n_x, n_z, 2 * prows, hid), back)
    outs = [(struct((half, d), BF), full((half, d)))] * 4 + [
        (slots, slot_block),
        (slots, slot_block),
        (struct((own, d), F32), full((own, d))),
        (struct((8, d), F32), full((8, d))),
        (struct((16, PAIR), F32), full((16, PAIR))),
    ]
    ins = [(n2, whole(n2)), (r2, whole(r2))] + [(c, whole(c)) for c in cots] + [
        (w, pl.BlockSpec((dc, 1, 2, prows, hid), lambda p, t, _: (0, t, 0, 0, 0)), True),
        (bias, whole(bias)),
        (vec, whole(vec)),
    ]
    scratch = [
        pltpu.VMEM((own, d), BF),
        pltpu.VMEM((d, own), BF),
        pltpu.VMEM((parts, own, hid), BF),
        pltpu.VMEM((parts, own, hid), F32),
        pltpu.VMEM((own, d), F32),
        pltpu.VMEM((own, d), BF),
        pltpu.VMEM((d, own), BF),
        pltpu.VMEM((own, d), F32),
    ]
    return launch(
        ffn_both, "ffn_both", (2, parts), ranks, ins, outs, scratch,
        cost=COSTS["ffn_both"],
    )


def bwd_scratch(own, keys, d):
    return [
        pltpu.VMEM((own, d), BF),
        pltpu.VMEM((d, own), BF),
        pltpu.VMEM((d, own), BF),
        pltpu.VMEM((own, d), F32),
        pltpu.VMEM((keys, PAIR), F32),
        pltpu.VMEM((keys, PAIR), F32),
    ]


def per_pair(a, first=0):
    return (a, pl.BlockSpec((1,) + a.shape[1:], lambda s, _: (s + first, 0, 0)), True)


def run_cross_bwd(ranks, dz, w_own, w_peer, vec, saved, n, r, n_x, n_z, deps):
    pairs, own, _ = saved[0].shape
    keys = saved[1].shape[1]
    d = dz.shape[1]
    prows = w_own.shape[3]
    kv_spec = pl.BlockSpec((2, 1, own, PAIR), lambda s, _: (0, s, 0, 0))
    outs = slot_outs(n_x, n_z, 2 * prows) + [
        (struct((2, pairs, own, PAIR), F32), kv_spec, True),
        (struct((2, pairs, own, PAIR), BF), kv_spec, True),
        (struct((own, d), F32), full((own, d))),
        (struct((8, d), F32), full((8, d))),
        (struct((pairs, 1, PAIR), F32), pl.BlockSpec((1, 1, PAIR), lambda s, _: (s, 0, 0))),
    ]
    ins = [
        (n, whole(n)),
        (r, whole(r)),
        (dz, whole(dz)),
        (w_own, half_spec(w_own, False), True),
        (w_peer, half_spec(w_peer, True), True),
        (vec, whole(vec)),
        *[per_pair(a) for a in saved],
    ]
    return launch(
        cross_bwd, "cross_bwd", (pairs,), ranks, ins, outs, bwd_scratch(own, keys, d), deps,
        cost=COSTS["cross_bwd"],
    )


def run_self_bwd(first, ranks, act, dz, part, w, saved, n_x, n_z, deps):
    _, own, _ = saved[0].shape
    keys = saved[1].shape[1]
    d = dz.shape[1]
    prows = w.shape[3]
    pairs = 2
    kv_spec = pl.BlockSpec((2, 1, own, PAIR), lambda s, _: (0, s, 0, 0))
    slots = (1, n_x, n_z, 2 * prows, PAIR)
    outs = [
        (struct((2,) + slots[1:], BF), pl.BlockSpec(slots, lambda s, _: (s, 0, 0, 0, 0))),
        (struct((2, pairs, own, PAIR), F32), kv_spec, True),
        (struct((2, pairs, own, PAIR), BF), kv_spec, True),
        (struct((own, d), F32), full((own, d))),
        (struct((pairs, 1, PAIR), F32), pl.BlockSpec((1, 1, PAIR), lambda s, _: (s, 0, 0))),
    ]
    ins = [
        (act, whole(act)),
        (dz, whole(dz)),
        (part, whole(part)),
        (w, pl.BlockSpec((1,) + w.shape[1:], lambda s, _: (s, 0, 0, 0, 0)), True),
        *[per_pair(a, first) for a in saved],
    ]
    return launch(
        self_bwd, "self_bwd", (pairs,), ranks, ins, outs, bwd_scratch(own, keys, d), deps,
        cost=COSTS["self_bwd"],
    )


def run_kv_back(name, ranks, act, parts, w_own, w_peer, extra, lanes, blen, n_x, n_z, deps):
    own, d = act.shape
    pairs = 2 * w_own.shape[0]
    prows = w_own.shape[3]
    final = bool(extra)
    rows = 2 * prows + (16 if final else 0)
    half = own // 4
    outs = [(struct((half, d), BF), full((half, d)))] * 4
    scratch = [pltpu.VMEM((d, own), BF), pltpu.VMEM((own, d), F32)]
    block = (2, 1, own, PAIR)
    if final:
        slots = struct((2, n_x, n_z, rows, PAIR), BF)
        outs += [(slots, whole(slots))] * 2
        scratch += [pltpu.VMEM((pairs, 1, PAIR), F32), pltpu.VMEM((pairs, 16, PAIR), F32)]
        low = pl.BlockSpec(block, lambda s, _: (0, jnp.minimum(s, 1), 0, 0))
        high = pl.BlockSpec(block, lambda s, _: (0, jnp.maximum(s - 2, 0), 0, 0))
        specs = [low, low, high, high]
    else:
        outs += slot_outs(n_x, n_z, rows)
        outs.append(
            (struct((pairs, 1, PAIR), F32), pl.BlockSpec((1, 1, PAIR), lambda s, _: (s, 0, 0)))
        )
        specs = [pl.BlockSpec(block, lambda s, _: (0, s, 0, 0)),
                 pl.BlockSpec(block, lambda s, _: (0, s ^ 2, 0, 0))]
    ins = [
        (act, whole(act)),
        (w_own, half_spec(w_own, False), True),
        (w_peer, half_spec(w_peer, True), True),
        *[(a, spec, True) for a, spec in zip(parts, specs)],
        *[(a, whole(a)) for a in extra],
    ]
    return launch(
        functools.partial(kv_back, final, lanes, blen), name, (pairs,), ranks, ins, outs,
        scratch, deps, cost=COSTS[name],
    )


ALL = ("dp", "ctx", "ty", "tc")


def shards(
    inputs, memory, cotangent, wq_self, wk_self, wv_self, wo_self, wq_cross, wk_cross, wv_cross,
    wo_cross, w_in, w_out, gains, shifts, ffn_bias,
):
    seqs, block, d = inputs.shape
    n_x, n_z, n_y, n_c = (lax.axis_size(a) for a in ALL)
    pairs = n_y * n_c
    half = block // n_c
    own = n_z * half
    x_rank, z_rank, y_rank, c_rank = (lax.axis_index(a) for a in ALL)
    ranks = jnp.stack([x_rank, z_rank, y_rank, c_rank, y_rank * n_c + c_rank]).astype(jnp.int32)
    prows, lanes, blen = wq_self.shape[0], gains.shape[1], ffn_bias.shape[0]
    hid = w_in.shape[1]
    x_bits = [1 << i for i in range((n_x - 1).bit_length())]

    def send(array, axis, bit):
        return lax.ppermute(array, axis, [(i, i ^ bit) for i in range(lax.axis_size(axis))])

    def rows_of(r):
        return pl.BlockSpec((1, half, d), lambda i, ref: (ref[2] * 4 + (ref[1] ^ r), ref[3], 0))

    def packed_rows(array):
        return [(array, rows_of(r), True) for r in range(n_z)]

    def around_z(parts):
        return [parts[0]] + [send(parts[r], "ctx", r) for r in range(1, n_z)]

    row_part = struct((half, d), BF)

    def sent_rows(array, name, deps):
        *parts, token = launch(
            pack_rows, name, (1,), ranks, packed_rows(array), [(row_part, whole(row_part))] * n_z,
            deps=deps, limit=SMALL_LIMIT,
        )
        return around_z(parts), token

    x_got, token = sent_rows(inputs, "pack_x", [])
    s_pack, c_pack, token = local(
        functools.partial(pack_weights, lanes, blen), "pack_weights",
        [struct((4 * prows + 32, PAIR), BF), struct((4 * prows, PAIR), BF)],
        wq_self, wk_self, wv_self, wo_self.T, wq_cross, wk_cross, wv_cross, wo_cross.T,
        gains, shifts, ffn_bias.reshape(1, -1), ranks=ranks, deps=[token],
        scratch=[pltpu.VMEM((16, PAIR), F32), pltpu.VMEM((16, PAIR), F32)],
    )
    s_got = around_z([s_pack] * n_z)
    cuts_s = ((0, 2 * prows), (2 * prows, 4 * prows + 32))
    cuts_c = ((0, 2 * prows), (2 * prows, 4 * prows))

    def z_slots(cuts):
        return [struct((1, 1, n_z, hi - lo, PAIR), BF) for lo, hi in cuts]

    def doubled(array, axis):
        shape = list(array.shape)
        shape[axis] *= 2
        return struct(tuple(shape), BF)

    steps_a = [("dp", bit) for bit in x_bits] + [("ty", 1)]
    steps_b = [("ty", 1)] + [("dp", bit) for bit in x_bits]
    axis_of = {"ty": 0, "dp": 1}
    axes_at = [(axis_of[sa[0]], axis_of[sb[0]]) for sa, sb in zip(steps_a, steps_b)]

    def step(i, a, b):
        return [a, send(a, *steps_a[i]), b, send(b, *steps_b[i])]

    def more(ins, deps):
        for i in range(len(steps_a) - 1):
            a, b, token = local(
                functools.partial(double_both, axes_at[i]), "double",
                [doubled(ins[0], axes_at[i][0]), doubled(ins[2], axes_at[i][1])], *ins, deps=deps,
            )
            ins, deps = step(i + 1, a, b), [token]
        return ins, token

    sa, sb, xo, token = local(
        functools.partial(start_one, cuts_s), "start_one",
        z_slots(cuts_s) + [struct((own, d), BF)], *s_got, *x_got, ranks=ranks,
    )
    xp = send(xo, "tc", 1)
    c_got = around_z([c_pack] * n_z)
    sa, sb, ca, cb, token = local(
        functools.partial(start_two, axes_at[0], cuts_c), "start_two",
        [doubled(sa, axes_at[0][0]), doubled(sb, axes_at[0][1])] + z_slots(cuts_c),
        *step(0, sa, sb), *c_got, deps=[token],
    )
    s_last = step(1, sa, sb)
    c_last = step(0, ca, cb)
    for i in range(1, len(steps_a) - 1):
        sa, sb, token = local(
            functools.partial(double_both, axes_at[i]), "double",
            [doubled(s_last[0], axes_at[i][0]), doubled(s_last[2], axes_at[i][1])],
            *s_last, deps=[token],
        )
        s_last = step(i + 1, sa, sb)
    f_shape = struct((2, prows, hid), BF)
    *packed, f_pack, token = launch(
        pack_rest, "pack_rest", (1,), ranks,
        packed_rows(memory) + packed_rows(cotangent) + [(a, whole(a)) for a in (w_in, w_out.T)],
        [(row_part, whole(row_part))] * (2 * n_z) + [(f_shape, whole(f_shape), True)],
        deps=[token], limit=SMALL_LIMIT,
    )
    w_ffn = lax.all_gather(f_pack, ALL, axis=0, tiled=False).reshape(
        n_x * n_z, pairs, 2, prows, hid
    )
    m_got, cots = around_z(packed[:n_z]), around_z(packed[n_z:])
    w_shape = struct((2, 4, n_x * n_z, prows, PAIR), BF)
    ws_own, v_own, token = local(
        functools.partial(assemble, lanes), "assemble",
        [w_shape, struct((pairs + 1, 16, PAIR), BF)], *s_last, ranks=ranks,
        scratch=[pltpu.VMEM((pairs + 1, 16, PAIR), F32)], deps=[token], pinned=(0,),
    )
    v_peer, ws_peer = send(v_own, "tc", 1), send(ws_own, "tc", 1)
    c_last, token = more(c_last, [token])
    *saved_self, n1, r1, vec, bias, token = run_attn_fwd(
        True, ranks, (xo, xp), ws_own, ws_peer, (v_own, v_peer), pairs, [token]
    )
    wc_own, mo, token = local(
        functools.partial(start_five, lanes), "start_five", [w_shape, struct((own, d), BF)],
        *c_last, *m_got, ranks=ranks, deps=[token], pinned=(0,),
    )
    wc_peer, mp = send(wc_own, "tc", 1), send(mo, "tc", 1)
    *saved_cross, n2, r2, token = run_attn_fwd(
        False, ranks, (n1, mo, mp), wc_own, wc_peer, (vec,), pairs, [token]
    )
    *out_rows, f_keep, f_send, dz2, vg_ffn, bg, token = run_ffn(
        ranks, n2, r2, cots, w_ffn, bias, vec, n_x, n_z
    )

    def home_rows(got, deps, cost=SMALL_COST):
        here, token = local(
            order_home, "order_home", [struct((own, d), BF)], *got, ranks=ranks, deps=deps,
            cost=cost,
        )
        return here.reshape(n_z, half, d), token

    def home_all(here):
        return lax.all_gather(here, ("ty", "tc"), axis=0, tiled=False)

    def home_last(every, dtype, deps):
        return launch(
            home_body, "home", (n_y,), None,
            [(every, pl.BlockSpec((n_c, n_z, half, d), lambda y: (y, 0, 0, 0)), True)],
            [(struct((seqs, block, d), dtype),
              pl.BlockSpec((n_z, block, d), lambda y: (y, 0, 0)), True)],
            deps=deps, limit=2 * SMALL_LIMIT,
        )

    def to_core(*arrays):
        return [send(a, "tc", 1) for a in arrays]

    back_a = [("ty", 1)] + [("dp", bit) for bit in reversed(x_bits)]
    back_b = [("dp", bit) for bit in reversed(x_bits)] + [("ty", 1)]
    rounds = len(back_a)

    def shape_at(i, rows, lanes_in, steps):
        shape = [2, n_x, n_z, rows, lanes_in]
        for axis, _ in steps[: i + 1]:
            shape[axis_of[axis]] //= 2
        return tuple(shape)

    def halve(i, ins, cuts, rows, deps, cost=SMALL_COST):
        width = ins[0].shape[4]
        shape_a = shape_at(i, rows[0], width, back_a)
        shape_b = shape_at(i, rows[1], width, back_b)
        to_a, keep_a, to_b, keep_b, token = local(
            functools.partial(
                halve_body, axis_of[back_a[i][0]], axis_of[back_b[i][0]], cuts
            ),
            "halve",
            [struct(shape_a, BF), struct(shape_a, F32), struct(shape_b, BF), struct(shape_b, F32)],
            *ins, deps=deps, limit=2 * SMALL_LIMIT, cost=cost,
        )
        return [keep_a, send(to_a, *back_a[i]), keep_b, send(to_b, *back_b[i])], token

    def halve_more(groups, rows, deps, cost=SMALL_COST):
        ins, cuts = sum(groups, []), (None,) * len(groups)
        for i in range(1, rounds):
            ins, token = halve(i, ins, cuts, rows, deps, cost)
            cuts, deps = (None,), [token]
        return ins, token

    def spread(ins, deps):
        rows, width = sum(a.shape[3] for a in ins[::2]), ins[0].shape[4]
        *sends, keep, token = local(
            spread_body, "spread",
            [struct((rows, width), BF)] * 3 + [struct((rows, width), F32)], *ins, deps=deps,
        )
        return [keep] + [send(sends[r - 1], "ctx", r) for r in range(1, n_z)], token

    def finish(ins, plan, extra, deps):
        width = ins[0].shape[1]
        outs = [struct((size, width), F32) for turn, size in plan if turn != 2] + extra
        return local(
            functools.partial(finish_body, plan, lanes, blen), "finish", outs, *ins,
            ranks=ranks, deps=deps,
        )

    out_got = around_z(out_rows)
    rows_f = (prows, prows)
    ffn, token = halve(0, [f_keep, to_core(f_send)[0]], (prows,), rows_f, [token])
    c_keep, c_send, c_own, c_peer, dz1, vg_cross, qgc, token = run_cross_bwd(
        ranks, dz2, wc_own, wc_peer, vec, saved_cross, n1, r1, n_x, n_z, [token]
    )
    c_got, c_add = to_core(c_peer, c_send)
    ffn, token = halve_more([ffn], rows_f, [token])
    s_send, own_hi, peer_hi, base, qgs_hi, token = run_self_bwd(
        2, ranks, xo, dz1, dz1, ws_peer, saved_self, n_x, n_z, [token]
    )
    ffn, token = spread(ffn, [token])
    *mem_rows, m_keep, m_send, vgc, token = run_kv_back(
        "mem_back", ranks, mo, (c_own, c_got), wc_own, wc_peer, (), lanes, blen, n_x, n_z, [token]
    )
    mem_got = around_z(mem_rows)
    out_here, token = home_rows(out_got, [token])
    out_every = home_all(out_here)
    got_low, s_add = to_core(peer_hi, s_send)
    s_keep, own_low, peer_low, base, qgs, token = run_self_bwd(
        0, ranks, xo, dz1, base, ws_own, saved_self, n_x, n_z, [token]
    )
    (m_add,) = to_core(m_send)
    rows_one = (3 * prows, 3 * prows)
    one, token = halve(
        0, [c_keep, c_add, m_keep, m_add, s_keep, s_add], (prows,) * 3, rows_one, [token]
    )
    mem_here, token = home_rows(mem_got, [token], COVER)
    mem_every = home_all(mem_here)
    (got_hi,) = to_core(peer_low)
    *in_rows, i_keep, i_send, token = run_kv_back(
        "in_back", ranks, xo, (own_low, got_low, own_hi, got_hi), ws_own, ws_peer,
        (base, vg_cross, vg_ffn, bg, qgs, qgs_hi, qgc, vgc), lanes, blen, n_x, n_z, [token],
    )
    in_got = around_z(in_rows)
    one, token = halve_more([one], rows_one, [token], COVER)
    rows_two = (prows, prows + 16)
    two, token = halve(0, [i_keep, to_core(i_send)[0]], (prows,), rows_two, [token])
    in_here, token = home_rows(in_got, [token], COVER)
    in_every = home_all(in_here)
    two, token = halve_more([two], rows_two, [token])
    out, token = home_last(out_every, BF, [token])
    g_in, g_out, token = finish(ffn, ((0, prows),) * 2, [], [token])
    sums, token = spread(one + two, [token])
    grad_memory, token = home_last(mem_every, F32, [token])
    grad_inputs, token = home_last(in_every, F32, [token])
    gqc, gkc, gqs, goc, gvc, gos, gks, gvs, g_gains, g_shifts, g_bias, _ = finish(
        sums, ((0, prows),) * 8 + ((2, 16),),
        [struct(gains.shape, F32), struct(shifts.shape, F32), struct((1, blen), F32)], [token],
    )
    return (
        out, grad_inputs, grad_memory, gqs, gks, gvs, gos.T, gqc, gkc, gvc, goc.T,
        g_in, g_out.T, g_gains, g_shifts, g_bias.reshape(-1),
    )


def solution(mesh):
    sizes = mesh.devices.shape
    inner = jax.sharding.Mesh(
        mesh.devices.reshape(sizes[0], sizes[1], sizes[2] // 2, 2), ALL
    )
    rows = P("dp", "ctx", None)
    tp = ("ty", "tc")
    col = P(("dp", "ctx"), tp)
    row = P(tp, ("dp", "ctx"))
    small = P(None, ALL)
    weights = (col, col, col, row, col, col, col, row, col, row)
    tail = (small, small, P(ALL))
    return jax.shard_map(
        shards,
        mesh=inner,
        in_specs=(rows, rows, rows) + weights + tail,
        out_specs=(rows, rows, rows) + weights + tail,
        check_vma=False,
    )
```

time: 310 us -> 268 us (0.86)
  waiting for transfers between devices: 96.1 us -> 45.6 us
  Pallas kernels: 111 us -> 126 us
  local copies, waits for them, and re-layouts: 18.7 us -> 11.7 us
    ppermute x64 -> x63, waiting for transfers between devices: 96 us -> 41.9 us  [send(): lax.ppermute(array, axis, [(i, i ^ bit) for i in range(lax.axis_size(axis...]
    pallas_call x30 -> x32, Pallas kernels: 111 us -> 126 us  [launch(): return call(*args) if ranks is None else call(ranks, *args)]
    unnamed x88 -> x96, local copies, waits for them, and re-layouts: 17.9 us -> 11.6 us
    all_gather x1, waiting for transfers between devices: 0.01 us -> 3.6 us  [shards(): lax.all_gather(f_pack, ALL, axis=0, tiled=False)]
    ppermute x64 -> x63, starting transfers between devices: 67.5 us -> 69.3 us  [send(): lax.ppermute(array, axis, [(i, i ^ bit) for i in range(lax.axis_size(axis...]
  transfers between devices with their start and end apart: 66 -> 67, of which waited for: 23 -> 15; matrix products, arithmetic and copies ran while one was open for 0% -> 0% of each run, Pallas kernels for 30% -> 38%
where the time goes in v3:
time: 268 us; the launch traced here: 267 us
  Pallas kernels  126 us (47%)
  starting transfers between devices  69.4 us (26%)
  waiting for transfers between devices  45.6 us (17%)
  between operations  14.6 us (5%)
  local copies, waits for them, and re-layouts  11.7 us (4%)
    pallas_call x32, Pallas kernels, launch(): return call(*args) if ranks is None else call(ranks, *args)  126 us
    ppermute x63, starting transfers between devices, send(): lax.ppermute(array, axis, [(i, i ^ bit) for i in range(lax.axis_size(axis...  69.3 us
    ppermute x63, waiting for transfers between devices, send(): lax.ppermute(array, axis, [(i, i ^ bit) for i in range(lax.axis_size(axis...  41.9 us
    unnamed x96, local copies, waits for them, and re-layouts  11.6 us
  transfers between devices with their start and end apart: 67, of which 15 were waited for; matrix products, arithmetic and copies ran while one was open for 0% of the time, Pallas kernels for 38%

profile of v3, /device:TPU:0, one launch (start us, length us, event | category | flops | bytes accessed | tf_op | source)
XLA Modules:
  0.0 267.0 jit_solution(15854285684530460980)
XLA Ops:
  10.4 5.0 %collective-permute-start.2 = (bf16[288,128]{1,0:T(8,128)(2,1)S(1)}, bf16[288,128]{1,0:T(8,128)(2,1)S(1)}, u32[]{:S(2)}, u32[]{:S(2)}) collective-permute-start(bf16[288,128]{1,0:T(8,128)(2,1)S(1)} %get-tuple-element.190.refs_1_), channel_id=1, source_target_pairs={{0,12},{4,8},{8,4},{12,0},{1,13},{5,9},{9,5},{13,1},{2,14},{6,10},... | collective-permute-start | bytes 221192 | tf_op jit(solution)/shard_map/ppermute | solution.py:935
  16.0 3.8 %collective-permute-start.5 = (bf16[128,512]{1,0:T(8,128)(2,1)S(1)}, bf16[128,512]{1,0:T(8,128)(2,1)S(1)}, u32[]{:S(2)}, u32[]{:S(2)}) collective-permute-start(bf16[128,512]{1,0:T(8,128)(2,1)S(1)} %get-tuple-element.194), channel_id=1, source_target_pairs={{0,12},{4,8},{8,4},{12,0},{1,13},{5,9},{9,5},{13,1},{2,14},{6,10},... | collective-permute-start | bytes 393224 | tf_op jit(solution)/shard_map/ppermute | solution.py:935
  20.4 12.6 %collective-permute-done.1.refs_3_ = bf16[288,128]{1,0:T(8,128)(2,1)S(1)} collective-permute-done((bf16[288,128]{1,0:T(8,128)(2,1)S(1)}, bf16[288,128]{1,0:T(8,128)(2,1)S(1)}, u32[]{:S(2)}, u32[]{:S(2)}) %collective-permute-start.1) | collective-permute-done | bytes 73760 | tf_op jit(solution)/shard_map/ppermute | solution.py:935
  36.8 2.6 collective-permute-start.11
  45.0 2.5 pack_rest.1
  48.6 6.0 %collective-permute-done.12.refs_2_ = bf16[1,2,4,128,128]{4,3,2,1,0:T(8,128)(2,1)S(1)} collective-permute-done((bf16[1,2,4,128,128]{4,3,2,1,0:T(8,128)(2,1)S(1)}, bf16[1,2,4,128,128]{4,3,2,1,0:T(8,128)(2,1)S(1)}, u32[]{:S(2)}, u32[]{:S(2)}) %collective-permute-start.12) | collective-permute-done | bytes 262176 | tf_op jit(solution)/shard_map/ppermute | solution.py:935
  59.3 3.0 %collective-permute-done.16.refs_1_ = bf16[1,1,4,128,128]{4,3,2,1,0:T(8,128)(2,1)S(1)} collective-permute-done((bf16[1,1,4,128,128]{4,3,2,1,0:T(8,128)(2,1)S(1)}, bf16[1,1,4,128,128]{4,3,2,1,0:T(8,128)(2,1)S(1)}, u32[]{:S(2)}, u32[]{:S(2)}) %collective-permute-start.16) | collective-permute-done | bytes 131104 | tf_op jit(solution)/shard_map/ppermute | solution.py:935
  62.3 2.0 collective-permute-start.21
  68.3 15.0 %self_fwd.1 = (bf16[4,512,128]{2,1,0:T(8,128)(2,1)}, bf16[4,1024,128]{2,1,0:T(8,128)(2,1)}, bf16[4,1024,128]{2,1,0:T(8,128)(2,1)}, bf16[4,256,256]{2,1,0:T(8,128...) custom-call(s32[5]{0:T(128)S(1)} %stack.23.refs_0_, ...), custom_call_target="tpu_custom_call" | custom-call | flops 24000000000 | bytes 1 | tf_op jit(solution)/shard_map/self_fwd/pallas_call | solution.py:567
  86.1 2.6 collective-permute-start.26
  90.9 17.6 %cross_fwd.1 = (bf16[4,512,128]{2,1,0:T(8,128)(2,1)}, bf16[4,1024,128]{2,1,0:T(8,128)(2,1)}, bf16[4,1024,128]{2,1,0:T(8,128)(2,1)}, bf16[4,1024,256]{2,1,0:T(8,1...) custom-call(s32[5]{0:T(128)S(1)} %stack.23.refs_0_, ...), custom_call_target="tpu_custom_call" | custom-call | flops 28000000000 | bytes 1 | tf_op jit(solution)/shard_map/cross_fwd/pallas_call | solution.py:567
  110.2 3.6 %all-gather.12.cloned.1.call-done = bf16[64,64,512]{2,1,0:T(8,128)(2,1)} async-done(((bf16[2,64,512]{2,1,0:T(8,128)(2,1)}), bf16[64,64,512]{2,1,0:T(8,128)(2,1)}) %all-gather.12.cloned.1.call-update) | async-done | bytes 4194320 | tf_op jit(solution)/shard_map/all_gather | solution.py:1019
  116.0 14.6 %ffn_both.1 = (bf16[128,512]{1,0:T(8,128)(2,1)S(1)}, bf16[128,512]{1,0:T(8,128)(2,1)S(1)}, bf16[128,512]{1,0:T(8,128)(2,1)S(1)}, bf16[128,512]{1,0:T(8,128)(2,1)...) custom-call(s32[5]{0:T(128)S(1)} %stack.23.refs_0_, ...), custom_call_target="tpu_custom_call" | custom-call | flops 24999999488 | bytes 1 | tf_op jit(solution)/shard_map/ffn_both/pallas_call | solution.py:567
  138.0 19.5 %cross_bwd.1 = (bf16[2,2,4,128,128]{4,3,2,1,0:T(8,128)(2,1)S(1)}, bf16[2,2,4,128,128]{4,3,2,1,0:T(8,128)(2,1)S(1)}, f32[2,4,512,128]{3,2,1,0:T(8,128)}, bf16[2,4...) custom-call(s32[5]{0:T(128)S(1)} %stack.23.refs_0_, ...), custom_call_target="tpu_custom_call" | custom-call | flops 30000001024 | bytes 1 | tf_op jit(solution)/shard_map/cross_bwd/pallas_call | solution.py:567
  159.4 8.9 %self_bwd.2 = (bf16[2,2,4,128,128]{4,3,2,1,0:T(8,128)(2,1)S(1)}, f32[2,2,512,128]{3,2,1,0:T(8,128)}, bf16[2,2,512,128]{3,2,1,0:T(8,128)(2,1)}, f32[512,512]{1,0:...) custom-call(s32[5]{0:T(128)S(1)} %stack.23.refs_0_, bf16[512,512]{1,0:T(8,128)(2,1)S(1)} %get-tuple-element.195.refs_1_, ...), custom_call_target="tpu_custom_call" | custom-call | flops 16000000000 | bytes 1 | tf_op jit(solution)/shard_map/self_bwd/pallas_call | solution.py:567
  168.9 2.4 collective-permute-start.30
  172.4 6.6 %mem_back.1 = (bf16[128,512]{1,0:T(8,128)(2,1)S(1)}, bf16[128,512]{1,0:T(8,128)(2,1)S(1)}, bf16[128,512]{1,0:T(8,128)(2,1)S(1)}, bf16[128,512]{1,0:T(8,128)(2,1)...) custom-call(s32[5]{0:T(128)S(1)} %stack.23.refs_0_, ...), custom_call_target="tpu_custom_call" | custom-call | flops 8999999488 | bytes 1 | tf_op jit(solution)/shard_map/mem_back/pallas_call | solution.py:567
  181.6 2.0 collective-permute-start.40
  183.7 2.4 collective-permute-start.41
  188.7 9.1 %self_bwd.3 = (bf16[2,2,4,128,128]{4,3,2,1,0:T(8,128)(2,1)S(1)}, f32[2,2,512,128]{3,2,1,0:T(8,128)}, bf16[2,2,512,128]{3,2,1,0:T(8,128)(2,1)}, f32[512,512]{1,0:...) custom-call(s32[5]{0:T(128)S(1)} %stack.23.refs_0_, bf16[512,512]{1,0:T(8,128)(2,1)S(1)} %get-tuple-element.195.refs_1_, ...), custom_call_target="tpu_custom_call" | custom-call | flops 16000000000 | bytes 1 | tf_op jit(solution)/shard_map/self_bwd/pallas_call | solution.py:567
  204.9 7.1 %in_back.1 = (bf16[128,512]{1,0:T(8,128)(2,1)S(1)}, bf16[128,512]{1,0:T(8,128)(2,1)S(1)}, bf16[128,512]{1,0:T(8,128)(2,1)S(1)}, bf16[128,512]{1,0:T(8,128)(2,1)S...) custom-call(s32[5]{0:T(128)S(1)} %stack.23.refs_0_, ...), custom_call_target="tpu_custom_call" | custom-call | flops 8999999488 | bytes 1 | tf_op jit(solution)/shard_map/in_back/pallas_call | solution.py:567
  212.1 2.3 collective-permute-start.51
  214.4 2.1 collective-permute-start.52
  219.2 5.9 %collective-permute-done.51.refs_3_ = bf16[128,512]{1,0:T(8,128)(2,1)S(1)} collective-permute-done((bf16[128,512]{1,0:T(8,128)(2,1)S(1)}, bf16[128,512]{1,0:T(8,128)(2,1)S(1)}, u32[]{:S(2)}, u32[]{:S(2)}) %collective-permute-start.51) | collective-permute-done | bytes 131104 | tf_op jit(solution)/shard_map/ppermute | solution.py:935
  228.1 2.3 collective-permute-start.57
  230.4 2.4 collective-permute-start.59
  235.4 2.9 %home.3 = (bf16[8,256,512]{2,1,0:T(8,128)(2,1)}, f32[8,128]{1,0:T(8,128)S(1)}) custom-call(bf16[4,4,128,512]{3,2,1,0:T(8,128)(2,1)} %all-gather.6.cloned.1.call-done.refs_0_, f32[8,128]{1,0:T(8,128)S(1)} %get-tuple-element.322.refs_1_), custom_call_target="tpu_custom_call" | custom-call | flops 1000000000 | bytes 1 | tf_op jit(solution)/shard_map/home/pallas_call | solution.py:567
  239.2 2.3 collective-permute-done.58.refs_3_
  244.3 3.4 %collective-permute-done.56.refs_7_ = bf16[1,1,4,80,128]{4,3,2,1,0:T(8,128)(2,1)S(1)} collective-permute-done((bf16[1,1,4,80,128]{4,3,2,1,0:T(8,128)(2,1)S(1)}, bf16[1,1,4,80,128]{4,3,2,1,0:T(8,128)(2,1)S(1)}, u32[]{:S(2)}, u32[]{:S(2)}) %collective-permute-start.56) | collective-permute-done | bytes 81952 | tf_op jit(solution)/shard_map/ppermute | solution.py:935
  250.2 2.0 collective-permute-start.62
  252.2 3.4 %home.4 = (f32[8,256,512]{2,1,0:T(8,128)}, f32[8,128]{1,0:T(8,128)S(1)}) custom-call(bf16[4,4,128,512]{3,2,1,0:T(8,128)(2,1)} %all-gather.10.cloned.1.call-done.refs_0_, f32[8,128]{1,0:T(8,128)S(1)} %get-tuple-element.340.refs_1_), custom_call_target="tpu_custom_call" | custom-call | flops 1000000000 | bytes 1 | tf_op jit(solution)/shard_map/home/pallas_call | solution.py:567
  255.6 3.4 %home.5 = (f32[8,256,512]{2,1,0:T(8,128)}, f32[8,128]{1,0:T(8,128)S(1)}) custom-call(bf16[4,4,128,512]{3,2,1,0:T(8,128)(2,1)} %all-gather.8.cloned.1.call-done.refs_0_, f32[8,128]{1,0:T(8,128)S(1)} %get-tuple-element.341.refs_1_), custom_call_target="tpu_custom_call" | custom-call | flops 1000000000 | bytes 1 | tf_op jit(solution)/shard_map/home/pallas_call | solution.py:567
  (235 shorter events, 71.5 us)
Async XLA Ops:
  7.2 106.6 %all-gather.12.cloned.1.call-start = ((), (), s32[]{:S(2)}) async-start(), calls=%async_computation.3 | async-start | bytes 4325376 | tf_op jit(solution)/shard_map/all_gather | solution.py:1019
  15.4 17.6 %collective-permute-start.3 = (bf16[128,512]{1,0:T(8,128)(2,1)S(1)}, bf16[128,512]{1,0:T(8,128)(2,1)S(1)}, u32[]{:S(2)}, u32[]{:S(2)}) collective-permute-start(bf16[128,512]{1,0:T(8,128)(2,1)S(1)} %get-tuple-element.192), channel_id=1, source_target_pairs={{0,4},{4,0},{8,12},{12,8},{1,5},{5,1},{9,13},{13,9},{2,6},{6,2},{1... | collective-permute-start | bytes 393224 | tf_op jit(solution)/shard_map/ppermute | solution.py:935
  15.4 17.6 %collective-permute-start.4 = (bf16[128,512]{1,0:T(8,128)(2,1)S(1)}, bf16[128,512]{1,0:T(8,128)(2,1)S(1)}, u32[]{:S(2)}, u32[]{:S(2)}) collective-permute-start(bf16[128,512]{1,0:T(8,128)(2,1)S(1)} %get-tuple-element.193), channel_id=1, source_target_pairs={{0,8},{4,12},{8,0},{12,4},{1,9},{5,13},{9,1},{13,5},{2,10},{6,14},... | collective-permute-start | bytes 393224 | tf_op jit(solution)/shard_map/ppermute | solution.py:935
  16.0 17.0 %collective-permute-start.5 = (bf16[128,512]{1,0:T(8,128)(2,1)S(1)}, bf16[128,512]{1,0:T(8,128)(2,1)S(1)}, u32[]{:S(2)}, u32[]{:S(2)}) collective-permute-start(bf16[128,512]{1,0:T(8,128)(2,1)S(1)} %get-tuple-element.194), channel_id=1, source_target_pairs={{0,12},{4,8},{8,4},{12,0},{1,13},{5,9},{9,5},{13,1},{2,14},{6,10},... | collective-permute-start | bytes 393224 | tf_op jit(solution)/shard_map/ppermute | solution.py:935
  19.8 13.2 %collective-permute-start.1 = (bf16[288,128]{1,0:T(8,128)(2,1)S(1)}, bf16[288,128]{1,0:T(8,128)(2,1)S(1)}, u32[]{:S(2)}, u32[]{:S(2)}) collective-permute-start(bf16[288,128]{1,0:T(8,128)(2,1)S(1)} %get-tuple-element.190.refs_1_), channel_id=1, source_target_pairs={{0,8},{4,12},{8,0},{12,4},{1,9},{5,13},{9,1},{13,5},{2,10},{6,14},... | collective-permute-start | bytes 221192 | tf_op jit(solution)/shard_map/ppermute | solution.py:935
  19.8 13.2 %collective-permute-start = (bf16[288,128]{1,0:T(8,128)(2,1)S(1)}, bf16[288,128]{1,0:T(8,128)(2,1)S(1)}, u32[]{:S(2)}, u32[]{:S(2)}) collective-permute-start(bf16[288,128]{1,0:T(8,128)(2,1)S(1)} %get-tuple-element.190.refs_1_), channel_id=1, source_target_pairs={{0,4},{4,0},{8,12},{12,8},{1,5},{5,1},{9,13},{13,9},{2,6},{6,2},{1... | collective-permute-start | bytes 221192 | tf_op jit(solution)/shard_map/ppermute | solution.py:935
  47.6 187.8 %all-gather.6.cloned.1.call-start = ((), (), s32[]{:S(2)}) async-start(), calls=%async_computation | async-start | bytes 2621440 | tf_op jit(solution)/shard_map/all_gather | solution.py:1054
  58.8 24.5 %collective-permute-start.20 = (bf16[128,512]{1,0:T(8,128)(2,1)S(1)}, bf16[128,512]{1,0:T(8,128)(2,1)S(1)}, u32[]{:S(2)}, u32[]{:S(2)}) collective-permute-start(bf16[128,512]{1,0:T(8,128)(2,1)S(1)} %get-tuple-element.214), channel_id=1, source_target_pairs={{0,4},{4,0},{8,12},{12,8},{1,5},{5,1},{9,13},{13,9},{2,6},{6,2},{1... | collective-permute-start | bytes 393224 | tf_op jit(solution)/shard_map/ppermute | solution.py:935
  62.3 21.0 %collective-permute-start.21 = (bf16[128,512]{1,0:T(8,128)(2,1)S(1)}, bf16[128,512]{1,0:T(8,128)(2,1)S(1)}, u32[]{:S(2)}, u32[]{:S(2)}) collective-permute-start(bf16[128,512]{1,0:T(8,128)(2,1)S(1)} %get-tuple-element.215), channel_id=1, source_target_pairs={{0,8},{4,12},{8,0},{12,4},{1,9},{5,13},{9,1},{13,5},{2,10},{6,14},... | collective-permute-start | bytes 393224 | tf_op jit(solution)/shard_map/ppermute | solution.py:935
  65.6 17.7 %collective-permute-start.22 = (bf16[128,512]{1,0:T(8,128)(2,1)S(1)}, bf16[128,512]{1,0:T(8,128)(2,1)S(1)}, u32[]{:S(2)}, u32[]{:S(2)}) collective-permute-start(bf16[128,512]{1,0:T(8,128)(2,1)S(1)} %get-tuple-element.216), channel_id=1, source_target_pairs={{0,12},{4,8},{8,4},{12,0},{1,13},{5,9},{9,5},{13,1},{2,14},{6,10},... | collective-permute-start | bytes 393224 | tf_op jit(solution)/shard_map/ppermute | solution.py:935
  66.6 16.7 %collective-permute-start.18 = (bf16[1,2,4,128,128]{4,3,2,1,0:T(8,128)(2,1)S(1)}, bf16[1,2,4,128,128]{4,3,2,1,0:T(8,128)(2,1)S(1)}, u32[]{:S(2)}, u32[]{:S(2)}) collective-permute-start(bf16[1,2,4,128,128]{4,3,2,1,0:T(8,128)(2,1)S(1)} %get-tuple-element.211.refs_1_), channel_id=1, source_target_pairs={{0,2},{2,0},{1,3},{3,1},{4,6},{6,4},{5,7},{7,5},{8,10},{10,8},{9,1... | collective-permute-start | bytes 786440 | tf_op jit(solution)/shard_map/ppermute | solution.py:935
  67.1 16.2 %collective-permute-start.19 = (bf16[2,1,4,128,128]{4,3,2,1,0:T(8,128)(2,1)S(1)}, bf16[2,1,4,128,128]{4,3,2,1,0:T(8,128)(2,1)S(1)}, u32[]{:S(2)}, u32[]{:S(2)}) collective-permute-start(bf16[2,1,4,128,128]{4,3,2,1,0:T(8,128)(2,1)S(1)} %get-tuple-element.212.refs_3_), channel_id=1, source_target_pairs={{0,16},{16,0},{1,17},{17,1},{2,18},{18,2},{3,19},{19,3},{4,20},{20... | collective-permute-start | bytes 786440 | tf_op jit(solution)/shard_map/ppermute | solution.py:935
  85.5 24.7 %collective-permute-start.25 = (bf16[128,512]{1,0:T(8,128)(2,1)S(1)}, bf16[128,512]{1,0:T(8,128)(2,1)S(1)}, u32[]{:S(2)}, u32[]{:S(2)}) collective-permute-start(bf16[128,512]{1,0:T(8,128)(2,1)S(1)} %get-tuple-element.225), channel_id=1, source_target_pairs={{0,4},{4,0},{8,12},{12,8},{1,5},{5,1},{9,13},{13,9},{2,6},{6,2},{1... | collective-permute-start | bytes 393224 | tf_op jit(solution)/shard_map/ppermute | solution.py:935
  86.1 24.1 %collective-permute-start.26 = (bf16[128,512]{1,0:T(8,128)(2,1)S(1)}, bf16[128,512]{1,0:T(8,128)(2,1)S(1)}, u32[]{:S(2)}, u32[]{:S(2)}) collective-permute-start(bf16[128,512]{1,0:T(8,128)(2,1)S(1)} %get-tuple-element.226), channel_id=1, source_target_pairs={{0,8},{4,12},{8,0},{12,4},{1,9},{5,13},{9,1},{13,5},{2,10},{6,14},... | collective-permute-start | bytes 393224 | tf_op jit(solution)/shard_map/ppermute | solution.py:935
  88.7 21.6 %collective-permute-start.27 = (bf16[128,512]{1,0:T(8,128)(2,1)S(1)}, bf16[128,512]{1,0:T(8,128)(2,1)S(1)}, u32[]{:S(2)}, u32[]{:S(2)}) collective-permute-start(bf16[128,512]{1,0:T(8,128)(2,1)S(1)} %get-tuple-element.227), channel_id=1, source_target_pairs={{0,12},{4,8},{8,4},{12,0},{1,13},{5,9},{9,5},{13,1},{2,14},{6,10},... | collective-permute-start | bytes 393224 | tf_op jit(solution)/shard_map/ppermute | solution.py:935
  130.9 48.6 %collective-permute-start.28 = (bf16[128,512]{1,0:T(8,128)(2,1)S(1)}, bf16[128,512]{1,0:T(8,128)(2,1)S(1)}, u32[]{:S(2)}, u32[]{:S(2)}) collective-permute-start(bf16[128,512]{1,0:T(8,128)(2,1)S(1)} %get-tuple-element.231), channel_id=1, source_target_pairs={{0,4},{4,0},{8,12},{12,8},{1,5},{5,1},{9,13},{13,9},{2,6},{6,2},{1... | collective-permute-start | bytes 393224 | tf_op jit(solution)/shard_map/ppermute | solution.py:935
  132.2 47.3 %collective-permute-start.29 = (bf16[128,512]{1,0:T(8,128)(2,1)S(1)}, bf16[128,512]{1,0:T(8,128)(2,1)S(1)}, u32[]{:S(2)}, u32[]{:S(2)}) collective-permute-start(bf16[128,512]{1,0:T(8,128)(2,1)S(1)} %get-tuple-element.232), channel_id=1, source_target_pairs={{0,8},{4,12},{8,0},{12,4},{1,9},{5,13},{9,1},{13,5},{2,10},{6,14},... | collective-permute-start | bytes 393224 | tf_op jit(solution)/shard_map/ppermute | solution.py:935
  135.4 22.2 %collective-permute-start.33 = (bf16[1,2,4,64,512]{4,3,2,1,0:T(8,128)(2,1)S(1)}, bf16[1,2,4,64,512]{4,3,2,1,0:T(8,128)(2,1)S(1)}, u32[]{:S(2)}, u32[]{:S(2)}) collective-permute-start(bf16[1,2,4,64,512]{4,3,2,1,0:T(8,128)(2,1)S(1)} %get-tuple-element.253), channel_id=1, source_target_pairs={{0,2},{2,0},{1,3},{3,1},{4,6},{6,4},{5,7},{7,5},{8,10},{10,8},{9,1... | collective-permute-start | bytes 1572872 | tf_op jit(solution)/shard_map/ppermute | solution.py:935
  136.8 20.9 %collective-permute-start.34 = (bf16[2,1,4,64,512]{4,3,2,1,0:T(8,128)(2,1)S(1)}, bf16[2,1,4,64,512]{4,3,2,1,0:T(8,128)(2,1)S(1)}, u32[]{:S(2)}, u32[]{:S(2)}) collective-permute-start(bf16[2,1,4,64,512]{4,3,2,1,0:T(8,128)(2,1)S(1)} %get-tuple-element.255), channel_id=1, source_target_pairs={{0,16},{16,0},{1,17},{17,1},{2,18},{18,2},{3,19},{19,3},{4,20},{20... | collective-permute-start | bytes 1572872 | tf_op jit(solution)/shard_map/ppermute | solution.py:935
  157.5 13.8 %collective-permute-start.32 = (bf16[2,4,512,128]{3,2,1,0:T(8,128)(2,1)}, bf16[2,4,512,128]{3,2,1,0:T(8,128)(2,1)S(1)}, u32[]{:S(2)}, u32[]{:S(2)}) collective-permute-start(bf16[2,4,512,128]{3,2,1,0:T(8,128)(2,1)} %get-tuple-element.251), channel_id=1, source_target_pairs={{0,1},{1,0},{2,3},{3,2},{4,5},{5,4},{6,7},{7,6},{8,9},{9,8},{10,11... | collective-permute-start | bytes 3145736 | tf_op jit(solution)/shard_map/ppermute | solution.py:935
  158.7 12.5 %collective-permute-start.36 = (bf16[1,1,4,64,512]{4,3,2,1,0:T(8,128)(2,1)S(1)}, bf16[1,1,4,64,512]{4,3,2,1,0:T(8,128)(2,1)S(1)}, u32[]{:S(2)}, u32[]{:S(2)}) collective-permute-start(bf16[1,1,4,64,512]{4,3,2,1,0:T(8,128)(2,1)S(1)} %get-tuple-element.260), channel_id=1, source_target_pairs={{0,2},{2,0},{1,3},{3,1},{4,6},{6,4},{5,7},{7,5},{8,10},{10,8},{9,1... | collective-permute-start | bytes 786440 | tf_op jit(solution)/shard_map/ppermute | solution.py:935
  181.0 71.2 %all-gather.10.cloned.1.call-start = ((), (), s32[]{:S(2)}) async-start(), calls=%async_computation.2 | async-start | bytes 2621440 | tf_op jit(solution)/shard_map/all_gather | solution.py:1054
  181.1 16.7 %collective-permute-start.44 = (bf16[2,2,4,128,128]{4,3,2,1,0:T(8,128)(2,1)S(1)}, bf16[2,2,4,128,128]{4,3,2,1,0:T(8,128)(2,1)S(1)}, u32[]{:S(2)}, u32[]{:S(2)}) collective-permute-start(bf16[2,2,4,128,128]{4,3,2,1,0:T(8,128)(2,1)S(1)} %get-tuple-element.300), channel_id=1, source_target_pairs={{0,1},{1,0},{2,3},{3,2},{4,5},{5,4},{6,7},{7,6},{8,9},{9,8},{10,11... | collective-permute-start | bytes 1572872 | tf_op jit(solution)/shard_map/ppermute | solution.py:935
  181.6 17.2 %collective-permute-start.39 = (bf16[128,512]{1,0:T(8,128)(2,1)S(1)}, bf16[128,512]{1,0:T(8,128)(2,1)S(1)}, u32[]{:S(2)}, u32[]{:S(2)}) collective-permute-start(bf16[128,512]{1,0:T(8,128)(2,1)S(1)} %get-tuple-element.292), channel_id=1, source_target_pairs={{0,4},{4,0},{8,12},{12,8},{1,5},{5,1},{9,13},{13,9},{2,6},{6,2},{1... | collective-permute-start | bytes 393224 | tf_op jit(solution)/shard_map/ppermute | solution.py:935
  181.6 17.2 %collective-permute-start.40 = (bf16[128,512]{1,0:T(8,128)(2,1)S(1)}, bf16[128,512]{1,0:T(8,128)(2,1)S(1)}, u32[]{:S(2)}, u32[]{:S(2)}) collective-permute-start(bf16[128,512]{1,0:T(8,128)(2,1)S(1)} %get-tuple-element.293), channel_id=1, source_target_pairs={{0,8},{4,12},{8,0},{12,4},{1,9},{5,13},{9,1},{13,5},{2,10},{6,14},... | collective-permute-start | bytes 393224 | tf_op jit(solution)/shard_map/ppermute | solution.py:935
  183.7 15.2 %collective-permute-start.41 = (bf16[128,512]{1,0:T(8,128)(2,1)S(1)}, bf16[128,512]{1,0:T(8,128)(2,1)S(1)}, u32[]{:S(2)}, u32[]{:S(2)}) collective-permute-start(bf16[128,512]{1,0:T(8,128)(2,1)S(1)} %get-tuple-element.294), channel_id=1, source_target_pairs={{0,12},{4,8},{8,4},{12,0},{1,13},{5,9},{9,5},{13,1},{2,14},{6,10},... | collective-permute-start | bytes 393224 | tf_op jit(solution)/shard_map/ppermute | solution.py:935
  186.0 12.3 %collective-permute-start.43 = (bf16[2,2,4,128,128]{4,3,2,1,0:T(8,128)(2,1)S(1)}, bf16[2,2,4,128,128]{4,3,2,1,0:T(8,128)(2,1)S(1)}, u32[]{:S(2)}, u32[]{:S(2)}) collective-permute-start(bf16[2,2,4,128,128]{4,3,2,1,0:T(8,128)(2,1)S(1)} %get-tuple-element.298), channel_id=1, source_target_pairs={{0,1},{1,0},{2,3},{3,2},{4,5},{5,4},{6,7},{7,6},{8,9},{9,8},{10,11... | collective-permute-start | bytes 1572872 | tf_op jit(solution)/shard_map/ppermute | solution.py:935
  200.4 55.2 %all-gather.8.cloned.1.call-start = ((), (), s32[]{:S(2)}) async-start(), calls=%async_computation.1 | async-start | bytes 2621440 | tf_op jit(solution)/shard_map/all_gather | solution.py:1054
  200.4 16.1 %collective-permute-start.46 = (bf16[1,2,4,192,128]{4,3,2,1,0:T(8,128)(2,1)S(1)}, bf16[1,2,4,192,128]{4,3,2,1,0:T(8,128)(2,1)S(1)}, u32[]{:S(2)}, u32[]{:S(2)}) collective-permute-start(bf16[1,2,4,192,128]{4,3,2,1,0:T(8,128)(2,1)S(1)} %get-tuple-element.307), channel_id=1, source_target_pairs={{0,2},{2,0},{1,3},{3,1},{4,6},{6,4},{5,7},{7,5},{8,10},{10,8},{9,1... | collective-permute-start | bytes 1179656 | tf_op jit(solution)/shard_map/ppermute | solution.py:935
  202.1 14.3 %collective-permute-start.47 = (bf16[2,1,4,192,128]{4,3,2,1,0:T(8,128)(2,1)S(1)}, bf16[2,1,4,192,128]{4,3,2,1,0:T(8,128)(2,1)S(1)}, u32[]{:S(2)}, u32[]{:S(2)}) collective-permute-start(bf16[2,1,4,192,128]{4,3,2,1,0:T(8,128)(2,1)S(1)} %get-tuple-element.309), channel_id=1, source_target_pairs={{0,16},{16,0},{1,17},{17,1},{2,18},{18,2},{3,19},{19,3},{4,20},{20... | collective-permute-start | bytes 1179656 | tf_op jit(solution)/shard_map/ppermute | solution.py:935
  212.1 13.0 %collective-permute-start.51 = (bf16[128,512]{1,0:T(8,128)(2,1)S(1)}, bf16[128,512]{1,0:T(8,128)(2,1)S(1)}, u32[]{:S(2)}, u32[]{:S(2)}) collective-permute-start(bf16[128,512]{1,0:T(8,128)(2,1)S(1)} %get-tuple-element.318), channel_id=1, source_target_pairs={{0,8},{4,12},{8,0},{12,4},{1,9},{5,13},{9,1},{13,5},{2,10},{6,14},... | collective-permute-start | bytes 393224 | tf_op jit(solution)/shard_map/ppermute | solution.py:935
  230.4 12.6 %collective-permute-start.59 = (bf16[128,512]{1,0:T(8,128)(2,1)S(1)}, bf16[128,512]{1,0:T(8,128)(2,1)S(1)}, u32[]{:S(2)}, u32[]{:S(2)}) collective-permute-start(bf16[128,512]{1,0:T(8,128)(2,1)S(1)} %get-tuple-element.337), channel_id=1, source_target_pairs={{0,12},{4,8},{8,4},{12,0},{1,13},{5,9},{9,5},{13,1},{2,14},{6,10},... | collective-permute-start | bytes 393224 | tf_op jit(solution)/shard_map/ppermute | solution.py:935
  (83 other events, 448.4 us)
Sparse Core Ops, SparseCore 0:
  47.7 66.1 all-gather.11
  181.1 21.2 all-gather.5
  204.0 22.5 all-gather.9
  228.6 25.1 all-gather.7

commit v4 on v3

--- a/solution.py
+++ b/solution.py
@@ -94,7 +94,7 @@
 
 def attn_fwd_body(
     causal, q_rows, kv_parts, w, biases,
-    q_ref, k_ref, v_ref, p_refs, ot_ref, o_ref, il_ref, acc_ref,
+    q_ref, k_ref, v_ref, p_refs, ot_ref, o_ref, il_ref, o_all, wo_all,
 ):
     wq, wk, wv, wo = w
     kv = nn(kv_parts, jnp.concatenate([wk, wv], axis=1))
@@ -110,9 +110,16 @@
     keys = k.shape[0]
     for b in range(blocks):
         n = keys // blocks * (b + 1) if causal else keys
-        s = nt(k[:n], split_pair(q[b * rows : (b + 1) * rows]))
-        top = jnp.max(s, axis=0, keepdims=True)
-        p = jnp.exp(s - top)
+        scores = nt(k[:n], split_pair(q[b * rows : (b + 1) * rows]))
+        if causal:
+            last = rows
+            lane = lax.broadcasted_iota(jnp.int32, (last, 2 * rows), 1)
+            hidden = lane % rows < rows // 2
+            scores = jnp.concatenate(
+                [scores[: n - last], jnp.where(hidden, -1e30, scores[n - last :])], axis=0
+            )
+        top = jnp.max(scores, axis=0, keepdims=True)
+        p = jnp.exp(scores - top)
         inv = 1.0 / jnp.sum(p, axis=0, keepdims=True)
         pb = p.astype(BF)
         p_refs[b][0] = pb
@@ -122,17 +129,23 @@
         o_ref[0, span, :] = ot.T.astype(BF)
         il_ref[0, 0:1, span] = inv[:, :rows]
         il_ref[0, 1:2, span] = inv[:, rows:]
-    acc_ref[...] += nt(o_ref[0], wo)
-
-
-def finish_norm(acc_ref, n_ref, r_ref):
-    normed, inv = norm_stats(acc_ref[...])
+    s = pl.program_id(0)
+    o_all[s] = o_ref[0]
+    wo_all[s] = wo
+
+
+def wide(ref):
+    return jnp.concatenate([ref[i] for i in range(ref.shape[0])], axis=1)
+
+
+def finish_norm(z, n_ref, r_ref):
+    normed, inv = norm_stats(z)
     n_ref[...] = normed
     r_ref[...] = jnp.broadcast_to(inv, r_ref.shape)
 
 
 def self_fwd(ranks_ref, xo_ref, xp_ref, wa_ref, wb_ref, va_ref, vb_ref, *refs):
-    saved, (n_ref, r_ref, vec_ref, bias_ref, x_all, acc_ref) = refs[:10], refs[10:]
+    saved, (n_ref, r_ref, vec_ref, bias_ref, x_all, acc_ref, o_all, wo_all) = refs[:8], refs[8:]
     q_ref, k_ref, v_ref, *p_refs, ot_ref, o_ref, il_ref = saved
     s = pl.program_id(0)
     blocks = 4
@@ -152,15 +165,15 @@
     w = [pick(wa_ref, wb_ref, i, s >= 2) for i in range(4)]
     t = swap(s) ^ ranks_ref[4]
     attn_fwd_body(True, xo_ref[...], x_all[...], w, (vec_ref[t, 3:4], vec_ref[t, 4:5]),
-                  q_ref, k_ref, v_ref, p_refs, ot_ref, o_ref, il_ref, acc_ref)
+                  q_ref, k_ref, v_ref, p_refs, ot_ref, o_ref, il_ref, o_all, wo_all)
 
     @pl.when(s == pl.num_programs(0) - 1)
     def _():
-        finish_norm(acc_ref, n_ref, r_ref)
+        finish_norm(acc_ref[...] + nt(wide(o_all), wide(wo_all)), n_ref, r_ref)
 
 
 def cross_fwd(ranks_ref, n1_ref, mo_ref, mp_ref, wa_ref, wb_ref, vec_ref, *refs):
-    saved, (n_ref, r_ref, m_all, h_low, acc_ref) = refs[:10], refs[10:]
+    saved, (n_ref, r_ref, m_all, h_low, acc_ref, o_all, wo_all) = refs[:7], refs[7:]
     q_ref, k_ref, v_ref, *p_refs, ot_ref, o_ref, il_ref = saved
     s = pl.program_id(0)
     half = mo_ref.shape[0]
@@ -176,11 +189,11 @@
     w = [pick(wa_ref, wb_ref, i, s >= 2) for i in range(4)]
     t = swap(s) ^ ranks_ref[4]
     attn_fwd_body(False, h_low[...], m_all[...], w, (vec_ref[t, 7:8], vec_ref[t, 8:9]),
-                  q_ref, k_ref, v_ref, p_refs, ot_ref, o_ref, il_ref, acc_ref)
+                  q_ref, k_ref, v_ref, p_refs, ot_ref, o_ref, il_ref, o_all, wo_all)
 
     @pl.when(s == pl.num_programs(0) - 1)
     def _():
-        finish_norm(acc_ref, n_ref, r_ref)
+        finish_norm(acc_ref[...] + nt(wide(o_all), wide(wo_all)), n_ref, r_ref)
 
 
 def ffn_both(ranks_ref, n2_ref, r2_ref, c0, c1, c2, c3, w_ref, bias_ref, vec_ref,
@@ -279,7 +292,7 @@
 
 
 def self_bwd(ranks_ref, act_ref, dz_ref, part_ref, w_ref, *refs):
-    saved, (slot_ref, own_ref, peer_ref, out_ref, qg_ref, *scratch) = refs[:10], refs[10:]
+    saved, (slot_ref, own_ref, peer_ref, out_ref, qg_ref, *scratch) = refs[:8], refs[8:]
     shape = w_ref.shape
     w = [w_ref[0, i].reshape(shape[2] * shape[3], shape[4]) for i in (0, 3)]
 
@@ -299,8 +312,8 @@
 
 
 def cross_bwd(ranks_ref, n_ref, r_ref, dz_ref, wa_ref, wb_ref, vec_ref, *refs):
-    saved = refs[:10]
-    keep_ref, send_ref, own_ref, peer_ref, out_ref, vg_ref, qg_ref, *scratch = refs[10:]
+    saved = refs[:7]
+    keep_ref, send_ref, own_ref, peer_ref, out_ref, vg_ref, qg_ref, *scratch = refs[7:]
     s = pl.program_id(0)
     odd = s >= 2
 
@@ -335,10 +348,9 @@
 
 
 def attn_bwd(causal, first, w, saved, store, last, piece, own_ref, peer_ref, qg_ref,
-             dy, dy_t, act_t, acc, dk_ref, dv_ref):
+             dy, dy_t, act_t, acc, dk_ref, dv_ref, dq_all, wq_all):
     s = pl.program_id(0)
-    q_ref, k_ref, v_ref, p0, p1, p2, p3, ot_ref, o_ref, il_ref = saved
-    p_refs = (p0, p1, p2, p3)
+    q_ref, k_ref, v_ref, *p_refs, ot_ref, o_ref, il_ref = saved
     blocks = len(p_refs)
     wq, wo = w
 
@@ -387,109 +399,92 @@
     g_q = nn(act_t[...], dq).astype(BF)
     store(g_q, g_o, piece)
     qg_ref[0] = rows_sum(dq.astype(F32))
-    acc[...] += nt(dq, wq)
+    dq_all[s] = dq
+    wq_all[s] = wq
     for i, ref in enumerate((dk_ref, dv_ref)):
         if causal:
-            for b in range(blocks):
-                at = 2 * b * rows
-                own_ref[i, 0, b * rows : (b + 1) * rows] = ref[at : at + rows]
-                peer_ref[i, 0, b * rows : (b + 1) * rows] = ref[at + rows : at + 2 * rows].astype(BF)
+            part = keys // 8
+            for b in range(4):
+                at, to = 2 * b * part, slice(b * part, (b + 1) * part)
+                own_ref[i, 0, to] = ref[at : at + part].astype(BF)
+                peer_ref[i, 0, to] = ref[at + part : at + 2 * part].astype(BF)
         else:
-            own_ref[i, 0] = ref[: keys // 2]
+            own_ref[i, 0] = ref[: keys // 2].astype(BF)
             peer_ref[i, 0] = ref[keys // 2 :].astype(BF)
 
     @pl.when(s == pl.num_programs(0) - 1)
     def _():
-        last(acc[...])
-
-
-def kv_back(final, lanes, blen, ranks_ref, act_ref, wa_ref, wb_ref, *rest):
+        last(acc[...] + nt(wide(dq_all), wide(wq_all)))
+
+
+def kv_back(final, lanes, blen, ranks_ref, act_ref, *refs):
+    (wk_own, wv_own, wk_peer, wv_peer), rest = refs[:4], refs[4:]
     if final:
-        (own_ref, got_ref, own_hi, got_hi, base_ref, vgc_ref, vgf_ref, bg_ref, qgs_ref, qgs_hi,
-         qgc_ref, vg_mem_ref,
-         h0, h1, h2, h3, keep_ref, send_ref, act_t, acc, vg_self, tiles) = rest
+        (own_low, got_low, own_hi, got_hi, base_ref, vgc_ref, vgf_ref, bg_ref, qgs_ref, qgs_hi,
+         qgc_ref, vg_mem_ref, h0, h1, h2, h3, keep_ref, send_ref, acc, tiles) = rest
+        parts = [(own_low, 0, got_low, 0), (own_low, 1, got_low, 1),
+                 (own_hi, 0, got_hi, 0), (own_hi, 1, got_hi, 1)]
     else:
-        own_ref, got_ref, h0, h1, h2, h3, keep_ref, send_ref, vgrad_ref, act_t, acc = rest
-    s = pl.program_id(0)
-    odd = s >= 2
-    wk = pick(wa_ref, wb_ref, 1, odd)
-    wv = pick(wa_ref, wb_ref, 2, odd)
-
-    @pl.when(s == 0)
-    def _():
-        act_t[...] = act_ref[...].T
-        if final:
-            acc[...] = base_ref[...]
-        else:
-            acc[...] = jnp.zeros_like(acc)
-
-    dk, dv = (own_ref[i, 0] + got_ref[i, 0].astype(F32) for i in range(2))
-    if final:
-        dk = jnp.where(odd, own_hi[0, 0] + got_hi[0, 0].astype(F32), dk)
-        dv = jnp.where(odd, own_hi[1, 0] + got_hi[1, 0].astype(F32), dv)
-    dk, dv = dk.astype(BF), dv.astype(BF)
-    dkv = jnp.concatenate([dk, dv], axis=1)
-    gkv = nn(act_t[...], dkv).astype(BF)
-    piece = gkv.shape[0] // (keep_ref.shape[1] * keep_ref.shape[2])
-    at = s % 2 if final else 0
-
-    @pl.when(jnp.logical_not(odd))
-    def _():
-        put_pieces(keep_ref, at, 0, gkv[:, :PAIR], ranks_ref)
-        put_pieces(keep_ref, at, piece, gkv[:, PAIR:], ranks_ref)
-
-    @pl.when(odd)
-    def _():
-        put_pieces(send_ref, at, 0, gkv[:, :PAIR], ranks_ref)
-        put_pieces(send_ref, at, piece, gkv[:, PAIR:], ranks_ref)
-
-    sums = rows_sum(dv.astype(F32))
-    acc[...] += nt(dkv, jnp.concatenate([wk, wv], axis=1))
+        own_ref, got_ref, h0, h1, h2, h3, keep_ref, send_ref, vgrad_ref, acc = rest
+        parts = [(own_ref, s, got_ref, s ^ 2) for s in range(4)]
+    pairs = len(parts)
+    d = act_ref.shape[1]
+
+    def gathered(own, i, got, j, kind):
+        return (own[kind, i].astype(F32) + got[kind, j].astype(F32)).astype(BF)
+
+    def weight(ref, ry):
+        return ref[ry, 0].reshape(d, PAIR)
+
+    dkv = [gathered(*part, kind) for part in parts for kind in range(2)]
+    wkv = [weight(ref, ry) for refs in ((wk_own, wv_own), (wk_peer, wv_peer))
+           for ry in range(2) for ref in refs]
+    dkv_all = jnp.concatenate(dkv, axis=1)
+    gkv = nn(act_ref[...].T, dkv_all).astype(BF)
+    total = nt(dkv_all, jnp.concatenate(wkv, axis=1))
+    acc[...] = total + base_ref[...] if final else total
+    put_home(acc, (h0, h1, h2, h3), ranks_ref)
+    n_x, n_z = keep_ref.shape[1], keep_ref.shape[2]
+    piece = d // (n_x * n_z)
+    for s in range(pairs):
+        ref = keep_ref if s < 2 else send_ref
+        for kind in range(2):
+            at = (2 * s + kind) * PAIR
+            put_pieces(ref, s % 2, kind * piece, gkv[:, at : at + PAIR], ranks_ref)
+    sums = [rows_sum(dkv[2 * s + 1].astype(F32)) for s in range(pairs)]
     if not final:
-        vgrad_ref[0] = sums
-    else:
-        vg_self[s] = sums
-        pairs = vg_self.shape[0]
-
-        @pl.when(s == 0)
-        def _():
-            for j in range(pairs):
-                at = slice(j * PAIR, (j + 1) * PAIR)
-                rel = swap(j ^ ranks_ref[4])
-                tiles[j, 0:1] = vgc_ref[0:1, at]
-                tiles[j, 1:2] = vgf_ref[3:4, at]
-                tiles[j, 2:3] = vgf_ref[0:1, at]
-                tiles[j, 3:4] = jnp.where(rel < 2, qgs_ref[rel % 2], qgs_hi[rel % 2])
-                tiles[j, 5:6] = vgc_ref[2:3, at]
-                tiles[j, 6:7] = vgc_ref[1:2, at]
-                tiles[j, 7:8] = qgc_ref[rel]
-                tiles[j, 8:9] = vg_mem_ref[rel]
-                tiles[j, 9:10] = vgf_ref[5:6, at]
-                tiles[j, 10:11] = vgf_ref[4:5, at]
-                tiles[j, 11:12] = vgf_ref[2:3, at]
-                tiles[j, 12:13] = vgf_ref[1:2, at]
-                tiles[j, 13:16] = jnp.zeros((3, PAIR), F32)
-
-        tiles[swap(s) ^ ranks_ref[4], 4:5] = sums
-        rows_at = lax.broadcasted_iota(jnp.int32, (16, PAIR), 0)
-        n_x, n_z = keep_ref.shape[1], keep_ref.shape[2]
-
-        @pl.when(s == pairs - 1)
-        def _():
-            for ry in range(2):
-                for rc, ref in enumerate((keep_ref, send_ref)):
-                    for i in range(n_x):
-                        for k in range(n_z):
-                            dc = (i ^ ranks_ref[0]) * n_z + (k ^ ranks_ref[1])
-                            p = dc * pairs + ((2 * ry + rc) ^ ranks_ref[4])
-                            tile = tiles[lax.div(p * lanes, PAIR)]
-                            bias = bg_ref[pl.ds(lax.div(p * blen, PAIR), 1), :]
-                            both = jnp.where(rows_at == 13, bias, tile).astype(BF)
-                            ref[ry, i, k, 2 * piece : 2 * piece + 16] = both
-
-    @pl.when(s == pl.num_programs(0) - 1)
-    def _():
-        put_home(acc, (h0, h1, h2, h3), ranks_ref)
+        for s in range(pairs):
+            vgrad_ref[s] = sums[s]
+        return
+    for j in range(pairs):
+        at = slice(j * PAIR, (j + 1) * PAIR)
+        rel = swap(j ^ ranks_ref[4])
+        tiles[j, 0:1] = vgc_ref[0:1, at]
+        tiles[j, 1:2] = vgf_ref[3:4, at]
+        tiles[j, 2:3] = vgf_ref[0:1, at]
+        tiles[j, 3:4] = jnp.where(rel < 2, qgs_ref[rel % 2], qgs_hi[rel % 2])
+        tiles[j, 5:6] = vgc_ref[2:3, at]
+        tiles[j, 6:7] = vgc_ref[1:2, at]
+        tiles[j, 7:8] = qgc_ref[rel]
+        tiles[j, 8:9] = vg_mem_ref[rel]
+        tiles[j, 9:10] = vgf_ref[5:6, at]
+        tiles[j, 10:11] = vgf_ref[4:5, at]
+        tiles[j, 11:12] = vgf_ref[2:3, at]
+        tiles[j, 12:13] = vgf_ref[1:2, at]
+        tiles[j, 13:16] = jnp.zeros((3, PAIR), F32)
+    for s in range(pairs):
+        tiles[swap(s) ^ ranks_ref[4], 4:5] = sums[s]
+    rows_at = lax.broadcasted_iota(jnp.int32, (16, PAIR), 0)
+    for ry in range(2):
+        for rc, ref in enumerate((keep_ref, send_ref)):
+            for i in range(n_x):
+                for k in range(n_z):
+                    dc = (i ^ ranks_ref[0]) * n_z + (k ^ ranks_ref[1])
+                    p = dc * pairs + ((2 * ry + rc) ^ ranks_ref[4])
+                    tile = tiles[lax.div(p * lanes, PAIR)]
+                    bias = bg_ref[pl.ds(lax.div(p * blen, PAIR), 1), :]
+                    both = jnp.where(rows_at == 13, bias, tile).astype(BF)
+                    ref[ry, i, k, 2 * piece : 2 * piece + 16] = both
 
 
 def pack_rows(*refs):
@@ -499,15 +494,14 @@
 
 
 def pack_rest(*refs):
-    ins, (win, wout), outs, f_ref = refs[1:9], refs[9:11], refs[11:19], refs[19]
-    for ref, out in zip(ins, outs):
+    for ref, out in zip(refs[1:9], refs[9:17]):
         out[...] = ref[0]
+
+
+def pack_weights(lanes, blen, ranks_ref, wqs, wks, wvs, wos, wqc, wkc, wvc, woc, win, wout,
+                 gains, shifts, bias, s_ref, c_ref, f_ref, va, vb):
     f_ref[0] = win[...]
     f_ref[1] = wout[...]
-
-
-def pack_weights(lanes, blen, ranks_ref, wqs, wks, wvs, wos, wqc, wkc, wvc, woc,
-                 gains, shifts, bias, s_ref, c_ref, va, vb):
     n = wqs.shape[0]
     for i, ref in enumerate((wqc, wkc, wvc, woc)):
         c_ref[i * n : (i + 1) * n] = ref[...]
@@ -739,7 +733,7 @@
 def run_attn_fwd(causal, ranks, rows_in, w_own, w_peer, vecs, pairs, deps):
     own, d = rows_in[0].shape
     keys = 2 * own
-    blocks = 4
+    blocks = 2 if causal else 1
     ns = [keys // blocks * (b + 1) if causal else keys for b in range(blocks)]
     qn = 2 * own // blocks
 
@@ -762,6 +756,7 @@
     ins += [(a, whole(a)) for a in vecs]
     scratch = [pltpu.VMEM((keys, d), BF)] + ([] if causal else [pltpu.VMEM((own, d), BF)])
     scratch.append(pltpu.VMEM((own, d), F32))
+    scratch += [pltpu.VMEM((pairs, own, PAIR), BF), pltpu.VMEM((pairs, d, PAIR), BF)]
 
     return launch(
         self_fwd if causal else cross_fwd, "self_fwd" if causal else "cross_fwd",
@@ -805,7 +800,7 @@
     )
 
 
-def bwd_scratch(own, keys, d):
+def bwd_scratch(own, keys, d, pairs):
     return [
         pltpu.VMEM((own, d), BF),
         pltpu.VMEM((d, own), BF),
@@ -813,6 +808,8 @@
         pltpu.VMEM((own, d), F32),
         pltpu.VMEM((keys, PAIR), F32),
         pltpu.VMEM((keys, PAIR), F32),
+        pltpu.VMEM((pairs, own, PAIR), BF),
+        pltpu.VMEM((pairs, d, PAIR), BF),
     ]
 
 
@@ -827,7 +824,7 @@
     prows = w_own.shape[3]
     kv_spec = pl.BlockSpec((2, 1, own, PAIR), lambda s, _: (0, s, 0, 0))
     outs = slot_outs(n_x, n_z, 2 * prows) + [
-        (struct((2, pairs, own, PAIR), F32), kv_spec, True),
+        (struct((2, pairs, own, PAIR), BF), kv_spec, True),
         (struct((2, pairs, own, PAIR), BF), kv_spec, True),
         (struct((own, d), F32), full((own, d))),
         (struct((8, d), F32), full((8, d))),
@@ -843,7 +840,7 @@
         *[per_pair(a) for a in saved],
     ]
     return launch(
-        cross_bwd, "cross_bwd", (pairs,), ranks, ins, outs, bwd_scratch(own, keys, d), deps,
+        cross_bwd, "cross_bwd", (pairs,), ranks, ins, outs, bwd_scratch(own, keys, d, pairs), deps,
         cost=COSTS["cross_bwd"],
     )
 
@@ -858,7 +855,7 @@
     slots = (1, n_x, n_z, 2 * prows, PAIR)
     outs = [
         (struct((2,) + slots[1:], BF), pl.BlockSpec(slots, lambda s, _: (s, 0, 0, 0, 0))),
-        (struct((2, pairs, own, PAIR), F32), kv_spec, True),
+        (struct((2, pairs, own, PAIR), BF), kv_spec, True),
         (struct((2, pairs, own, PAIR), BF), kv_spec, True),
         (struct((own, d), F32), full((own, d))),
         (struct((pairs, 1, PAIR), F32), pl.BlockSpec((1, 1, PAIR), lambda s, _: (s, 0, 0))),
@@ -871,7 +868,7 @@
         *[per_pair(a, first) for a in saved],
     ]
     return launch(
-        self_bwd, "self_bwd", (pairs,), ranks, ins, outs, bwd_scratch(own, keys, d), deps,
+        self_bwd, "self_bwd", (pairs,), ranks, ins, outs, bwd_scratch(own, keys, d, pairs), deps,
         cost=COSTS["self_bwd"],
     )
 
@@ -883,32 +880,26 @@
     final = bool(extra)
     rows = 2 * prows + (16 if final else 0)
     half = own // 4
-    outs = [(struct((half, d), BF), full((half, d)))] * 4
-    scratch = [pltpu.VMEM((d, own), BF), pltpu.VMEM((own, d), F32)]
-    block = (2, 1, own, PAIR)
+    slots = struct((2, n_x, n_z, rows, PAIR), BF)
+    outs = [(struct((half, d), BF), full((half, d)))] * 4 + [(slots, whole(slots))] * 2
+    scratch = [pltpu.VMEM((own, d), F32)]
     if final:
-        slots = struct((2, n_x, n_z, rows, PAIR), BF)
-        outs += [(slots, whole(slots))] * 2
-        scratch += [pltpu.VMEM((pairs, 1, PAIR), F32), pltpu.VMEM((pairs, 16, PAIR), F32)]
-        low = pl.BlockSpec(block, lambda s, _: (0, jnp.minimum(s, 1), 0, 0))
-        high = pl.BlockSpec(block, lambda s, _: (0, jnp.maximum(s - 2, 0), 0, 0))
-        specs = [low, low, high, high]
+        scratch.append(pltpu.VMEM((pairs, 16, PAIR), F32))
     else:
-        outs += slot_outs(n_x, n_z, rows)
-        outs.append(
-            (struct((pairs, 1, PAIR), F32), pl.BlockSpec((1, 1, PAIR), lambda s, _: (s, 0, 0)))
-        )
-        specs = [pl.BlockSpec(block, lambda s, _: (0, s, 0, 0)),
-                 pl.BlockSpec(block, lambda s, _: (0, s ^ 2, 0, 0))]
+        outs.append((struct((pairs, 1, PAIR), F32), full((pairs, 1, PAIR))))
+
+    def mat(w, i):
+        block = (w.shape[0], 1) + w.shape[2:]
+        return (w, pl.BlockSpec(block, lambda *_: (0, i, 0, 0, 0)), True)
+
     ins = [
         (act, whole(act)),
-        (w_own, half_spec(w_own, False), True),
-        (w_peer, half_spec(w_peer, True), True),
-        *[(a, spec, True) for a, spec in zip(parts, specs)],
+        mat(w_own, 1), mat(w_own, 2), mat(w_peer, 1), mat(w_peer, 2),
+        *[(a, whole(a), True) for a in parts],
         *[(a, whole(a)) for a in extra],
     ]
     return launch(
-        functools.partial(kv_back, final, lanes, blen), name, (pairs,), ranks, ins, outs,
+        functools.partial(kv_back, final, lanes, blen), name, (1,), ranks, ins, outs,
         scratch, deps, cost=COSTS[name],
     )
 
@@ -953,14 +944,19 @@
         return around_z(parts), token
 
     x_got, token = sent_rows(inputs, "pack_x", [])
-    s_pack, c_pack, token = local(
+    f_shape = struct((2, prows, hid), BF)
+    s_pack, c_pack, f_pack, token = local(
         functools.partial(pack_weights, lanes, blen), "pack_weights",
-        [struct((4 * prows + 32, PAIR), BF), struct((4 * prows, PAIR), BF)],
+        [struct((4 * prows + 32, PAIR), BF), struct((4 * prows, PAIR), BF), f_shape],
         wq_self, wk_self, wv_self, wo_self.T, wq_cross, wk_cross, wv_cross, wo_cross.T,
-        gains, shifts, ffn_bias.reshape(1, -1), ranks=ranks, deps=[token],
+        w_in, w_out.T, gains, shifts, ffn_bias.reshape(1, -1), ranks=ranks, deps=[token],
+        pinned=(2,),
         scratch=[pltpu.VMEM((16, PAIR), F32), pltpu.VMEM((16, PAIR), F32)],
     )
     s_got = around_z([s_pack] * n_z)
+    w_ffn = lax.all_gather(f_pack, ALL, axis=0, tiled=False).reshape(
+        n_x * n_z, pairs, 2, prows, hid
+    )
     cuts_s = ((0, 2 * prows), (2 * prows, 4 * prows + 32))
     cuts_c = ((0, 2 * prows), (2 * prows, 4 * prows))
 
@@ -1009,15 +1005,9 @@
             *s_last, deps=[token],
         )
         s_last = step(i + 1, sa, sb)
-    f_shape = struct((2, prows, hid), BF)
-    *packed, f_pack, token = launch(
-        pack_rest, "pack_rest", (1,), ranks,
-        packed_rows(memory) + packed_rows(cotangent) + [(a, whole(a)) for a in (w_in, w_out.T)],
-        [(row_part, whole(row_part))] * (2 * n_z) + [(f_shape, whole(f_shape), True)],
-        deps=[token], limit=SMALL_LIMIT,
-    )
-    w_ffn = lax.all_gather(f_pack, ALL, axis=0, tiled=False).reshape(
-        n_x * n_z, pairs, 2, prows, hid
+    *packed, token = launch(
+        pack_rest, "pack_rest", (1,), ranks, packed_rows(memory) + packed_rows(cotangent),
+        [(row_part, whole(row_part))] * (2 * n_z), deps=[token], limit=SMALL_LIMIT,
     )
     m_got, cots = around_z(packed[:n_z]), around_z(packed[n_z:])
     w_shape = struct((2, 4, n_x * n_z, prows, PAIR), BF)

time: 268 us -> 256 us (0.955)
  Pallas kernels: 126 us -> 112 us
  waiting for transfers between devices: 45.6 us -> 48.9 us
    pallas_call x32, Pallas kernels: 126 us -> 112 us  [launch(): return call(*args) if ranks is None else call(ranks, *args)]
    ppermute x63, waiting for transfers between devices: 41.9 us -> 47.4 us  [send(): lax.ppermute(array, axis, [(i, i ^ bit) for i in range(lax.axis_size(axis...]
    all_gather x1, waiting for transfers between devices: 3.6 us -> 0.02 us  [shards(): lax.all_gather(f_pack, ALL, axis=0, tiled=False)]
    unnamed x96 -> x92, local copies, waits for them, and re-layouts: 11.6 us -> 10.4 us
  transfers between devices with their start and end apart: 67 -> 67, of which waited for: 15 -> 18; matrix products, arithmetic and copies ran while one was open for 0% -> 0% of each run, Pallas kernels for 38% -> 36%
where the time goes in v4:
time: 256 us; the launch traced here: 255 us
  Pallas kernels  112 us (44%)
  starting transfers between devices  69.4 us (27%)
  waiting for transfers between devices  48.9 us (19%)
  between operations  14.5 us (6%)
  local copies, waits for them, and re-layouts  10.5 us (4%)
    pallas_call x32, Pallas kernels, launch(): return call(*args) if ranks is None else call(ranks, *args)  112 us
    ppermute x63, starting transfers between devices, send(): lax.ppermute(array, axis, [(i, i ^ bit) for i in range(lax.axis_size(axis...  69.2 us
    ppermute x63, waiting for transfers between devices, send(): lax.ppermute(array, axis, [(i, i ^ bit) for i in range(lax.axis_size(axis...  47.4 us
    unnamed x92, local copies, waits for them, and re-layouts  10.4 us
  transfers between devices with their start and end apart: 67, of which 18 were waited for; matrix products, arithmetic and copies ran while one was open for 0% of the time, Pallas kernels for 36%

profile of v4, /device:TPU:0, one launch (start us, length us, event | category | flops | bytes accessed | tf_op | source)
XLA Modules:
  0.0 255.0 jit_solution(12976223753014594269)
XLA Ops:
  10.6 5.1 %collective-permute-start.2 = (bf16[288,128]{1,0:T(8,128)(2,1)S(1)}, bf16[288,128]{1,0:T(8,128)(2,1)S(1)}, u32[]{:S(2)}, u32[]{:S(2)}) collective-permute-start(bf16[288,128]{1,0:T(8,128)(2,1)S(1)} %get-tuple-element.185.refs_1_), channel_id=1, source_target_pairs={{0,12},{4,8},{8,4},{12,0},{1,13},{5,9},{9,5},{13,1},{2,14},{6,10},... | collective-permute-start | bytes 221192 | tf_op jit(solution)/shard_map/ppermute | solution.py:926
  16.3 3.7 %collective-permute-start.5 = (bf16[128,512]{1,0:T(8,128)(2,1)S(1)}, bf16[128,512]{1,0:T(8,128)(2,1)S(1)}, u32[]{:S(2)}, u32[]{:S(2)}) collective-permute-start(bf16[128,512]{1,0:T(8,128)(2,1)S(1)} %get-tuple-element.189), channel_id=1, source_target_pairs={{0,12},{4,8},{8,4},{12,0},{1,13},{5,9},{9,5},{13,1},{2,14},{6,10},... | collective-permute-start | bytes 393224 | tf_op jit(solution)/shard_map/ppermute | solution.py:926
  20.7 14.8 %collective-permute-done.1.refs_3_ = bf16[288,128]{1,0:T(8,128)(2,1)S(1)} collective-permute-done((bf16[288,128]{1,0:T(8,128)(2,1)S(1)}, bf16[288,128]{1,0:T(8,128)(2,1)S(1)}, u32[]{:S(2)}, u32[]{:S(2)}) %collective-permute-start.1) | collective-permute-done | bytes 73760 | tf_op jit(solution)/shard_map/ppermute | solution.py:926
  36.1 1.9 collective-permute-start.8
  39.6 2.8 %collective-permute-start.11 = (bf16[256,128]{1,0:T(8,128)(2,1)S(1)}, bf16[256,128]{1,0:T(8,128)(2,1)S(1)}, u32[]{:S(2)}, u32[]{:S(2)}) collective-permute-start(bf16[256,128]{1,0:T(8,128)(2,1)S(1)} %get-tuple-element.193.refs_4_), channel_id=1, source_target_pairs={{0,12},{4,8},{8,4},{12,0},{1,13},{5,9},{9,5},{13,1},{2,14},{6,10},... | collective-permute-start | bytes 196616 | tf_op jit(solution)/shard_map/ppermute | solution.py:926
  45.8 3.2 %collective-permute-done.10.refs_6_ = bf16[256,128]{1,0:T(8,128)(2,1)S(1)} collective-permute-done((bf16[256,128]{1,0:T(8,128)(2,1)S(1)}, bf16[256,128]{1,0:T(8,128)(2,1)S(1)}, u32[]{:S(2)}, u32[]{:S(2)}) %collective-permute-start.10) | collective-permute-done | bytes 65568 | tf_op jit(solution)/shard_map/ppermute | solution.py:926
  50.4 1.9 pack_rest.1
  52.3 3.9 %collective-permute-done.12.refs_2_ = bf16[1,2,4,128,128]{4,3,2,1,0:T(8,128)(2,1)S(1)} collective-permute-done((bf16[1,2,4,128,128]{4,3,2,1,0:T(8,128)(2,1)S(1)}, bf16[1,2,4,128,128]{4,3,2,1,0:T(8,128)(2,1)S(1)}, u32[]{:S(2)}, u32[]{:S(2)}) %collective-permute-start.12) | collective-permute-done | bytes 262176 | tf_op jit(solution)/shard_map/ppermute | solution.py:926
  61.2 3.1 %collective-permute-done.16.refs_1_ = bf16[1,1,4,128,128]{4,3,2,1,0:T(8,128)(2,1)S(1)} collective-permute-done((bf16[1,1,4,128,128]{4,3,2,1,0:T(8,128)(2,1)S(1)}, bf16[1,1,4,128,128]{4,3,2,1,0:T(8,128)(2,1)S(1)}, u32[]{:S(2)}, u32[]{:S(2)}) %collective-permute-start.16) | collective-permute-done | bytes 131104 | tf_op jit(solution)/shard_map/ppermute | solution.py:926
  71.1 12.6 %self_fwd.1 = (bf16[4,512,128]{2,1,0:T(8,128)(2,1)}, bf16[4,1024,128]{2,1,0:T(8,128)(2,1)}, bf16[4,1024,128]{2,1,0:T(8,128)(2,1)}, bf16[4,512,512]{2,1,0:T(8,128...) custom-call(s32[5]{0:T(128)S(1)} %stack.23.refs_0_, ...), custom_call_target="tpu_custom_call" | custom-call | flops 24000000000 | bytes 1 | tf_op jit(solution)/shard_map/self_fwd/pallas_call | solution.py:561
  86.4 3.9 %collective-permute-start.25 = (bf16[128,512]{1,0:T(8,128)(2,1)S(1)}, bf16[128,512]{1,0:T(8,128)(2,1)S(1)}, u32[]{:S(2)}, u32[]{:S(2)}) collective-permute-start(bf16[128,512]{1,0:T(8,128)(2,1)S(1)} %get-tuple-element.220), channel_id=1, source_target_pairs={{0,4},{4,0},{8,12},{12,8},{1,5},{5,1},{9,13},{13,9},{2,6},{6,2},{1... | collective-permute-start | bytes 393224 | tf_op jit(solution)/shard_map/ppermute | solution.py:926
  90.3 2.4 collective-permute-start.27
  93.7 14.5 %cross_fwd.1 = (bf16[4,512,128]{2,1,0:T(8,128)(2,1)}, bf16[4,1024,128]{2,1,0:T(8,128)(2,1)}, bf16[4,1024,128]{2,1,0:T(8,128)(2,1)}, bf16[4,1024,1024]{2,1,0:T(8,...) custom-call(s32[5]{0:T(128)S(1)} %stack.23.refs_0_, ...), custom_call_target="tpu_custom_call" | custom-call | flops 28000000000 | bytes 1 | tf_op jit(solution)/shard_map/cross_fwd/pallas_call | solution.py:561
  110.4 14.6 %ffn_both.1 = (bf16[128,512]{1,0:T(8,128)(2,1)S(1)}, bf16[128,512]{1,0:T(8,128)(2,1)S(1)}, bf16[128,512]{1,0:T(8,128)(2,1)S(1)}, bf16[128,512]{1,0:T(8,128)(2,1)...) custom-call(s32[5]{0:T(128)S(1)} %stack.23.refs_0_, ...), custom_call_target="tpu_custom_call" | custom-call | flops 24999999488 | bytes 1 | tf_op jit(solution)/shard_map/ffn_both/pallas_call | solution.py:561
  127.2 2.1 collective-permute-done.31.refs_1_
  132.8 17.5 %cross_bwd.1 = (bf16[2,2,4,128,128]{4,3,2,1,0:T(8,128)(2,1)S(1)}, bf16[2,2,4,128,128]{4,3,2,1,0:T(8,128)(2,1)S(1)}, bf16[2,4,512,128]{3,2,1,0:T(8,128)(2,1)}, bf...) custom-call(s32[5]{0:T(128)S(1)} %stack.23.refs_0_, ...), custom_call_target="tpu_custom_call" | custom-call | flops 30000001024 | bytes 1 | tf_op jit(solution)/shard_map/cross_bwd/pallas_call | solution.py:561
  151.8 9.0 %self_bwd.2 = (bf16[2,2,4,128,128]{4,3,2,1,0:T(8,128)(2,1)S(1)}, bf16[2,2,512,128]{3,2,1,0:T(8,128)(2,1)}, bf16[2,2,512,128]{3,2,1,0:T(8,128)(2,1)}, f32[512,512...) custom-call(s32[5]{0:T(128)S(1)} %stack.23.refs_0_, bf16[512,512]{1,0:T(8,128)(2,1)S(1)} %get-tuple-element.190.refs_1_, ...), custom_call_target="tpu_custom_call" | custom-call | flops 16000000000 | bytes 1 | tf_op jit(solution)/shard_map/self_bwd/pallas_call | solution.py:561
  164.0 3.8 %mem_back.1 = (bf16[128,512]{1,0:T(8,128)(2,1)S(1)}, bf16[128,512]{1,0:T(8,128)(2,1)S(1)}, bf16[128,512]{1,0:T(8,128)(2,1)S(1)}, bf16[128,512]{1,0:T(8,128)(2,1)...) custom-call(s32[5]{0:T(128)S(1)} %stack.23.refs_0_, ...), custom_call_target="tpu_custom_call" | custom-call | flops 8999999488 | bytes 1 | tf_op jit(solution)/shard_map/mem_back/pallas_call | solution.py:561
  170.6 2.0 collective-permute-start.39
  177.6 9.2 %self_bwd.3 = (bf16[2,2,4,128,128]{4,3,2,1,0:T(8,128)(2,1)S(1)}, bf16[2,2,512,128]{3,2,1,0:T(8,128)(2,1)}, bf16[2,2,512,128]{3,2,1,0:T(8,128)(2,1)}, f32[512,512...) custom-call(s32[5]{0:T(128)S(1)} %stack.23.refs_0_, bf16[512,512]{1,0:T(8,128)(2,1)S(1)} %get-tuple-element.190.refs_1_, ...), custom_call_target="tpu_custom_call" | custom-call | flops 16000000000 | bytes 1 | tf_op jit(solution)/shard_map/self_bwd/pallas_call | solution.py:561
  194.5 4.0 %in_back.1 = (bf16[128,512]{1,0:T(8,128)(2,1)S(1)}, bf16[128,512]{1,0:T(8,128)(2,1)S(1)}, bf16[128,512]{1,0:T(8,128)(2,1)S(1)}, bf16[128,512]{1,0:T(8,128)(2,1)S...) custom-call(s32[5]{0:T(128)S(1)} %stack.23.refs_0_, ...), custom_call_target="tpu_custom_call" | custom-call | flops 8999999488 | bytes 1 | tf_op jit(solution)/shard_map/in_back/pallas_call | solution.py:561
  199.7 2.0 collective-permute-start.51
  205.6 6.7 %collective-permute-done.51.refs_3_ = bf16[128,512]{1,0:T(8,128)(2,1)S(1)} collective-permute-done((bf16[128,512]{1,0:T(8,128)(2,1)S(1)}, bf16[128,512]{1,0:T(8,128)(2,1)S(1)}, u32[]{:S(2)}, u32[]{:S(2)}) %collective-permute-start.51) | collective-permute-done | bytes 131104 | tf_op jit(solution)/shard_map/ppermute | solution.py:926
  214.9 2.2 collective-permute-start.57
  217.5 2.0 collective-permute-start.59
  222.6 2.7 %home.3 = (bf16[8,256,512]{2,1,0:T(8,128)(2,1)}, f32[8,128]{1,0:T(8,128)S(1)}) custom-call(bf16[4,4,128,512]{3,2,1,0:T(8,128)(2,1)} %all-gather.6.cloned.1.call-done.refs_0_, f32[8,128]{1,0:T(8,128)S(1)} %get-tuple-element.312.refs_1_), custom_call_target="tpu_custom_call" | custom-call | flops 1000000000 | bytes 1 | tf_op jit(solution)/shard_map/home/pallas_call | solution.py:561
  225.8 2.7 %collective-permute-done.58.refs_3_ = bf16[128,512]{1,0:T(8,128)(2,1)S(1)} collective-permute-done((bf16[128,512]{1,0:T(8,128)(2,1)S(1)}, bf16[128,512]{1,0:T(8,128)(2,1)S(1)}, u32[]{:S(2)}, u32[]{:S(2)}) %collective-permute-start.58) | collective-permute-done | bytes 131104 | tf_op jit(solution)/shard_map/ppermute | solution.py:926
  231.2 3.4 %collective-permute-done.56.refs_7_ = bf16[1,1,4,80,128]{4,3,2,1,0:T(8,128)(2,1)S(1)} collective-permute-done((bf16[1,1,4,80,128]{4,3,2,1,0:T(8,128)(2,1)S(1)}, bf16[1,1,4,80,128]{4,3,2,1,0:T(8,128)(2,1)S(1)}, u32[]{:S(2)}, u32[]{:S(2)}) %collective-permute-start.56) | collective-permute-done | bytes 81952 | tf_op jit(solution)/shard_map/ppermute | solution.py:926
  234.7 2.4 collective-permute-start.61
  237.1 2.0 collective-permute-start.62
  239.1 3.4 %home.4 = (f32[8,256,512]{2,1,0:T(8,128)}, f32[8,128]{1,0:T(8,128)S(1)}) custom-call(bf16[4,4,128,512]{3,2,1,0:T(8,128)(2,1)} %all-gather.10.cloned.1.call-done.refs_0_, f32[8,128]{1,0:T(8,128)S(1)} %get-tuple-element.330.refs_1_), custom_call_target="tpu_custom_call" | custom-call | flops 1000000000 | bytes 1 | tf_op jit(solution)/shard_map/home/pallas_call | solution.py:561
  243.8 3.4 %home.5 = (f32[8,256,512]{2,1,0:T(8,128)}, f32[8,128]{1,0:T(8,128)S(1)}) custom-call(bf16[4,4,128,512]{3,2,1,0:T(8,128)(2,1)} %all-gather.8.cloned.1.call-done.refs_0_, f32[8,128]{1,0:T(8,128)S(1)} %get-tuple-element.331.refs_1_), custom_call_target="tpu_custom_call" | custom-call | flops 1000000000 | bytes 1 | tf_op jit(solution)/shard_map/home/pallas_call | solution.py:561
  (231 shorter events, 71.6 us)
Async XLA Ops:
  7.2 102.0 %all-gather.12.cloned.1.call-start = ((), (), s32[]{:S(2)}) async-start(), calls=%async_computation.3 | async-start | bytes 4325376 | tf_op jit(solution)/shard_map/all_gather | solution.py:957
  10.5 212.0 %all-gather.6.cloned.1.call-start = ((), (), s32[]{:S(2)}) async-start(), calls=%async_computation | async-start | bytes 2621440 | tf_op jit(solution)/shard_map/all_gather | solution.py:1044
  15.7 19.8 %collective-permute-start.3 = (bf16[128,512]{1,0:T(8,128)(2,1)S(1)}, bf16[128,512]{1,0:T(8,128)(2,1)S(1)}, u32[]{:S(2)}, u32[]{:S(2)}) collective-permute-start(bf16[128,512]{1,0:T(8,128)(2,1)S(1)} %get-tuple-element.187), channel_id=1, source_target_pairs={{0,4},{4,0},{8,12},{12,8},{1,5},{5,1},{9,13},{13,9},{2,6},{6,2},{1... | collective-permute-start | bytes 393224 | tf_op jit(solution)/shard_map/ppermute | solution.py:926
  15.7 19.8 %collective-permute-start.4 = (bf16[128,512]{1,0:T(8,128)(2,1)S(1)}, bf16[128,512]{1,0:T(8,128)(2,1)S(1)}, u32[]{:S(2)}, u32[]{:S(2)}) collective-permute-start(bf16[128,512]{1,0:T(8,128)(2,1)S(1)} %get-tuple-element.188), channel_id=1, source_target_pairs={{0,8},{4,12},{8,0},{12,4},{1,9},{5,13},{9,1},{13,5},{2,10},{6,14},... | collective-permute-start | bytes 393224 | tf_op jit(solution)/shard_map/ppermute | solution.py:926
  16.3 19.2 %collective-permute-start.5 = (bf16[128,512]{1,0:T(8,128)(2,1)S(1)}, bf16[128,512]{1,0:T(8,128)(2,1)S(1)}, u32[]{:S(2)}, u32[]{:S(2)}) collective-permute-start(bf16[128,512]{1,0:T(8,128)(2,1)S(1)} %get-tuple-element.189), channel_id=1, source_target_pairs={{0,12},{4,8},{8,4},{12,0},{1,13},{5,9},{9,5},{13,1},{2,14},{6,10},... | collective-permute-start | bytes 393224 | tf_op jit(solution)/shard_map/ppermute | solution.py:926
  20.1 15.4 %collective-permute-start.1 = (bf16[288,128]{1,0:T(8,128)(2,1)S(1)}, bf16[288,128]{1,0:T(8,128)(2,1)S(1)}, u32[]{:S(2)}, u32[]{:S(2)}) collective-permute-start(bf16[288,128]{1,0:T(8,128)(2,1)S(1)} %get-tuple-element.185.refs_1_), channel_id=1, source_target_pairs={{0,8},{4,12},{8,0},{12,4},{1,9},{5,13},{9,1},{13,5},{2,10},{6,14},... | collective-permute-start | bytes 221192 | tf_op jit(solution)/shard_map/ppermute | solution.py:926
  20.1 15.4 %collective-permute-start = (bf16[288,128]{1,0:T(8,128)(2,1)S(1)}, bf16[288,128]{1,0:T(8,128)(2,1)S(1)}, u32[]{:S(2)}, u32[]{:S(2)}) collective-permute-start(bf16[288,128]{1,0:T(8,128)(2,1)S(1)} %get-tuple-element.185.refs_1_), channel_id=1, source_target_pairs={{0,4},{4,0},{8,12},{12,8},{1,5},{5,1},{9,13},{13,9},{2,6},{6,2},{1... | collective-permute-start | bytes 221192 | tf_op jit(solution)/shard_map/ppermute | solution.py:926
  36.1 13.0 %collective-permute-start.8 = (bf16[1,1,4,160,128]{4,3,2,1,0:T(8,128)(2,1)S(1)}, bf16[1,1,4,160,128]{4,3,2,1,0:T(8,128)(2,1)S(1)}, u32[]{:S(2)}, u32[]{:S(2)}) collective-permute-start(bf16[1,1,4,160,128]{4,3,2,1,0:T(8,128)(2,1)S(1)} %get-tuple-element.192.refs_2_), channel_id=1, source_target_pairs={{0,2},{2,0},{1,3},{3,1},{4,6},{6,4},{5,7},{7,5},{8,10},{10,8},{9,1... | collective-permute-start | bytes 491528 | tf_op jit(solution)/shard_map/ppermute | solution.py:926
  60.3 23.5 %collective-permute-start.20 = (bf16[128,512]{1,0:T(8,128)(2,1)S(1)}, bf16[128,512]{1,0:T(8,128)(2,1)S(1)}, u32[]{:S(2)}, u32[]{:S(2)}) collective-permute-start(bf16[128,512]{1,0:T(8,128)(2,1)S(1)} %get-tuple-element.209), channel_id=1, source_target_pairs={{0,4},{4,0},{8,12},{12,8},{1,5},{5,1},{9,13},{13,9},{2,6},{6,2},{1... | collective-permute-start | bytes 393224 | tf_op jit(solution)/shard_map/ppermute | solution.py:926
  64.3 19.9 %collective-permute-start.21 = (bf16[128,512]{1,0:T(8,128)(2,1)S(1)}, bf16[128,512]{1,0:T(8,128)(2,1)S(1)}, u32[]{:S(2)}, u32[]{:S(2)}) collective-permute-start(bf16[128,512]{1,0:T(8,128)(2,1)S(1)} %get-tuple-element.210), channel_id=1, source_target_pairs={{0,8},{4,12},{8,0},{12,4},{1,9},{5,13},{9,1},{13,5},{2,10},{6,14},... | collective-permute-start | bytes 393224 | tf_op jit(solution)/shard_map/ppermute | solution.py:926
  67.8 16.5 %collective-permute-start.22 = (bf16[128,512]{1,0:T(8,128)(2,1)S(1)}, bf16[128,512]{1,0:T(8,128)(2,1)S(1)}, u32[]{:S(2)}, u32[]{:S(2)}) collective-permute-start(bf16[128,512]{1,0:T(8,128)(2,1)S(1)} %get-tuple-element.211), channel_id=1, source_target_pairs={{0,12},{4,8},{8,4},{12,0},{1,13},{5,9},{9,5},{13,1},{2,14},{6,10},... | collective-permute-start | bytes 393224 | tf_op jit(solution)/shard_map/ppermute | solution.py:926
  69.4 14.9 %collective-permute-start.18 = (bf16[1,2,4,128,128]{4,3,2,1,0:T(8,128)(2,1)S(1)}, bf16[1,2,4,128,128]{4,3,2,1,0:T(8,128)(2,1)S(1)}, u32[]{:S(2)}, u32[]{:S(2)}) collective-permute-start(bf16[1,2,4,128,128]{4,3,2,1,0:T(8,128)(2,1)S(1)} %get-tuple-element.206.refs_1_), channel_id=1, source_target_pairs={{0,2},{2,0},{1,3},{3,1},{4,6},{6,4},{5,7},{7,5},{8,10},{10,8},{9,1... | collective-permute-start | bytes 786440 | tf_op jit(solution)/shard_map/ppermute | solution.py:926
  70.2 14.1 %collective-permute-start.19 = (bf16[2,1,4,128,128]{4,3,2,1,0:T(8,128)(2,1)S(1)}, bf16[2,1,4,128,128]{4,3,2,1,0:T(8,128)(2,1)S(1)}, u32[]{:S(2)}, u32[]{:S(2)}) collective-permute-start(bf16[2,1,4,128,128]{4,3,2,1,0:T(8,128)(2,1)S(1)} %get-tuple-element.207.refs_3_), channel_id=1, source_target_pairs={{0,16},{16,0},{1,17},{17,1},{2,18},{18,2},{3,19},{19,3},{4,20},{20... | collective-permute-start | bytes 786440 | tf_op jit(solution)/shard_map/ppermute | solution.py:926
  86.4 22.8 %collective-permute-start.25 = (bf16[128,512]{1,0:T(8,128)(2,1)S(1)}, bf16[128,512]{1,0:T(8,128)(2,1)S(1)}, u32[]{:S(2)}, u32[]{:S(2)}) collective-permute-start(bf16[128,512]{1,0:T(8,128)(2,1)S(1)} %get-tuple-element.220), channel_id=1, source_target_pairs={{0,4},{4,0},{8,12},{12,8},{1,5},{5,1},{9,13},{13,9},{2,6},{6,2},{1... | collective-permute-start | bytes 393224 | tf_op jit(solution)/shard_map/ppermute | solution.py:926
  90.3 18.9 %collective-permute-start.26 = (bf16[128,512]{1,0:T(8,128)(2,1)S(1)}, bf16[128,512]{1,0:T(8,128)(2,1)S(1)}, u32[]{:S(2)}, u32[]{:S(2)}) collective-permute-start(bf16[128,512]{1,0:T(8,128)(2,1)S(1)} %get-tuple-element.221), channel_id=1, source_target_pairs={{0,8},{4,12},{8,0},{12,4},{1,9},{5,13},{9,1},{13,5},{2,10},{6,14},... | collective-permute-start | bytes 393224 | tf_op jit(solution)/shard_map/ppermute | solution.py:926
  90.3 18.9 %collective-permute-start.27 = (bf16[128,512]{1,0:T(8,128)(2,1)S(1)}, bf16[128,512]{1,0:T(8,128)(2,1)S(1)}, u32[]{:S(2)}, u32[]{:S(2)}) collective-permute-start(bf16[128,512]{1,0:T(8,128)(2,1)S(1)} %get-tuple-element.222), channel_id=1, source_target_pairs={{0,12},{4,8},{8,4},{12,0},{1,13},{5,9},{9,5},{13,1},{2,14},{6,10},... | collective-permute-start | bytes 393224 | tf_op jit(solution)/shard_map/ppermute | solution.py:926
  125.1 43.4 %collective-permute-start.28 = (bf16[128,512]{1,0:T(8,128)(2,1)S(1)}, bf16[128,512]{1,0:T(8,128)(2,1)S(1)}, u32[]{:S(2)}, u32[]{:S(2)}) collective-permute-start(bf16[128,512]{1,0:T(8,128)(2,1)S(1)} %get-tuple-element.226), channel_id=1, source_target_pairs={{0,4},{4,0},{8,12},{12,8},{1,5},{5,1},{9,13},{13,9},{2,6},{6,2},{1... | collective-permute-start | bytes 393224 | tf_op jit(solution)/shard_map/ppermute | solution.py:926
  126.3 42.2 %collective-permute-start.29 = (bf16[128,512]{1,0:T(8,128)(2,1)S(1)}, bf16[128,512]{1,0:T(8,128)(2,1)S(1)}, u32[]{:S(2)}, u32[]{:S(2)}) collective-permute-start(bf16[128,512]{1,0:T(8,128)(2,1)S(1)} %get-tuple-element.227), channel_id=1, source_target_pairs={{0,8},{4,12},{8,0},{12,4},{1,9},{5,13},{9,1},{13,5},{2,10},{6,14},... | collective-permute-start | bytes 393224 | tf_op jit(solution)/shard_map/ppermute | solution.py:926
  129.8 20.6 %collective-permute-start.33 = (bf16[1,2,4,64,512]{4,3,2,1,0:T(8,128)(2,1)S(1)}, bf16[1,2,4,64,512]{4,3,2,1,0:T(8,128)(2,1)S(1)}, u32[]{:S(2)}, u32[]{:S(2)}) collective-permute-start(bf16[1,2,4,64,512]{4,3,2,1,0:T(8,128)(2,1)S(1)} %get-tuple-element.245), channel_id=1, source_target_pairs={{0,2},{2,0},{1,3},{3,1},{4,6},{6,4},{5,7},{7,5},{8,10},{10,8},{9,1... | collective-permute-start | bytes 1572872 | tf_op jit(solution)/shard_map/ppermute | solution.py:926
  131.3 19.1 %collective-permute-start.34 = (bf16[2,1,4,64,512]{4,3,2,1,0:T(8,128)(2,1)S(1)}, bf16[2,1,4,64,512]{4,3,2,1,0:T(8,128)(2,1)S(1)}, u32[]{:S(2)}, u32[]{:S(2)}) collective-permute-start(bf16[2,1,4,64,512]{4,3,2,1,0:T(8,128)(2,1)S(1)} %get-tuple-element.247), channel_id=1, source_target_pairs={{0,16},{16,0},{1,17},{17,1},{2,18},{18,2},{3,19},{19,3},{4,20},{20... | collective-permute-start | bytes 1572872 | tf_op jit(solution)/shard_map/ppermute | solution.py:926
  150.3 12.6 %collective-permute-start.32 = (bf16[2,4,512,128]{3,2,1,0:T(8,128)(2,1)}, bf16[2,4,512,128]{3,2,1,0:T(8,128)(2,1)S(1)}, u32[]{:S(2)}, u32[]{:S(2)}) collective-permute-start(bf16[2,4,512,128]{3,2,1,0:T(8,128)(2,1)} %get-tuple-element.243), channel_id=1, source_target_pairs={{0,1},{1,0},{2,3},{3,2},{4,5},{5,4},{6,7},{7,6},{8,9},{9,8},{10,11... | collective-permute-start | bytes 3145736 | tf_op jit(solution)/shard_map/ppermute | solution.py:926
  170.0 69.1 %all-gather.10.cloned.1.call-start = ((), (), s32[]{:S(2)}) async-start(), calls=%async_computation.2 | async-start | bytes 2621440 | tf_op jit(solution)/shard_map/all_gather | solution.py:1044
  170.1 16.7 %collective-permute-start.44 = (bf16[2,2,4,128,128]{4,3,2,1,0:T(8,128)(2,1)S(1)}, bf16[2,2,4,128,128]{4,3,2,1,0:T(8,128)(2,1)S(1)}, u32[]{:S(2)}, u32[]{:S(2)}) collective-permute-start(bf16[2,2,4,128,128]{4,3,2,1,0:T(8,128)(2,1)S(1)} %get-tuple-element.290), channel_id=1, source_target_pairs={{0,1},{1,0},{2,3},{3,2},{4,5},{5,4},{6,7},{7,6},{8,9},{9,8},{10,11... | collective-permute-start | bytes 1572872 | tf_op jit(solution)/shard_map/ppermute | solution.py:926
  170.6 17.3 %collective-permute-start.39 = (bf16[128,512]{1,0:T(8,128)(2,1)S(1)}, bf16[128,512]{1,0:T(8,128)(2,1)S(1)}, u32[]{:S(2)}, u32[]{:S(2)}) collective-permute-start(bf16[128,512]{1,0:T(8,128)(2,1)S(1)} %get-tuple-element.282), channel_id=1, source_target_pairs={{0,4},{4,0},{8,12},{12,8},{1,5},{5,1},{9,13},{13,9},{2,6},{6,2},{1... | collective-permute-start | bytes 393224 | tf_op jit(solution)/shard_map/ppermute | solution.py:926
  172.7 15.3 %collective-permute-start.40 = (bf16[128,512]{1,0:T(8,128)(2,1)S(1)}, bf16[128,512]{1,0:T(8,128)(2,1)S(1)}, u32[]{:S(2)}, u32[]{:S(2)}) collective-permute-start(bf16[128,512]{1,0:T(8,128)(2,1)S(1)} %get-tuple-element.283), channel_id=1, source_target_pairs={{0,8},{4,12},{8,0},{12,4},{1,9},{5,13},{9,1},{13,5},{2,10},{6,14},... | collective-permute-start | bytes 393224 | tf_op jit(solution)/shard_map/ppermute | solution.py:926
  173.4 14.5 %collective-permute-start.41 = (bf16[128,512]{1,0:T(8,128)(2,1)S(1)}, bf16[128,512]{1,0:T(8,128)(2,1)S(1)}, u32[]{:S(2)}, u32[]{:S(2)}) collective-permute-start(bf16[128,512]{1,0:T(8,128)(2,1)S(1)} %get-tuple-element.284), channel_id=1, source_target_pairs={{0,12},{4,8},{8,4},{12,0},{1,13},{5,9},{9,5},{13,1},{2,14},{6,10},... | collective-permute-start | bytes 393224 | tf_op jit(solution)/shard_map/ppermute | solution.py:926
  175.0 12.4 %collective-permute-start.43 = (bf16[2,2,4,128,128]{4,3,2,1,0:T(8,128)(2,1)S(1)}, bf16[2,2,4,128,128]{4,3,2,1,0:T(8,128)(2,1)S(1)}, u32[]{:S(2)}, u32[]{:S(2)}) collective-permute-start(bf16[2,2,4,128,128]{4,3,2,1,0:T(8,128)(2,1)S(1)} %get-tuple-element.288), channel_id=1, source_target_pairs={{0,1},{1,0},{2,3},{3,2},{4,5},{5,4},{6,7},{7,6},{8,9},{9,8},{10,11... | collective-permute-start | bytes 1572872 | tf_op jit(solution)/shard_map/ppermute | solution.py:926
  189.4 54.4 %all-gather.8.cloned.1.call-start = ((), (), s32[]{:S(2)}) async-start(), calls=%async_computation.1 | async-start | bytes 2621440 | tf_op jit(solution)/shard_map/all_gather | solution.py:1044
  189.5 13.5 %collective-permute-start.46 = (bf16[1,2,4,192,128]{4,3,2,1,0:T(8,128)(2,1)S(1)}, bf16[1,2,4,192,128]{4,3,2,1,0:T(8,128)(2,1)S(1)}, u32[]{:S(2)}, u32[]{:S(2)}) collective-permute-start(bf16[1,2,4,192,128]{4,3,2,1,0:T(8,128)(2,1)S(1)} %get-tuple-element.297), channel_id=1, source_target_pairs={{0,2},{2,0},{1,3},{3,1},{4,6},{6,4},{5,7},{7,5},{8,10},{10,8},{9,1... | collective-permute-start | bytes 1179656 | tf_op jit(solution)/shard_map/ppermute | solution.py:926
  199.7 12.6 %collective-permute-start.51 = (bf16[128,512]{1,0:T(8,128)(2,1)S(1)}, bf16[128,512]{1,0:T(8,128)(2,1)S(1)}, u32[]{:S(2)}, u32[]{:S(2)}) collective-permute-start(bf16[128,512]{1,0:T(8,128)(2,1)S(1)} %get-tuple-element.308), channel_id=1, source_target_pairs={{0,8},{4,12},{8,0},{12,4},{1,9},{5,13},{9,1},{13,5},{2,10},{6,14},... | collective-permute-start | bytes 393224 | tf_op jit(solution)/shard_map/ppermute | solution.py:926
  234.7 12.6 %collective-permute-start.60 = (bf16[528,128]{1,0:T(8,128)(2,1)S(1)}, bf16[528,128]{1,0:T(8,128)(2,1)S(1)}, u32[]{:S(2)}, u32[]{:S(2)}) collective-permute-start(bf16[528,128]{1,0:T(8,128)(2,1)S(1)} %get-tuple-element.335), channel_id=1, source_target_pairs={{0,4},{4,0},{8,12},{12,8},{1,5},{5,1},{9,13},{13,9},{2,6},{6,2},{1... | collective-permute-start | bytes 405512 | tf_op jit(solution)/shard_map/ppermute | solution.py:926
  234.7 12.5 %collective-permute-start.61 = (bf16[528,128]{1,0:T(8,128)(2,1)S(1)}, bf16[528,128]{1,0:T(8,128)(2,1)S(1)}, u32[]{:S(2)}, u32[]{:S(2)}) collective-permute-start(bf16[528,128]{1,0:T(8,128)(2,1)S(1)} %get-tuple-element.336), channel_id=1, source_target_pairs={{0,8},{4,12},{8,0},{12,4},{1,9},{5,13},{9,1},{13,5},{2,10},{6,14},... | collective-permute-start | bytes 405512 | tf_op jit(solution)/shard_map/ppermute | solution.py:926
  (81 other events, 432.0 us)
Sparse Core Ops, SparseCore 0:
  11.5 78.1 all-gather.11
  170.1 22.4 all-gather.5
  194.2 23.4 all-gather.9
  219.7 24.0 all-gather.7

commit v5 on v4

--- a/solution.py
+++ b/solution.py
@@ -745,7 +745,7 @@
         saved((own, PAIR), BF), saved((keys, PAIR), BF), saved((keys, PAIR), BF),
         *[saved((n, qn), BF) for n in ns],
         saved((PAIR, own), BF), saved((own, PAIR), BF), saved((8, own), F32),
-        (struct((own, d), F32), full((own, d))),
+        (struct((own, d), F32), full((own, d))) + (() if causal else (True,)),
         (struct((own, PAIR), F32), full((own, PAIR))),
     ]
     if causal:
@@ -779,7 +779,7 @@
         (struct((8, d), F32), full((8, d))),
         (struct((16, PAIR), F32), full((16, PAIR))),
     ]
-    ins = [(n2, whole(n2)), (r2, whole(r2))] + [(c, whole(c)) for c in cots] + [
+    ins = [(n2, whole(n2), True), (r2, whole(r2))] + [(c, whole(c)) for c in cots] + [
         (w, pl.BlockSpec((dc, 1, 2, prows, hid), lambda p, t, _: (0, t, 0, 0, 0)), True),
         (bias, whole(bias)),
         (vec, whole(vec)),
@@ -857,13 +857,13 @@
         (struct((2,) + slots[1:], BF), pl.BlockSpec(slots, lambda s, _: (s, 0, 0, 0, 0))),
         (struct((2, pairs, own, PAIR), BF), kv_spec, True),
         (struct((2, pairs, own, PAIR), BF), kv_spec, True),
-        (struct((own, d), F32), full((own, d))),
+        (struct((own, d), F32), full((own, d)), True),
         (struct((pairs, 1, PAIR), F32), pl.BlockSpec((1, 1, PAIR), lambda s, _: (s, 0, 0))),
     ]
     ins = [
         (act, whole(act)),
-        (dz, whole(dz)),
-        (part, whole(part)),
+        (dz, whole(dz)) if first else (dz, whole(dz), True),
+        (part, whole(part)) if first else (part, whole(part), True),
         (w, pl.BlockSpec((1,) + w.shape[1:], lambda s, _: (s, 0, 0, 0, 0)), True),
         *[per_pair(a, first) for a in saved],
     ]
@@ -896,7 +896,7 @@
         (act, whole(act)),
         mat(w_own, 1), mat(w_own, 2), mat(w_peer, 1), mat(w_peer, 2),
         *[(a, whole(a), True) for a in parts],
-        *[(a, whole(a)) for a in extra],
+        *[(a, whole(a), True) if i == 0 else (a, whole(a)) for i, a in enumerate(extra)],
     ]
     return launch(
         functools.partial(kv_back, final, lanes, blen), name, (1,), ranks, ins, outs,
@@ -1010,6 +1010,7 @@
         [(row_part, whole(row_part))] * (2 * n_z), deps=[token], limit=SMALL_LIMIT,
     )
     m_got, cots = around_z(packed[:n_z]), around_z(packed[n_z:])
+    c_last, token = more(c_last, [token])
     w_shape = struct((2, 4, n_x * n_z, prows, PAIR), BF)
     ws_own, v_own, token = local(
         functools.partial(assemble, lanes), "assemble",
@@ -1017,7 +1018,6 @@
         scratch=[pltpu.VMEM((pairs + 1, 16, PAIR), F32)], deps=[token], pinned=(0,),
     )
     v_peer, ws_peer = send(v_own, "tc", 1), send(ws_own, "tc", 1)
-    c_last, token = more(c_last, [token])
     *saved_self, n1, r1, vec, bias, token = run_attn_fwd(
         True, ranks, (xo, xp), ws_own, ws_peer, (v_own, v_peer), pairs, [token]
     )
@@ -1113,13 +1113,13 @@
     s_send, own_hi, peer_hi, base, qgs_hi, token = run_self_bwd(
         2, ranks, xo, dz1, dz1, ws_peer, saved_self, n_x, n_z, [token]
     )
+    out_here, token = home_rows(out_got, [token])
+    out_every = home_all(out_here)
     ffn, token = spread(ffn, [token])
     *mem_rows, m_keep, m_send, vgc, token = run_kv_back(
         "mem_back", ranks, mo, (c_own, c_got), wc_own, wc_peer, (), lanes, blen, n_x, n_z, [token]
     )
     mem_got = around_z(mem_rows)
-    out_here, token = home_rows(out_got, [token])
-    out_every = home_all(out_here)
     got_low, s_add = to_core(peer_hi, s_send)
     s_keep, own_low, peer_low, base, qgs, token = run_self_bwd(
         0, ranks, xo, dz1, base, ws_own, saved_self, n_x, n_z, [token]

time: 256 us -> 250 us (0.977)
  waiting for transfers between devices: 48.9 us -> 37.8 us
  starting transfers between devices: 69.4 us -> 76.5 us
  local copies, waits for them, and re-layouts: 10.5 us -> 4.99 us
  Pallas kernels: 112 us -> 116 us
    ppermute x63, waiting for transfers between devices: 47.4 us -> 37.7 us  [send(): lax.ppermute(array, axis, [(i, i ^ bit) for i in range(lax.axis_size(axis...]
    ppermute x63, starting transfers between devices: 69.2 us -> 76.1 us  [send(): lax.ppermute(array, axis, [(i, i ^ bit) for i in range(lax.axis_size(axis...]
    unnamed x92 -> x76, local copies, waits for them, and re-layouts: 10.4 us -> 4.9 us
    pallas_call x32, Pallas kernels: 112 us -> 116 us  [launch(): return call(*args) if ranks is None else call(ranks, *args)]
  transfers between devices with their start and end apart: 67 -> 67, of which waited for: 18 -> 11; matrix products, arithmetic and copies ran while one was open for 0% -> 0% of each run, Pallas kernels for 36% -> 39%
where the time goes in v5:
time: 250 us
  Pallas kernels  116 us (46%)
  starting transfers between devices  76.5 us (31%)
  waiting for transfers between devices  37.8 us (15%)
  between operations  14.6 us (6%)
  local copies, waits for them, and re-layouts  4.99 us (2%)
    pallas_call x32, Pallas kernels, launch(): return call(*args) if ranks is None else call(ranks, *args)  116 us
    ppermute x63, starting transfers between devices, send(): lax.ppermute(array, axis, [(i, i ^ bit) for i in range(lax.axis_size(axis...  76.1 us
    ppermute x63, waiting for transfers between devices, send(): lax.ppermute(array, axis, [(i, i ^ bit) for i in range(lax.axis_size(axis...  37.7 us
  transfers between devices with their start and end apart: 67, of which 11 were waited for; matrix products, arithmetic and copies ran while one was open for 0% of the time, Pallas kernels for 39%

profile of v5, /device:TPU:0, one launch (start us, length us, event | category | flops | bytes accessed | tf_op | source)
XLA Modules:
  0.0 249.8 jit_solution(11444643587635470634)
XLA Ops:
  10.6 5.1 %collective-permute-start.2 = (bf16[288,128]{1,0:T(8,128)(2,1)S(1)}, bf16[288,128]{1,0:T(8,128)(2,1)S(1)}, u32[]{:S(2)}, u32[]{:S(2)}) collective-permute-start(bf16[288,128]{1,0:T(8,128)(2,1)S(1)} %get-tuple-element.185.refs_1_), channel_id=1, source_target_pairs={{0,12},{4,8},{8,4},{12,0},{1,13},{5,9},{9,5},{13,1},{2,14},{6,10},... | collective-permute-start | bytes 221192 | tf_op jit(solution)/shard_map/ppermute | solution.py:926
  16.3 3.7 %collective-permute-start.5 = (bf16[128,512]{1,0:T(8,128)(2,1)S(1)}, bf16[128,512]{1,0:T(8,128)(2,1)S(1)}, u32[]{:S(2)}, u32[]{:S(2)}) collective-permute-start(bf16[128,512]{1,0:T(8,128)(2,1)S(1)} %get-tuple-element.189), channel_id=1, source_target_pairs={{0,12},{4,8},{8,4},{12,0},{1,13},{5,9},{9,5},{13,1},{2,14},{6,10},... | collective-permute-start | bytes 393224 | tf_op jit(solution)/shard_map/ppermute | solution.py:926
  20.7 14.8 %collective-permute-done.1.refs_3_ = bf16[288,128]{1,0:T(8,128)(2,1)S(1)} collective-permute-done((bf16[288,128]{1,0:T(8,128)(2,1)S(1)}, bf16[288,128]{1,0:T(8,128)(2,1)S(1)}, u32[]{:S(2)}, u32[]{:S(2)}) %collective-permute-start.1) | collective-permute-done | bytes 73760 | tf_op jit(solution)/shard_map/ppermute | solution.py:926
  39.6 2.8 %collective-permute-start.11 = (bf16[256,128]{1,0:T(8,128)(2,1)S(1)}, bf16[256,128]{1,0:T(8,128)(2,1)S(1)}, u32[]{:S(2)}, u32[]{:S(2)}) collective-permute-start(bf16[256,128]{1,0:T(8,128)(2,1)S(1)} %get-tuple-element.193.refs_4_), channel_id=1, source_target_pairs={{0,12},{4,8},{8,4},{12,0},{1,13},{5,9},{9,5},{13,1},{2,14},{6,10},... | collective-permute-start | bytes 196616 | tf_op jit(solution)/shard_map/ppermute | solution.py:926
  45.8 3.2 %collective-permute-done.10.refs_6_ = bf16[256,128]{1,0:T(8,128)(2,1)S(1)} collective-permute-done((bf16[256,128]{1,0:T(8,128)(2,1)S(1)}, bf16[256,128]{1,0:T(8,128)(2,1)S(1)}, u32[]{:S(2)}, u32[]{:S(2)}) %collective-permute-start.10) | collective-permute-done | bytes 65568 | tf_op jit(solution)/shard_map/ppermute | solution.py:926
  55.3 3.2 %collective-permute-done.14.refs_1_ = bf16[1,1,4,128,128]{4,3,2,1,0:T(8,128)(2,1)S(1)} collective-permute-done((bf16[1,1,4,128,128]{4,3,2,1,0:T(8,128)(2,1)S(1)}, bf16[1,1,4,128,128]{4,3,2,1,0:T(8,128)(2,1)S(1)}, u32[]{:S(2)}, u32[]{:S(2)}) %collective-permute-start.14) | collective-permute-done | bytes 131104 | tf_op jit(solution)/shard_map/ppermute | solution.py:926
  60.6 2.6 %collective-permute-start.20 = (bf16[128,512]{1,0:T(8,128)(2,1)S(1)}, bf16[128,512]{1,0:T(8,128)(2,1)S(1)}, u32[]{:S(2)}, u32[]{:S(2)}) collective-permute-start(bf16[128,512]{1,0:T(8,128)(2,1)S(1)} %get-tuple-element.209), channel_id=1, source_target_pairs={{0,4},{4,0},{8,12},{12,8},{1,5},{5,1},{9,13},{13,9},{2,6},{6,2},{1... | collective-permute-start | bytes 393224 | tf_op jit(solution)/shard_map/ppermute | solution.py:926
  64.3 2.0 collective-permute-start.22
  68.8 12.6 %self_fwd.1 = (bf16[4,512,128]{2,1,0:T(8,128)(2,1)}, bf16[4,1024,128]{2,1,0:T(8,128)(2,1)}, bf16[4,1024,128]{2,1,0:T(8,128)(2,1)}, bf16[4,512,512]{2,1,0:T(8,128...) custom-call(s32[5]{0:T(128)S(1)} %stack.23.refs_0_, ...), custom_call_target="tpu_custom_call" | custom-call | flops 24000000000 | bytes 1 | tf_op jit(solution)/shard_map/self_fwd/pallas_call | solution.py:561
  84.3 6.0 %collective-permute-start.25 = (bf16[128,512]{1,0:T(8,128)(2,1)S(1)}, bf16[128,512]{1,0:T(8,128)(2,1)S(1)}, u32[]{:S(2)}, u32[]{:S(2)}) collective-permute-start(bf16[128,512]{1,0:T(8,128)(2,1)S(1)} %get-tuple-element.220), channel_id=1, source_target_pairs={{0,4},{4,0},{8,12},{12,8},{1,5},{5,1},{9,13},{13,9},{2,6},{6,2},{1... | collective-permute-start | bytes 393224 | tf_op jit(solution)/shard_map/ppermute | solution.py:926
  90.3 2.4 collective-permute-start.27
  93.7 14.8 %cross_fwd.1 = (bf16[4,512,128]{2,1,0:T(8,128)(2,1)}, bf16[4,1024,128]{2,1,0:T(8,128)(2,1)}, bf16[4,1024,128]{2,1,0:T(8,128)(2,1)}, bf16[4,1024,1024]{2,1,0:T(8,...) custom-call(s32[5]{0:T(128)S(1)} %stack.23.refs_0_, ...), custom_call_target="tpu_custom_call" | custom-call | flops 28000000000 | bytes 1 | tf_op jit(solution)/shard_map/cross_fwd/pallas_call | solution.py:561
  108.6 14.9 %ffn_both.1 = (bf16[128,512]{1,0:T(8,128)(2,1)S(1)}, bf16[128,512]{1,0:T(8,128)(2,1)S(1)}, bf16[128,512]{1,0:T(8,128)(2,1)S(1)}, bf16[128,512]{1,0:T(8,128)(2,1)...) custom-call(s32[5]{0:T(128)S(1)} %stack.23.refs_0_, ...), custom_call_target="tpu_custom_call" | custom-call | flops 24999999488 | bytes 1 | tf_op jit(solution)/shard_map/ffn_both/pallas_call | solution.py:561
  125.6 2.4 collective-permute-start.30
  131.3 17.5 %cross_bwd.1 = (bf16[2,2,4,128,128]{4,3,2,1,0:T(8,128)(2,1)S(1)}, bf16[2,2,4,128,128]{4,3,2,1,0:T(8,128)(2,1)S(1)}, bf16[2,4,512,128]{3,2,1,0:T(8,128)(2,1)}, bf...) custom-call(s32[5]{0:T(128)S(1)} %stack.23.refs_0_, ...), custom_call_target="tpu_custom_call" | custom-call | flops 30000001024 | bytes 1 | tf_op jit(solution)/shard_map/cross_bwd/pallas_call | solution.py:561
  151.1 9.4 %self_bwd.2 = (bf16[2,2,4,128,128]{4,3,2,1,0:T(8,128)(2,1)S(1)}, bf16[2,2,512,128]{3,2,1,0:T(8,128)(2,1)}, bf16[2,2,512,128]{3,2,1,0:T(8,128)(2,1)}, f32[512,512...) custom-call(s32[5]{0:T(128)S(1)} %stack.23.refs_0_, bf16[512,512]{1,0:T(8,128)(2,1)S(1)} %get-tuple-element.190.refs_1_, ...), custom_call_target="tpu_custom_call" | custom-call | flops 16000000000 | bytes 1 | tf_op jit(solution)/shard_map/self_bwd/pallas_call | solution.py:561
  165.9 4.0 %mem_back.1 = (bf16[128,512]{1,0:T(8,128)(2,1)S(1)}, bf16[128,512]{1,0:T(8,128)(2,1)S(1)}, bf16[128,512]{1,0:T(8,128)(2,1)S(1)}, bf16[128,512]{1,0:T(8,128)(2,1)...) custom-call(s32[5]{0:T(128)S(1)} %stack.23.refs_0_, ...), custom_call_target="tpu_custom_call" | custom-call | flops 8999999488 | bytes 1 | tf_op jit(solution)/shard_map/mem_back/pallas_call | solution.py:561
  171.9 2.5 %collective-permute-start.41 = (bf16[128,512]{1,0:T(8,128)(2,1)S(1)}, bf16[128,512]{1,0:T(8,128)(2,1)S(1)}, u32[]{:S(2)}, u32[]{:S(2)}) collective-permute-start(bf16[128,512]{1,0:T(8,128)(2,1)S(1)} %get-tuple-element.284), channel_id=1, source_target_pairs={{0,12},{4,8},{8,4},{12,0},{1,13},{5,9},{9,5},{13,1},{2,14},{6,10},... | collective-permute-start | bytes 393224 | tf_op jit(solution)/shard_map/ppermute | solution.py:926
  174.4 10.5 %self_bwd.3 = (bf16[2,2,4,128,128]{4,3,2,1,0:T(8,128)(2,1)S(1)}, bf16[2,2,512,128]{3,2,1,0:T(8,128)(2,1)}, bf16[2,2,512,128]{3,2,1,0:T(8,128)(2,1)}, f32[512,512...) custom-call(s32[5]{0:T(128)S(1)} %stack.23.refs_0_, bf16[512,512]{1,0:T(8,128)(2,1)S(1)} %get-tuple-element.190.refs_1_, ...), custom_call_target="tpu_custom_call" | custom-call | flops 16000000000 | bytes 1 | tf_op jit(solution)/shard_map/self_bwd/pallas_call | solution.py:561
  190.6 4.6 %in_back.1 = (bf16[128,512]{1,0:T(8,128)(2,1)S(1)}, bf16[128,512]{1,0:T(8,128)(2,1)S(1)}, bf16[128,512]{1,0:T(8,128)(2,1)S(1)}, bf16[128,512]{1,0:T(8,128)(2,1)S...) custom-call(s32[5]{0:T(128)S(1)} %stack.23.refs_0_, ...), custom_call_target="tpu_custom_call" | custom-call | flops 8999999488 | bytes 1 | tf_op jit(solution)/shard_map/in_back/pallas_call | solution.py:561
  197.2 2.4 collective-permute-start.52
  199.6 3.2 %collective-permute-done.46.refs_1_ = bf16[1,2,4,192,128]{4,3,2,1,0:T(8,128)(2,1)S(1)} collective-permute-done((bf16[1,2,4,192,128]{4,3,2,1,0:T(8,128)(2,1)S(1)}, bf16[1,2,4,192,128]{4,3,2,1,0:T(8,128)(2,1)S(1)}, u32[]{:S(2)}, u32[]{:S(2)}) %collective-permute-start.46) | collective-permute-done | bytes 393248 | tf_op jit(solution)/shard_map/ppermute | solution.py:926
  205.0 3.3 %collective-permute-done.51.refs_3_ = bf16[128,512]{1,0:T(8,128)(2,1)S(1)} collective-permute-done((bf16[128,512]{1,0:T(8,128)(2,1)S(1)}, bf16[128,512]{1,0:T(8,128)(2,1)S(1)}, u32[]{:S(2)}, u32[]{:S(2)}) %collective-permute-start.51) | collective-permute-done | bytes 131104 | tf_op jit(solution)/shard_map/ppermute | solution.py:926
  211.0 2.3 collective-permute-start.57
  213.3 2.4 collective-permute-start.59
  219.1 2.7 %home.3 = (bf16[8,256,512]{2,1,0:T(8,128)(2,1)}, f32[8,128]{1,0:T(8,128)S(1)}) custom-call(bf16[4,4,128,512]{3,2,1,0:T(8,128)(2,1)} %all-gather.6.cloned.1.call-done.refs_0_, f32[8,128]{1,0:T(8,128)S(1)} %get-tuple-element.312.refs_1_), custom_call_target="tpu_custom_call" | custom-call | flops 1000000000 | bytes 1 | tf_op jit(solution)/shard_map/home/pallas_call | solution.py:561
  222.6 2.0 collective-permute-done.58.refs_3_
  227.2 3.5 %collective-permute-done.56.refs_7_ = bf16[1,1,4,80,128]{4,3,2,1,0:T(8,128)(2,1)S(1)} collective-permute-done((bf16[1,1,4,80,128]{4,3,2,1,0:T(8,128)(2,1)S(1)}, bf16[1,1,4,80,128]{4,3,2,1,0:T(8,128)(2,1)S(1)}, u32[]{:S(2)}, u32[]{:S(2)}) %collective-permute-start.56) | collective-permute-done | bytes 81952 | tf_op jit(solution)/shard_map/ppermute | solution.py:926
  230.9 2.4 collective-permute-start.61
  233.3 2.0 collective-permute-start.62
  235.2 3.4 %home.4 = (f32[8,256,512]{2,1,0:T(8,128)}, f32[8,128]{1,0:T(8,128)S(1)}) custom-call(bf16[4,4,128,512]{3,2,1,0:T(8,128)(2,1)} %all-gather.10.cloned.1.call-done.refs_0_, f32[8,128]{1,0:T(8,128)S(1)} %get-tuple-element.330.refs_1_), custom_call_target="tpu_custom_call" | custom-call | flops 1000000000 | bytes 1 | tf_op jit(solution)/shard_map/home/pallas_call | solution.py:561
  238.6 3.4 %home.5 = (f32[8,256,512]{2,1,0:T(8,128)}, f32[8,128]{1,0:T(8,128)S(1)}) custom-call(bf16[4,4,128,512]{3,2,1,0:T(8,128)(2,1)} %all-gather.8.cloned.1.call-done.refs_0_, f32[8,128]{1,0:T(8,128)S(1)} %get-tuple-element.331.refs_1_), custom_call_target="tpu_custom_call" | custom-call | flops 1000000000 | bytes 1 | tf_op jit(solution)/shard_map/home/pallas_call | solution.py:561
  (215 shorter events, 63.4 us)
Async XLA Ops:
  7.2 101.4 %all-gather.12.cloned.1.call-start = ((), (), s32[]{:S(2)}) async-start(), calls=%async_computation.3 | async-start | bytes 4325376 | tf_op jit(solution)/shard_map/all_gather | solution.py:957
  10.5 208.6 %all-gather.6.cloned.1.call-start = ((), (), s32[]{:S(2)}) async-start(), calls=%async_computation | async-start | bytes 2621440 | tf_op jit(solution)/shard_map/all_gather | solution.py:1044
  15.7 19.8 %collective-permute-start.3 = (bf16[128,512]{1,0:T(8,128)(2,1)S(1)}, bf16[128,512]{1,0:T(8,128)(2,1)S(1)}, u32[]{:S(2)}, u32[]{:S(2)}) collective-permute-start(bf16[128,512]{1,0:T(8,128)(2,1)S(1)} %get-tuple-element.187), channel_id=1, source_target_pairs={{0,4},{4,0},{8,12},{12,8},{1,5},{5,1},{9,13},{13,9},{2,6},{6,2},{1... | collective-permute-start | bytes 393224 | tf_op jit(solution)/shard_map/ppermute | solution.py:926
  15.7 19.8 %collective-permute-start.4 = (bf16[128,512]{1,0:T(8,128)(2,1)S(1)}, bf16[128,512]{1,0:T(8,128)(2,1)S(1)}, u32[]{:S(2)}, u32[]{:S(2)}) collective-permute-start(bf16[128,512]{1,0:T(8,128)(2,1)S(1)} %get-tuple-element.188), channel_id=1, source_target_pairs={{0,8},{4,12},{8,0},{12,4},{1,9},{5,13},{9,1},{13,5},{2,10},{6,14},... | collective-permute-start | bytes 393224 | tf_op jit(solution)/shard_map/ppermute | solution.py:926
  16.3 19.2 %collective-permute-start.5 = (bf16[128,512]{1,0:T(8,128)(2,1)S(1)}, bf16[128,512]{1,0:T(8,128)(2,1)S(1)}, u32[]{:S(2)}, u32[]{:S(2)}) collective-permute-start(bf16[128,512]{1,0:T(8,128)(2,1)S(1)} %get-tuple-element.189), channel_id=1, source_target_pairs={{0,12},{4,8},{8,4},{12,0},{1,13},{5,9},{9,5},{13,1},{2,14},{6,10},... | collective-permute-start | bytes 393224 | tf_op jit(solution)/shard_map/ppermute | solution.py:926
  20.1 15.4 %collective-permute-start.1 = (bf16[288,128]{1,0:T(8,128)(2,1)S(1)}, bf16[288,128]{1,0:T(8,128)(2,1)S(1)}, u32[]{:S(2)}, u32[]{:S(2)}) collective-permute-start(bf16[288,128]{1,0:T(8,128)(2,1)S(1)} %get-tuple-element.185.refs_1_), channel_id=1, source_target_pairs={{0,8},{4,12},{8,0},{12,4},{1,9},{5,13},{9,1},{13,5},{2,10},{6,14},... | collective-permute-start | bytes 221192 | tf_op jit(solution)/shard_map/ppermute | solution.py:926
  20.1 15.4 %collective-permute-start = (bf16[288,128]{1,0:T(8,128)(2,1)S(1)}, bf16[288,128]{1,0:T(8,128)(2,1)S(1)}, u32[]{:S(2)}, u32[]{:S(2)}) collective-permute-start(bf16[288,128]{1,0:T(8,128)(2,1)S(1)} %get-tuple-element.185.refs_1_), channel_id=1, source_target_pairs={{0,4},{4,0},{8,12},{12,8},{1,5},{5,1},{9,13},{13,9},{2,6},{6,2},{1... | collective-permute-start | bytes 221192 | tf_op jit(solution)/shard_map/ppermute | solution.py:926
  36.1 13.0 %collective-permute-start.8 = (bf16[1,1,4,160,128]{4,3,2,1,0:T(8,128)(2,1)S(1)}, bf16[1,1,4,160,128]{4,3,2,1,0:T(8,128)(2,1)S(1)}, u32[]{:S(2)}, u32[]{:S(2)}) collective-permute-start(bf16[1,1,4,160,128]{4,3,2,1,0:T(8,128)(2,1)S(1)} %get-tuple-element.192.refs_2_), channel_id=1, source_target_pairs={{0,2},{2,0},{1,3},{3,1},{4,6},{6,4},{5,7},{7,5},{8,10},{10,8},{9,1... | collective-permute-start | bytes 491528 | tf_op jit(solution)/shard_map/ppermute | solution.py:926
  60.6 20.9 %collective-permute-start.20 = (bf16[128,512]{1,0:T(8,128)(2,1)S(1)}, bf16[128,512]{1,0:T(8,128)(2,1)S(1)}, u32[]{:S(2)}, u32[]{:S(2)}) collective-permute-start(bf16[128,512]{1,0:T(8,128)(2,1)S(1)} %get-tuple-element.209), channel_id=1, source_target_pairs={{0,4},{4,0},{8,12},{12,8},{1,5},{5,1},{9,13},{13,9},{2,6},{6,2},{1... | collective-permute-start | bytes 393224 | tf_op jit(solution)/shard_map/ppermute | solution.py:926
  63.2 18.3 %collective-permute-start.21 = (bf16[128,512]{1,0:T(8,128)(2,1)S(1)}, bf16[128,512]{1,0:T(8,128)(2,1)S(1)}, u32[]{:S(2)}, u32[]{:S(2)}) collective-permute-start(bf16[128,512]{1,0:T(8,128)(2,1)S(1)} %get-tuple-element.210), channel_id=1, source_target_pairs={{0,8},{4,12},{8,0},{12,4},{1,9},{5,13},{9,1},{13,5},{2,10},{6,14},... | collective-permute-start | bytes 393224 | tf_op jit(solution)/shard_map/ppermute | solution.py:926
  64.3 17.8 %collective-permute-start.22 = (bf16[128,512]{1,0:T(8,128)(2,1)S(1)}, bf16[128,512]{1,0:T(8,128)(2,1)S(1)}, u32[]{:S(2)}, u32[]{:S(2)}) collective-permute-start(bf16[128,512]{1,0:T(8,128)(2,1)S(1)} %get-tuple-element.211), channel_id=1, source_target_pairs={{0,12},{4,8},{8,4},{12,0},{1,13},{5,9},{9,5},{13,1},{2,14},{6,10},... | collective-permute-start | bytes 393224 | tf_op jit(solution)/shard_map/ppermute | solution.py:926
  66.4 15.8 %collective-permute-start.18 = (bf16[1,2,4,128,128]{4,3,2,1,0:T(8,128)(2,1)S(1)}, bf16[1,2,4,128,128]{4,3,2,1,0:T(8,128)(2,1)S(1)}, u32[]{:S(2)}, u32[]{:S(2)}) collective-permute-start(bf16[1,2,4,128,128]{4,3,2,1,0:T(8,128)(2,1)S(1)} %get-tuple-element.206.refs_1_), channel_id=1, source_target_pairs={{0,2},{2,0},{1,3},{3,1},{4,6},{6,4},{5,7},{7,5},{8,10},{10,8},{9,1... | collective-permute-start | bytes 786440 | tf_op jit(solution)/shard_map/ppermute | solution.py:926
  67.9 14.3 %collective-permute-start.19 = (bf16[2,1,4,128,128]{4,3,2,1,0:T(8,128)(2,1)S(1)}, bf16[2,1,4,128,128]{4,3,2,1,0:T(8,128)(2,1)S(1)}, u32[]{:S(2)}, u32[]{:S(2)}) collective-permute-start(bf16[2,1,4,128,128]{4,3,2,1,0:T(8,128)(2,1)S(1)} %get-tuple-element.207.refs_3_), channel_id=1, source_target_pairs={{0,16},{16,0},{1,17},{17,1},{2,18},{18,2},{3,19},{19,3},{4,20},{20... | collective-permute-start | bytes 786440 | tf_op jit(solution)/shard_map/ppermute | solution.py:926
  84.3 24.2 %collective-permute-start.25 = (bf16[128,512]{1,0:T(8,128)(2,1)S(1)}, bf16[128,512]{1,0:T(8,128)(2,1)S(1)}, u32[]{:S(2)}, u32[]{:S(2)}) collective-permute-start(bf16[128,512]{1,0:T(8,128)(2,1)S(1)} %get-tuple-element.220), channel_id=1, source_target_pairs={{0,4},{4,0},{8,12},{12,8},{1,5},{5,1},{9,13},{13,9},{2,6},{6,2},{1... | collective-permute-start | bytes 393224 | tf_op jit(solution)/shard_map/ppermute | solution.py:926
  90.3 18.2 %collective-permute-start.26 = (bf16[128,512]{1,0:T(8,128)(2,1)S(1)}, bf16[128,512]{1,0:T(8,128)(2,1)S(1)}, u32[]{:S(2)}, u32[]{:S(2)}) collective-permute-start(bf16[128,512]{1,0:T(8,128)(2,1)S(1)} %get-tuple-element.221), channel_id=1, source_target_pairs={{0,8},{4,12},{8,0},{12,4},{1,9},{5,13},{9,1},{13,5},{2,10},{6,14},... | collective-permute-start | bytes 393224 | tf_op jit(solution)/shard_map/ppermute | solution.py:926
  90.3 18.2 %collective-permute-start.27 = (bf16[128,512]{1,0:T(8,128)(2,1)S(1)}, bf16[128,512]{1,0:T(8,128)(2,1)S(1)}, u32[]{:S(2)}, u32[]{:S(2)}) collective-permute-start(bf16[128,512]{1,0:T(8,128)(2,1)S(1)} %get-tuple-element.222), channel_id=1, source_target_pairs={{0,12},{4,8},{8,4},{12,0},{1,13},{5,9},{9,5},{13,1},{2,14},{6,10},... | collective-permute-start | bytes 393224 | tf_op jit(solution)/shard_map/ppermute | solution.py:926
  123.5 27.0 %collective-permute-start.28 = (bf16[128,512]{1,0:T(8,128)(2,1)S(1)}, bf16[128,512]{1,0:T(8,128)(2,1)S(1)}, u32[]{:S(2)}, u32[]{:S(2)}) collective-permute-start(bf16[128,512]{1,0:T(8,128)(2,1)S(1)} %get-tuple-element.226), channel_id=1, source_target_pairs={{0,4},{4,0},{8,12},{12,8},{1,5},{5,1},{9,13},{13,9},{2,6},{6,2},{1... | collective-permute-start | bytes 393224 | tf_op jit(solution)/shard_map/ppermute | solution.py:926
  124.7 35.8 %collective-permute-start.29 = (bf16[128,512]{1,0:T(8,128)(2,1)S(1)}, bf16[128,512]{1,0:T(8,128)(2,1)S(1)}, u32[]{:S(2)}, u32[]{:S(2)}) collective-permute-start(bf16[128,512]{1,0:T(8,128)(2,1)S(1)} %get-tuple-element.227), channel_id=1, source_target_pairs={{0,8},{4,12},{8,0},{12,4},{1,9},{5,13},{9,1},{13,5},{2,10},{6,14},... | collective-permute-start | bytes 393224 | tf_op jit(solution)/shard_map/ppermute | solution.py:926
  125.6 35.0 %collective-permute-start.30 = (bf16[128,512]{1,0:T(8,128)(2,1)S(1)}, bf16[128,512]{1,0:T(8,128)(2,1)S(1)}, u32[]{:S(2)}, u32[]{:S(2)}) collective-permute-start(bf16[128,512]{1,0:T(8,128)(2,1)S(1)} %get-tuple-element.228), channel_id=1, source_target_pairs={{0,12},{4,8},{8,4},{12,0},{1,13},{5,9},{9,5},{13,1},{2,14},{6,10},... | collective-permute-start | bytes 393224 | tf_op jit(solution)/shard_map/ppermute | solution.py:926
  128.6 20.8 %collective-permute-start.32 = (bf16[1,2,4,64,512]{4,3,2,1,0:T(8,128)(2,1)S(1)}, bf16[1,2,4,64,512]{4,3,2,1,0:T(8,128)(2,1)S(1)}, u32[]{:S(2)}, u32[]{:S(2)}) collective-permute-start(bf16[1,2,4,64,512]{4,3,2,1,0:T(8,128)(2,1)S(1)} %get-tuple-element.252), channel_id=1, source_target_pairs={{0,2},{2,0},{1,3},{3,1},{4,6},{6,4},{5,7},{7,5},{8,10},{10,8},{9,1... | collective-permute-start | bytes 1572872 | tf_op jit(solution)/shard_map/ppermute | solution.py:926
  130.1 19.3 %collective-permute-start.33 = (bf16[2,1,4,64,512]{4,3,2,1,0:T(8,128)(2,1)S(1)}, bf16[2,1,4,64,512]{4,3,2,1,0:T(8,128)(2,1)S(1)}, u32[]{:S(2)}, u32[]{:S(2)}) collective-permute-start(bf16[2,1,4,64,512]{4,3,2,1,0:T(8,128)(2,1)S(1)} %get-tuple-element.254), channel_id=1, source_target_pairs={{0,16},{16,0},{1,17},{17,1},{2,18},{18,2},{3,19},{19,3},{4,20},{20... | collective-permute-start | bytes 1572872 | tf_op jit(solution)/shard_map/ppermute | solution.py:926
  149.3 16.5 %collective-permute-start.34 = (bf16[2,4,512,128]{3,2,1,0:T(8,128)(2,1)}, bf16[2,4,512,128]{3,2,1,0:T(8,128)(2,1)}, u32[]{:S(2)}, u32[]{:S(2)}) collective-permute-start(bf16[2,4,512,128]{3,2,1,0:T(8,128)(2,1)} %get-tuple-element.261), channel_id=1, source_target_pairs={{0,1},{1,0},{2,3},{3,2},{4,5},{5,4},{6,7},{7,6},{8,9},{9,8},{10,11... | collective-permute-start | bytes 3145736 | tf_op jit(solution)/shard_map/ppermute | solution.py:926
  149.7 13.1 %collective-permute-start.35 = (bf16[1,1,4,64,512]{4,3,2,1,0:T(8,128)(2,1)S(1)}, bf16[1,1,4,64,512]{4,3,2,1,0:T(8,128)(2,1)S(1)}, u32[]{:S(2)}, u32[]{:S(2)}) collective-permute-start(bf16[1,1,4,64,512]{4,3,2,1,0:T(8,128)(2,1)S(1)} %get-tuple-element.263), channel_id=1, source_target_pairs={{0,16},{16,0},{1,17},{17,1},{2,18},{18,2},{3,19},{19,3},{4,20},{20... | collective-permute-start | bytes 786440 | tf_op jit(solution)/shard_map/ppermute | solution.py:926
  160.6 13.8 %collective-permute-start.42 = (bf16[2,2,4,128,128]{4,3,2,1,0:T(8,128)(2,1)S(1)}, bf16[2,2,4,128,128]{4,3,2,1,0:T(8,128)(2,1)S(1)}, u32[]{:S(2)}, u32[]{:S(2)}) collective-permute-start(bf16[2,2,4,128,128]{4,3,2,1,0:T(8,128)(2,1)S(1)} %get-tuple-element.286), channel_id=1, source_target_pairs={{0,1},{1,0},{2,3},{3,2},{4,5},{5,4},{6,7},{7,6},{8,9},{9,8},{10,11... | collective-permute-start | bytes 1572872 | tf_op jit(solution)/shard_map/ppermute | solution.py:926
  162.1 73.1 %all-gather.10.cloned.1.call-start = ((), (), s32[]{:S(2)}) async-start(), calls=%async_computation.2 | async-start | bytes 2621440 | tf_op jit(solution)/shard_map/all_gather | solution.py:1044
  162.2 22.8 %collective-permute-start.44 = (bf16[2,2,4,128,128]{4,3,2,1,0:T(8,128)(2,1)S(1)}, bf16[2,2,4,128,128]{4,3,2,1,0:T(8,128)(2,1)S(1)}, u32[]{:S(2)}, u32[]{:S(2)}) collective-permute-start(bf16[2,2,4,128,128]{4,3,2,1,0:T(8,128)(2,1)S(1)} %get-tuple-element.290), channel_id=1, source_target_pairs={{0,1},{1,0},{2,3},{3,2},{4,5},{5,4},{6,7},{7,6},{8,9},{9,8},{10,11... | collective-permute-start | bytes 1572872 | tf_op jit(solution)/shard_map/ppermute | solution.py:926
  169.9 16.1 %collective-permute-start.39 = (bf16[128,512]{1,0:T(8,128)(2,1)S(1)}, bf16[128,512]{1,0:T(8,128)(2,1)S(1)}, u32[]{:S(2)}, u32[]{:S(2)}) collective-permute-start(bf16[128,512]{1,0:T(8,128)(2,1)S(1)} %get-tuple-element.282), channel_id=1, source_target_pairs={{0,4},{4,0},{8,12},{12,8},{1,5},{5,1},{9,13},{13,9},{2,6},{6,2},{1... | collective-permute-start | bytes 393224 | tf_op jit(solution)/shard_map/ppermute | solution.py:926
  170.7 15.4 %collective-permute-start.40 = (bf16[128,512]{1,0:T(8,128)(2,1)S(1)}, bf16[128,512]{1,0:T(8,128)(2,1)S(1)}, u32[]{:S(2)}, u32[]{:S(2)}) collective-permute-start(bf16[128,512]{1,0:T(8,128)(2,1)S(1)} %get-tuple-element.283), channel_id=1, source_target_pairs={{0,8},{4,12},{8,0},{12,4},{1,9},{5,13},{9,1},{13,5},{2,10},{6,14},... | collective-permute-start | bytes 393224 | tf_op jit(solution)/shard_map/ppermute | solution.py:926
  171.9 14.2 %collective-permute-start.41 = (bf16[128,512]{1,0:T(8,128)(2,1)S(1)}, bf16[128,512]{1,0:T(8,128)(2,1)S(1)}, u32[]{:S(2)}, u32[]{:S(2)}) collective-permute-start(bf16[128,512]{1,0:T(8,128)(2,1)S(1)} %get-tuple-element.284), channel_id=1, source_target_pairs={{0,12},{4,8},{8,4},{12,0},{1,13},{5,9},{9,5},{13,1},{2,14},{6,10},... | collective-permute-start | bytes 393224 | tf_op jit(solution)/shard_map/ppermute | solution.py:926
  187.6 51.0 %all-gather.8.cloned.1.call-start = ((), (), s32[]{:S(2)}) async-start(), calls=%async_computation.1 | async-start | bytes 2621440 | tf_op jit(solution)/shard_map/all_gather | solution.py:1044
  187.9 14.9 %collective-permute-start.46 = (bf16[1,2,4,192,128]{4,3,2,1,0:T(8,128)(2,1)S(1)}, bf16[1,2,4,192,128]{4,3,2,1,0:T(8,128)(2,1)S(1)}, u32[]{:S(2)}, u32[]{:S(2)}) collective-permute-start(bf16[1,2,4,192,128]{4,3,2,1,0:T(8,128)(2,1)S(1)} %get-tuple-element.297), channel_id=1, source_target_pairs={{0,2},{2,0},{1,3},{3,1},{4,6},{6,4},{5,7},{7,5},{8,10},{10,8},{9,1... | collective-permute-start | bytes 1179656 | tf_op jit(solution)/shard_map/ppermute | solution.py:926
  189.4 13.4 %collective-permute-start.47 = (bf16[2,1,4,192,128]{4,3,2,1,0:T(8,128)(2,1)S(1)}, bf16[2,1,4,192,128]{4,3,2,1,0:T(8,128)(2,1)S(1)}, u32[]{:S(2)}, u32[]{:S(2)}) collective-permute-start(bf16[2,1,4,192,128]{4,3,2,1,0:T(8,128)(2,1)S(1)} %get-tuple-element.299), channel_id=1, source_target_pairs={{0,16},{16,0},{1,17},{17,1},{2,18},{18,2},{3,19},{19,3},{4,20},{20... | collective-permute-start | bytes 1179656 | tf_op jit(solution)/shard_map/ppermute | solution.py:926
  (73 other events, 470.4 us)
Sparse Core Ops, SparseCore 0:
  11.5 77.7 all-gather.11
  162.2 21.6 all-gather.5
  187.7 24.4 all-gather.9
  214.2 23.4 all-gather.7

commit v6 on v5

--- a/solution.py
+++ b/solution.py
@@ -1145,8 +1145,8 @@
     two, token = halve_more([two], rows_two, [token])
     out, token = home_last(out_every, BF, [token])
     g_in, g_out, token = finish(ffn, ((0, prows),) * 2, [], [token])
+    grad_memory, token = home_last(mem_every, F32, [token])
     sums, token = spread(one + two, [token])
-    grad_memory, token = home_last(mem_every, F32, [token])
     grad_inputs, token = home_last(in_every, F32, [token])
     gqc, gkc, gqs, goc, gvc, gos, gks, gvs, g_gains, g_shifts, g_bias, _ = finish(
         sums, ((0, prows),) * 8 + ((2, 16),),

time: 250 us -> 252 us (level)
    unnamed x76 -> x80, local copies, waits for them, and re-layouts: 4.9 us -> 5.57 us
  transfers between devices with their start and end apart: 67 -> 67, of which waited for: 11 -> 12; matrix products, arithmetic and copies ran while one was open for 0% -> 0% of each run, Pallas kernels for 39% -> 39%
where the time goes in v6:
time: 252 us; the launch traced here: 251 us
  Pallas kernels  116 us (46%)
  starting transfers between devices  76.6 us (30%)
  waiting for transfers between devices  38.7 us (15%)
  between operations  14.6 us (6%)
  local copies, waits for them, and re-layouts  5.65 us (2%)
    pallas_call x32, Pallas kernels, launch(): return call(*args) if ranks is None else call(ranks, *args)  116 us
    ppermute x63, starting transfers between devices, send(): lax.ppermute(array, axis, [(i, i ^ bit) for i in range(lax.axis_size(axis...  76.2 us
    ppermute x63, waiting for transfers between devices, send(): lax.ppermute(array, axis, [(i, i ^ bit) for i in range(lax.axis_size(axis...  36.2 us
    unnamed x80, local copies, waits for them, and re-layouts  5.57 us
  transfers between devices with their start and end apart: 67, of which 12 were waited for; matrix products, arithmetic and copies ran while one was open for 0% of the time, Pallas kernels for 39%

profile of v6, /device:TPU:0, one launch (start us, length us, event | category | flops | bytes accessed | tf_op | source)
XLA Modules:
  0.0 251.5 jit_solution(6799883579624066659)
XLA Ops:
  10.6 5.1 %collective-permute-start.2 = (bf16[288,128]{1,0:T(8,128)(2,1)S(1)}, bf16[288,128]{1,0:T(8,128)(2,1)S(1)}, u32[]{:S(2)}, u32[]{:S(2)}) collective-permute-start(bf16[288,128]{1,0:T(8,128)(2,1)S(1)} %get-tuple-element.185.refs_1_), channel_id=1, source_target_pairs={{0,12},{4,8},{8,4},{12,0},{1,13},{5,9},{9,5},{13,1},{2,14},{6,10},... | collective-permute-start | bytes 221192 | tf_op jit(solution)/shard_map/ppermute | solution.py:926
  16.3 3.7 %collective-permute-start.5 = (bf16[128,512]{1,0:T(8,128)(2,1)S(1)}, bf16[128,512]{1,0:T(8,128)(2,1)S(1)}, u32[]{:S(2)}, u32[]{:S(2)}) collective-permute-start(bf16[128,512]{1,0:T(8,128)(2,1)S(1)} %get-tuple-element.189), channel_id=1, source_target_pairs={{0,12},{4,8},{8,4},{12,0},{1,13},{5,9},{9,5},{13,1},{2,14},{6,10},... | collective-permute-start | bytes 393224 | tf_op jit(solution)/shard_map/ppermute | solution.py:926
  20.7 14.8 %collective-permute-done.1.refs_3_ = bf16[288,128]{1,0:T(8,128)(2,1)S(1)} collective-permute-done((bf16[288,128]{1,0:T(8,128)(2,1)S(1)}, bf16[288,128]{1,0:T(8,128)(2,1)S(1)}, u32[]{:S(2)}, u32[]{:S(2)}) %collective-permute-start.1) | collective-permute-done | bytes 73760 | tf_op jit(solution)/shard_map/ppermute | solution.py:926
  39.6 2.8 %collective-permute-start.11 = (bf16[256,128]{1,0:T(8,128)(2,1)S(1)}, bf16[256,128]{1,0:T(8,128)(2,1)S(1)}, u32[]{:S(2)}, u32[]{:S(2)}) collective-permute-start(bf16[256,128]{1,0:T(8,128)(2,1)S(1)} %get-tuple-element.193.refs_4_), channel_id=1, source_target_pairs={{0,12},{4,8},{8,4},{12,0},{1,13},{5,9},{9,5},{13,1},{2,14},{6,10},... | collective-permute-start | bytes 196616 | tf_op jit(solution)/shard_map/ppermute | solution.py:926
  45.8 3.2 %collective-permute-done.10.refs_6_ = bf16[256,128]{1,0:T(8,128)(2,1)S(1)} collective-permute-done((bf16[256,128]{1,0:T(8,128)(2,1)S(1)}, bf16[256,128]{1,0:T(8,128)(2,1)S(1)}, u32[]{:S(2)}, u32[]{:S(2)}) %collective-permute-start.10) | collective-permute-done | bytes 65568 | tf_op jit(solution)/shard_map/ppermute | solution.py:926
  55.3 3.2 %collective-permute-done.14.refs_1_ = bf16[1,1,4,128,128]{4,3,2,1,0:T(8,128)(2,1)S(1)} collective-permute-done((bf16[1,1,4,128,128]{4,3,2,1,0:T(8,128)(2,1)S(1)}, bf16[1,1,4,128,128]{4,3,2,1,0:T(8,128)(2,1)S(1)}, u32[]{:S(2)}, u32[]{:S(2)}) %collective-permute-start.14) | collective-permute-done | bytes 131104 | tf_op jit(solution)/shard_map/ppermute | solution.py:926
  60.6 2.6 %collective-permute-start.20 = (bf16[128,512]{1,0:T(8,128)(2,1)S(1)}, bf16[128,512]{1,0:T(8,128)(2,1)S(1)}, u32[]{:S(2)}, u32[]{:S(2)}) collective-permute-start(bf16[128,512]{1,0:T(8,128)(2,1)S(1)} %get-tuple-element.209), channel_id=1, source_target_pairs={{0,4},{4,0},{8,12},{12,8},{1,5},{5,1},{9,13},{13,9},{2,6},{6,2},{1... | collective-permute-start | bytes 393224 | tf_op jit(solution)/shard_map/ppermute | solution.py:926
  64.3 2.0 collective-permute-start.22
  68.9 12.6 %self_fwd.1 = (bf16[4,512,128]{2,1,0:T(8,128)(2,1)}, bf16[4,1024,128]{2,1,0:T(8,128)(2,1)}, bf16[4,1024,128]{2,1,0:T(8,128)(2,1)}, bf16[4,512,512]{2,1,0:T(8,128...) custom-call(s32[5]{0:T(128)S(1)} %stack.23.refs_0_, ...), custom_call_target="tpu_custom_call" | custom-call | flops 24000000000 | bytes 1 | tf_op jit(solution)/shard_map/self_fwd/pallas_call | solution.py:561
  84.4 6.0 %collective-permute-start.25 = (bf16[128,512]{1,0:T(8,128)(2,1)S(1)}, bf16[128,512]{1,0:T(8,128)(2,1)S(1)}, u32[]{:S(2)}, u32[]{:S(2)}) collective-permute-start(bf16[128,512]{1,0:T(8,128)(2,1)S(1)} %get-tuple-element.220), channel_id=1, source_target_pairs={{0,4},{4,0},{8,12},{12,8},{1,5},{5,1},{9,13},{13,9},{2,6},{6,2},{1... | collective-permute-start | bytes 393224 | tf_op jit(solution)/shard_map/ppermute | solution.py:926
  90.3 2.4 collective-permute-start.27
  93.7 14.8 %cross_fwd.1 = (bf16[4,512,128]{2,1,0:T(8,128)(2,1)}, bf16[4,1024,128]{2,1,0:T(8,128)(2,1)}, bf16[4,1024,128]{2,1,0:T(8,128)(2,1)}, bf16[4,1024,1024]{2,1,0:T(8,...) custom-call(s32[5]{0:T(128)S(1)} %stack.23.refs_0_, ...), custom_call_target="tpu_custom_call" | custom-call | flops 28000000000 | bytes 1 | tf_op jit(solution)/shard_map/cross_fwd/pallas_call | solution.py:561
  108.6 14.9 %ffn_both.1 = (bf16[128,512]{1,0:T(8,128)(2,1)S(1)}, bf16[128,512]{1,0:T(8,128)(2,1)S(1)}, bf16[128,512]{1,0:T(8,128)(2,1)S(1)}, bf16[128,512]{1,0:T(8,128)(2,1)...) custom-call(s32[5]{0:T(128)S(1)} %stack.23.refs_0_, ...), custom_call_target="tpu_custom_call" | custom-call | flops 24999999488 | bytes 1 | tf_op jit(solution)/shard_map/ffn_both/pallas_call | solution.py:561
  125.7 2.4 collective-permute-start.30
  131.3 17.5 %cross_bwd.1 = (bf16[2,2,4,128,128]{4,3,2,1,0:T(8,128)(2,1)S(1)}, bf16[2,2,4,128,128]{4,3,2,1,0:T(8,128)(2,1)S(1)}, bf16[2,4,512,128]{3,2,1,0:T(8,128)(2,1)}, bf...) custom-call(s32[5]{0:T(128)S(1)} %stack.23.refs_0_, ...), custom_call_target="tpu_custom_call" | custom-call | flops 30000001024 | bytes 1 | tf_op jit(solution)/shard_map/cross_bwd/pallas_call | solution.py:561
  151.1 9.4 %self_bwd.2 = (bf16[2,2,4,128,128]{4,3,2,1,0:T(8,128)(2,1)S(1)}, bf16[2,2,512,128]{3,2,1,0:T(8,128)(2,1)}, bf16[2,2,512,128]{3,2,1,0:T(8,128)(2,1)}, f32[512,512...) custom-call(s32[5]{0:T(128)S(1)} %stack.23.refs_0_, bf16[512,512]{1,0:T(8,128)(2,1)S(1)} %get-tuple-element.190.refs_1_, ...), custom_call_target="tpu_custom_call" | custom-call | flops 16000000000 | bytes 1 | tf_op jit(solution)/shard_map/self_bwd/pallas_call | solution.py:561
  165.9 4.1 %mem_back.1 = (bf16[128,512]{1,0:T(8,128)(2,1)S(1)}, bf16[128,512]{1,0:T(8,128)(2,1)S(1)}, bf16[128,512]{1,0:T(8,128)(2,1)S(1)}, bf16[128,512]{1,0:T(8,128)(2,1)...) custom-call(s32[5]{0:T(128)S(1)} %stack.23.refs_0_, ...), custom_call_target="tpu_custom_call" | custom-call | flops 8999999488 | bytes 1 | tf_op jit(solution)/shard_map/mem_back/pallas_call | solution.py:561
  171.9 2.6 %collective-permute-start.41 = (bf16[128,512]{1,0:T(8,128)(2,1)S(1)}, bf16[128,512]{1,0:T(8,128)(2,1)S(1)}, u32[]{:S(2)}, u32[]{:S(2)}) collective-permute-start(bf16[128,512]{1,0:T(8,128)(2,1)S(1)} %get-tuple-element.284), channel_id=1, source_target_pairs={{0,12},{4,8},{8,4},{12,0},{1,13},{5,9},{9,5},{13,1},{2,14},{6,10},... | collective-permute-start | bytes 393224 | tf_op jit(solution)/shard_map/ppermute | solution.py:926
  174.5 10.5 %self_bwd.3 = (bf16[2,2,4,128,128]{4,3,2,1,0:T(8,128)(2,1)S(1)}, bf16[2,2,512,128]{3,2,1,0:T(8,128)(2,1)}, bf16[2,2,512,128]{3,2,1,0:T(8,128)(2,1)}, f32[512,512...) custom-call(s32[5]{0:T(128)S(1)} %stack.23.refs_0_, bf16[512,512]{1,0:T(8,128)(2,1)S(1)} %get-tuple-element.190.refs_1_, ...), custom_call_target="tpu_custom_call" | custom-call | flops 16000000000 | bytes 1 | tf_op jit(solution)/shard_map/self_bwd/pallas_call | solution.py:561
  190.6 4.6 %in_back.1 = (bf16[128,512]{1,0:T(8,128)(2,1)S(1)}, bf16[128,512]{1,0:T(8,128)(2,1)S(1)}, bf16[128,512]{1,0:T(8,128)(2,1)S(1)}, bf16[128,512]{1,0:T(8,128)(2,1)S...) custom-call(s32[5]{0:T(128)S(1)} %stack.23.refs_0_, ...), custom_call_target="tpu_custom_call" | custom-call | flops 8999999488 | bytes 1 | tf_op jit(solution)/shard_map/in_back/pallas_call | solution.py:561
  195.3 1.9 collective-permute-start.51
  197.2 2.4 collective-permute-start.52
  199.7 3.2 %collective-permute-done.46.refs_1_ = bf16[1,2,4,192,128]{4,3,2,1,0:T(8,128)(2,1)S(1)} collective-permute-done((bf16[1,2,4,192,128]{4,3,2,1,0:T(8,128)(2,1)S(1)}, bf16[1,2,4,192,128]{4,3,2,1,0:T(8,128)(2,1)S(1)}, u32[]{:S(2)}, u32[]{:S(2)}) %collective-permute-start.46) | collective-permute-done | bytes 393248 | tf_op jit(solution)/shard_map/ppermute | solution.py:926
  205.0 3.2 %collective-permute-done.51.refs_3_ = bf16[128,512]{1,0:T(8,128)(2,1)S(1)} collective-permute-done((bf16[128,512]{1,0:T(8,128)(2,1)S(1)}, bf16[128,512]{1,0:T(8,128)(2,1)S(1)}, u32[]{:S(2)}, u32[]{:S(2)}) %collective-permute-start.51) | collective-permute-done | bytes 131104 | tf_op jit(solution)/shard_map/ppermute | solution.py:926
  211.0 2.3 collective-permute-start.57
  213.3 2.4 collective-permute-start.59
  219.7 2.7 %home.3 = (bf16[8,256,512]{2,1,0:T(8,128)(2,1)}, f32[8,128]{1,0:T(8,128)S(1)}) custom-call(bf16[4,4,128,512]{3,2,1,0:T(8,128)(2,1)} %all-gather.6.cloned.1.call-done.refs_0_, f32[8,128]{1,0:T(8,128)S(1)} %get-tuple-element.312.refs_1_), custom_call_target="tpu_custom_call" | custom-call | flops 1000000000 | bytes 1 | tf_op jit(solution)/shard_map/home/pallas_call | solution.py:561
  227.2 3.4 %home.4 = (f32[8,256,512]{2,1,0:T(8,128)}, f32[8,128]{1,0:T(8,128)S(1)}) custom-call(bf16[4,4,128,512]{3,2,1,0:T(8,128)(2,1)} %all-gather.10.cloned.1.call-done.refs_0_, f32[8,128]{1,0:T(8,128)S(1)} %get-tuple-element.329.refs_1_), custom_call_target="tpu_custom_call" | custom-call | flops 1000000000 | bytes 1 | tf_op jit(solution)/shard_map/home/pallas_call | solution.py:561
  233.3 2.0 collective-permute-start.62
  235.3 2.4 all-gather.8.cloned.1.call-done.refs_0_
  237.7 3.4 %home.5 = (f32[8,256,512]{2,1,0:T(8,128)}, f32[8,128]{1,0:T(8,128)S(1)}) custom-call(bf16[4,4,128,512]{3,2,1,0:T(8,128)(2,1)} %all-gather.8.cloned.1.call-done.refs_0_, f32[8,128]{1,0:T(8,128)S(1)} %get-tuple-element.331.refs_1_), custom_call_target="tpu_custom_call" | custom-call | flops 1000000000 | bytes 1 | tf_op jit(solution)/shard_map/home/pallas_call | solution.py:561
  241.1 2.6 %collective-permute-done.61.refs_3_ = bf16[528,128]{1,0:T(8,128)(2,1)S(1)} collective-permute-done((bf16[528,128]{1,0:T(8,128)(2,1)S(1)}, bf16[528,128]{1,0:T(8,128)(2,1)S(1)}, u32[]{:S(2)}, u32[]{:S(2)}) %collective-permute-start.61) | collective-permute-done | bytes 135200 | tf_op jit(solution)/shard_map/ppermute | solution.py:926
  (219 shorter events, 65.9 us)
Async XLA Ops:
  7.2 101.4 %all-gather.12.cloned.1.call-start = ((), (), s32[]{:S(2)}) async-start(), calls=%async_computation.3 | async-start | bytes 4325376 | tf_op jit(solution)/shard_map/all_gather | solution.py:957
  10.5 209.2 %all-gather.6.cloned.1.call-start = ((), (), s32[]{:S(2)}) async-start(), calls=%async_computation | async-start | bytes 2621440 | tf_op jit(solution)/shard_map/all_gather | solution.py:1044
  15.7 19.8 %collective-permute-start.3 = (bf16[128,512]{1,0:T(8,128)(2,1)S(1)}, bf16[128,512]{1,0:T(8,128)(2,1)S(1)}, u32[]{:S(2)}, u32[]{:S(2)}) collective-permute-start(bf16[128,512]{1,0:T(8,128)(2,1)S(1)} %get-tuple-element.187), channel_id=1, source_target_pairs={{0,4},{4,0},{8,12},{12,8},{1,5},{5,1},{9,13},{13,9},{2,6},{6,2},{1... | collective-permute-start | bytes 393224 | tf_op jit(solution)/shard_map/ppermute | solution.py:926
  15.7 19.8 %collective-permute-start.4 = (bf16[128,512]{1,0:T(8,128)(2,1)S(1)}, bf16[128,512]{1,0:T(8,128)(2,1)S(1)}, u32[]{:S(2)}, u32[]{:S(2)}) collective-permute-start(bf16[128,512]{1,0:T(8,128)(2,1)S(1)} %get-tuple-element.188), channel_id=1, source_target_pairs={{0,8},{4,12},{8,0},{12,4},{1,9},{5,13},{9,1},{13,5},{2,10},{6,14},... | collective-permute-start | bytes 393224 | tf_op jit(solution)/shard_map/ppermute | solution.py:926
  16.3 19.2 %collective-permute-start.5 = (bf16[128,512]{1,0:T(8,128)(2,1)S(1)}, bf16[128,512]{1,0:T(8,128)(2,1)S(1)}, u32[]{:S(2)}, u32[]{:S(2)}) collective-permute-start(bf16[128,512]{1,0:T(8,128)(2,1)S(1)} %get-tuple-element.189), channel_id=1, source_target_pairs={{0,12},{4,8},{8,4},{12,0},{1,13},{5,9},{9,5},{13,1},{2,14},{6,10},... | collective-permute-start | bytes 393224 | tf_op jit(solution)/shard_map/ppermute | solution.py:926
  20.1 15.4 %collective-permute-start.1 = (bf16[288,128]{1,0:T(8,128)(2,1)S(1)}, bf16[288,128]{1,0:T(8,128)(2,1)S(1)}, u32[]{:S(2)}, u32[]{:S(2)}) collective-permute-start(bf16[288,128]{1,0:T(8,128)(2,1)S(1)} %get-tuple-element.185.refs_1_), channel_id=1, source_target_pairs={{0,8},{4,12},{8,0},{12,4},{1,9},{5,13},{9,1},{13,5},{2,10},{6,14},... | collective-permute-start | bytes 221192 | tf_op jit(solution)/shard_map/ppermute | solution.py:926
  20.1 15.4 %collective-permute-start = (bf16[288,128]{1,0:T(8,128)(2,1)S(1)}, bf16[288,128]{1,0:T(8,128)(2,1)S(1)}, u32[]{:S(2)}, u32[]{:S(2)}) collective-permute-start(bf16[288,128]{1,0:T(8,128)(2,1)S(1)} %get-tuple-element.185.refs_1_), channel_id=1, source_target_pairs={{0,4},{4,0},{8,12},{12,8},{1,5},{5,1},{9,13},{13,9},{2,6},{6,2},{1... | collective-permute-start | bytes 221192 | tf_op jit(solution)/shard_map/ppermute | solution.py:926
  60.6 20.9 %collective-permute-start.20 = (bf16[128,512]{1,0:T(8,128)(2,1)S(1)}, bf16[128,512]{1,0:T(8,128)(2,1)S(1)}, u32[]{:S(2)}, u32[]{:S(2)}) collective-permute-start(bf16[128,512]{1,0:T(8,128)(2,1)S(1)} %get-tuple-element.209), channel_id=1, source_target_pairs={{0,4},{4,0},{8,12},{12,8},{1,5},{5,1},{9,13},{13,9},{2,6},{6,2},{1... | collective-permute-start | bytes 393224 | tf_op jit(solution)/shard_map/ppermute | solution.py:926
  63.2 18.3 %collective-permute-start.21 = (bf16[128,512]{1,0:T(8,128)(2,1)S(1)}, bf16[128,512]{1,0:T(8,128)(2,1)S(1)}, u32[]{:S(2)}, u32[]{:S(2)}) collective-permute-start(bf16[128,512]{1,0:T(8,128)(2,1)S(1)} %get-tuple-element.210), channel_id=1, source_target_pairs={{0,8},{4,12},{8,0},{12,4},{1,9},{5,13},{9,1},{13,5},{2,10},{6,14},... | collective-permute-start | bytes 393224 | tf_op jit(solution)/shard_map/ppermute | solution.py:926
  64.3 17.8 %collective-permute-start.22 = (bf16[128,512]{1,0:T(8,128)(2,1)S(1)}, bf16[128,512]{1,0:T(8,128)(2,1)S(1)}, u32[]{:S(2)}, u32[]{:S(2)}) collective-permute-start(bf16[128,512]{1,0:T(8,128)(2,1)S(1)} %get-tuple-element.211), channel_id=1, source_target_pairs={{0,12},{4,8},{8,4},{12,0},{1,13},{5,9},{9,5},{13,1},{2,14},{6,10},... | collective-permute-start | bytes 393224 | tf_op jit(solution)/shard_map/ppermute | solution.py:926
  66.4 15.8 %collective-permute-start.18 = (bf16[1,2,4,128,128]{4,3,2,1,0:T(8,128)(2,1)S(1)}, bf16[1,2,4,128,128]{4,3,2,1,0:T(8,128)(2,1)S(1)}, u32[]{:S(2)}, u32[]{:S(2)}) collective-permute-start(bf16[1,2,4,128,128]{4,3,2,1,0:T(8,128)(2,1)S(1)} %get-tuple-element.206.refs_1_), channel_id=1, source_target_pairs={{0,2},{2,0},{1,3},{3,1},{4,6},{6,4},{5,7},{7,5},{8,10},{10,8},{9,1... | collective-permute-start | bytes 786440 | tf_op jit(solution)/shard_map/ppermute | solution.py:926
  67.9 14.3 %collective-permute-start.19 = (bf16[2,1,4,128,128]{4,3,2,1,0:T(8,128)(2,1)S(1)}, bf16[2,1,4,128,128]{4,3,2,1,0:T(8,128)(2,1)S(1)}, u32[]{:S(2)}, u32[]{:S(2)}) collective-permute-start(bf16[2,1,4,128,128]{4,3,2,1,0:T(8,128)(2,1)S(1)} %get-tuple-element.207.refs_3_), channel_id=1, source_target_pairs={{0,16},{16,0},{1,17},{17,1},{2,18},{18,2},{3,19},{19,3},{4,20},{20... | collective-permute-start | bytes 786440 | tf_op jit(solution)/shard_map/ppermute | solution.py:926
  84.4 24.2 %collective-permute-start.25 = (bf16[128,512]{1,0:T(8,128)(2,1)S(1)}, bf16[128,512]{1,0:T(8,128)(2,1)S(1)}, u32[]{:S(2)}, u32[]{:S(2)}) collective-permute-start(bf16[128,512]{1,0:T(8,128)(2,1)S(1)} %get-tuple-element.220), channel_id=1, source_target_pairs={{0,4},{4,0},{8,12},{12,8},{1,5},{5,1},{9,13},{13,9},{2,6},{6,2},{1... | collective-permute-start | bytes 393224 | tf_op jit(solution)/shard_map/ppermute | solution.py:926
  90.3 18.2 %collective-permute-start.26 = (bf16[128,512]{1,0:T(8,128)(2,1)S(1)}, bf16[128,512]{1,0:T(8,128)(2,1)S(1)}, u32[]{:S(2)}, u32[]{:S(2)}) collective-permute-start(bf16[128,512]{1,0:T(8,128)(2,1)S(1)} %get-tuple-element.221), channel_id=1, source_target_pairs={{0,8},{4,12},{8,0},{12,4},{1,9},{5,13},{9,1},{13,5},{2,10},{6,14},... | collective-permute-start | bytes 393224 | tf_op jit(solution)/shard_map/ppermute | solution.py:926
  90.3 18.2 %collective-permute-start.27 = (bf16[128,512]{1,0:T(8,128)(2,1)S(1)}, bf16[128,512]{1,0:T(8,128)(2,1)S(1)}, u32[]{:S(2)}, u32[]{:S(2)}) collective-permute-start(bf16[128,512]{1,0:T(8,128)(2,1)S(1)} %get-tuple-element.222), channel_id=1, source_target_pairs={{0,12},{4,8},{8,4},{12,0},{1,13},{5,9},{9,5},{13,1},{2,14},{6,10},... | collective-permute-start | bytes 393224 | tf_op jit(solution)/shard_map/ppermute | solution.py:926
  123.6 27.0 %collective-permute-start.28 = (bf16[128,512]{1,0:T(8,128)(2,1)S(1)}, bf16[128,512]{1,0:T(8,128)(2,1)S(1)}, u32[]{:S(2)}, u32[]{:S(2)}) collective-permute-start(bf16[128,512]{1,0:T(8,128)(2,1)S(1)} %get-tuple-element.226), channel_id=1, source_target_pairs={{0,4},{4,0},{8,12},{12,8},{1,5},{5,1},{9,13},{13,9},{2,6},{6,2},{1... | collective-permute-start | bytes 393224 | tf_op jit(solution)/shard_map/ppermute | solution.py:926
  124.8 35.9 %collective-permute-start.29 = (bf16[128,512]{1,0:T(8,128)(2,1)S(1)}, bf16[128,512]{1,0:T(8,128)(2,1)S(1)}, u32[]{:S(2)}, u32[]{:S(2)}) collective-permute-start(bf16[128,512]{1,0:T(8,128)(2,1)S(1)} %get-tuple-element.227), channel_id=1, source_target_pairs={{0,8},{4,12},{8,0},{12,4},{1,9},{5,13},{9,1},{13,5},{2,10},{6,14},... | collective-permute-start | bytes 393224 | tf_op jit(solution)/shard_map/ppermute | solution.py:926
  125.7 35.0 %collective-permute-start.30 = (bf16[128,512]{1,0:T(8,128)(2,1)S(1)}, bf16[128,512]{1,0:T(8,128)(2,1)S(1)}, u32[]{:S(2)}, u32[]{:S(2)}) collective-permute-start(bf16[128,512]{1,0:T(8,128)(2,1)S(1)} %get-tuple-element.228), channel_id=1, source_target_pairs={{0,12},{4,8},{8,4},{12,0},{1,13},{5,9},{9,5},{13,1},{2,14},{6,10},... | collective-permute-start | bytes 393224 | tf_op jit(solution)/shard_map/ppermute | solution.py:926
  128.6 20.8 %collective-permute-start.32 = (bf16[1,2,4,64,512]{4,3,2,1,0:T(8,128)(2,1)S(1)}, bf16[1,2,4,64,512]{4,3,2,1,0:T(8,128)(2,1)S(1)}, u32[]{:S(2)}, u32[]{:S(2)}) collective-permute-start(bf16[1,2,4,64,512]{4,3,2,1,0:T(8,128)(2,1)S(1)} %get-tuple-element.252), channel_id=1, source_target_pairs={{0,2},{2,0},{1,3},{3,1},{4,6},{6,4},{5,7},{7,5},{8,10},{10,8},{9,1... | collective-permute-start | bytes 1572872 | tf_op jit(solution)/shard_map/ppermute | solution.py:926
  130.1 19.3 %collective-permute-start.33 = (bf16[2,1,4,64,512]{4,3,2,1,0:T(8,128)(2,1)S(1)}, bf16[2,1,4,64,512]{4,3,2,1,0:T(8,128)(2,1)S(1)}, u32[]{:S(2)}, u32[]{:S(2)}) collective-permute-start(bf16[2,1,4,64,512]{4,3,2,1,0:T(8,128)(2,1)S(1)} %get-tuple-element.254), channel_id=1, source_target_pairs={{0,16},{16,0},{1,17},{17,1},{2,18},{18,2},{3,19},{19,3},{4,20},{20... | collective-permute-start | bytes 1572872 | tf_op jit(solution)/shard_map/ppermute | solution.py:926
  149.3 16.6 %collective-permute-start.34 = (bf16[2,4,512,128]{3,2,1,0:T(8,128)(2,1)}, bf16[2,4,512,128]{3,2,1,0:T(8,128)(2,1)}, u32[]{:S(2)}, u32[]{:S(2)}) collective-permute-start(bf16[2,4,512,128]{3,2,1,0:T(8,128)(2,1)} %get-tuple-element.261), channel_id=1, source_target_pairs={{0,1},{1,0},{2,3},{3,2},{4,5},{5,4},{6,7},{7,6},{8,9},{9,8},{10,11... | collective-permute-start | bytes 3145736 | tf_op jit(solution)/shard_map/ppermute | solution.py:926
  160.6 13.8 %collective-permute-start.42 = (bf16[2,2,4,128,128]{4,3,2,1,0:T(8,128)(2,1)S(1)}, bf16[2,2,4,128,128]{4,3,2,1,0:T(8,128)(2,1)S(1)}, u32[]{:S(2)}, u32[]{:S(2)}) collective-permute-start(bf16[2,2,4,128,128]{4,3,2,1,0:T(8,128)(2,1)S(1)} %get-tuple-element.286), channel_id=1, source_target_pairs={{0,1},{1,0},{2,3},{3,2},{4,5},{5,4},{6,7},{7,6},{8,9},{9,8},{10,11... | collective-permute-start | bytes 1572872 | tf_op jit(solution)/shard_map/ppermute | solution.py:926
  162.2 65.1 %all-gather.10.cloned.1.call-start = ((), (), s32[]{:S(2)}) async-start(), calls=%async_computation.2 | async-start | bytes 2621440 | tf_op jit(solution)/shard_map/all_gather | solution.py:1044
  162.2 22.8 %collective-permute-start.44 = (bf16[2,2,4,128,128]{4,3,2,1,0:T(8,128)(2,1)S(1)}, bf16[2,2,4,128,128]{4,3,2,1,0:T(8,128)(2,1)S(1)}, u32[]{:S(2)}, u32[]{:S(2)}) collective-permute-start(bf16[2,2,4,128,128]{4,3,2,1,0:T(8,128)(2,1)S(1)} %get-tuple-element.290), channel_id=1, source_target_pairs={{0,1},{1,0},{2,3},{3,2},{4,5},{5,4},{6,7},{7,6},{8,9},{9,8},{10,11... | collective-permute-start | bytes 1572872 | tf_op jit(solution)/shard_map/ppermute | solution.py:926
  170.0 16.1 %collective-permute-start.39 = (bf16[128,512]{1,0:T(8,128)(2,1)S(1)}, bf16[128,512]{1,0:T(8,128)(2,1)S(1)}, u32[]{:S(2)}, u32[]{:S(2)}) collective-permute-start(bf16[128,512]{1,0:T(8,128)(2,1)S(1)} %get-tuple-element.282), channel_id=1, source_target_pairs={{0,4},{4,0},{8,12},{12,8},{1,5},{5,1},{9,13},{13,9},{2,6},{6,2},{1... | collective-permute-start | bytes 393224 | tf_op jit(solution)/shard_map/ppermute | solution.py:926
  170.7 15.4 %collective-permute-start.40 = (bf16[128,512]{1,0:T(8,128)(2,1)S(1)}, bf16[128,512]{1,0:T(8,128)(2,1)S(1)}, u32[]{:S(2)}, u32[]{:S(2)}) collective-permute-start(bf16[128,512]{1,0:T(8,128)(2,1)S(1)} %get-tuple-element.283), channel_id=1, source_target_pairs={{0,8},{4,12},{8,0},{12,4},{1,9},{5,13},{9,1},{13,5},{2,10},{6,14},... | collective-permute-start | bytes 393224 | tf_op jit(solution)/shard_map/ppermute | solution.py:926
  171.9 14.2 %collective-permute-start.41 = (bf16[128,512]{1,0:T(8,128)(2,1)S(1)}, bf16[128,512]{1,0:T(8,128)(2,1)S(1)}, u32[]{:S(2)}, u32[]{:S(2)}) collective-permute-start(bf16[128,512]{1,0:T(8,128)(2,1)S(1)} %get-tuple-element.284), channel_id=1, source_target_pairs={{0,12},{4,8},{8,4},{12,0},{1,13},{5,9},{9,5},{13,1},{2,14},{6,10},... | collective-permute-start | bytes 393224 | tf_op jit(solution)/shard_map/ppermute | solution.py:926
  187.6 50.1 %all-gather.8.cloned.1.call-start = ((), (), s32[]{:S(2)}) async-start(), calls=%async_computation.1 | async-start | bytes 2621440 | tf_op jit(solution)/shard_map/all_gather | solution.py:1044
  187.9 14.9 %collective-permute-start.46 = (bf16[1,2,4,192,128]{4,3,2,1,0:T(8,128)(2,1)S(1)}, bf16[1,2,4,192,128]{4,3,2,1,0:T(8,128)(2,1)S(1)}, u32[]{:S(2)}, u32[]{:S(2)}) collective-permute-start(bf16[1,2,4,192,128]{4,3,2,1,0:T(8,128)(2,1)S(1)} %get-tuple-element.297), channel_id=1, source_target_pairs={{0,2},{2,0},{1,3},{3,1},{4,6},{6,4},{5,7},{7,5},{8,10},{10,8},{9,1... | collective-permute-start | bytes 1179656 | tf_op jit(solution)/shard_map/ppermute | solution.py:926
  189.4 13.4 %collective-permute-start.47 = (bf16[2,1,4,192,128]{4,3,2,1,0:T(8,128)(2,1)S(1)}, bf16[2,1,4,192,128]{4,3,2,1,0:T(8,128)(2,1)S(1)}, u32[]{:S(2)}, u32[]{:S(2)}) collective-permute-start(bf16[2,1,4,192,128]{4,3,2,1,0:T(8,128)(2,1)S(1)} %get-tuple-element.299), channel_id=1, source_target_pairs={{0,16},{16,0},{1,17},{17,1},{2,18},{18,2},{3,19},{19,3},{4,20},{20... | collective-permute-start | bytes 1179656 | tf_op jit(solution)/shard_map/ppermute | solution.py:926
  215.7 15.0 %collective-permute-start.53 = (bf16[1,1,4,192,128]{4,3,2,1,0:T(8,128)(2,1)S(1)}, bf16[1,1,4,192,128]{4,3,2,1,0:T(8,128)(2,1)S(1)}, u32[]{:S(2)}, u32[]{:S(2)}) collective-permute-start(bf16[1,1,4,192,128]{4,3,2,1,0:T(8,128)(2,1)S(1)} %get-tuple-element.316), channel_id=1, source_target_pairs={{0,16},{16,0},{1,17},{17,1},{2,18},{18,2},{3,19},{19,3},{4,20},{20... | collective-permute-start | bytes 589832 | tf_op jit(solution)/shard_map/ppermute | solution.py:926
  217.2 13.5 %collective-permute-start.54 = (bf16[1,1,4,192,128]{4,3,2,1,0:T(8,128)(2,1)S(1)}, bf16[1,1,4,192,128]{4,3,2,1,0:T(8,128)(2,1)S(1)}, u32[]{:S(2)}, u32[]{:S(2)}) collective-permute-start(bf16[1,1,4,192,128]{4,3,2,1,0:T(8,128)(2,1)S(1)} %get-tuple-element.318), channel_id=1, source_target_pairs={{0,2},{2,0},{1,3},{3,1},{4,6},{6,4},{5,7},{7,5},{8,10},{10,8},{9,1... | collective-permute-start | bytes 589832 | tf_op jit(solution)/shard_map/ppermute | solution.py:926
  (75 other events, 478.3 us)
Sparse Core Ops, SparseCore 0:
  11.5 77.7 all-gather.11
  162.3 21.6 all-gather.5
  187.7 24.4 all-gather.9
  214.2 23.4 all-gather.7
